TPU v7x, 32 devices: a whole 2x2x4 slice. The times are simulated.
32 devices in a mesh: groups: 2 (over y), tiles: 4 (over z), rhs: 2 (over x), sub: 2 (over core).
Axes of the slice: x: 2, y: 2, z: 4, core: 2. Of those that a mesh axis runs over, the one named last changes fastest.
Arguments:
- sources: bfloat16 [256, 8192], P('rhs', ('groups', 'tiles', 'sub')), parts along dimension 1, may hold values from -6 to 6
- basis_out: bfloat16 [384, 64, 512], P(('groups', 'tiles', 'rhs', 'sub')), parts along dimension 0, may hold values from -0.15625 to 0.15625
- basis_in: bfloat16 [384, 64, 512], P(('groups', 'tiles', 'rhs', 'sub')), parts along dimension 0, may hold values from -0.25 to 0.25
- tile_rank: int32 [384], P(('groups', 'tiles', 'rhs', 'sub')), parts along dimension 0, may hold values from 1 to 64, as said below
- tile_row: int32 [384], P(('groups', 'tiles', 'rhs', 'sub')), parts along dimension 0, may hold values from 0 to 7
- tile_col: int32 [384], P(('groups', 'tiles', 'rhs', 'sub')), parts along dimension 0, may hold values from 0 to 7
- near_blocks: bfloat16 [16, 16, 512, 512], P(('groups', 'tiles', 'sub')), parts along dimension 0, may hold values from -0.0625 to 0.0625
- near_col: int32 [16, 16], P(('groups', 'tiles', 'sub')), parts along dimension 0, may hold values from 0 to 7
- jacobi_inverse: bfloat16 [64, 128, 128], P(('groups', 'tiles', 'sub')), parts along dimension 0
Outputs:
- first_result: bfloat16 [256, 8192], P('rhs', ('groups', 'tiles', 'sub')), parts along dimension 1
- second_result: bfloat16 [256, 8192], P('rhs', ('groups', 'tiles', 'sub')), parts along dimension 1
There are 2 independent parts, one for each index of `groups`. A program takes and returns all parts, laid end to end along the dimension named above; each array names one. Nothing has to cross between parts.
Inputs may be any that keep to these rules, and one draw needn't show every extreme that they name: `tile_rank`: every rank lies in 1 to 64, and some tile has rank 64.
All inputs are finite; a program needn't handle non-finite values.
Results may differ from a plain program's by a relative error of at most 0.03.
Values may be sent and summed in bfloat16 or wider, within the bound.
No kernel may reach another device: no remote copies, remote signals or barrier semaphores. Data moves between devices by JAX's collectives and lax.ppermute only.
A program may use at most 128 MiB of HBM per device.

v0:
```python
import jax
import jax.numpy as jnp
from jax import lax
from jax.sharding import PartitionSpec as P

BLK = 512
RMAX = 64
JB = 128


def tile_terms(running, pieces, gathered):
    basis_out, basis_in, tile_rank, tile_row, tile_col = pieces
    picked = jnp.take(gathered, tile_col, axis=1)
    coefficients = jnp.einsum("ctq,trq->ctr", picked, basis_in, preferred_element_type=jnp.float32)
    rank_iota = lax.broadcasted_iota(jnp.int32, (1, tile_rank.shape[0], RMAX), 2)
    kept_mask = rank_iota < tile_rank[None, :, None]
    coefficients = jnp.where(kept_mask, coefficients, jnp.zeros_like(coefficients)).astype(
        jnp.bfloat16
    )
    contrib = jnp.einsum(
        "ctr,trp->ctp", coefficients, basis_out, preferred_element_type=jnp.float32
    )
    upper = contrib.astype(jnp.bfloat16)
    lower = (contrib - upper.astype(jnp.float32)).astype(jnp.bfloat16)
    block_iota = lax.broadcasted_iota(jnp.int32, (1, running.shape[1]), 1)
    onehot = (tile_row[:, None] == block_iota).astype(jnp.bfloat16)
    placed_upper = jnp.einsum("ctp,tb->cbp", upper, onehot, preferred_element_type=jnp.float32)
    placed_lower = jnp.einsum("ctp,tb->cbp", lower, onehot, preferred_element_type=jnp.float32)
    return placed_upper + placed_lower


def apply_operator(vector, tile_apply, near_blocks, near_col):
    columns = vector.shape[0]
    gathered = lax.all_gather(vector, ("tiles", "sub"), axis=1, tiled=True).reshape(
        columns, -1, BLK
    )
    zero_sums = jnp.zeros(gathered.shape, jnp.float32)
    far_field = tile_apply(zero_sums, gathered).reshape(columns, -1)
    far_field = lax.psum_scatter(
        far_field.astype(jnp.bfloat16), ("tiles", "sub"), scatter_dimension=1, tiled=True
    ).astype(jnp.float32)
    picked = jnp.take(gathered, near_col, axis=1)
    near_field = jnp.einsum(
        "cikq,ikpq->cip", picked, near_blocks, preferred_element_type=jnp.float32
    )
    return (far_field + near_field.reshape(columns, -1)).astype(jnp.bfloat16)


def precondition(field, jacobi_inverse):
    columns = field.shape[0]
    grouped = field.reshape(columns, -1, JB)
    result = jnp.einsum("cgq,gpq->cgp", grouped, jacobi_inverse, preferred_element_type=jnp.float32)
    return result.astype(jnp.bfloat16).reshape(columns, -1)


def local(
    sources,
    basis_out,
    basis_in,
    tile_rank,
    tile_row,
    tile_col,
    near_blocks,
    near_col,
    jacobi_inverse,
):

    def tile_apply(running, gathered):
        return tile_terms(
            running,
            (
                lax.all_gather(basis_out, "rhs", axis=0, tiled=True),
                lax.all_gather(basis_in, "rhs", axis=0, tiled=True),
                lax.all_gather(tile_rank, "rhs", axis=0, tiled=True),
                lax.all_gather(tile_row, "rhs", axis=0, tiled=True),
                lax.all_gather(tile_col, "rhs", axis=0, tiled=True),
            ),
            gathered,
        )

    first_result = precondition(
        apply_operator(sources, tile_apply, near_blocks, near_col), jacobi_inverse
    )
    second_result = precondition(
        apply_operator(first_result, tile_apply, near_blocks, near_col), jacobi_inverse
    )
    return (first_result, second_result)


def solution(mesh):
    return jax.shard_map(
        local,
        mesh=mesh,
        in_specs=(
            P("rhs", ("groups", "tiles", "sub")),
            P(("groups", "tiles", "rhs", "sub"), None, None),
            P(("groups", "tiles", "rhs", "sub"), None, None),
            P(("groups", "tiles", "rhs", "sub")),
            P(("groups", "tiles", "rhs", "sub")),
            P(("groups", "tiles", "rhs", "sub")),
            P(("groups", "tiles", "sub"), None, None, None),
            P(("groups", "tiles", "sub"), None),
            P(("groups", "tiles", "sub"), None, None),
        ),
        out_specs=(P("rhs", ("groups", "tiles", "sub")), P("rhs", ("groups", "tiles", "sub"))),
        check_vma=False,
    )
```

profile of v0, /device:TPU:0, one launch (start us, length us, event | category | flops | bytes accessed | tf_op | source)
XLA Modules:
  0.0 233.3 jit_solution(618950563438700425)
XLA Ops:
  7.2 0.0 copy-start
  7.2 0.0 all-gather.5.cloned.1.call-start
  7.2 1.7 copy.40
  8.9 0.0 all-gather.5.cloned.1.call-update
  8.9 0.0 all-gather.7.cloned.1.call-start
  9.0 0.7 all-gather.7.cloned.1.call-update
  9.7 0.0 all-gather.9.cloned.1.call-start
  9.7 0.7 all-gather.9.cloned.1.call-update
  10.4 0.0 reduce-scatter.3.cloned.1.call-start
  10.5 1.2 dynamic-slice
  12.4 0.9 dynamic-update-slice
  13.2 0.8 dynamic-update-slice.1
  14.1 0.8 dynamic-update-slice.2
  14.9 5.2 %all-reduce.3 = (s32[24]{0:T(128)S(1)}, s32[24]{0:T(128)S(1)}, s32[24]{0:T(128)S(1)}) all-reduce(s32[24]{0:T(128)S(1)} %dynamic-update-slice.2, s32[24]{0:T(128)S(1)} %dynamic-update-slice.1, s32[24]{0:T(128)S(1)} %dynamic-update-slice), channel_id=1, replica_groups=mesh['groups'=2,'tiles'=4,'rhs'=2,'sub'=2] {'rhs'}, use_global_device_ids=true, to_apply=%add.2 | all-reduce | flops 72 | bytes 576
  20.1 0.1 iota_compare_fusion
  20.2 14.8 %all-gather.5.cloned.1.call-done = bf16[128,4096]{0,1:T(8,128)(2,1)} async-done(((bf16[128,512]{0,1:T(8,128)(2,1)}), bf16[128,4096]{0,1:T(8,128)(2,1)}) %all-gather.5.cloned.1.call-update) | async-done | bytes 1048592 | tf_op jit(solution)/shard_map/all_gather | solution.py:34
  35.0 1.5 copy.41
  36.5 2.5 %gather_fusion = bf16[24,128,512]{2,1,0:T(8,128)(2,1)} fusion(bf16[128,8,512]{2,0,1:T(8,128)(2,1)S(1)} %copy.41, s32[1024]{0:T(1024)S(1)} %pad_clamp_fusion.1), kind=kCustom, calls=%fused_computation.clone | custom fusion | bytes 6291552 | tf_op jit(solution)/shard_map/jit(_take)/gather | solution.py:13
  39.0 24.4 %all-gather.7.cloned.1.call-done = bf16[24,64,512]{2,1,0:T(8,128)(2,1)} async-done(((bf16[12,64,512]{2,1,0:T(8,128)(2,1)}), bf16[24,64,512]{2,1,0:T(8,128)(2,1)}) %all-gather.7.cloned.1.call-update) | async-done | bytes 1572880 | tf_op jit(solution)/shard_map/all_gather | solution.py:73
  63.4 28.8 %all-gather.9.cloned.1.call-done = bf16[24,64,512]{2,1,0:T(8,128)(2,1)} async-done(((bf16[12,64,512]{2,1,0:T(8,128)(2,1)}), bf16[24,64,512]{2,1,0:T(8,128)(2,1)}) %all-gather.9.cloned.1.call-update) | async-done | bytes 1572880 | tf_op jit(solution)/shard_map/all_gather | solution.py:72
  92.2 7.7 %fusion.5 = (bf16[128,24,512]{2,0,1:T(8,128)(2,1)}, bf16[128,24,512]{2,0,1:T(8,128)(2,1)}) fusion(bf16[24,64,512]{2,1,0:T(8,128)(2,1)} %all-gather.9.cloned.1.call-done, bf16[24,64,512]{2,1,0:T(8,128)(2,1)} %all-gather.7.cloned.1.call-done, bf16[24,128,512]{2,1,0:T(8,128)(2,1)} %gather_fusion, pred[24]{0:T(512)(128)(4,1)S(1)} %compare_and_fusion, ...), kind=kOutput, calls=%fused_computation.13 | convolution fusion | flops 410910720 | bytes 12584472 | tf_op jit(solution)/shard_map/ctr,trp->ctp/dot_general | solution.py:20
  100.0 4.3 %fusion.14 = f32[8,128,512]{2,0,1:T(8,128)S(1)} fusion(bf16[128,24,512]{2,0,1:T(8,128)(2,1)} %get-tuple-element.17, s32[24]{0:T(128)S(1)} %get-tuple-element.14), kind=kOutput, calls=%fused_computation.22 | convolution fusion | flops 25166016 | bytes 5242976 | tf_op jit(solution)/shard_map/ctp,tb->cbp/dot_general | solution.py:28
  104.2 0.0 copy-done.2
  104.2 2.3 add_convert_fusion.1
  106.5 1.4 copy.56
  107.9 0.0 reduce-scatter.3.cloned.1.call-update
  107.9 0.0 all-gather.11.cloned.1.call-start
  108.0 0.0 copy-done.4
  108.0 0.7 gather_fusion.1
  108.7 31.8 %reduce-scatter.3.cloned.1.call-done = bf16[128,512]{1,0:T(8,128)(2,1)} async-done(((bf16[128,4096]{1,0:T(8,128)(2,1)}), bf16[128,512]{1,0:T(8,128)(2,1)}) %reduce-scatter.3.cloned.1.call-update) | async-done | bytes 131088 | tf_op jit(solution)/shard_map/reduce_scatter | solution.py:39
  140.6 6.2 %fusion.93 = bf16[16,4,8,128]{3,2,1,0:T(8,128)(2,1)S(1)} fusion(bf16[1,16,512,512]{3,2,1,0:T(8,128)(2,1)} %param.19, bf16[16,128,512]{2,1,0:T(8,128)(2,1)S(1)} %gather_fusion.1, pred[16]{0:T(512)(128)(4,1)S(1)} %and_bitcast_fusion, bf16[128,512]{1,0:T(8,128)(2,1)} %reduce-scatter.3.cloned.1.call-done), kind=kOutput, calls=%fused_computation.57 | convolution fusion | flops 1074987008 | bytes 10747920 | tf_op jit(solution)/shard_map/cikq,ikpq->cip/dot_general | solution.py:43
  146.8 0.9 convolution_convert_fusion.1
  147.7 0.0 all-gather.11.cloned.1.call-update
  147.7 0.2 reduce-scatter.5.cloned.1.call-start
  147.9 20.2 %all-gather.11.cloned.1.call-done = bf16[128,4096]{0,1:T(8,128)(2,1)} async-done(((bf16[128,512]{0,1:T(8,128)(2,1)}), bf16[128,4096]{0,1:T(8,128)(2,1)}) %all-gather.11.cloned.1.call-update) | async-done | bytes 1048592 | tf_op jit(solution)/shard_map/all_gather | solution.py:34
  168.1 3.9 %gather_fusion.2 = bf16[24,128,512]{1,2,0:T(8,128)(2,1)} fusion(bf16[128,8,512]{0,2,1:T(8,128)(2,1)} %bitcast.182, s32[1024]{0:T(1024)S(1)} %pad_clamp_fusion.1), kind=kCustom, calls=%fused_computation.2.clone | custom fusion | bytes 6291552 | tf_op jit(solution)/shard_map/jit(_take)/gather | solution.py:13
  172.0 6.7 %fusion.4 = (bf16[128,24,512]{2,0,1:T(8,128)(2,1)}, bf16[128,24,512]{2,0,1:T(8,128)(2,1)S(1)}) fusion(bf16[24,64,512]{2,1,0:T(8,128)(2,1)} %all-gather.9.cloned.1.call-done, bf16[24,64,512]{2,1,0:T(8,128)(2,1)} %all-gather.7.cloned.1.call-done, bf16[24,128,512]{1,2,0:T(8,128)(2,1)} %gather_fusion.2, pred[24]{0:T(512)(128)(4,1)S(1)} %compare_and_fusion, ...), kind=kOutput, calls=%fused_computation.10 | convolution fusion | flops 410910720 | bytes 12584472 | tf_op jit(solution)/shard_map/ctr,trp->ctp/dot_general | solution.py:20
  178.7 4.1 %fusion.10 = f32[8,128,512]{2,0,1:T(8,128)S(1)} fusion(bf16[128,24,512]{2,0,1:T(8,128)(2,1)} %get-tuple-element.15, s32[24]{0:T(128)S(1)} %get-tuple-element.14), kind=kOutput, calls=%fused_computation.18 | convolution fusion | flops 25166016 | bytes 5242976 | tf_op jit(solution)/shard_map/ctp,tb->cbp/dot_general | solution.py:28
  182.8 2.3 add_convert_fusion
  185.2 1.4 copy.57
  186.5 0.0 reduce-scatter.5.cloned.1.call-update
  186.5 0.8 copy.51
  187.3 0.5 copy.49
  187.8 2.0 gather_fusion.3
  189.9 28.8 %reduce-scatter.5.cloned.1.call-done = bf16[128,512]{1,0:T(8,128)(2,1)} async-done(((bf16[128,4096]{1,0:T(8,128)(2,1)}), bf16[128,512]{1,0:T(8,128)(2,1)}) %reduce-scatter.5.cloned.1.call-update) | async-done | bytes 131088 | tf_op jit(solution)/shard_map/reduce_scatter | solution.py:39
  218.7 6.8 %fusion.88 = bf16[16,4,8,128]{3,2,1,0:T(8,128)(2,1)S(1)} fusion(bf16[1,16,512,512]{3,2,1,0:T(8,128)(2,1)} %param.19, bf16[16,128,512]{2,1,0:T(8,128)(2,1)} %gather_fusion.3, pred[16]{0:T(512)(128)(4,1)S(1)} %and_bitcast_fusion, bf16[128,512]{1,0:T(8,128)(2,1)} %reduce-scatter.5.cloned.1.call-done), kind=kOutput, calls=%fused_computation.56 | convolution fusion | flops 1074987008 | bytes 10747920 | tf_op jit(solution)/shard_map/cikq,ikpq->cip/dot_general | solution.py:43
  225.5 0.2 convolution_convert_fusion
  225.7 0.8 copy.52
  (16 shorter events, 0.1 us)
Async XLA Ops:
  7.2 139.6 %copy-start = (bf16[4,128,128]{2,1,0:T(8,128)(2,1)S(1)}, bf16[4,128,128]{2,1,0:T(8,128)(2,1)}, u32[]{:S(2)}) copy-start(bf16[4,128,128]{2,1,0:T(8,128)(2,1)} %param.21) | copy-start | bytes 393220
  7.2 27.8 %all-gather.5.cloned.1.call-start = ((), (), s32[]{:S(2)}) async-start(), calls=%async_computation.2 | async-start | bytes 1179648 | tf_op jit(solution)/shard_map/all_gather | solution.py:34
  8.9 54.5 %all-gather.7.cloned.1.call-start = ((), (), s32[]{:S(2)}) async-start(), calls=%async_computation.3 | async-start | bytes 2359296 | tf_op jit(solution)/shard_map/all_gather | solution.py:73
  9.7 82.5 %all-gather.9.cloned.1.call-start = ((), (), s32[]{:S(2)}) async-start(), calls=%async_computation.4 | async-start | bytes 2359296 | tf_op jit(solution)/shard_map/all_gather | solution.py:72
  10.4 130.1 %reduce-scatter.3.cloned.1.call-start = ((), (), s32[]{:S(2)}) async-start(), calls=%async_computation.5 | async-start | bytes 1179648 | tf_op jit(solution)/shard_map/reduce_scatter | solution.py:39
  100.0 4.3 %copy-start.2 = (bf16[128,24,512]{2,0,1:T(8,128)(2,1)S(1)}, bf16[128,24,512]{2,0,1:T(8,128)(2,1)}, u32[]{:S(2)}) copy-start(bf16[128,24,512]{2,0,1:T(8,128)(2,1)} %get-tuple-element.18) | copy-start | bytes 9437188
  106.5 1.5 copy-start.4
  107.9 60.2 %all-gather.11.cloned.1.call-start = ((), (), s32[]{:S(2)}) async-start(), calls=%async_computation.6 | async-start | bytes 1179648 | tf_op jit(solution)/shard_map/all_gather | solution.py:34
  147.7 71.0 %reduce-scatter.5.cloned.1.call-start = ((), (), s32[]{:S(2)}) async-start(), calls=%async_computation.7 | async-start | bytes 1179648 | tf_op jit(solution)/shard_map/reduce_scatter | solution.py:39
  185.1 1.4 copy-start.3
  185.1 2.2 copy-start.1
Sparse Core Ops, SparseCore 0:
  10.2 24.7 all-gather.4
  36.6 26.8 all-gather.6
  65.0 27.1 all-gather.8
  108.0 32.4 reduce-scatter.2
  147.8 20.2 all-gather.10
  186.7 31.9 reduce-scatter.4
where the time goes:
time: 234 us; the launch traced here: 233 us
  waiting for transfers between devices  150 us (64%)
  matrix products  41.5 us (18%)
  local copies, waits for them, and re-layouts  20.9 us (9%)
  between operations  14.9 us (6%)
  blocking collectives  5.19 us (2%)
    reduce_scatter x2, waiting for transfers between devices, apply_operator(): lax.psum_scatter(far_field.astype(jnp.bfloat16), ('tiles', 'sub'), scatte...  60.7 us
    all_gather x2, waiting for transfers between devices, apply_operator(): lax.all_gather(vector, ('tiles', 'sub'), axis=1, tiled=True)  35 us
    all_gather x1, waiting for transfers between devices, tile_apply(): lax.all_gather(basis_out, 'rhs', axis=0, tiled=True)  28.8 us
    all_gather x1, waiting for transfers between devices, tile_apply(): lax.all_gather(basis_in, 'rhs', axis=0, tiled=True)  24.4 us
    dot_general x2, matrix products, tile_terms(): jnp.einsum('ctr,trp->ctp', coefficients, basis_out, preferred_element_typ...  14.4 us
    dot_general x2, matrix products, apply_operator(): jnp.einsum('cikq,ikpq->cip', picked, near_blocks, preferred_element_type=...  13 us
    unnamed x22, local copies, waits for them, and re-layouts  9.77 us
    dot_general x2, matrix products, tile_terms(): jnp.einsum('ctp,tb->cbp', lower, onehot, preferred_element_type=jnp.float32)  8.39 us
  transfers between devices with their start and end apart: 6, of which 6 were waited for; matrix products, arithmetic and copies ran while one was open for 5% of the time, Pallas kernels for 0%

commit v1 on v0

v1 whole, which is shorter than its diff:
```python
import functools

import jax
import jax.numpy as jnp
from jax import lax
from jax.experimental import pallas as pl
from jax.experimental.pallas import tpu as pltpu
from jax.sharding import PartitionSpec as P

BLK = 512
RMAX = 64
JB = 128
NCHUNK = 256
BF16 = jnp.bfloat16
F32 = jnp.float32
VMEM_LIMIT = 48 * 1024 * 1024
CONTRACT_LAST = (((1,), (1,)), ((), ()))


def shifted(value, axis, size, amount):
    return lax.ppermute(value, axis, [(i, (i + amount) % size) for i in range(size)])


def fetch(pieces, stacked, sems):
    rows = pieces[0].shape[0]
    copies = [
        pltpu.make_async_copy(piece, stacked.at[pl.ds(i * rows, rows)], sems.at[i])
        for i, piece in enumerate(pieces)
    ]
    for copy in copies:
        copy.start()
    for copy in copies:
        copy.wait()


def far_kernel(n_pieces, n_parts, n_keep, col_ref, row_ref, *refs):
    pieces = refs[:n_pieces]
    ins = refs[n_pieces : n_pieces + n_parts]
    outs = refs[n_pieces + n_parts : n_pieces + 2 * n_parts]
    keep_ref, send_ref, stacked, coeff, masked, sems = refs[n_pieces + 2 * n_parts :]
    rows = pieces[0].shape[0]
    width = ins[0].shape[0]
    fetch(pieces, stacked, sems)
    for part in range(n_parts):
        for chunk in range(width // NCHUNK):
            here = pl.ds(chunk * NCHUNK, NCHUNK)
            there = pl.ds(part * width + chunk * NCHUNK, NCHUNK)
            products = lax.dot_general(
                stacked[...], ins[part][here, :], CONTRACT_LAST, preferred_element_type=F32
            )
            column = col_ref[:, there]
            chosen = products[:rows]
            for piece in range(1, n_pieces):
                chosen = jnp.where(
                    column == piece, products[piece * rows : (piece + 1) * rows], chosen
                )
            coeff[:, there] = chosen
    for target in range(n_pieces):
        for chunk in range(n_parts * width // NCHUNK):
            there = pl.ds(chunk * NCHUNK, NCHUNK)
            masked[pl.ds(target * rows, rows), there] = jnp.where(
                row_ref[:, there] == target, coeff[:, there], 0.0
            ).astype(BF16)
    total = jnp.dot(masked[:, :width], outs[0][...], preferred_element_type=F32)
    for part in range(1, n_parts):
        total += jnp.dot(
            masked[:, part * width : (part + 1) * width],
            outs[part][...],
            preferred_element_type=F32,
        )
    total = total.astype(BF16)
    keep_ref[...] = total[: n_keep * rows]
    send_ref[...] = total[n_keep * rows :]


def far_field(pieces, ins, outs, columns, rows_of, n_keep):
    rows = pieces[0].shape[0]
    n_pieces, n_parts, width = len(pieces), len(ins), ins[0].shape[0]
    whole = pl.BlockSpec(memory_space=pltpu.VMEM)
    anywhere = pl.BlockSpec(memory_space=pl.ANY)
    flops = 4 * n_pieces * rows * n_parts * width * BLK
    return pl.pallas_call(
        functools.partial(far_kernel, n_pieces, n_parts, n_keep),
        out_shape=(
            jax.ShapeDtypeStruct((n_keep * rows, BLK), BF16),
            jax.ShapeDtypeStruct(((n_pieces - n_keep) * rows, BLK), BF16),
        ),
        in_specs=[whole, whole] + [anywhere] * n_pieces + [whole] * (2 * n_parts),
        out_specs=(whole, whole),
        scratch_shapes=[
            pltpu.VMEM((n_pieces * rows, BLK), BF16),
            pltpu.VMEM((rows, n_parts * width), F32),
            pltpu.VMEM((n_pieces * rows, n_parts * width), BF16),
            pltpu.SemaphoreType.DMA((n_pieces,)),
        ],
        compiler_params=pltpu.CompilerParams(vmem_limit_bytes=VMEM_LIMIT),
        cost_estimate=pl.CostEstimate(
            flops=flops,
            transcendentals=0,
            bytes_accessed=2 * BLK * (2 * n_pieces * rows + 2 * n_parts * width),
        ),
        name="far_field",
    )(columns, rows_of, *pieces, *ins, *outs)


def near_kernel(n_pieces, per_step, slot_ref, *refs):
    pieces = refs[:n_pieces]
    blocks_ref, out_ref, stacked, sems = refs[n_pieces:]
    rows = pieces[0].shape[0]
    step = pl.program_id(0)

    @pl.when(step == 0)
    def _():
        fetch(pieces, stacked, sems)
        out_ref[...] = jnp.zeros_like(out_ref)

    total = out_ref[...]
    for k in range(per_step):
        start = pl.multiple_of(slot_ref[step * per_step + k] * rows, rows)
        total += lax.dot_general(
            stacked[pl.ds(start, rows), :],
            blocks_ref[k],
            CONTRACT_LAST,
            preferred_element_type=F32,
        )
    out_ref[...] = total


def near_field(pieces, near_blocks, slots):
    rows = pieces[0].shape[0]
    n_pieces, near = len(pieces), near_blocks.shape[0]
    per_step = 4 if near % 4 == 0 else 1
    anywhere = pl.BlockSpec(memory_space=pl.ANY)
    return pl.pallas_call(
        functools.partial(near_kernel, n_pieces, per_step),
        out_shape=jax.ShapeDtypeStruct((rows, BLK), F32),
        grid_spec=pltpu.PrefetchScalarGridSpec(
            num_scalar_prefetch=1,
            grid=(near // per_step,),
            in_specs=[anywhere] * n_pieces
            + [pl.BlockSpec((per_step, BLK, BLK), lambda step, slot: (step, 0, 0))],
            out_specs=pl.BlockSpec((rows, BLK), lambda step, slot: (0, 0)),
            scratch_shapes=[
                pltpu.VMEM((n_pieces * rows, BLK), BF16),
                pltpu.SemaphoreType.DMA((n_pieces,)),
            ],
        ),
        compiler_params=pltpu.CompilerParams(vmem_limit_bytes=VMEM_LIMIT),
        cost_estimate=pl.CostEstimate(
            flops=2 * near * rows * BLK * BLK,
            transcendentals=0,
            bytes_accessed=2 * BLK * (near * BLK + n_pieces * rows + 2 * rows),
        ),
        name="near_field",
    )(slots, *pieces, near_blocks)


def finish_kernel(n_sums, *refs):
    sums, (near_ref, jacobi_ref, out_ref) = refs[:n_sums], refs[n_sums:]
    total = near_ref[...]
    for part in sums:
        total += part[...].astype(F32)
    field = total.astype(BF16)
    for group in range(jacobi_ref.shape[0]):
        here = slice(group * JB, (group + 1) * JB)
        out_ref[:, here] = lax.dot_general(
            field[:, here], jacobi_ref[group], CONTRACT_LAST, preferred_element_type=F32
        ).astype(BF16)


def finish(sums, near, jacobi_inverse):
    whole = pl.BlockSpec(memory_space=pltpu.VMEM)
    return pl.pallas_call(
        functools.partial(finish_kernel, len(sums)),
        out_shape=jax.ShapeDtypeStruct(near.shape, BF16),
        in_specs=[whole] * (len(sums) + 2),
        out_specs=whole,
        name="finish",
    )(*sums, near, jacobi_inverse)


def local(
    n_tiles,
    n_rhs,
    n_sub,
    sources,
    basis_out,
    basis_in,
    tile_rank,
    tile_row,
    tile_col,
    near_blocks,
    near_col,
    jacobi_inverse,
):
    z = lax.axis_index("tiles")
    s = lax.axis_index("sub")
    rows = sources.shape[0]
    basis_in = basis_in.reshape(-1, BLK)
    basis_out = basis_out.reshape(-1, BLK)

    def source_slot(block):
        return (s - block % n_sub) % n_sub * n_tiles + (z - block // n_sub) % n_tiles

    def target_slot(block):
        return (block % n_sub - s) % n_sub * n_tiles + (block // n_sub - z) % n_tiles

    def gather(field):
        along = [field] + [shifted(field, "tiles", n_tiles, d) for d in range(1, n_tiles)]
        pieces = list(along)
        for e in range(1, n_sub):
            pieces += [shifted(piece, "sub", n_sub, e) for piece in along]
        return pieces

    pieces = gather(sources)
    numbers = jnp.stack([tile_rank, tile_row, tile_col])
    ins, outs, tables = [basis_in], [basis_out], [numbers]
    for d in range(1, n_rhs):
        tables.append(shifted(numbers, "rhs", n_rhs, d))
        ins.append(shifted(basis_in, "rhs", n_rhs, d))
        outs.append(shifted(basis_out, "rhs", n_rhs, d))
    ranks, block_rows, block_cols = jnp.concatenate(tables, axis=1)
    kept = lax.broadcasted_iota(jnp.int32, (ranks.shape[0], RMAX), 1) < ranks[:, None]
    rows_of = jnp.where(kept, target_slot(block_rows)[:, None], -1).reshape(1, -1)
    columns = jnp.broadcast_to(source_slot(block_cols)[:, None], kept.shape).reshape(1, -1)
    near_slots = source_slot(near_col[0])
    near_blocks = near_blocks[0]

    def apply_once(pieces):
        keep, send = far_field(pieces, ins, outs, columns, rows_of, n_tiles)
        total = keep.astype(F32)
        for e in range(1, n_sub):
            size = n_tiles * rows
            total += shifted(send[(e - 1) * size : e * size], "sub", n_sub, e).astype(F32)
        sums = []
        for d in range(n_tiles):
            part = total[d * rows : (d + 1) * rows].astype(BF16)
            sums.append(shifted(part, "tiles", n_tiles, d) if d else part)
        near = near_field(pieces, near_blocks, near_slots)
        return finish(sums, near, jacobi_inverse)

    first_result = apply_once(pieces)
    second_result = apply_once(gather(first_result))
    return (first_result, second_result)


def solution(mesh):
    sizes = mesh.shape
    return jax.shard_map(
        functools.partial(local, sizes["tiles"], sizes["rhs"], sizes["sub"]),
        mesh=mesh,
        in_specs=(
            P("rhs", ("groups", "tiles", "sub")),
            P(("groups", "tiles", "rhs", "sub"), None, None),
            P(("groups", "tiles", "rhs", "sub"), None, None),
            P(("groups", "tiles", "rhs", "sub")),
            P(("groups", "tiles", "rhs", "sub")),
            P(("groups", "tiles", "rhs", "sub")),
            P(("groups", "tiles", "sub"), None, None, None),
            P(("groups", "tiles", "sub"), None),
            P(("groups", "tiles", "sub"), None, None),
        ),
        out_specs=(P("rhs", ("groups", "tiles", "sub")), P("rhs", ("groups", "tiles", "sub"))),
        check_vma=False,
    )
```

time: 234 us -> 124 us (0.53)
  waiting for transfers between devices: 150 us -> 58.6 us
  matrix products: 41.5 us -> 0 us
  Pallas kernels: 0 us -> 29.4 us
  starting transfers between devices: 0.42 us -> 21.6 us
  between operations: 14.9 us -> 0.77 us
  local copies, waits for them, and re-layouts: 20.9 us -> 11.2 us
  blocking collectives: 5.19 us -> 0 us
    all_gather x4 -> x0, waiting for transfers between devices: 88.2 us -> none  [the longest x2 35 us: apply_operator(): lax.all_gather(vector, ('tiles', 'sub'), axis=1, tiled=True)]
    reduce_scatter x2 -> x0, waiting for transfers between devices: 60.7 us -> none  [apply_operator(): lax.psum_scatter(far_field.astype(jnp.bfloat16), ('tiles', 'sub'), scatte...]
    ppermute x0 -> x25, waiting for transfers between devices: none -> 58.6 us  [shifted(): lax.ppermute(value, axis, [(i, (i + amount) % size) for i in range(size)])]
    dot_general x10 -> x0, matrix products: 41.5 us -> none  [the longest x2 14.4 us: tile_terms(): jnp.einsum('ctr,trp->ctp', coefficients, basis_out, preferred_element_typ...]
    pallas_call x0 -> x6, Pallas kernels: none -> 29.4 us  [the longest x2 15.5 us: near_field(): pl.pallas_call(functools.partial(near_kernel, n_pieces, per_step), out_sh...]
    ppermute x0 -> x25, starting transfers between devices: none -> 21.6 us  [shifted(): lax.ppermute(value, axis, [(i, (i + amount) % size) for i in range(size)])]
    gather x4 -> x0, local copies, waits for them, and re-layouts: 9.13 us -> none  [the longest x2 6.43 us: tile_terms(): picked = jnp.take(gathered, tile_col, axis=1)]
    unnamed x1 -> x0, blocking collectives: 5.19 us -> none
  transfers between devices with their start and end apart: 6 -> 25, of which waited for: 6 -> 12; matrix products, arithmetic and copies ran while one was open for 5% -> 1% of each run, Pallas kernels for 0% -> 13%
where the time goes in v1:
time: 124 us; the launch traced here: 123 us
  waiting for transfers between devices  58.6 us (47%)
  Pallas kernels  29.4 us (24%)
  starting transfers between devices  21.6 us (17%)
  local copies, waits for them, and re-layouts  11.2 us (9%)
  other arithmetic  1.84 us (1%)
    ppermute x25, waiting for transfers between devices, shifted(): lax.ppermute(value, axis, [(i, (i + amount) % size) for i in range(size)])  58.6 us
    ppermute x25, starting transfers between devices, shifted(): lax.ppermute(value, axis, [(i, (i + amount) % size) for i in range(size)])  21.6 us
    pallas_call x2, Pallas kernels, near_field(): pl.pallas_call(functools.partial(near_kernel, n_pieces, per_step), out_sh...  15.5 us
    pallas_call x2, Pallas kernels, far_field(): pl.pallas_call(functools.partial(far_kernel, n_pieces, n_parts, n_keep),...  9.72 us
    unnamed x34, local copies, waits for them, and re-layouts  9.54 us
    pallas_call x2, Pallas kernels, finish(): pl.pallas_call(functools.partial(finish_kernel, len(sums)), out_shape=jax...  4.21 us
  transfers between devices with their start and end apart: 25, of which 12 were waited for; matrix products, arithmetic and copies ran while one was open for 1% of the time, Pallas kernels for 13%

profile of v1, /device:TPU:0, one launch (start us, length us, event | category | flops | bytes accessed | tf_op | source)
XLA Modules:
  0.0 123.4 jit_solution(3358662079683790917)
XLA Ops:
  0.6 0.5 collective-permute-start.4
  1.2 4.7 %collective-permute-start.3 = (bf16[128,512]{1,0:T(8,128)(2,1)}, bf16[128,512]{1,0:T(8,128)(2,1)S(1)}, u32[]{:S(2)}, u32[]{:S(2)}) collective-permute-start(bf16[128,512]{1,0:T(8,128)(2,1)} %refs_0_.3), channel_id=1, source_target_pairs={{0,12},{4,0},{8,4},{12,8},{1,13},{5,1},{9,5},{13,9},{2,14},{6,2},{... | collective-permute-start | bytes 393224 | tf_op jit(solution)/shard_map/ppermute | solution.py:21
  5.8 1.5 %collective-permute-start.9 = (bf16[768,512]{1,0:T(8,128)(2,1)}, bf16[768,512]{1,0:T(8,128)(2,1)S(1)}, u32[]{:S(2)}, u32[]{:S(2)}) collective-permute-start(bf16[768,512]{1,0:T(8,128)(2,1)} %bitcast.50), channel_id=1, source_target_pairs={{0,2},{2,0},{1,3},{3,1},{4,6},{6,4},{5,7},{7,5},{8,10},{10,8},{9,1... | collective-permute-start | bytes 2359304 | tf_op jit(solution)/shard_map/ppermute | solution.py:21
  7.3 0.5 collective-permute-start.8
  7.8 0.7 pad_add_fusion
  8.5 1.5 %collective-permute-start = (s32[3,12]{1,0:T(4,128)S(1)}, s32[3,12]{1,0:T(4,128)S(1)}, u32[]{:S(2)}, u32[]{:S(2)}) collective-permute-start(s32[3,12]{1,0:T(4,128)S(1)} %pad_add_fusion), channel_id=1, source_target_pairs={{0,2},{2,0},{1,3},{3,1},{4,6},{6,4},{5,7},{7,5},{8,10},{10,8},{9,1... | collective-permute-start | bytes 440 | tf_op jit(solution)/shard_map/ppermute | solution.py:21
  10.1 32.5 %collective-permute-done = s32[3,12]{1,0:T(4,128)S(1)} collective-permute-done((s32[3,12]{1,0:T(4,128)S(1)}, s32[3,12]{1,0:T(4,128)S(1)}, u32[]{:S(2)}, u32[]{:S(2)}) %collective-permute-start) | collective-permute-done | bytes 176 | tf_op jit(solution)/shard_map/ppermute | solution.py:21
  42.5 0.8 pad_add_fusion.1
  43.3 1.1 collective-permute-start.1
  44.4 7.5 %collective-permute-done.2.refs_2_ = bf16[128,512]{1,0:T(8,128)(2,1)S(1)} collective-permute-done((bf16[128,512]{1,0:T(8,128)(2,1)}, bf16[128,512]{1,0:T(8,128)(2,1)S(1)}, u32[]{:S(2)}, u32[]{:S(2)}) %collective-permute-start.2) | collective-permute-done | bytes 131104 | tf_op jit(solution)/shard_map/ppermute | solution.py:21
  51.9 0.5 collective-permute-start.5
  52.8 0.5 collective-permute-done.6.refs_6_
  53.5 0.9 copy-done.3
  54.4 1.1 copy-done.4
  55.5 1.1 copy-done.6
  56.6 4.9 %far_field.2 = (bf16[512,512]{1,0:T(8,128)(2,1)S(1)}, bf16[512,512]{1,0:T(8,128)(2,1)S(1)}) custom-call(s32[1,1536]{1,0:T(1,128)S(1)} %reshape.199.col_ref, s32[1,1536]{1,0:T(1,128)S(1)} %select_n.109.row_ref, bf16[128,512]{1,0:T(8,128)(2,1)S(1)} %copy-done.3, bf16[128,512]{1,0:T(8,128)(2,1)S(1)} %collective-permute-done.1.refs_1_, ...), custom_call_target="tpu_custom_call" | custom-call | flops 3221225472 | bytes 5242880 | tf_op jit(solution)/shard_map/far_field/pallas_call | solution.py:82
  61.5 0.9 copy-done.8
  62.4 0.3 collective-permute-start.10
  62.7 1.6 %collective-permute-done.10 = bf16[512,512]{1,0:T(8,128)(2,1)S(1)} collective-permute-done((bf16[512,512]{1,0:T(8,128)(2,1)S(1)}, bf16[512,512]{1,0:T(8,128)(2,1)S(1)}, u32[]{:S(2)}, u32[]{:S(2)}) %collective-permute-start.10) | collective-permute-done | bytes 524320 | tf_op jit(solution)/shard_map/ppermute | solution.py:21
  64.5 0.7 fusion.17
  65.2 0.6 collective-permute-start.13
  65.8 0.8 collective-permute-start.12
  66.6 2.0 %collective-permute-start.11 = (bf16[128,512]{1,0:T(8,128)(2,1)S(1)}, bf16[128,512]{1,0:T(8,128)(2,1)S(1)}, u32[]{:S(2)}, u32[]{:S(2)}) collective-permute-start(bf16[128,512]{1,0:T(8,128)(2,1)S(1)} %get-tuple-element.16), channel_id=1, source_target_pairs={{0,4},{4,8},{8,12},{12,0},{1,5},{5,9},{9,13},{13,1},{2,6},{6,10},{... | collective-permute-start | bytes 393224 | tf_op jit(solution)/shard_map/ppermute | solution.py:21
  68.6 7.8 %near_field.2.refs_4_ = f32[128,512]{1,0:T(8,128)S(1)} custom-call(s32[16]{0:T(128)S(1)} %fusion.3.slot_ref, bf16[128,512]{1,0:T(8,128)(2,1)S(1)} %copy-done.3, bf16[128,512]{1,0:T(8,128)(2,1)S(1)} %collective-permute-done.1.refs_1_, bf16[128,512]{1,0:T(8,128)(2,1)S(1)} %collective-permute-done.2.refs_2_, ...), custom_call_target="tpu_custom_call" | custom-call | flops 1073741824 | bytes 9699328 | tf_op jit(solution)/shard_map/near_field/pallas_call | solution.py:134
  76.4 0.7 copy-done.1
  77.1 1.7 %collective-permute-done.12.refs_2_ = bf16[128,512]{1,0:T(8,128)(2,1)S(1)} collective-permute-done((bf16[128,512]{1,0:T(8,128)(2,1)S(1)}, bf16[128,512]{1,0:T(8,128)(2,1)S(1)}, u32[]{:S(2)}, u32[]{:S(2)}) %collective-permute-start.12) | collective-permute-done | bytes 131104 | tf_op jit(solution)/shard_map/ppermute | solution.py:21
  78.8 0.7 copy-done.12
  79.5 0.6 copy-done.14
  80.1 2.1 %finish.2.refs_0_ = bf16[128,512]{1,0:T(8,128)(2,1)} custom-call(bf16[128,512]{1,0:T(8,128)(2,1)} %get-tuple-element.17.refs_0_, bf16[128,512]{1,0:T(8,128)(2,1)} %copy-done.14, bf16[128,512]{1,0:T(8,128)(2,1)} %copy-done.12, bf16[128,512]{1,0:T(8,128)(2,1)} %copy-done.10, f32[128,512]{1,0:T(8,128)} %copy-done.1, bf16[4,128,128]{2,1,0:T(8,128)(2,1)} %refs_5_.3), custom_call_target="tpu_custom_call" | custom-call | tf_op jit(solution)/shard_map/finish/pallas_call | solution.py:173
  82.4 1.2 collective-permute-start.15
  83.6 2.0 %collective-permute-start.14 = (bf16[128,512]{1,0:T(8,128)(2,1)}, bf16[128,512]{1,0:T(8,128)(2,1)S(1)}, u32[]{:S(2)}, u32[]{:S(2)}) collective-permute-start(bf16[128,512]{1,0:T(8,128)(2,1)} %finish.2.refs_0_), channel_id=1, source_target_pairs={{0,4},{4,8},{8,12},{12,0},{1,5},{5,9},{9,13},{13,1},{2,6},{6,10},{... | collective-permute-start | bytes 393224 | tf_op jit(solution)/shard_map/ppermute | solution.py:21
  85.6 2.4 %collective-permute-done.16.refs_3_ = bf16[128,512]{1,0:T(8,128)(2,1)S(1)} collective-permute-done((bf16[128,512]{1,0:T(8,128)(2,1)}, bf16[128,512]{1,0:T(8,128)(2,1)S(1)}, u32[]{:S(2)}, u32[]{:S(2)}) %collective-permute-start.16) | collective-permute-done | bytes 131104 | tf_op jit(solution)/shard_map/ppermute | solution.py:21
  88.0 7.9 %collective-permute-done.15.refs_2_ = bf16[128,512]{1,0:T(8,128)(2,1)S(1)} collective-permute-done((bf16[128,512]{1,0:T(8,128)(2,1)}, bf16[128,512]{1,0:T(8,128)(2,1)S(1)}, u32[]{:S(2)}, u32[]{:S(2)}) %collective-permute-start.15) | collective-permute-done | bytes 131104 | tf_op jit(solution)/shard_map/ppermute | solution.py:21
  95.9 0.5 collective-permute-start.18
  96.4 0.8 collective-permute-done.19.refs_6_
  97.4 0.9 copy-done.2
  98.3 1.1 copy-done.9
  99.5 4.9 %far_field.3 = (bf16[512,512]{1,0:T(8,128)(2,1)S(1)}, bf16[512,512]{1,0:T(8,128)(2,1)S(1)}) custom-call(s32[1,1536]{1,0:T(1,128)S(1)} %reshape.199.col_ref, s32[1,1536]{1,0:T(1,128)S(1)} %select_n.109.row_ref, bf16[128,512]{1,0:T(8,128)(2,1)S(1)} %copy-done.2, bf16[128,512]{1,0:T(8,128)(2,1)S(1)} %collective-permute-done.14.refs_1_, ...), custom_call_target="tpu_custom_call" | custom-call | flops 3221225472 | bytes 5242880 | tf_op jit(solution)/shard_map/far_field/pallas_call | solution.py:82
  104.3 0.4 collective-permute-start.21
  104.7 1.6 %collective-permute-done.21 = bf16[512,512]{1,0:T(8,128)(2,1)S(1)} collective-permute-done((bf16[512,512]{1,0:T(8,128)(2,1)S(1)}, bf16[512,512]{1,0:T(8,128)(2,1)S(1)}, u32[]{:S(2)}, u32[]{:S(2)}) %collective-permute-start.21) | collective-permute-done | bytes 524320 | tf_op jit(solution)/shard_map/ppermute | solution.py:21
  106.4 0.7 fusion.16
  107.1 1.2 collective-permute-start.23
  108.3 2.0 %collective-permute-start.22 = (bf16[128,512]{1,0:T(8,128)(2,1)S(1)}, bf16[128,512]{1,0:T(8,128)(2,1)S(1)}, u32[]{:S(2)}, u32[]{:S(2)}) collective-permute-start(bf16[128,512]{1,0:T(8,128)(2,1)S(1)} %get-tuple-element.12), channel_id=1, source_target_pairs={{0,4},{4,8},{8,12},{12,0},{1,5},{5,9},{9,13},{13,1},{2,6},{6,10},{... | collective-permute-start | bytes 393224 | tf_op jit(solution)/shard_map/ppermute | solution.py:21
  110.4 7.7 %near_field.3.refs_4_ = f32[128,512]{1,0:T(8,128)S(1)} custom-call(s32[16]{0:T(128)S(1)} %fusion.3.slot_ref, bf16[128,512]{1,0:T(8,128)(2,1)S(1)} %copy-done.2, bf16[128,512]{1,0:T(8,128)(2,1)S(1)} %collective-permute-done.14.refs_1_, bf16[128,512]{1,0:T(8,128)(2,1)S(1)} %collective-permute-done.15.refs_2_, ...), custom_call_target="tpu_custom_call" | custom-call | flops 1073741824 | bytes 9699328 | tf_op jit(solution)/shard_map/near_field/pallas_call | solution.py:134
  118.1 0.7 copy-done
  118.8 1.7 %collective-permute-done.23.refs_2_ = bf16[128,512]{1,0:T(8,128)(2,1)S(1)} collective-permute-done((bf16[128,512]{1,0:T(8,128)(2,1)S(1)}, bf16[128,512]{1,0:T(8,128)(2,1)S(1)}, u32[]{:S(2)}, u32[]{:S(2)}) %collective-permute-start.23) | collective-permute-done | bytes 131104 | tf_op jit(solution)/shard_map/ppermute | solution.py:21
  120.6 0.6 copy-done.13
  121.3 2.1 %finish.3 = bf16[128,512]{1,0:T(8,128)(2,1)} custom-call(bf16[128,512]{1,0:T(8,128)(2,1)} %get-tuple-element.13.refs_0_, bf16[128,512]{1,0:T(8,128)(2,1)} %copy-done.15, bf16[128,512]{1,0:T(8,128)(2,1)} %copy-done.13, bf16[128,512]{1,0:T(8,128)(2,1)} %copy-done.11, f32[128,512]{1,0:T(8,128)} %copy-done, bf16[4,128,128]{2,1,0:T(8,128)(2,1)} %refs_5_.3), custom_call_target="tpu_custom_call" | custom-call | tf_op jit(solution)/shard_map/finish/pallas_call | solution.py:173
  (55 shorter events, 1.3 us)
Async XLA Ops:
  0.6 68.0 %copy-start.16 = (s32[1,16]{1,0:T(1,128)S(1)}, s32[1,16]{1,0:T(1,128)}, u32[]{:S(2)}) copy-start(s32[1,16]{1,0:T(1,128)} %param.16) | copy-start | bytes 196
  0.6 42.7 %collective-permute-start.4 = (bf16[128,512]{1,0:T(8,128)(2,1)}, bf16[128,512]{1,0:T(8,128)(2,1)S(1)}, u32[]{:S(2)}, u32[]{:S(2)}) collective-permute-start(bf16[128,512]{1,0:T(8,128)(2,1)} %refs_0_.3), channel_id=1, source_target_pairs={{0,1},{1,0},{2,3},{3,2},{4,5},{5,4},{6,7},{7,6},{8,9},{9,8},{10,11... | collective-permute-start | bytes 393224 | tf_op jit(solution)/shard_map/ppermute | solution.py:21
  1.2 43.3 %collective-permute-start.3 = (bf16[128,512]{1,0:T(8,128)(2,1)}, bf16[128,512]{1,0:T(8,128)(2,1)S(1)}, u32[]{:S(2)}, u32[]{:S(2)}) collective-permute-start(bf16[128,512]{1,0:T(8,128)(2,1)} %refs_0_.3), channel_id=1, source_target_pairs={{0,12},{4,0},{8,4},{12,8},{1,13},{5,1},{9,5},{13,9},{2,14},{6,2},{... | collective-permute-start | bytes 393224 | tf_op jit(solution)/shard_map/ppermute | solution.py:21
  5.8 47.6 %collective-permute-start.9 = (bf16[768,512]{1,0:T(8,128)(2,1)}, bf16[768,512]{1,0:T(8,128)(2,1)S(1)}, u32[]{:S(2)}, u32[]{:S(2)}) collective-permute-start(bf16[768,512]{1,0:T(8,128)(2,1)} %bitcast.50), channel_id=1, source_target_pairs={{0,2},{2,0},{1,3},{3,1},{4,6},{6,4},{5,7},{7,5},{8,10},{10,8},{9,1... | collective-permute-start | bytes 2359304 | tf_op jit(solution)/shard_map/ppermute | solution.py:21
  7.3 46.2 %collective-permute-start.8 = (bf16[768,512]{1,0:T(8,128)(2,1)}, bf16[768,512]{1,0:T(8,128)(2,1)S(1)}, u32[]{:S(2)}, u32[]{:S(2)}) collective-permute-start(bf16[768,512]{1,0:T(8,128)(2,1)} %bitcast.47), channel_id=1, source_target_pairs={{0,2},{2,0},{1,3},{3,1},{4,6},{6,4},{5,7},{7,5},{8,10},{10,8},{9,1... | collective-permute-start | bytes 2359304 | tf_op jit(solution)/shard_map/ppermute | solution.py:21
  8.5 34.0 %collective-permute-start = (s32[3,12]{1,0:T(4,128)S(1)}, s32[3,12]{1,0:T(4,128)S(1)}, u32[]{:S(2)}, u32[]{:S(2)}) collective-permute-start(s32[3,12]{1,0:T(4,128)S(1)} %pad_add_fusion), channel_id=1, source_target_pairs={{0,2},{2,0},{1,3},{3,1},{4,6},{6,4},{5,7},{7,5},{8,10},{10,8},{9,1... | collective-permute-start | bytes 440 | tf_op jit(solution)/shard_map/ppermute | solution.py:21
  42.5 9.4 %collective-permute-start.2 = (bf16[128,512]{1,0:T(8,128)(2,1)}, bf16[128,512]{1,0:T(8,128)(2,1)S(1)}, u32[]{:S(2)}, u32[]{:S(2)}) collective-permute-start(bf16[128,512]{1,0:T(8,128)(2,1)} %refs_0_.3), channel_id=1, source_target_pairs={{0,8},{4,12},{8,0},{12,4},{1,9},{5,13},{9,1},{13,5},{2,10},{6,14},... | collective-permute-start | bytes 393224 | tf_op jit(solution)/shard_map/ppermute | solution.py:21
  43.3 8.6 %collective-permute-start.1 = (bf16[128,512]{1,0:T(8,128)(2,1)}, bf16[128,512]{1,0:T(8,128)(2,1)S(1)}, u32[]{:S(2)}, u32[]{:S(2)}) collective-permute-start(bf16[128,512]{1,0:T(8,128)(2,1)} %refs_0_.3), channel_id=1, source_target_pairs={{0,4},{4,8},{8,12},{12,0},{1,5},{5,9},{9,13},{13,1},{2,6},{6,10},{... | collective-permute-start | bytes 393224 | tf_op jit(solution)/shard_map/ppermute | solution.py:21
  44.4 8.3 %collective-permute-start.7 = (bf16[128,512]{1,0:T(8,128)(2,1)S(1)}, bf16[128,512]{1,0:T(8,128)(2,1)S(1)}, u32[]{:S(2)}, u32[]{:S(2)}) collective-permute-start(bf16[128,512]{1,0:T(8,128)(2,1)S(1)} %collective-permute-done.3.refs_3_), channel_id=1, source_target_pairs={{0,1},{1,0},{2,3},{3,2},{4,5},{5,4},{6,7},{7,6},{8,9},{9,8},{10,11... | collective-permute-start | bytes 393224 | tf_op jit(solution)/shard_map/ppermute | solution.py:21
  51.9 1.3 %collective-permute-start.6 = (bf16[128,512]{1,0:T(8,128)(2,1)S(1)}, bf16[128,512]{1,0:T(8,128)(2,1)S(1)}, u32[]{:S(2)}, u32[]{:S(2)}) collective-permute-start(bf16[128,512]{1,0:T(8,128)(2,1)S(1)} %collective-permute-done.2.refs_2_), channel_id=1, source_target_pairs={{0,1},{1,0},{2,3},{3,2},{4,5},{5,4},{6,7},{7,6},{8,9},{9,8},{10,11... | collective-permute-start | bytes 393224 | tf_op jit(solution)/shard_map/ppermute | solution.py:21
  51.9 1.5 %collective-permute-start.5 = (bf16[128,512]{1,0:T(8,128)(2,1)S(1)}, bf16[128,512]{1,0:T(8,128)(2,1)S(1)}, u32[]{:S(2)}, u32[]{:S(2)}) collective-permute-start(bf16[128,512]{1,0:T(8,128)(2,1)S(1)} %collective-permute-done.1.refs_1_), channel_id=1, source_target_pairs={{0,1},{1,0},{2,3},{3,2},{4,5},{5,4},{6,7},{7,6},{8,9},{9,8},{10,11... | collective-permute-start | bytes 393224 | tf_op jit(solution)/shard_map/ppermute | solution.py:21
  53.5 0.9 copy-start.3
  54.4 1.1 copy-start.4
  55.5 1.1 copy-start.6
  61.5 0.9 copy-start.8
  62.4 35.0 %copy-start.5 = (bf16[12,64,512]{2,1,0:T(8,128)(2,1)S(1)}, bf16[12,64,512]{2,1,0:T(8,128)(2,1)}, u32[]{:S(2)}) copy-start(bf16[12,64,512]{2,1,0:T(8,128)(2,1)} %param.11) | copy-start | bytes 2359300
  62.4 35.0 %copy-start.7 = (bf16[12,64,512]{2,1,0:T(8,128)(2,1)S(1)}, bf16[12,64,512]{2,1,0:T(8,128)(2,1)}, u32[]{:S(2)}) copy-start(bf16[12,64,512]{2,1,0:T(8,128)(2,1)} %param.10) | copy-start | bytes 2359300
  62.4 1.9 %collective-permute-start.10 = (bf16[512,512]{1,0:T(8,128)(2,1)S(1)}, bf16[512,512]{1,0:T(8,128)(2,1)S(1)}, u32[]{:S(2)}, u32[]{:S(2)}) collective-permute-start(bf16[512,512]{1,0:T(8,128)(2,1)S(1)} %get-tuple-element.7), channel_id=1, source_target_pairs={{0,1},{1,0},{2,3},{3,2},{4,5},{5,4},{6,7},{7,6},{8,9},{9,8},{10,11... | collective-permute-start | bytes 1572872 | tf_op jit(solution)/shard_map/ppermute | solution.py:21
  65.2 12.0 %collective-permute-start.13 = (bf16[128,512]{1,0:T(8,128)(2,1)S(1)}, bf16[128,512]{1,0:T(8,128)(2,1)S(1)}, u32[]{:S(2)}, u32[]{:S(2)}) collective-permute-start(bf16[128,512]{1,0:T(8,128)(2,1)S(1)} %get-tuple-element.14), channel_id=1, source_target_pairs={{0,12},{4,0},{8,4},{12,8},{1,13},{5,1},{9,5},{13,9},{2,14},{6,2},{... | collective-permute-start | bytes 393224 | tf_op jit(solution)/shard_map/ppermute | solution.py:21
  65.8 13.1 %collective-permute-start.12 = (bf16[128,512]{1,0:T(8,128)(2,1)S(1)}, bf16[128,512]{1,0:T(8,128)(2,1)S(1)}, u32[]{:S(2)}, u32[]{:S(2)}) collective-permute-start(bf16[128,512]{1,0:T(8,128)(2,1)S(1)} %get-tuple-element.15), channel_id=1, source_target_pairs={{0,8},{4,12},{8,0},{12,4},{1,9},{5,13},{9,1},{13,5},{2,10},{6,14},... | collective-permute-start | bytes 393224 | tf_op jit(solution)/shard_map/ppermute | solution.py:21
  66.6 12.2 %collective-permute-start.11 = (bf16[128,512]{1,0:T(8,128)(2,1)S(1)}, bf16[128,512]{1,0:T(8,128)(2,1)S(1)}, u32[]{:S(2)}, u32[]{:S(2)}) collective-permute-start(bf16[128,512]{1,0:T(8,128)(2,1)S(1)} %get-tuple-element.16), channel_id=1, source_target_pairs={{0,4},{4,8},{8,12},{12,0},{1,5},{5,9},{9,13},{13,1},{2,6},{6,10},{... | collective-permute-start | bytes 393224 | tf_op jit(solution)/shard_map/ppermute | solution.py:21
  76.4 0.7 copy-start.1
  77.1 3.0 %copy-start.10 = (bf16[128,512]{1,0:T(8,128)(2,1)}, bf16[128,512]{1,0:T(8,128)(2,1)S(1)}, u32[]{:S(2)}) copy-start(bf16[128,512]{1,0:T(8,128)(2,1)S(1)} %collective-permute-done.13.refs_3_) | copy-start | bytes 393220
  78.8 0.7 copy-start.12
  79.5 0.6 copy-start.14
  82.2 5.8 %collective-permute-start.16 = (bf16[128,512]{1,0:T(8,128)(2,1)}, bf16[128,512]{1,0:T(8,128)(2,1)S(1)}, u32[]{:S(2)}, u32[]{:S(2)}) collective-permute-start(bf16[128,512]{1,0:T(8,128)(2,1)} %finish.2.refs_0_), channel_id=1, source_target_pairs={{0,12},{4,0},{8,4},{12,8},{1,13},{5,1},{9,5},{13,9},{2,14},{6,2},{... | collective-permute-start | bytes 393224 | tf_op jit(solution)/shard_map/ppermute | solution.py:21
  82.4 13.5 %collective-permute-start.15 = (bf16[128,512]{1,0:T(8,128)(2,1)}, bf16[128,512]{1,0:T(8,128)(2,1)S(1)}, u32[]{:S(2)}, u32[]{:S(2)}) collective-permute-start(bf16[128,512]{1,0:T(8,128)(2,1)} %finish.2.refs_0_), channel_id=1, source_target_pairs={{0,8},{4,12},{8,0},{12,4},{1,9},{5,13},{9,1},{13,5},{2,10},{6,14},... | collective-permute-start | bytes 393224 | tf_op jit(solution)/shard_map/ppermute | solution.py:21
  83.6 12.3 %collective-permute-start.14 = (bf16[128,512]{1,0:T(8,128)(2,1)}, bf16[128,512]{1,0:T(8,128)(2,1)S(1)}, u32[]{:S(2)}, u32[]{:S(2)}) collective-permute-start(bf16[128,512]{1,0:T(8,128)(2,1)} %finish.2.refs_0_), channel_id=1, source_target_pairs={{0,4},{4,8},{8,12},{12,0},{1,5},{5,9},{9,13},{13,1},{2,6},{6,10},{... | collective-permute-start | bytes 393224 | tf_op jit(solution)/shard_map/ppermute | solution.py:21
  85.6 10.8 %collective-permute-start.17 = (bf16[128,512]{1,0:T(8,128)(2,1)}, bf16[128,512]{1,0:T(8,128)(2,1)S(1)}, u32[]{:S(2)}, u32[]{:S(2)}) collective-permute-start(bf16[128,512]{1,0:T(8,128)(2,1)} %finish.2.refs_0_), channel_id=1, source_target_pairs={{0,1},{1,0},{2,3},{3,2},{4,5},{5,4},{6,7},{7,6},{8,9},{9,8},{10,11... | collective-permute-start | bytes 393224 | tf_op jit(solution)/shard_map/ppermute | solution.py:21
  88.0 8.4 %collective-permute-start.20 = (bf16[128,512]{1,0:T(8,128)(2,1)S(1)}, bf16[128,512]{1,0:T(8,128)(2,1)S(1)}, u32[]{:S(2)}, u32[]{:S(2)}) collective-permute-start(bf16[128,512]{1,0:T(8,128)(2,1)S(1)} %collective-permute-done.16.refs_3_), channel_id=1, source_target_pairs={{0,1},{1,0},{2,3},{3,2},{4,5},{5,4},{6,7},{7,6},{8,9},{9,8},{10,11... | collective-permute-start | bytes 393224 | tf_op jit(solution)/shard_map/ppermute | solution.py:21
  95.9 1.3 %collective-permute-start.19 = (bf16[128,512]{1,0:T(8,128)(2,1)S(1)}, bf16[128,512]{1,0:T(8,128)(2,1)S(1)}, u32[]{:S(2)}, u32[]{:S(2)}) collective-permute-start(bf16[128,512]{1,0:T(8,128)(2,1)S(1)} %collective-permute-done.15.refs_2_), channel_id=1, source_target_pairs={{0,1},{1,0},{2,3},{3,2},{4,5},{5,4},{6,7},{7,6},{8,9},{9,8},{10,11... | collective-permute-start | bytes 393224 | tf_op jit(solution)/shard_map/ppermute | solution.py:21
  95.9 1.5 %collective-permute-start.18 = (bf16[128,512]{1,0:T(8,128)(2,1)S(1)}, bf16[128,512]{1,0:T(8,128)(2,1)S(1)}, u32[]{:S(2)}, u32[]{:S(2)}) collective-permute-start(bf16[128,512]{1,0:T(8,128)(2,1)S(1)} %collective-permute-done.14.refs_1_), channel_id=1, source_target_pairs={{0,1},{1,0},{2,3},{3,2},{4,5},{5,4},{6,7},{7,6},{8,9},{9,8},{10,11... | collective-permute-start | bytes 393224 | tf_op jit(solution)/shard_map/ppermute | solution.py:21
  97.4 0.9 copy-start.2
  98.3 1.1 copy-start.9
  104.3 2.0 %collective-permute-start.21 = (bf16[512,512]{1,0:T(8,128)(2,1)S(1)}, bf16[512,512]{1,0:T(8,128)(2,1)S(1)}, u32[]{:S(2)}, u32[]{:S(2)}) collective-permute-start(bf16[512,512]{1,0:T(8,128)(2,1)S(1)} %get-tuple-element.9), channel_id=1, source_target_pairs={{0,1},{1,0},{2,3},{3,2},{4,5},{5,4},{6,7},{7,6},{8,9},{9,8},{10,11... | collective-permute-start | bytes 1572872 | tf_op jit(solution)/shard_map/ppermute | solution.py:21
  107.1 11.7 %collective-permute-start.24 = (bf16[128,512]{1,0:T(8,128)(2,1)S(1)}, bf16[128,512]{1,0:T(8,128)(2,1)S(1)}, u32[]{:S(2)}, u32[]{:S(2)}) collective-permute-start(bf16[128,512]{1,0:T(8,128)(2,1)S(1)} %get-tuple-element.10), channel_id=1, source_target_pairs={{0,12},{4,0},{8,4},{12,8},{1,13},{5,1},{9,5},{13,9},{2,14},{6,2},{... | collective-permute-start | bytes 393224 | tf_op jit(solution)/shard_map/ppermute | solution.py:21
  107.1 13.4 %collective-permute-start.23 = (bf16[128,512]{1,0:T(8,128)(2,1)S(1)}, bf16[128,512]{1,0:T(8,128)(2,1)S(1)}, u32[]{:S(2)}, u32[]{:S(2)}) collective-permute-start(bf16[128,512]{1,0:T(8,128)(2,1)S(1)} %get-tuple-element.11), channel_id=1, source_target_pairs={{0,8},{4,12},{8,0},{12,4},{1,9},{5,13},{9,1},{13,5},{2,10},{6,14},... | collective-permute-start | bytes 393224 | tf_op jit(solution)/shard_map/ppermute | solution.py:21
  108.3 12.2 %collective-permute-start.22 = (bf16[128,512]{1,0:T(8,128)(2,1)S(1)}, bf16[128,512]{1,0:T(8,128)(2,1)S(1)}, u32[]{:S(2)}, u32[]{:S(2)}) collective-permute-start(bf16[128,512]{1,0:T(8,128)(2,1)S(1)} %get-tuple-element.12), channel_id=1, source_target_pairs={{0,4},{4,8},{8,12},{12,0},{1,5},{5,9},{9,13},{13,1},{2,6},{6,10},{... | collective-permute-start | bytes 393224 | tf_op jit(solution)/shard_map/ppermute | solution.py:21
  118.1 0.7 copy-start
  118.8 1.8 %copy-start.11 = (bf16[128,512]{1,0:T(8,128)(2,1)}, bf16[128,512]{1,0:T(8,128)(2,1)S(1)}, u32[]{:S(2)}) copy-start(bf16[128,512]{1,0:T(8,128)(2,1)S(1)} %collective-permute-done.24.refs_3_) | copy-start | bytes 393220
  120.6 0.7 copy-start.13
  120.6 0.7 copy-start.15

commit v2 on v1

--- a/solution.py
+++ b/solution.py
@@ -13,7 +13,6 @@
 NCHUNK = 256
 BF16 = jnp.bfloat16
 F32 = jnp.float32
-VMEM_LIMIT = 48 * 1024 * 1024
 CONTRACT_LAST = (((1,), (1,)), ((), ()))
 
 
@@ -33,74 +32,121 @@
         copy.wait()
 
 
-def far_kernel(n_pieces, n_parts, n_keep, col_ref, row_ref, *refs):
-    pieces = refs[:n_pieces]
-    ins = refs[n_pieces : n_pieces + n_parts]
-    outs = refs[n_pieces + n_parts : n_pieces + 2 * n_parts]
-    keep_ref, send_ref, stacked, coeff, masked, sems = refs[n_pieces + 2 * n_parts :]
+def spread(values):
+    tile = lax.broadcasted_iota(jnp.int32, (1, NCHUNK), 1) // RMAX
+    out = jnp.full((1, NCHUNK), values[0], jnp.int32)
+    for i, value in enumerate(values[1:], 1):
+        out = jnp.where(tile == i, value, out)
+    return out
+
+
+def far_kernel(sizes, n_parts, has_partial, final, place_ref, *refs):
+    n_tiles, n_sub = sizes
+    n_pieces = n_tiles * n_sub
+    tables, refs = refs[:n_parts], refs[n_parts:]
+    pieces, refs = refs[:n_pieces], refs[n_pieces:]
+    ins, refs = refs[:n_parts], refs[n_parts:]
+    outs, refs = refs[:n_parts], refs[n_parts:]
+    partial, refs = refs[:has_partial], refs[has_partial:]
+    results, (stacked, masked, sems) = refs[:-3], refs[-3:]
+    z, s = place_ref[0], place_ref[1]
     rows = pieces[0].shape[0]
     width = ins[0].shape[0]
+    per_chunk = NCHUNK // RMAX
     fetch(pieces, stacked, sems)
+    lane = lax.broadcasted_iota(jnp.int32, (1, NCHUNK), 1) % RMAX
     for part in range(n_parts):
         for chunk in range(width // NCHUNK):
-            here = pl.ds(chunk * NCHUNK, NCHUNK)
-            there = pl.ds(part * width + chunk * NCHUNK, NCHUNK)
+            tiles = range(chunk * per_chunk, (chunk + 1) * per_chunk)
+            ranks = spread([tables[part][0, t] for t in tiles])
+            block_rows = [tables[part][1, t] for t in tiles]
+            block_cols = [tables[part][2, t] for t in tiles]
+            column = spread(
+                [
+                    lax.rem(s + n_sub - lax.rem(j, n_sub), n_sub) * n_tiles
+                    + lax.rem(z + n_tiles - lax.div(j, n_sub), n_tiles)
+                    for j in block_cols
+                ]
+            )
+            target = spread(
+                [
+                    lax.rem(lax.rem(j, n_sub) + n_sub - s, n_sub) * n_tiles
+                    + lax.rem(lax.div(j, n_sub) + n_tiles - z, n_tiles)
+                    for j in block_rows
+                ]
+            )
+            target = jnp.where(lane < ranks, target, -1)
             products = lax.dot_general(
-                stacked[...], ins[part][here, :], CONTRACT_LAST, preferred_element_type=F32
+                stacked[...],
+                ins[part][chunk * NCHUNK : (chunk + 1) * NCHUNK, :],
+                CONTRACT_LAST,
+                preferred_element_type=F32,
             )
-            column = col_ref[:, there]
             chosen = products[:rows]
             for piece in range(1, n_pieces):
                 chosen = jnp.where(
                     column == piece, products[piece * rows : (piece + 1) * rows], chosen
                 )
-            coeff[:, there] = chosen
-    for target in range(n_pieces):
-        for chunk in range(n_parts * width // NCHUNK):
-            there = pl.ds(chunk * NCHUNK, NCHUNK)
-            masked[pl.ds(target * rows, rows), there] = jnp.where(
-                row_ref[:, there] == target, coeff[:, there], 0.0
-            ).astype(BF16)
-    total = jnp.dot(masked[:, :width], outs[0][...], preferred_element_type=F32)
-    for part in range(1, n_parts):
-        total += jnp.dot(
+            first = part * width + chunk * NCHUNK
+            for piece in range(n_pieces):
+                masked[piece * rows : (piece + 1) * rows, first : first + NCHUNK] = jnp.where(
+                    target == piece, chosen, 0.0
+                ).astype(BF16)
+    total = partial[0][...] if has_partial else None
+    for part in range(n_parts):
+        added = jnp.dot(
             masked[:, part * width : (part + 1) * width],
             outs[part][...],
             preferred_element_type=F32,
         )
-    total = total.astype(BF16)
-    keep_ref[...] = total[: n_keep * rows]
-    send_ref[...] = total[n_keep * rows :]
-
-
-def far_field(pieces, ins, outs, columns, rows_of, n_keep):
+        total = added if total is None else total + added
+    if final:
+        keep_ref, send_ref = results
+        total = total.astype(BF16)
+        keep_ref[...] = total[: n_tiles * rows]
+        send_ref[...] = total[n_tiles * rows :]
+    else:
+        results[0][...] = total
+
+
+def far_field(sizes, place, tables, pieces, ins, outs, partial=None, final=True):
     rows = pieces[0].shape[0]
     n_pieces, n_parts, width = len(pieces), len(ins), ins[0].shape[0]
+    n_keep = sizes[0]
     whole = pl.BlockSpec(memory_space=pltpu.VMEM)
+    scalars = pl.BlockSpec(memory_space=pltpu.SMEM)
     anywhere = pl.BlockSpec(memory_space=pl.ANY)
-    flops = 4 * n_pieces * rows * n_parts * width * BLK
-    return pl.pallas_call(
-        functools.partial(far_kernel, n_pieces, n_parts, n_keep),
-        out_shape=(
+    if final:
+        out_shape = (
             jax.ShapeDtypeStruct((n_keep * rows, BLK), BF16),
             jax.ShapeDtypeStruct(((n_pieces - n_keep) * rows, BLK), BF16),
-        ),
-        in_specs=[whole, whole] + [anywhere] * n_pieces + [whole] * (2 * n_parts),
-        out_specs=(whole, whole),
+        )
+    else:
+        out_shape = (jax.ShapeDtypeStruct((n_pieces * rows, BLK), F32),)
+    partials = [] if partial is None else [partial]
+    limit = n_pieces * rows * (2 * BLK + 2 * n_parts * width + 16 * BLK + 4 * NCHUNK)
+    limit += 4 * n_parts * width * BLK + (4 << 20)
+    out = pl.pallas_call(
+        functools.partial(far_kernel, sizes, n_parts, len(partials), final),
+        out_shape=out_shape,
+        in_specs=[scalars] * (1 + n_parts)
+        + [anywhere] * n_pieces
+        + [whole] * (2 * n_parts + len(partials)),
+        out_specs=(whole,) * len(out_shape),
         scratch_shapes=[
             pltpu.VMEM((n_pieces * rows, BLK), BF16),
-            pltpu.VMEM((rows, n_parts * width), F32),
             pltpu.VMEM((n_pieces * rows, n_parts * width), BF16),
             pltpu.SemaphoreType.DMA((n_pieces,)),
         ],
-        compiler_params=pltpu.CompilerParams(vmem_limit_bytes=VMEM_LIMIT),
+        compiler_params=pltpu.CompilerParams(vmem_limit_bytes=limit),
         cost_estimate=pl.CostEstimate(
-            flops=flops,
+            flops=4 * n_pieces * rows * n_parts * width * BLK,
             transcendentals=0,
             bytes_accessed=2 * BLK * (2 * n_pieces * rows + 2 * n_parts * width),
         ),
         name="far_field",
-    )(columns, rows_of, *pieces, *ins, *outs)
+    )(place, *tables, *pieces, *ins, *outs, *partials)
+    return out if final else out[0]
 
 
 def near_kernel(n_pieces, per_step, slot_ref, *refs):
@@ -145,7 +191,7 @@
                 pltpu.SemaphoreType.DMA((n_pieces,)),
             ],
         ),
-        compiler_params=pltpu.CompilerParams(vmem_limit_bytes=VMEM_LIMIT),
+        compiler_params=pltpu.CompilerParams(vmem_limit_bytes=12 << 20),
         cost_estimate=pl.CostEstimate(
             flops=2 * near * rows * BLK * BLK,
             transcendentals=0,
@@ -175,6 +221,7 @@
         out_shape=jax.ShapeDtypeStruct(near.shape, BF16),
         in_specs=[whole] * (len(sums) + 2),
         out_specs=whole,
+        compiler_params=pltpu.CompilerParams(vmem_limit_bytes=4 << 20),
         name="finish",
     )(*sums, near, jacobi_inverse)
 
@@ -202,9 +249,6 @@
     def source_slot(block):
         return (s - block % n_sub) % n_sub * n_tiles + (z - block // n_sub) % n_tiles
 
-    def target_slot(block):
-        return (block % n_sub - s) % n_sub * n_tiles + (block // n_sub - z) % n_tiles
-
     def gather(field):
         along = [field] + [shifted(field, "tiles", n_tiles, d) for d in range(1, n_tiles)]
         pieces = list(along)
@@ -219,15 +263,12 @@
         tables.append(shifted(numbers, "rhs", n_rhs, d))
         ins.append(shifted(basis_in, "rhs", n_rhs, d))
         outs.append(shifted(basis_out, "rhs", n_rhs, d))
-    ranks, block_rows, block_cols = jnp.concatenate(tables, axis=1)
-    kept = lax.broadcasted_iota(jnp.int32, (ranks.shape[0], RMAX), 1) < ranks[:, None]
-    rows_of = jnp.where(kept, target_slot(block_rows)[:, None], -1).reshape(1, -1)
-    columns = jnp.broadcast_to(source_slot(block_cols)[:, None], kept.shape).reshape(1, -1)
+    sizes = (n_tiles, n_sub)
+    place = jnp.stack([z, s])
     near_slots = source_slot(near_col[0])
     near_blocks = near_blocks[0]
 
-    def apply_once(pieces):
-        keep, send = far_field(pieces, ins, outs, columns, rows_of, n_tiles)
+    def reduce_and_finish(pieces, keep, send):
         total = keep.astype(F32)
         for e in range(1, n_sub):
             size = n_tiles * rows
@@ -239,8 +280,12 @@
         near = near_field(pieces, near_blocks, near_slots)
         return finish(sums, near, jacobi_inverse)
 
-    first_result = apply_once(pieces)
-    second_result = apply_once(gather(first_result))
+    partial = far_field(sizes, place, tables[:1], pieces, ins[:1], outs[:1], final=False)
+    keep, send = far_field(sizes, place, tables[1:], pieces, ins[1:], outs[1:], partial=partial)
+    first_result = reduce_and_finish(pieces, keep, send)
+    pieces = gather(first_result)
+    keep, send = far_field(sizes, place, tables, pieces, ins, outs)
+    second_result = reduce_and_finish(pieces, keep, send)
     return (first_result, second_result)
 
 

time: 124 us -> 98.9 us (0.80)
  waiting for transfers between devices: 58.6 us -> 36.6 us
  starting transfers between devices: 21.6 us -> 29.2 us
  local copies, waits for them, and re-layouts: 11.2 us -> 5.07 us
  Pallas kernels: 29.4 us -> 25.5 us
    ppermute x25, waiting for transfers between devices: 58.6 us -> 36.6 us  [shifted(): lax.ppermute(value, axis, [(i, (i + amount) % size) for i in range(size)])]
    ppermute x25, starting transfers between devices: 21.6 us -> 29.2 us  [shifted(): lax.ppermute(value, axis, [(i, (i + amount) % size) for i in range(size)])]
    pallas_call x2, Pallas kernels: 15.5 us -> 10.6 us  [near_field(): pl.pallas_call(functools.partial(near_kernel, n_pieces, per_step), out_sh...]
    unnamed x34 -> x20, local copies, waits for them, and re-layouts: 9.54 us -> 5 us
    pallas_call x2 -> x3, Pallas kernels: 9.72 us -> 13.1 us  [far_field(): pl.pallas_call(functools.partial(far_kernel, sizes, n_parts, len(partials...]
    pallas_call x2, Pallas kernels: 4.21 us -> 1.78 us  [finish(): pl.pallas_call(functools.partial(finish_kernel, len(sums)), out_shape=jax...]
    slice x2, local copies, waits for them, and re-layouts: 1.38 us -> 0.07 us  [reduce_and_finish(): part = total[d * rows:(d + 1) * rows].astype(BF16)]
  transfers between devices with their start and end apart: 25 -> 25, of which waited for: 12 -> 12; matrix products, arithmetic and copies ran while one was open for 1% -> 1% of each run, Pallas kernels for 13% -> 15%
where the time goes in v2:
time: 98.9 us; the launch traced here: 98.2 us
  waiting for transfers between devices  36.6 us (37%)
  starting transfers between devices  29.2 us (30%)
  Pallas kernels  25.5 us (26%)
  local copies, waits for them, and re-layouts  5.07 us (5%)
  other arithmetic  1.06 us (1%)
    ppermute x25, waiting for transfers between devices, shifted(): lax.ppermute(value, axis, [(i, (i + amount) % size) for i in range(size)])  36.6 us
    ppermute x25, starting transfers between devices, shifted(): lax.ppermute(value, axis, [(i, (i + amount) % size) for i in range(size)])  29.2 us
    pallas_call x3, Pallas kernels, far_field(): pl.pallas_call(functools.partial(far_kernel, sizes, n_parts, len(partials...  13.1 us
    pallas_call x2, Pallas kernels, near_field(): pl.pallas_call(functools.partial(near_kernel, n_pieces, per_step), out_sh...  10.6 us
    unnamed x20, local copies, waits for them, and re-layouts  5 us
  transfers between devices with their start and end apart: 25, of which 12 were waited for; matrix products, arithmetic and copies ran while one was open for 1% of the time, Pallas kernels for 15%

profile of v2, /device:TPU:0, one launch (start us, length us, event | category | flops | bytes accessed | tf_op | source)
XLA Modules:
  0.0 98.2 jit_solution(6801861999075645812)
XLA Ops:
  0.6 3.0 %collective-permute-start.8 = (bf16[768,512]{1,0:T(8,128)(2,1)}, bf16[768,512]{1,0:T(8,128)(2,1)S(1)}, u32[]{:S(2)}, u32[]{:S(2)}) collective-permute-start(bf16[768,512]{1,0:T(8,128)(2,1)} %bitcast.23), channel_id=1, source_target_pairs={{0,2},{2,0},{1,3},{3,1},{4,6},{6,4},{5,7},{7,5},{8,10},{10,8},{9,1... | collective-permute-start | bytes 2359304 | tf_op jit(solution)/shard_map/ppermute | solution.py:20
  3.6 0.1 collective-permute-start.9
  3.7 2.0 %collective-permute-start.1 = (bf16[128,512]{1,0:T(8,128)(2,1)}, bf16[128,512]{1,0:T(8,128)(2,1)S(1)}, u32[]{:S(2)}, u32[]{:S(2)}) collective-permute-start(bf16[128,512]{1,0:T(8,128)(2,1)} %refs_0_.1), channel_id=1, source_target_pairs={{0,4},{4,8},{8,12},{12,0},{1,5},{5,9},{9,13},{13,1},{2,6},{6,10},{... | collective-permute-start | bytes 393224 | tf_op jit(solution)/shard_map/ppermute | solution.py:20
  5.8 2.6 %collective-permute-start.2 = (bf16[128,512]{1,0:T(8,128)(2,1)}, bf16[128,512]{1,0:T(8,128)(2,1)S(1)}, u32[]{:S(2)}, u32[]{:S(2)}) collective-permute-start(bf16[128,512]{1,0:T(8,128)(2,1)} %refs_0_.1), channel_id=1, source_target_pairs={{0,8},{4,12},{8,0},{12,4},{1,9},{5,13},{9,1},{13,5},{2,10},{6,14},... | collective-permute-start | bytes 393224 | tf_op jit(solution)/shard_map/ppermute | solution.py:20
  8.3 1.3 %collective-permute-start.3 = (bf16[128,512]{1,0:T(8,128)(2,1)}, bf16[128,512]{1,0:T(8,128)(2,1)S(1)}, u32[]{:S(2)}, u32[]{:S(2)}) collective-permute-start(bf16[128,512]{1,0:T(8,128)(2,1)} %refs_0_.1), channel_id=1, source_target_pairs={{0,12},{4,0},{8,4},{12,8},{1,13},{5,1},{9,5},{13,9},{2,14},{6,2},{... | collective-permute-start | bytes 393224 | tf_op jit(solution)/shard_map/ppermute | solution.py:20
  9.7 2.8 %collective-permute-done.1.refs_2_.refs_1_ = bf16[128,512]{1,0:T(8,128)(2,1)S(1)} collective-permute-done((bf16[128,512]{1,0:T(8,128)(2,1)}, bf16[128,512]{1,0:T(8,128)(2,1)S(1)}, u32[]{:S(2)}, u32[]{:S(2)}) %collective-permute-start.1) | collective-permute-done | bytes 131104 | tf_op jit(solution)/shard_map/ppermute | solution.py:20
  12.5 4.1 %collective-permute-done.2.refs_3_.refs_2_ = bf16[128,512]{1,0:T(8,128)(2,1)S(1)} collective-permute-done((bf16[128,512]{1,0:T(8,128)(2,1)}, bf16[128,512]{1,0:T(8,128)(2,1)S(1)}, u32[]{:S(2)}, u32[]{:S(2)}) %collective-permute-start.2) | collective-permute-done | bytes 131104 | tf_op jit(solution)/shard_map/ppermute | solution.py:20
  16.6 0.1 collective-permute-done.3.refs_4_.refs_3_
  16.7 0.5 collective-permute-start.6
  17.2 0.1 collective-permute-start.7
  17.2 0.1 pad_add_fusion.1.place_ref
  17.3 0.7 pad_add_fusion.refs_0_
  18.0 1.6 %collective-permute-start = (s32[3,12]{1,0:T(4,128)S(1)}, s32[3,12]{1,0:T(4,128)S(1)}, u32[]{:S(2)}, u32[]{:S(2)}) collective-permute-start(s32[3,12]{1,0:T(4,128)S(1)} %pad_add_fusion.refs_0_), channel_id=1, source_target_pairs={{0,2},{2,0},{1,3},{3,1},{4,6},{6,4},{5,7},{7,5},{8,10},{10,8},{9,1... | collective-permute-start | bytes 440 | tf_op jit(solution)/shard_map/ppermute | solution.py:20
  19.7 0.9 copy-done.3
  20.6 1.1 %copy-done.5 = bf16[12,64,512]{2,1,0:T(8,128)(2,1)S(1)} copy-done((bf16[12,64,512]{2,1,0:T(8,128)(2,1)S(1)}, bf16[12,64,512]{2,1,0:T(8,128)(2,1)}, u32[]{:S(2)}) %copy-start.5) | copy-done | bytes 786456
  21.7 1.1 %copy-done.7 = bf16[12,64,512]{2,1,0:T(8,128)(2,1)S(1)} copy-done((bf16[12,64,512]{2,1,0:T(8,128)(2,1)S(1)}, bf16[12,64,512]{2,1,0:T(8,128)(2,1)}, u32[]{:S(2)}) %copy-start.7) | copy-done | bytes 786456
  22.8 3.8 %far_field.3.refs_11_ = f32[1024,512]{1,0:T(8,128)S(1)} custom-call(s32[2]{0:T(128)S(1)} %pad_add_fusion.1.place_ref, s32[3,12]{1,0:T(4,128)S(1)} %pad_add_fusion.refs_0_, bf16[128,512]{1,0:T(8,128)(2,1)S(1)} %copy-done.3, bf16[128,512]{1,0:T(8,128)(2,1)S(1)} %collective-permute-done.1.refs_2_.refs_1_, ...), custom_call_target="tpu_custom_call" | custom-call | flops 1610612736 | bytes 3670016 | tf_op jit(solution)/shard_map/far_field/pallas_call | solution.py:129
  26.7 11.6 %collective-permute-done.refs_0_.refs_1_ = s32[3,12]{1,0:T(4,128)S(1)} collective-permute-done((s32[3,12]{1,0:T(4,128)S(1)}, s32[3,12]{1,0:T(4,128)S(1)}, u32[]{:S(2)}, u32[]{:S(2)}) %collective-permute-start) | collective-permute-done | bytes 176 | tf_op jit(solution)/shard_map/ppermute | solution.py:20
  38.3 0.9 copy-done.4
  39.2 3.8 %far_field.4 = (bf16[512,512]{1,0:T(8,128)(2,1)S(1)}, bf16[512,512]{1,0:T(8,128)(2,1)S(1)}) custom-call(s32[2]{0:T(128)S(1)} %pad_add_fusion.1.place_ref, s32[3,12]{1,0:T(4,128)S(1)} %collective-permute-done.refs_0_.refs_1_, bf16[128,512]{1,0:T(8,128)(2,1)S(1)} %copy-done.4, bf16[128,512]{1,0:T(8,128)(2,1)S(1)} %collective-permute-done.1.refs_2_.refs_1_, ...), custom_call_target="tpu_custom_call" | custom-call | flops 1610612736 | bytes 3670016 | tf_op jit(solution)/shard_map/far_field/pallas_call | solution.py:129
  43.1 0.1 collective-permute-start.10
  43.1 1.9 %collective-permute-done.10 = bf16[512,512]{1,0:T(8,128)(2,1)S(1)} collective-permute-done((bf16[512,512]{1,0:T(8,128)(2,1)S(1)}, bf16[512,512]{1,0:T(8,128)(2,1)S(1)}, u32[]{:S(2)}, u32[]{:S(2)}) %collective-permute-start.10) | collective-permute-done | bytes 524320 | tf_op jit(solution)/shard_map/ppermute | solution.py:20
  45.0 0.1 add_convert_fusion.1
  45.2 1.9 %collective-permute-start.11 = (bf16[128,512]{1,0:T(8,128)(2,1)S(1)}, bf16[128,512]{1,0:T(8,128)(2,1)S(1)}, u32[]{:S(2)}, u32[]{:S(2)}) collective-permute-start(bf16[128,512]{1,0:T(8,128)(2,1)S(1)} %get-tuple-element.16), channel_id=1, source_target_pairs={{0,4},{4,8},{8,12},{12,0},{1,5},{5,9},{9,13},{13,1},{2,6},{6,10},{... | collective-permute-start | bytes 393224 | tf_op jit(solution)/shard_map/ppermute | solution.py:20
  47.1 2.6 %collective-permute-start.12 = (bf16[128,512]{1,0:T(8,128)(2,1)S(1)}, bf16[128,512]{1,0:T(8,128)(2,1)S(1)}, u32[]{:S(2)}, u32[]{:S(2)}) collective-permute-start(bf16[128,512]{1,0:T(8,128)(2,1)S(1)} %get-tuple-element.15), channel_id=1, source_target_pairs={{0,8},{4,12},{8,0},{12,4},{1,9},{5,13},{9,1},{13,5},{2,10},{6,14},... | collective-permute-start | bytes 393224 | tf_op jit(solution)/shard_map/ppermute | solution.py:20
  49.7 1.4 %collective-permute-start.13 = (bf16[128,512]{1,0:T(8,128)(2,1)S(1)}, bf16[128,512]{1,0:T(8,128)(2,1)S(1)}, u32[]{:S(2)}, u32[]{:S(2)}) collective-permute-start(bf16[128,512]{1,0:T(8,128)(2,1)S(1)} %get-tuple-element.14), channel_id=1, source_target_pairs={{0,12},{4,0},{8,4},{12,8},{1,13},{5,1},{9,5},{13,9},{2,14},{6,2},{... | collective-permute-start | bytes 393224 | tf_op jit(solution)/shard_map/ppermute | solution.py:20
  51.1 5.3 %near_field.2.refs_4_ = f32[128,512]{1,0:T(8,128)S(1)} custom-call(s32[16]{0:T(128)S(1)} %fusion.slot_ref, bf16[128,512]{1,0:T(8,128)(2,1)S(1)} %copy-done.4, bf16[128,512]{1,0:T(8,128)(2,1)S(1)} %collective-permute-done.1.refs_2_.refs_1_, bf16[128,512]{1,0:T(8,128)(2,1)S(1)} %collective-permute-done.2.refs_3_.refs_2_, ...), custom_call_target="tpu_custom_call" | custom-call | flops 1073741824 | bytes 9699328 | tf_op jit(solution)/shard_map/near_field/pallas_call | solution.py:180
  56.4 2.3 %collective-permute-done.12.refs_2_ = bf16[128,512]{1,0:T(8,128)(2,1)S(1)} collective-permute-done((bf16[128,512]{1,0:T(8,128)(2,1)S(1)}, bf16[128,512]{1,0:T(8,128)(2,1)S(1)}, u32[]{:S(2)}, u32[]{:S(2)}) %collective-permute-start.12) | collective-permute-done | bytes 131104 | tf_op jit(solution)/shard_map/ppermute | solution.py:20
  58.6 0.9 finish.2.refs_2_.refs_0_
  59.5 3.3 %collective-permute-start.14 = (bf16[128,512]{1,0:T(8,128)(2,1)}, bf16[128,512]{1,0:T(8,128)(2,1)S(1)}, u32[]{:S(2)}, u32[]{:S(2)}) collective-permute-start(bf16[128,512]{1,0:T(8,128)(2,1)} %finish.2.refs_2_.refs_0_), channel_id=1, source_target_pairs={{0,4},{4,8},{8,12},{12,0},{1,5},{5,9},{9,13},{13,1},{2,6},{6,10},{... | collective-permute-start | bytes 393224 | tf_op jit(solution)/shard_map/ppermute | solution.py:20
  62.8 1.6 %collective-permute-start.15 = (bf16[128,512]{1,0:T(8,128)(2,1)}, bf16[128,512]{1,0:T(8,128)(2,1)S(1)}, u32[]{:S(2)}, u32[]{:S(2)}) collective-permute-start(bf16[128,512]{1,0:T(8,128)(2,1)} %finish.2.refs_2_.refs_0_), channel_id=1, source_target_pairs={{0,8},{4,12},{8,0},{12,4},{1,9},{5,13},{9,1},{13,5},{2,10},{6,14},... | collective-permute-start | bytes 393224 | tf_op jit(solution)/shard_map/ppermute | solution.py:20
  64.4 0.7 collective-permute-start.16
  65.2 3.1 %collective-permute-done.14.refs_3_.refs_1_ = bf16[128,512]{1,0:T(8,128)(2,1)S(1)} collective-permute-done((bf16[128,512]{1,0:T(8,128)(2,1)}, bf16[128,512]{1,0:T(8,128)(2,1)S(1)}, u32[]{:S(2)}, u32[]{:S(2)}) %collective-permute-start.14) | collective-permute-done | bytes 131104 | tf_op jit(solution)/shard_map/ppermute | solution.py:20
  68.2 4.5 %collective-permute-done.15.refs_4_.refs_2_ = bf16[128,512]{1,0:T(8,128)(2,1)S(1)} collective-permute-done((bf16[128,512]{1,0:T(8,128)(2,1)}, bf16[128,512]{1,0:T(8,128)(2,1)S(1)}, u32[]{:S(2)}, u32[]{:S(2)}) %collective-permute-start.15) | collective-permute-done | bytes 131104 | tf_op jit(solution)/shard_map/ppermute | solution.py:20
  72.8 0.5 collective-permute-start.20
  73.3 0.8 collective-permute-done.19.refs_8_.refs_6_
  74.1 0.2 collective-permute-done.20.refs_9_.refs_7_
  74.3 0.9 copy-done.1
  75.2 5.5 %far_field.5 = (bf16[512,512]{1,0:T(8,128)(2,1)S(1)}, bf16[512,512]{1,0:T(8,128)(2,1)S(1)}) custom-call(s32[2]{0:T(128)S(1)} %pad_add_fusion.1.place_ref, s32[3,12]{1,0:T(4,128)S(1)} %pad_add_fusion.refs_0_, s32[3,12]{1,0:T(4,128)S(1)} %collective-permute-done.refs_0_.refs_1_, bf16[128,512]{1,0:T(8,128)(2,1)S(1)} %copy-done.1, ...), custom_call_target="tpu_custom_call" | custom-call | flops 3221225472 | bytes 5242880 | tf_op jit(solution)/shard_map/far_field/pallas_call | solution.py:129
  80.7 0.4 collective-permute-start.21
  81.1 1.6 %collective-permute-done.21 = bf16[512,512]{1,0:T(8,128)(2,1)S(1)} collective-permute-done((bf16[512,512]{1,0:T(8,128)(2,1)S(1)}, bf16[512,512]{1,0:T(8,128)(2,1)S(1)}, u32[]{:S(2)}, u32[]{:S(2)}) %collective-permute-start.21) | collective-permute-done | bytes 524320 | tf_op jit(solution)/shard_map/ppermute | solution.py:20
  82.7 0.1 add_convert_fusion
  82.8 3.1 %collective-permute-start.22 = (bf16[128,512]{1,0:T(8,128)(2,1)S(1)}, bf16[128,512]{1,0:T(8,128)(2,1)S(1)}, u32[]{:S(2)}, u32[]{:S(2)}) collective-permute-start(bf16[128,512]{1,0:T(8,128)(2,1)S(1)} %get-tuple-element.12), channel_id=1, source_target_pairs={{0,4},{4,8},{8,12},{12,0},{1,5},{5,9},{9,13},{13,1},{2,6},{6,10},{... | collective-permute-start | bytes 393224 | tf_op jit(solution)/shard_map/ppermute | solution.py:20
  86.0 2.2 %collective-permute-start.23 = (bf16[128,512]{1,0:T(8,128)(2,1)S(1)}, bf16[128,512]{1,0:T(8,128)(2,1)S(1)}, u32[]{:S(2)}, u32[]{:S(2)}) collective-permute-start(bf16[128,512]{1,0:T(8,128)(2,1)S(1)} %get-tuple-element.11), channel_id=1, source_target_pairs={{0,8},{4,12},{8,0},{12,4},{1,9},{5,13},{9,1},{13,5},{2,10},{6,14},... | collective-permute-start | bytes 393224 | tf_op jit(solution)/shard_map/ppermute | solution.py:20
  88.2 0.3 collective-permute-start.24
  88.4 5.3 %near_field.3.refs_4_ = f32[128,512]{1,0:T(8,128)S(1)} custom-call(s32[16]{0:T(128)S(1)} %fusion.slot_ref, bf16[128,512]{1,0:T(8,128)(2,1)S(1)} %copy-done.1, bf16[128,512]{1,0:T(8,128)(2,1)S(1)} %collective-permute-done.14.refs_3_.refs_1_, bf16[128,512]{1,0:T(8,128)(2,1)S(1)} %collective-permute-done.15.refs_4_.refs_2_, ...), custom_call_target="tpu_custom_call" | custom-call | flops 1073741824 | bytes 9699328 | tf_op jit(solution)/shard_map/near_field/pallas_call | solution.py:180
  93.7 3.6 %collective-permute-done.23.refs_2_ = bf16[128,512]{1,0:T(8,128)(2,1)S(1)} collective-permute-done((bf16[128,512]{1,0:T(8,128)(2,1)S(1)}, bf16[128,512]{1,0:T(8,128)(2,1)S(1)}, u32[]{:S(2)}, u32[]{:S(2)}) %collective-permute-start.23) | collective-permute-done | bytes 131104 | tf_op jit(solution)/shard_map/ppermute | solution.py:20
  97.3 0.9 finish.3
  (36 shorter events, 0.2 us)
Async XLA Ops:
  0.6 50.4 %copy-start.9 = (s32[1,16]{1,0:T(1,128)S(1)}, s32[1,16]{1,0:T(1,128)}, u32[]{:S(2)}) copy-start(s32[1,16]{1,0:T(1,128)} %param.16) | copy-start | bytes 196
  0.6 37.7 %collective-permute-start.8 = (bf16[768,512]{1,0:T(8,128)(2,1)}, bf16[768,512]{1,0:T(8,128)(2,1)S(1)}, u32[]{:S(2)}, u32[]{:S(2)}) collective-permute-start(bf16[768,512]{1,0:T(8,128)(2,1)} %bitcast.23), channel_id=1, source_target_pairs={{0,2},{2,0},{1,3},{3,1},{4,6},{6,4},{5,7},{7,5},{8,10},{10,8},{9,1... | collective-permute-start | bytes 2359304 | tf_op jit(solution)/shard_map/ppermute | solution.py:20
  3.6 34.7 %collective-permute-start.9 = (bf16[768,512]{1,0:T(8,128)(2,1)}, bf16[768,512]{1,0:T(8,128)(2,1)S(1)}, u32[]{:S(2)}, u32[]{:S(2)}) collective-permute-start(bf16[768,512]{1,0:T(8,128)(2,1)} %bitcast.26), channel_id=1, source_target_pairs={{0,2},{2,0},{1,3},{3,1},{4,6},{6,4},{5,7},{7,5},{8,10},{10,8},{9,1... | collective-permute-start | bytes 2359304 | tf_op jit(solution)/shard_map/ppermute | solution.py:20
  3.7 8.8 %collective-permute-start.1 = (bf16[128,512]{1,0:T(8,128)(2,1)}, bf16[128,512]{1,0:T(8,128)(2,1)S(1)}, u32[]{:S(2)}, u32[]{:S(2)}) collective-permute-start(bf16[128,512]{1,0:T(8,128)(2,1)} %refs_0_.1), channel_id=1, source_target_pairs={{0,4},{4,8},{8,12},{12,0},{1,5},{5,9},{9,13},{13,1},{2,6},{6,10},{... | collective-permute-start | bytes 393224 | tf_op jit(solution)/shard_map/ppermute | solution.py:20
  5.8 10.9 %collective-permute-start.2 = (bf16[128,512]{1,0:T(8,128)(2,1)}, bf16[128,512]{1,0:T(8,128)(2,1)S(1)}, u32[]{:S(2)}, u32[]{:S(2)}) collective-permute-start(bf16[128,512]{1,0:T(8,128)(2,1)} %refs_0_.1), channel_id=1, source_target_pairs={{0,8},{4,12},{8,0},{12,4},{1,9},{5,13},{9,1},{13,5},{2,10},{6,14},... | collective-permute-start | bytes 393224 | tf_op jit(solution)/shard_map/ppermute | solution.py:20
  8.3 8.4 %collective-permute-start.3 = (bf16[128,512]{1,0:T(8,128)(2,1)}, bf16[128,512]{1,0:T(8,128)(2,1)S(1)}, u32[]{:S(2)}, u32[]{:S(2)}) collective-permute-start(bf16[128,512]{1,0:T(8,128)(2,1)} %refs_0_.1), channel_id=1, source_target_pairs={{0,12},{4,0},{8,4},{12,8},{1,13},{5,1},{9,5},{13,9},{2,14},{6,2},{... | collective-permute-start | bytes 393224 | tf_op jit(solution)/shard_map/ppermute | solution.py:20
  12.5 4.6 %collective-permute-start.4 = (bf16[128,512]{1,0:T(8,128)(2,1)}, bf16[128,512]{1,0:T(8,128)(2,1)S(1)}, u32[]{:S(2)}, u32[]{:S(2)}) collective-permute-start(bf16[128,512]{1,0:T(8,128)(2,1)} %refs_0_.1), channel_id=1, source_target_pairs={{0,1},{1,0},{2,3},{3,2},{4,5},{5,4},{6,7},{7,6},{8,9},{9,8},{10,11... | collective-permute-start | bytes 393224 | tf_op jit(solution)/shard_map/ppermute | solution.py:20
  12.5 38.5 %copy-start = (bf16[1,16,512,512]{3,2,1,0:T(8,128)(2,1)S(1)}, bf16[1,16,512,512]{3,2,1,0:T(8,128)(2,1)}, u32[]{:S(2)}) copy-start(bf16[1,16,512,512]{3,2,1,0:T(8,128)(2,1)} %param.15) | copy-start | bytes 25165828
  16.6 1.4 %collective-permute-start.5 = (bf16[128,512]{1,0:T(8,128)(2,1)S(1)}, bf16[128,512]{1,0:T(8,128)(2,1)S(1)}, u32[]{:S(2)}, u32[]{:S(2)}) collective-permute-start(bf16[128,512]{1,0:T(8,128)(2,1)S(1)} %collective-permute-done.1.refs_2_.refs_1_), channel_id=1, source_target_pairs={{0,1},{1,0},{2,3},{3,2},{4,5},{5,4},{6,7},{7,6},{8,9},{9,8},{10,11... | collective-permute-start | bytes 393224 | tf_op jit(solution)/shard_map/ppermute | solution.py:20
  16.7 3.0 %collective-permute-start.6 = (bf16[128,512]{1,0:T(8,128)(2,1)S(1)}, bf16[128,512]{1,0:T(8,128)(2,1)S(1)}, u32[]{:S(2)}, u32[]{:S(2)}) collective-permute-start(bf16[128,512]{1,0:T(8,128)(2,1)S(1)} %collective-permute-done.2.refs_3_.refs_2_), channel_id=1, source_target_pairs={{0,1},{1,0},{2,3},{3,2},{4,5},{5,4},{6,7},{7,6},{8,9},{9,8},{10,11... | collective-permute-start | bytes 393224 | tf_op jit(solution)/shard_map/ppermute | solution.py:20
  17.2 2.5 %collective-permute-start.7 = (bf16[128,512]{1,0:T(8,128)(2,1)S(1)}, bf16[128,512]{1,0:T(8,128)(2,1)S(1)}, u32[]{:S(2)}, u32[]{:S(2)}) collective-permute-start(bf16[128,512]{1,0:T(8,128)(2,1)S(1)} %collective-permute-done.3.refs_4_.refs_3_), channel_id=1, source_target_pairs={{0,1},{1,0},{2,3},{3,2},{4,5},{5,4},{6,7},{7,6},{8,9},{9,8},{10,11... | collective-permute-start | bytes 393224 | tf_op jit(solution)/shard_map/ppermute | solution.py:20
  18.0 20.3 %collective-permute-start = (s32[3,12]{1,0:T(4,128)S(1)}, s32[3,12]{1,0:T(4,128)S(1)}, u32[]{:S(2)}, u32[]{:S(2)}) collective-permute-start(s32[3,12]{1,0:T(4,128)S(1)} %pad_add_fusion.refs_0_), channel_id=1, source_target_pairs={{0,2},{2,0},{1,3},{3,1},{4,6},{6,4},{5,7},{7,5},{8,10},{10,8},{9,1... | collective-permute-start | bytes 440 | tf_op jit(solution)/shard_map/ppermute | solution.py:20
  19.7 0.9 copy-start.3
  20.6 1.1 %copy-start.5 = (bf16[12,64,512]{2,1,0:T(8,128)(2,1)S(1)}, bf16[12,64,512]{2,1,0:T(8,128)(2,1)}, u32[]{:S(2)}) copy-start(bf16[12,64,512]{2,1,0:T(8,128)(2,1)} %param.11) | copy-start | bytes 2359300
  21.7 1.1 %copy-start.7 = (bf16[12,64,512]{2,1,0:T(8,128)(2,1)S(1)}, bf16[12,64,512]{2,1,0:T(8,128)(2,1)}, u32[]{:S(2)}) copy-start(bf16[12,64,512]{2,1,0:T(8,128)(2,1)} %param.10) | copy-start | bytes 2359300
  26.7 32.0 %copy-start.2 = (bf16[4,128,128]{2,1,0:T(8,128)(2,1)S(1)}, bf16[4,128,128]{2,1,0:T(8,128)(2,1)}, u32[]{:S(2)}) copy-start(bf16[4,128,128]{2,1,0:T(8,128)(2,1)} %refs_5_.3) | copy-start | bytes 393220
  38.3 0.9 copy-start.4
  39.2 35.1 %copy-start.6 = (bf16[12,64,512]{2,1,0:T(8,128)(2,1)S(1)}, bf16[12,64,512]{2,1,0:T(8,128)(2,1)}, u32[]{:S(2)}) copy-start(bf16[12,64,512]{2,1,0:T(8,128)(2,1)} %param.11) | copy-start | bytes 2359300
  39.2 35.1 %copy-start.8 = (bf16[12,64,512]{2,1,0:T(8,128)(2,1)S(1)}, bf16[12,64,512]{2,1,0:T(8,128)(2,1)}, u32[]{:S(2)}) copy-start(bf16[12,64,512]{2,1,0:T(8,128)(2,1)} %param.10) | copy-start | bytes 2359300
  43.1 2.0 %collective-permute-start.10 = (bf16[512,512]{1,0:T(8,128)(2,1)S(1)}, bf16[512,512]{1,0:T(8,128)(2,1)S(1)}, u32[]{:S(2)}, u32[]{:S(2)}) collective-permute-start(bf16[512,512]{1,0:T(8,128)(2,1)S(1)} %get-tuple-element.7), channel_id=1, source_target_pairs={{0,1},{1,0},{2,3},{3,2},{4,5},{5,4},{6,7},{7,6},{8,9},{9,8},{10,11... | collective-permute-start | bytes 1572872 | tf_op jit(solution)/shard_map/ppermute | solution.py:20
  45.2 11.1 %collective-permute-start.11 = (bf16[128,512]{1,0:T(8,128)(2,1)S(1)}, bf16[128,512]{1,0:T(8,128)(2,1)S(1)}, u32[]{:S(2)}, u32[]{:S(2)}) collective-permute-start(bf16[128,512]{1,0:T(8,128)(2,1)S(1)} %get-tuple-element.16), channel_id=1, source_target_pairs={{0,4},{4,8},{8,12},{12,0},{1,5},{5,9},{9,13},{13,1},{2,6},{6,10},{... | collective-permute-start | bytes 393224 | tf_op jit(solution)/shard_map/ppermute | solution.py:20
  47.1 11.5 %collective-permute-start.12 = (bf16[128,512]{1,0:T(8,128)(2,1)S(1)}, bf16[128,512]{1,0:T(8,128)(2,1)S(1)}, u32[]{:S(2)}, u32[]{:S(2)}) collective-permute-start(bf16[128,512]{1,0:T(8,128)(2,1)S(1)} %get-tuple-element.15), channel_id=1, source_target_pairs={{0,8},{4,12},{8,0},{12,4},{1,9},{5,13},{9,1},{13,5},{2,10},{6,14},... | collective-permute-start | bytes 393224 | tf_op jit(solution)/shard_map/ppermute | solution.py:20
  49.7 8.9 %collective-permute-start.13 = (bf16[128,512]{1,0:T(8,128)(2,1)S(1)}, bf16[128,512]{1,0:T(8,128)(2,1)S(1)}, u32[]{:S(2)}, u32[]{:S(2)}) collective-permute-start(bf16[128,512]{1,0:T(8,128)(2,1)S(1)} %get-tuple-element.14), channel_id=1, source_target_pairs={{0,12},{4,0},{8,4},{12,8},{1,13},{5,1},{9,5},{13,9},{2,14},{6,2},{... | collective-permute-start | bytes 393224 | tf_op jit(solution)/shard_map/ppermute | solution.py:20
  59.5 8.7 %collective-permute-start.14 = (bf16[128,512]{1,0:T(8,128)(2,1)}, bf16[128,512]{1,0:T(8,128)(2,1)S(1)}, u32[]{:S(2)}, u32[]{:S(2)}) collective-permute-start(bf16[128,512]{1,0:T(8,128)(2,1)} %finish.2.refs_2_.refs_0_), channel_id=1, source_target_pairs={{0,4},{4,8},{8,12},{12,0},{1,5},{5,9},{9,13},{13,1},{2,6},{6,10},{... | collective-permute-start | bytes 393224 | tf_op jit(solution)/shard_map/ppermute | solution.py:20
  62.8 10.0 %collective-permute-start.15 = (bf16[128,512]{1,0:T(8,128)(2,1)}, bf16[128,512]{1,0:T(8,128)(2,1)S(1)}, u32[]{:S(2)}, u32[]{:S(2)}) collective-permute-start(bf16[128,512]{1,0:T(8,128)(2,1)} %finish.2.refs_2_.refs_0_), channel_id=1, source_target_pairs={{0,8},{4,12},{8,0},{12,4},{1,9},{5,13},{9,1},{13,5},{2,10},{6,14},... | collective-permute-start | bytes 393224 | tf_op jit(solution)/shard_map/ppermute | solution.py:20
  64.4 8.3 %collective-permute-start.16 = (bf16[128,512]{1,0:T(8,128)(2,1)}, bf16[128,512]{1,0:T(8,128)(2,1)S(1)}, u32[]{:S(2)}, u32[]{:S(2)}) collective-permute-start(bf16[128,512]{1,0:T(8,128)(2,1)} %finish.2.refs_2_.refs_0_), channel_id=1, source_target_pairs={{0,12},{4,0},{8,4},{12,8},{1,13},{5,1},{9,5},{13,9},{2,14},{6,2},{... | collective-permute-start | bytes 393224 | tf_op jit(solution)/shard_map/ppermute | solution.py:20
  65.2 8.1 %collective-permute-start.17 = (bf16[128,512]{1,0:T(8,128)(2,1)}, bf16[128,512]{1,0:T(8,128)(2,1)S(1)}, u32[]{:S(2)}, u32[]{:S(2)}) collective-permute-start(bf16[128,512]{1,0:T(8,128)(2,1)} %finish.2.refs_2_.refs_0_), channel_id=1, source_target_pairs={{0,1},{1,0},{2,3},{3,2},{4,5},{5,4},{6,7},{7,6},{8,9},{9,8},{10,11... | collective-permute-start | bytes 393224 | tf_op jit(solution)/shard_map/ppermute | solution.py:20
  68.2 5.0 %collective-permute-start.18 = (bf16[128,512]{1,0:T(8,128)(2,1)S(1)}, bf16[128,512]{1,0:T(8,128)(2,1)S(1)}, u32[]{:S(2)}, u32[]{:S(2)}) collective-permute-start(bf16[128,512]{1,0:T(8,128)(2,1)S(1)} %collective-permute-done.14.refs_3_.refs_1_), channel_id=1, source_target_pairs={{0,1},{1,0},{2,3},{3,2},{4,5},{5,4},{6,7},{7,6},{8,9},{9,8},{10,11... | collective-permute-start | bytes 393224 | tf_op jit(solution)/shard_map/ppermute | solution.py:20
  72.7 1.3 %collective-permute-start.19 = (bf16[128,512]{1,0:T(8,128)(2,1)S(1)}, bf16[128,512]{1,0:T(8,128)(2,1)S(1)}, u32[]{:S(2)}, u32[]{:S(2)}) collective-permute-start(bf16[128,512]{1,0:T(8,128)(2,1)S(1)} %collective-permute-done.15.refs_4_.refs_2_), channel_id=1, source_target_pairs={{0,1},{1,0},{2,3},{3,2},{4,5},{5,4},{6,7},{7,6},{8,9},{9,8},{10,11... | collective-permute-start | bytes 393224 | tf_op jit(solution)/shard_map/ppermute | solution.py:20
  72.8 1.5 %collective-permute-start.20 = (bf16[128,512]{1,0:T(8,128)(2,1)S(1)}, bf16[128,512]{1,0:T(8,128)(2,1)S(1)}, u32[]{:S(2)}, u32[]{:S(2)}) collective-permute-start(bf16[128,512]{1,0:T(8,128)(2,1)S(1)} %collective-permute-done.16.refs_5_.refs_3_), channel_id=1, source_target_pairs={{0,1},{1,0},{2,3},{3,2},{4,5},{5,4},{6,7},{7,6},{8,9},{9,8},{10,11... | collective-permute-start | bytes 393224 | tf_op jit(solution)/shard_map/ppermute | solution.py:20
  74.3 0.9 copy-start.1
  80.7 2.0 %collective-permute-start.21 = (bf16[512,512]{1,0:T(8,128)(2,1)S(1)}, bf16[512,512]{1,0:T(8,128)(2,1)S(1)}, u32[]{:S(2)}, u32[]{:S(2)}) collective-permute-start(bf16[512,512]{1,0:T(8,128)(2,1)S(1)} %get-tuple-element.9), channel_id=1, source_target_pairs={{0,1},{1,0},{2,3},{3,2},{4,5},{5,4},{6,7},{7,6},{8,9},{9,8},{10,11... | collective-permute-start | bytes 1572872 | tf_op jit(solution)/shard_map/ppermute | solution.py:20
  82.8 10.9 %collective-permute-start.22 = (bf16[128,512]{1,0:T(8,128)(2,1)S(1)}, bf16[128,512]{1,0:T(8,128)(2,1)S(1)}, u32[]{:S(2)}, u32[]{:S(2)}) collective-permute-start(bf16[128,512]{1,0:T(8,128)(2,1)S(1)} %get-tuple-element.12), channel_id=1, source_target_pairs={{0,4},{4,8},{8,12},{12,0},{1,5},{5,9},{9,13},{13,1},{2,6},{6,10},{... | collective-permute-start | bytes 393224 | tf_op jit(solution)/shard_map/ppermute | solution.py:20
  86.0 11.3 %collective-permute-start.23 = (bf16[128,512]{1,0:T(8,128)(2,1)S(1)}, bf16[128,512]{1,0:T(8,128)(2,1)S(1)}, u32[]{:S(2)}, u32[]{:S(2)}) collective-permute-start(bf16[128,512]{1,0:T(8,128)(2,1)S(1)} %get-tuple-element.11), channel_id=1, source_target_pairs={{0,8},{4,12},{8,0},{12,4},{1,9},{5,13},{9,1},{13,5},{2,10},{6,14},... | collective-permute-start | bytes 393224 | tf_op jit(solution)/shard_map/ppermute | solution.py:20
  88.2 9.1 %collective-permute-start.24 = (bf16[128,512]{1,0:T(8,128)(2,1)S(1)}, bf16[128,512]{1,0:T(8,128)(2,1)S(1)}, u32[]{:S(2)}, u32[]{:S(2)}) collective-permute-start(bf16[128,512]{1,0:T(8,128)(2,1)S(1)} %get-tuple-element.10), channel_id=1, source_target_pairs={{0,12},{4,0},{8,4},{12,8},{1,13},{5,1},{9,5},{13,9},{2,14},{6,2},{... | collective-permute-start | bytes 393224 | tf_op jit(solution)/shard_map/ppermute | solution.py:20

commit v3 on v2

--- a/solution.py
+++ b/solution.py
@@ -20,16 +20,10 @@
     return lax.ppermute(value, axis, [(i, (i + amount) % size) for i in range(size)])
 
 
-def fetch(pieces, stacked, sems):
+def stack(pieces, stacked):
     rows = pieces[0].shape[0]
-    copies = [
-        pltpu.make_async_copy(piece, stacked.at[pl.ds(i * rows, rows)], sems.at[i])
-        for i, piece in enumerate(pieces)
-    ]
-    for copy in copies:
-        copy.start()
-    for copy in copies:
-        copy.wait()
+    for i, piece in enumerate(pieces):
+        stacked[i * rows : (i + 1) * rows, :] = piece[...]
 
 
 def spread(values):
@@ -48,12 +42,12 @@
     ins, refs = refs[:n_parts], refs[n_parts:]
     outs, refs = refs[:n_parts], refs[n_parts:]
     partial, refs = refs[:has_partial], refs[has_partial:]
-    results, (stacked, masked, sems) = refs[:-3], refs[-3:]
+    results, (stacked, masked) = refs[:-2], refs[-2:]
     z, s = place_ref[0], place_ref[1]
     rows = pieces[0].shape[0]
     width = ins[0].shape[0]
     per_chunk = NCHUNK // RMAX
-    fetch(pieces, stacked, sems)
+    stack(pieces, stacked)
     lane = lax.broadcasted_iota(jnp.int32, (1, NCHUNK), 1) % RMAX
     for part in range(n_parts):
         for chunk in range(width // NCHUNK):
@@ -109,13 +103,13 @@
         results[0][...] = total
 
 
-def far_field(sizes, place, tables, pieces, ins, outs, partial=None, final=True):
+def far_field(sizes, place, parts, pieces, partial=None, final=True):
+    tables, ins, outs = zip(*parts)
     rows = pieces[0].shape[0]
     n_pieces, n_parts, width = len(pieces), len(ins), ins[0].shape[0]
     n_keep = sizes[0]
     whole = pl.BlockSpec(memory_space=pltpu.VMEM)
     scalars = pl.BlockSpec(memory_space=pltpu.SMEM)
-    anywhere = pl.BlockSpec(memory_space=pl.ANY)
     if final:
         out_shape = (
             jax.ShapeDtypeStruct((n_keep * rows, BLK), BF16),
@@ -130,13 +124,11 @@
         functools.partial(far_kernel, sizes, n_parts, len(partials), final),
         out_shape=out_shape,
         in_specs=[scalars] * (1 + n_parts)
-        + [anywhere] * n_pieces
-        + [whole] * (2 * n_parts + len(partials)),
+        + [whole] * (n_pieces + 2 * n_parts + len(partials)),
         out_specs=(whole,) * len(out_shape),
         scratch_shapes=[
             pltpu.VMEM((n_pieces * rows, BLK), BF16),
             pltpu.VMEM((n_pieces * rows, n_parts * width), BF16),
-            pltpu.SemaphoreType.DMA((n_pieces,)),
         ],
         compiler_params=pltpu.CompilerParams(vmem_limit_bytes=limit),
         cost_estimate=pl.CostEstimate(
@@ -149,81 +141,98 @@
     return out if final else out[0]
 
 
-def near_kernel(n_pieces, per_step, slot_ref, *refs):
-    pieces = refs[:n_pieces]
-    blocks_ref, out_ref, stacked, sems = refs[n_pieces:]
+def near_kernel(n_halves, n_pieces, per_step, slot_ref, *refs):
+    pieces, (blocks_ref, *results, stacked, total) = (
+        refs[: n_halves * n_pieces],
+        refs[n_halves * n_pieces :],
+    )
     rows = pieces[0].shape[0]
     step = pl.program_id(0)
 
     @pl.when(step == 0)
     def _():
-        fetch(pieces, stacked, sems)
-        out_ref[...] = jnp.zeros_like(out_ref)
-
-    total = out_ref[...]
+        for half in range(n_halves):
+            for i in range(n_pieces):
+                stacked[i, half * rows : (half + 1) * rows, :] = pieces[half * n_pieces + i][...]
+        total[...] = jnp.zeros_like(total)
+
+    added = total[...]
     for k in range(per_step):
-        start = pl.multiple_of(slot_ref[step * per_step + k] * rows, rows)
-        total += lax.dot_general(
-            stacked[pl.ds(start, rows), :],
+        added += lax.dot_general(
+            stacked[slot_ref[step * per_step + k]],
             blocks_ref[k],
             CONTRACT_LAST,
             preferred_element_type=F32,
         )
-    out_ref[...] = total
-
-
-def near_field(pieces, near_blocks, slots):
-    rows = pieces[0].shape[0]
-    n_pieces, near = len(pieces), near_blocks.shape[0]
+    total[...] = added
+
+    @pl.when(step == pl.num_programs(0) - 1)
+    def _():
+        for half, result in enumerate(results):
+            result[...] = total[half * rows : (half + 1) * rows, :]
+
+
+def near_field(halves, near_blocks, slots):
+    rows = halves[0][0].shape[0]
+    n_halves, n_pieces, near = len(halves), len(halves[0]), near_blocks.shape[0]
     per_step = 4 if near % 4 == 0 else 1
-    anywhere = pl.BlockSpec(memory_space=pl.ANY)
+    whole = pl.BlockSpec(memory_space=pltpu.VMEM)
     return pl.pallas_call(
-        functools.partial(near_kernel, n_pieces, per_step),
-        out_shape=jax.ShapeDtypeStruct((rows, BLK), F32),
+        functools.partial(near_kernel, n_halves, n_pieces, per_step),
+        out_shape=(jax.ShapeDtypeStruct((rows, BLK), F32),) * n_halves,
         grid_spec=pltpu.PrefetchScalarGridSpec(
             num_scalar_prefetch=1,
             grid=(near // per_step,),
-            in_specs=[anywhere] * n_pieces
+            in_specs=[whole] * (n_halves * n_pieces)
             + [pl.BlockSpec((per_step, BLK, BLK), lambda step, slot: (step, 0, 0))],
-            out_specs=pl.BlockSpec((rows, BLK), lambda step, slot: (0, 0)),
+            out_specs=(whole,) * n_halves,
             scratch_shapes=[
-                pltpu.VMEM((n_pieces * rows, BLK), BF16),
-                pltpu.SemaphoreType.DMA((n_pieces,)),
+                pltpu.VMEM((n_pieces, n_halves * rows, BLK), BF16),
+                pltpu.VMEM((n_halves * rows, BLK), F32),
             ],
         ),
-        compiler_params=pltpu.CompilerParams(vmem_limit_bytes=12 << 20),
+        compiler_params=pltpu.CompilerParams(vmem_limit_bytes=14 << 20),
         cost_estimate=pl.CostEstimate(
-            flops=2 * near * rows * BLK * BLK,
+            flops=2 * near * n_halves * rows * BLK * BLK,
             transcendentals=0,
-            bytes_accessed=2 * BLK * (near * BLK + n_pieces * rows + 2 * rows),
+            bytes_accessed=2 * BLK * near * BLK,
         ),
         name="near_field",
-    )(slots, *pieces, near_blocks)
-
-
-def finish_kernel(n_sums, *refs):
-    sums, (near_ref, jacobi_ref, out_ref) = refs[:n_sums], refs[n_sums:]
+    )(slots, *[piece for half in halves for piece in half], near_blocks)
+
+
+def finish_kernel(n_sums, n_before, *refs):
+    sums, (near_ref, jacobi_ref), refs = refs[:n_sums], refs[n_sums : n_sums + 2], refs[n_sums + 2 :]
+    before, (field_ref, *results) = refs[:n_before], refs[n_before:]
     total = near_ref[...]
     for part in sums:
         total += part[...].astype(F32)
+    rows = total.shape[0]
     field = total.astype(BF16)
     for group in range(jacobi_ref.shape[0]):
         here = slice(group * JB, (group + 1) * JB)
-        out_ref[:, here] = lax.dot_general(
+        field_ref[:, here] = lax.dot_general(
             field[:, here], jacobi_ref[group], CONTRACT_LAST, preferred_element_type=F32
         ).astype(BF16)
-
-
-def finish(sums, near, jacobi_inverse):
+    for result in results:
+        for i, ref in enumerate([*before, field_ref]):
+            result[i * rows : (i + 1) * rows, :] = ref[...]
+
+
+def finish(sums, near, jacobi_inverse, before=(), last=False):
     whole = pl.BlockSpec(memory_space=pltpu.VMEM)
+    rows = near.shape[0]
+    out_shape = [jax.ShapeDtypeStruct(near.shape, BF16)]
+    if last:
+        out_shape.append(jax.ShapeDtypeStruct(((len(before) + 1) * rows, BLK), BF16))
     return pl.pallas_call(
-        functools.partial(finish_kernel, len(sums)),
-        out_shape=jax.ShapeDtypeStruct(near.shape, BF16),
-        in_specs=[whole] * (len(sums) + 2),
-        out_specs=whole,
+        functools.partial(finish_kernel, len(sums), len(before) if last else 0),
+        out_shape=tuple(out_shape),
+        in_specs=[whole] * (len(sums) + 2 + (len(before) if last else 0)),
+        out_specs=(whole,) * len(out_shape),
         compiler_params=pltpu.CompilerParams(vmem_limit_bytes=4 << 20),
         name="finish",
-    )(*sums, near, jacobi_inverse)
+    )(*sums, near, jacobi_inverse, *(before if last else ()))
 
 
 def local(
@@ -242,7 +251,6 @@
 ):
     z = lax.axis_index("tiles")
     s = lax.axis_index("sub")
-    rows = sources.shape[0]
     basis_in = basis_in.reshape(-1, BLK)
     basis_out = basis_out.reshape(-1, BLK)
 
@@ -256,19 +264,19 @@
             pieces += [shifted(piece, "sub", n_sub, e) for piece in along]
         return pieces
 
-    pieces = gather(sources)
+    n_halves = 1
+    rows = sources.shape[0] // n_halves
     numbers = jnp.stack([tile_rank, tile_row, tile_col])
-    ins, outs, tables = [basis_in], [basis_out], [numbers]
-    for d in range(1, n_rhs):
-        tables.append(shifted(numbers, "rhs", n_rhs, d))
-        ins.append(shifted(basis_in, "rhs", n_rhs, d))
-        outs.append(shifted(basis_out, "rhs", n_rhs, d))
+    parts = [(numbers, basis_in, basis_out)]
+    for e in range(1, n_rhs):
+        parts.append(tuple(shifted(array, "rhs", n_rhs, e) for array in parts[0]))
+    halves = [gather(sources[h * rows : (h + 1) * rows]) for h in range(n_halves)]
     sizes = (n_tiles, n_sub)
     place = jnp.stack([z, s])
     near_slots = source_slot(near_col[0])
     near_blocks = near_blocks[0]
 
-    def reduce_and_finish(pieces, keep, send):
+    def exchange(keep, send):
         total = keep.astype(F32)
         for e in range(1, n_sub):
             size = n_tiles * rows
@@ -277,15 +285,26 @@
         for d in range(n_tiles):
             part = total[d * rows : (d + 1) * rows].astype(BF16)
             sums.append(shifted(part, "tiles", n_tiles, d) if d else part)
-        near = near_field(pieces, near_blocks, near_slots)
-        return finish(sums, near, jacobi_inverse)
-
-    partial = far_field(sizes, place, tables[:1], pieces, ins[:1], outs[:1], final=False)
-    keep, send = far_field(sizes, place, tables[1:], pieces, ins[1:], outs[1:], partial=partial)
-    first_result = reduce_and_finish(pieces, keep, send)
-    pieces = gather(first_result)
-    keep, send = far_field(sizes, place, tables, pieces, ins, outs)
-    second_result = reduce_and_finish(pieces, keep, send)
+        return sums
+
+    def finish_all(sums, nears):
+        fields = []
+        for h in range(n_halves):
+            out = finish(sums[h], nears[h], jacobi_inverse, fields, h == n_halves - 1)
+            fields.append(out[0])
+        return fields, out[1]
+
+    nears = near_field(halves, near_blocks, near_slots)
+    partials = [far_field(sizes, place, parts[:1], half, final=False) for half in halves]
+    sums = [
+        exchange(*far_field(sizes, place, parts[1:], half, partial=partial))
+        for half, partial in zip(halves, partials)
+    ]
+    fields, first_result = finish_all(sums, nears)
+    halves = [gather(field) for field in fields]
+    sums = [exchange(*far_field(sizes, place, parts, half)) for half in halves]
+    nears = near_field(halves, near_blocks, near_slots)
+    fields, second_result = finish_all(sums, nears)
     return (first_result, second_result)
 
 

time: 98.9 us -> 95 us (0.961)
  Pallas kernels: 25.5 us -> 18.5 us
  waiting for transfers between devices: 36.6 us -> 40.5 us
    pallas_call x3, Pallas kernels: 13.1 us -> 8.86 us  [far_field(): pl.pallas_call(functools.partial(far_kernel, sizes, n_parts, len(partials...]
    ppermute x25, waiting for transfers between devices: 36.6 us -> 40.5 us  [shifted(): lax.ppermute(value, axis, [(i, (i + amount) % size) for i in range(size)])]
    pallas_call x4, Pallas kernels: 12.3 us -> 9.63 us  [the longest x2 7.81 us: near_field(): pl.pallas_call(functools.partial(near_kernel, n_halves, n_pieces, per_ste...]
    unnamed x20 -> x18, local copies, waits for them, and re-layouts: 5 us -> 4.09 us
  transfers between devices with their start and end apart: 25 -> 25, of which waited for: 12 -> 12; matrix products, arithmetic and copies ran while one was open for 1% -> 1% of each run, Pallas kernels for 15% -> 11%
where the time goes in v3:
time: 95 us; the launch traced here: 94.3 us
  waiting for transfers between devices  40.5 us (43%)
  starting transfers between devices  29.2 us (31%)
  Pallas kernels  18.5 us (19%)
  local copies, waits for them, and re-layouts  4.17 us (4%)
  other arithmetic  1.06 us (1%)
    ppermute x25, waiting for transfers between devices, shifted(): lax.ppermute(value, axis, [(i, (i + amount) % size) for i in range(size)])  40.5 us
    ppermute x25, starting transfers between devices, shifted(): lax.ppermute(value, axis, [(i, (i + amount) % size) for i in range(size)])  29.2 us
    pallas_call x3, Pallas kernels, far_field(): pl.pallas_call(functools.partial(far_kernel, sizes, n_parts, len(partials...  8.86 us
    pallas_call x2, Pallas kernels, near_field(): pl.pallas_call(functools.partial(near_kernel, n_halves, n_pieces, per_ste...  7.81 us
    unnamed x18, local copies, waits for them, and re-layouts  4.09 us
  transfers between devices with their start and end apart: 25, of which 12 were waited for; matrix products, arithmetic and copies ran while one was open for 1% of the time, Pallas kernels for 11%

profile of v3, /device:TPU:0, one launch (start us, length us, event | category | flops | bytes accessed | tf_op | source)
XLA Modules:
  0.0 94.3 jit_solution(3117330036546606849)
XLA Ops:
  0.6 3.0 %collective-permute-start.8 = (bf16[768,512]{1,0:T(8,128)(2,1)}, bf16[768,512]{1,0:T(8,128)(2,1)S(1)}, u32[]{:S(2)}, u32[]{:S(2)}) collective-permute-start(bf16[768,512]{1,0:T(8,128)(2,1)} %bitcast.23), channel_id=1, source_target_pairs={{0,2},{2,0},{1,3},{3,1},{4,6},{6,4},{5,7},{7,5},{8,10},{10,8},{9,1... | collective-permute-start | bytes 2359304 | tf_op jit(solution)/shard_map/ppermute | solution.py:20
  3.6 0.1 collective-permute-start.9
  3.7 2.0 %collective-permute-start.1 = (bf16[128,512]{1,0:T(8,128)(2,1)}, bf16[128,512]{1,0:T(8,128)(2,1)S(1)}, u32[]{:S(2)}, u32[]{:S(2)}) collective-permute-start(bf16[128,512]{1,0:T(8,128)(2,1)} %refs_0_.1), channel_id=1, source_target_pairs={{0,4},{4,8},{8,12},{12,0},{1,5},{5,9},{9,13},{13,1},{2,6},{6,10},{... | collective-permute-start | bytes 393224 | tf_op jit(solution)/shard_map/ppermute | solution.py:20
  5.8 2.6 %collective-permute-start.2 = (bf16[128,512]{1,0:T(8,128)(2,1)}, bf16[128,512]{1,0:T(8,128)(2,1)S(1)}, u32[]{:S(2)}, u32[]{:S(2)}) collective-permute-start(bf16[128,512]{1,0:T(8,128)(2,1)} %refs_0_.1), channel_id=1, source_target_pairs={{0,8},{4,12},{8,0},{12,4},{1,9},{5,13},{9,1},{13,5},{2,10},{6,14},... | collective-permute-start | bytes 393224 | tf_op jit(solution)/shard_map/ppermute | solution.py:20
  8.3 1.3 %collective-permute-start.3 = (bf16[128,512]{1,0:T(8,128)(2,1)}, bf16[128,512]{1,0:T(8,128)(2,1)S(1)}, u32[]{:S(2)}, u32[]{:S(2)}) collective-permute-start(bf16[128,512]{1,0:T(8,128)(2,1)} %refs_0_.1), channel_id=1, source_target_pairs={{0,12},{4,0},{8,4},{12,8},{1,13},{5,1},{9,5},{13,9},{2,14},{6,2},{... | collective-permute-start | bytes 393224 | tf_op jit(solution)/shard_map/ppermute | solution.py:20
  9.7 2.8 %collective-permute-done.1.refs_2_.refs_1_ = bf16[128,512]{1,0:T(8,128)(2,1)S(1)} collective-permute-done((bf16[128,512]{1,0:T(8,128)(2,1)}, bf16[128,512]{1,0:T(8,128)(2,1)S(1)}, u32[]{:S(2)}, u32[]{:S(2)}) %collective-permute-start.1) | collective-permute-done | bytes 131104 | tf_op jit(solution)/shard_map/ppermute | solution.py:20
  12.5 4.1 %collective-permute-done.2.refs_3_.refs_2_ = bf16[128,512]{1,0:T(8,128)(2,1)S(1)} collective-permute-done((bf16[128,512]{1,0:T(8,128)(2,1)}, bf16[128,512]{1,0:T(8,128)(2,1)S(1)}, u32[]{:S(2)}, u32[]{:S(2)}) %collective-permute-start.2) | collective-permute-done | bytes 131104 | tf_op jit(solution)/shard_map/ppermute | solution.py:20
  16.6 0.1 collective-permute-done.3.refs_4_.refs_3_
  16.7 0.5 collective-permute-start.6
  17.2 0.1 collective-permute-start.7
  17.2 0.1 pad_add_fusion.1.place_ref
  17.3 0.7 pad_add_fusion.refs_0_
  18.0 1.6 %collective-permute-start = (s32[3,12]{1,0:T(4,128)S(1)}, s32[3,12]{1,0:T(4,128)S(1)}, u32[]{:S(2)}, u32[]{:S(2)}) collective-permute-start(s32[3,12]{1,0:T(4,128)S(1)} %pad_add_fusion.refs_0_), channel_id=1, source_target_pairs={{0,2},{2,0},{1,3},{3,1},{4,6},{6,4},{5,7},{7,5},{8,10},{10,8},{9,1... | collective-permute-start | bytes 440 | tf_op jit(solution)/shard_map/ppermute | solution.py:20
  19.7 0.9 copy-done.2
  20.6 1.1 %copy-done.4 = bf16[12,64,512]{2,1,0:T(8,128)(2,1)S(1)} copy-done((bf16[12,64,512]{2,1,0:T(8,128)(2,1)S(1)}, bf16[12,64,512]{2,1,0:T(8,128)(2,1)}, u32[]{:S(2)}) %copy-start.4) | copy-done | bytes 786456
  21.7 1.1 %copy-done.6 = bf16[12,64,512]{2,1,0:T(8,128)(2,1)S(1)} copy-done((bf16[12,64,512]{2,1,0:T(8,128)(2,1)S(1)}, bf16[12,64,512]{2,1,0:T(8,128)(2,1)}, u32[]{:S(2)}) %copy-start.6) | copy-done | bytes 786456
  22.8 2.4 %far_field.3.refs_11_ = f32[1024,512]{1,0:T(8,128)S(1)} custom-call(s32[2]{0:T(128)S(1)} %pad_add_fusion.1.place_ref, s32[3,12]{1,0:T(4,128)S(1)} %pad_add_fusion.refs_0_, bf16[128,512]{1,0:T(8,128)(2,1)S(1)} %copy-done.2, bf16[128,512]{1,0:T(8,128)(2,1)S(1)} %collective-permute-done.1.refs_2_.refs_1_, ...), custom_call_target="tpu_custom_call" | custom-call | flops 1610612736 | bytes 3670016 | tf_op jit(solution)/shard_map/far_field/pallas_call | solution.py:123
  25.2 0.0 copy-start.1
  25.2 13.1 %collective-permute-done.refs_0_.refs_1_ = s32[3,12]{1,0:T(4,128)S(1)} collective-permute-done((s32[3,12]{1,0:T(4,128)S(1)}, s32[3,12]{1,0:T(4,128)S(1)}, u32[]{:S(2)}, u32[]{:S(2)}) %collective-permute-start) | collective-permute-done | bytes 176 | tf_op jit(solution)/shard_map/ppermute | solution.py:20
  38.3 0.9 copy-done.3
  39.2 2.4 %far_field.4 = (bf16[512,512]{1,0:T(8,128)(2,1)S(1)}, bf16[512,512]{1,0:T(8,128)(2,1)S(1)}) custom-call(s32[2]{0:T(128)S(1)} %pad_add_fusion.1.place_ref, s32[3,12]{1,0:T(4,128)S(1)} %collective-permute-done.refs_0_.refs_1_, bf16[128,512]{1,0:T(8,128)(2,1)S(1)} %copy-done.3, bf16[128,512]{1,0:T(8,128)(2,1)S(1)} %collective-permute-done.1.refs_2_.refs_1_, ...), custom_call_target="tpu_custom_call" | custom-call | flops 1610612736 | bytes 3670016 | tf_op jit(solution)/shard_map/far_field/pallas_call | solution.py:123
  41.6 0.1 collective-permute-start.10
  41.7 1.9 %collective-permute-done.10 = bf16[512,512]{1,0:T(8,128)(2,1)S(1)} collective-permute-done((bf16[512,512]{1,0:T(8,128)(2,1)S(1)}, bf16[512,512]{1,0:T(8,128)(2,1)S(1)}, u32[]{:S(2)}, u32[]{:S(2)}) %collective-permute-start.10) | collective-permute-done | bytes 524320 | tf_op jit(solution)/shard_map/ppermute | solution.py:20
  43.6 0.1 add_convert_fusion.1
  43.8 1.9 %collective-permute-start.11 = (bf16[128,512]{1,0:T(8,128)(2,1)S(1)}, bf16[128,512]{1,0:T(8,128)(2,1)S(1)}, u32[]{:S(2)}, u32[]{:S(2)}) collective-permute-start(bf16[128,512]{1,0:T(8,128)(2,1)S(1)} %get-tuple-element.22), channel_id=1, source_target_pairs={{0,4},{4,8},{8,12},{12,0},{1,5},{5,9},{9,13},{13,1},{2,6},{6,10},{... | collective-permute-start | bytes 393224 | tf_op jit(solution)/shard_map/ppermute | solution.py:20
  45.6 2.6 %collective-permute-start.12 = (bf16[128,512]{1,0:T(8,128)(2,1)S(1)}, bf16[128,512]{1,0:T(8,128)(2,1)S(1)}, u32[]{:S(2)}, u32[]{:S(2)}) collective-permute-start(bf16[128,512]{1,0:T(8,128)(2,1)S(1)} %get-tuple-element.21), channel_id=1, source_target_pairs={{0,8},{4,12},{8,0},{12,4},{1,9},{5,13},{9,1},{13,5},{2,10},{6,14},... | collective-permute-start | bytes 393224 | tf_op jit(solution)/shard_map/ppermute | solution.py:20
  48.2 1.3 %collective-permute-start.13 = (bf16[128,512]{1,0:T(8,128)(2,1)S(1)}, bf16[128,512]{1,0:T(8,128)(2,1)S(1)}, u32[]{:S(2)}, u32[]{:S(2)}) collective-permute-start(bf16[128,512]{1,0:T(8,128)(2,1)S(1)} %get-tuple-element.20), channel_id=1, source_target_pairs={{0,12},{4,0},{8,4},{12,8},{1,13},{5,1},{9,5},{13,9},{2,14},{6,2},{... | collective-permute-start | bytes 393224 | tf_op jit(solution)/shard_map/ppermute | solution.py:20
  49.6 3.9 %near_field.2.refs_4_ = f32[128,512]{1,0:T(8,128)S(1)} custom-call(s32[16]{0:T(128)S(1)} %fusion.slot_ref, bf16[128,512]{1,0:T(8,128)(2,1)S(1)} %copy-done.3, bf16[128,512]{1,0:T(8,128)(2,1)S(1)} %collective-permute-done.1.refs_2_.refs_1_, bf16[128,512]{1,0:T(8,128)(2,1)S(1)} %collective-permute-done.2.refs_3_.refs_2_, ...), custom_call_target="tpu_custom_call" | custom-call | flops 1073741824 | bytes 8388608 | tf_op jit(solution)/shard_map/near_field/pallas_call | solution.py:180
  53.5 3.6 %collective-permute-done.12.refs_2_ = bf16[128,512]{1,0:T(8,128)(2,1)S(1)} collective-permute-done((bf16[128,512]{1,0:T(8,128)(2,1)S(1)}, bf16[128,512]{1,0:T(8,128)(2,1)S(1)}, u32[]{:S(2)}, u32[]{:S(2)}) %collective-permute-start.12) | collective-permute-done | bytes 131104 | tf_op jit(solution)/shard_map/ppermute | solution.py:20
  57.2 0.9 finish.2
  58.1 3.3 %collective-permute-start.14 = (bf16[128,512]{1,0:T(8,128)(2,1)S(1)}, bf16[128,512]{1,0:T(8,128)(2,1)S(1)}, u32[]{:S(2)}, u32[]{:S(2)}) collective-permute-start(bf16[128,512]{1,0:T(8,128)(2,1)S(1)} %get-tuple-element.12.refs_2_.refs_0_), channel_id=1, source_target_pairs={{0,4},{4,8},{8,12},{12,0},{1,5},{5,9},{9,13},{13,1},{2,6},{6,10},{... | collective-permute-start | bytes 393224 | tf_op jit(solution)/shard_map/ppermute | solution.py:20
  61.4 1.6 %collective-permute-start.15 = (bf16[128,512]{1,0:T(8,128)(2,1)S(1)}, bf16[128,512]{1,0:T(8,128)(2,1)S(1)}, u32[]{:S(2)}, u32[]{:S(2)}) collective-permute-start(bf16[128,512]{1,0:T(8,128)(2,1)S(1)} %get-tuple-element.12.refs_2_.refs_0_), channel_id=1, source_target_pairs={{0,8},{4,12},{8,0},{12,4},{1,9},{5,13},{9,1},{13,5},{2,10},{6,14},... | collective-permute-start | bytes 393224 | tf_op jit(solution)/shard_map/ppermute | solution.py:20
  63.0 0.7 collective-permute-start.16
  63.7 2.8 %collective-permute-done.14.refs_3_.refs_1_ = bf16[128,512]{1,0:T(8,128)(2,1)S(1)} collective-permute-done((bf16[128,512]{1,0:T(8,128)(2,1)S(1)}, bf16[128,512]{1,0:T(8,128)(2,1)S(1)}, u32[]{:S(2)}, u32[]{:S(2)}) %collective-permute-start.14) | collective-permute-done | bytes 131104 | tf_op jit(solution)/shard_map/ppermute | solution.py:20
  66.6 4.5 %collective-permute-done.15.refs_4_.refs_2_ = bf16[128,512]{1,0:T(8,128)(2,1)S(1)} collective-permute-done((bf16[128,512]{1,0:T(8,128)(2,1)S(1)}, bf16[128,512]{1,0:T(8,128)(2,1)S(1)}, u32[]{:S(2)}, u32[]{:S(2)}) %collective-permute-start.15) | collective-permute-done | bytes 131104 | tf_op jit(solution)/shard_map/ppermute | solution.py:20
  71.1 0.5 collective-permute-start.20
  71.6 0.8 collective-permute-done.19.refs_8_.refs_6_
  72.4 0.2 collective-permute-done.20.refs_9_.refs_7_
  72.6 4.1 %far_field.5 = (bf16[512,512]{1,0:T(8,128)(2,1)S(1)}, bf16[512,512]{1,0:T(8,128)(2,1)S(1)}) custom-call(s32[2]{0:T(128)S(1)} %pad_add_fusion.1.place_ref, s32[3,12]{1,0:T(4,128)S(1)} %pad_add_fusion.refs_0_, s32[3,12]{1,0:T(4,128)S(1)} %collective-permute-done.refs_0_.refs_1_, bf16[128,512]{1,0:T(8,128)(2,1)S(1)} %get-tuple-element.12.refs_2_.refs_0_, ...), custom_call_target="tpu_custom_call" | custom-call | flops 3221225472 | bytes 5242880 | tf_op jit(solution)/shard_map/far_field/pallas_call | solution.py:123
  76.7 0.4 collective-permute-start.21
  77.1 1.6 %collective-permute-done.21 = bf16[512,512]{1,0:T(8,128)(2,1)S(1)} collective-permute-done((bf16[512,512]{1,0:T(8,128)(2,1)S(1)}, bf16[512,512]{1,0:T(8,128)(2,1)S(1)}, u32[]{:S(2)}, u32[]{:S(2)}) %collective-permute-start.21) | collective-permute-done | bytes 524320 | tf_op jit(solution)/shard_map/ppermute | solution.py:20
  78.7 0.1 add_convert_fusion
  78.9 3.1 %collective-permute-start.22 = (bf16[128,512]{1,0:T(8,128)(2,1)S(1)}, bf16[128,512]{1,0:T(8,128)(2,1)S(1)}, u32[]{:S(2)}, u32[]{:S(2)}) collective-permute-start(bf16[128,512]{1,0:T(8,128)(2,1)S(1)} %get-tuple-element.18), channel_id=1, source_target_pairs={{0,4},{4,8},{8,12},{12,0},{1,5},{5,9},{9,13},{13,1},{2,6},{6,10},{... | collective-permute-start | bytes 393224 | tf_op jit(solution)/shard_map/ppermute | solution.py:20
  82.0 2.2 %collective-permute-start.23 = (bf16[128,512]{1,0:T(8,128)(2,1)S(1)}, bf16[128,512]{1,0:T(8,128)(2,1)S(1)}, u32[]{:S(2)}, u32[]{:S(2)}) collective-permute-start(bf16[128,512]{1,0:T(8,128)(2,1)S(1)} %get-tuple-element.17), channel_id=1, source_target_pairs={{0,8},{4,12},{8,0},{12,4},{1,9},{5,13},{9,1},{13,5},{2,10},{6,14},... | collective-permute-start | bytes 393224 | tf_op jit(solution)/shard_map/ppermute | solution.py:20
  84.2 0.2 collective-permute-start.24
  84.5 3.9 %near_field.3.refs_4_ = f32[128,512]{1,0:T(8,128)S(1)} custom-call(s32[16]{0:T(128)S(1)} %fusion.slot_ref, bf16[128,512]{1,0:T(8,128)(2,1)S(1)} %get-tuple-element.12.refs_2_.refs_0_, bf16[128,512]{1,0:T(8,128)(2,1)S(1)} %collective-permute-done.14.refs_3_.refs_1_, bf16[128,512]{1,0:T(8,128)(2,1)S(1)} %collective-permute-done.15.refs_4_.refs_2_, ...), custom_call_target="tpu_custom_call" | custom-call | flops 1073741824 | bytes 8388608 | tf_op jit(solution)/shard_map/near_field/pallas_call | solution.py:180
  88.4 5.0 %collective-permute-done.23.refs_2_ = bf16[128,512]{1,0:T(8,128)(2,1)S(1)} collective-permute-done((bf16[128,512]{1,0:T(8,128)(2,1)S(1)}, bf16[128,512]{1,0:T(8,128)(2,1)S(1)}, u32[]{:S(2)}, u32[]{:S(2)}) %collective-permute-start.23) | collective-permute-done | bytes 131104 | tf_op jit(solution)/shard_map/ppermute | solution.py:20
  93.4 0.9 finish.3
  (34 shorter events, 0.2 us)
Async XLA Ops:
  0.6 49.0 %copy-start.8 = (s32[1,16]{1,0:T(1,128)S(1)}, s32[1,16]{1,0:T(1,128)}, u32[]{:S(2)}) copy-start(s32[1,16]{1,0:T(1,128)} %param.16) | copy-start | bytes 196
  0.6 37.7 %collective-permute-start.8 = (bf16[768,512]{1,0:T(8,128)(2,1)}, bf16[768,512]{1,0:T(8,128)(2,1)S(1)}, u32[]{:S(2)}, u32[]{:S(2)}) collective-permute-start(bf16[768,512]{1,0:T(8,128)(2,1)} %bitcast.23), channel_id=1, source_target_pairs={{0,2},{2,0},{1,3},{3,1},{4,6},{6,4},{5,7},{7,5},{8,10},{10,8},{9,1... | collective-permute-start | bytes 2359304 | tf_op jit(solution)/shard_map/ppermute | solution.py:20
  3.6 34.7 %collective-permute-start.9 = (bf16[768,512]{1,0:T(8,128)(2,1)}, bf16[768,512]{1,0:T(8,128)(2,1)S(1)}, u32[]{:S(2)}, u32[]{:S(2)}) collective-permute-start(bf16[768,512]{1,0:T(8,128)(2,1)} %bitcast.26), channel_id=1, source_target_pairs={{0,2},{2,0},{1,3},{3,1},{4,6},{6,4},{5,7},{7,5},{8,10},{10,8},{9,1... | collective-permute-start | bytes 2359304 | tf_op jit(solution)/shard_map/ppermute | solution.py:20
  3.7 8.8 %collective-permute-start.1 = (bf16[128,512]{1,0:T(8,128)(2,1)}, bf16[128,512]{1,0:T(8,128)(2,1)S(1)}, u32[]{:S(2)}, u32[]{:S(2)}) collective-permute-start(bf16[128,512]{1,0:T(8,128)(2,1)} %refs_0_.1), channel_id=1, source_target_pairs={{0,4},{4,8},{8,12},{12,0},{1,5},{5,9},{9,13},{13,1},{2,6},{6,10},{... | collective-permute-start | bytes 393224 | tf_op jit(solution)/shard_map/ppermute | solution.py:20
  5.8 10.9 %collective-permute-start.2 = (bf16[128,512]{1,0:T(8,128)(2,1)}, bf16[128,512]{1,0:T(8,128)(2,1)S(1)}, u32[]{:S(2)}, u32[]{:S(2)}) collective-permute-start(bf16[128,512]{1,0:T(8,128)(2,1)} %refs_0_.1), channel_id=1, source_target_pairs={{0,8},{4,12},{8,0},{12,4},{1,9},{5,13},{9,1},{13,5},{2,10},{6,14},... | collective-permute-start | bytes 393224 | tf_op jit(solution)/shard_map/ppermute | solution.py:20
  8.3 8.4 %collective-permute-start.3 = (bf16[128,512]{1,0:T(8,128)(2,1)}, bf16[128,512]{1,0:T(8,128)(2,1)S(1)}, u32[]{:S(2)}, u32[]{:S(2)}) collective-permute-start(bf16[128,512]{1,0:T(8,128)(2,1)} %refs_0_.1), channel_id=1, source_target_pairs={{0,12},{4,0},{8,4},{12,8},{1,13},{5,1},{9,5},{13,9},{2,14},{6,2},{... | collective-permute-start | bytes 393224 | tf_op jit(solution)/shard_map/ppermute | solution.py:20
  12.5 4.6 %collective-permute-start.4 = (bf16[128,512]{1,0:T(8,128)(2,1)}, bf16[128,512]{1,0:T(8,128)(2,1)S(1)}, u32[]{:S(2)}, u32[]{:S(2)}) collective-permute-start(bf16[128,512]{1,0:T(8,128)(2,1)} %refs_0_.1), channel_id=1, source_target_pairs={{0,1},{1,0},{2,3},{3,2},{4,5},{5,4},{6,7},{7,6},{8,9},{9,8},{10,11... | collective-permute-start | bytes 393224 | tf_op jit(solution)/shard_map/ppermute | solution.py:20
  12.5 37.1 %copy-start = (bf16[1,16,512,512]{3,2,1,0:T(8,128)(2,1)S(1)}, bf16[1,16,512,512]{3,2,1,0:T(8,128)(2,1)}, u32[]{:S(2)}) copy-start(bf16[1,16,512,512]{3,2,1,0:T(8,128)(2,1)} %param.15) | copy-start | bytes 25165828
  16.6 1.4 %collective-permute-start.5 = (bf16[128,512]{1,0:T(8,128)(2,1)S(1)}, bf16[128,512]{1,0:T(8,128)(2,1)S(1)}, u32[]{:S(2)}, u32[]{:S(2)}) collective-permute-start(bf16[128,512]{1,0:T(8,128)(2,1)S(1)} %collective-permute-done.1.refs_2_.refs_1_), channel_id=1, source_target_pairs={{0,1},{1,0},{2,3},{3,2},{4,5},{5,4},{6,7},{7,6},{8,9},{9,8},{10,11... | collective-permute-start | bytes 393224 | tf_op jit(solution)/shard_map/ppermute | solution.py:20
  16.7 3.0 %collective-permute-start.6 = (bf16[128,512]{1,0:T(8,128)(2,1)S(1)}, bf16[128,512]{1,0:T(8,128)(2,1)S(1)}, u32[]{:S(2)}, u32[]{:S(2)}) collective-permute-start(bf16[128,512]{1,0:T(8,128)(2,1)S(1)} %collective-permute-done.2.refs_3_.refs_2_), channel_id=1, source_target_pairs={{0,1},{1,0},{2,3},{3,2},{4,5},{5,4},{6,7},{7,6},{8,9},{9,8},{10,11... | collective-permute-start | bytes 393224 | tf_op jit(solution)/shard_map/ppermute | solution.py:20
  17.2 2.5 %collective-permute-start.7 = (bf16[128,512]{1,0:T(8,128)(2,1)S(1)}, bf16[128,512]{1,0:T(8,128)(2,1)S(1)}, u32[]{:S(2)}, u32[]{:S(2)}) collective-permute-start(bf16[128,512]{1,0:T(8,128)(2,1)S(1)} %collective-permute-done.3.refs_4_.refs_3_), channel_id=1, source_target_pairs={{0,1},{1,0},{2,3},{3,2},{4,5},{5,4},{6,7},{7,6},{8,9},{9,8},{10,11... | collective-permute-start | bytes 393224 | tf_op jit(solution)/shard_map/ppermute | solution.py:20
  18.0 20.3 %collective-permute-start = (s32[3,12]{1,0:T(4,128)S(1)}, s32[3,12]{1,0:T(4,128)S(1)}, u32[]{:S(2)}, u32[]{:S(2)}) collective-permute-start(s32[3,12]{1,0:T(4,128)S(1)} %pad_add_fusion.refs_0_), channel_id=1, source_target_pairs={{0,2},{2,0},{1,3},{3,1},{4,6},{6,4},{5,7},{7,5},{8,10},{10,8},{9,1... | collective-permute-start | bytes 440 | tf_op jit(solution)/shard_map/ppermute | solution.py:20
  19.7 0.9 copy-start.2
  20.6 1.1 %copy-start.4 = (bf16[12,64,512]{2,1,0:T(8,128)(2,1)S(1)}, bf16[12,64,512]{2,1,0:T(8,128)(2,1)}, u32[]{:S(2)}) copy-start(bf16[12,64,512]{2,1,0:T(8,128)(2,1)} %param.11) | copy-start | bytes 2359300
  21.7 1.1 %copy-start.6 = (bf16[12,64,512]{2,1,0:T(8,128)(2,1)S(1)}, bf16[12,64,512]{2,1,0:T(8,128)(2,1)}, u32[]{:S(2)}) copy-start(bf16[12,64,512]{2,1,0:T(8,128)(2,1)} %param.10) | copy-start | bytes 2359300
  25.2 32.0 %copy-start.1 = (bf16[4,128,128]{2,1,0:T(8,128)(2,1)S(1)}, bf16[4,128,128]{2,1,0:T(8,128)(2,1)}, u32[]{:S(2)}) copy-start(bf16[4,128,128]{2,1,0:T(8,128)(2,1)} %refs_5_.3) | copy-start | bytes 393220
  38.3 0.9 copy-start.3
  39.2 33.4 %copy-start.5 = (bf16[12,64,512]{2,1,0:T(8,128)(2,1)S(1)}, bf16[12,64,512]{2,1,0:T(8,128)(2,1)}, u32[]{:S(2)}) copy-start(bf16[12,64,512]{2,1,0:T(8,128)(2,1)} %param.11) | copy-start | bytes 2359300
  39.2 33.4 %copy-start.7 = (bf16[12,64,512]{2,1,0:T(8,128)(2,1)S(1)}, bf16[12,64,512]{2,1,0:T(8,128)(2,1)}, u32[]{:S(2)}) copy-start(bf16[12,64,512]{2,1,0:T(8,128)(2,1)} %param.10) | copy-start | bytes 2359300
  41.6 2.0 %collective-permute-start.10 = (bf16[512,512]{1,0:T(8,128)(2,1)S(1)}, bf16[512,512]{1,0:T(8,128)(2,1)S(1)}, u32[]{:S(2)}, u32[]{:S(2)}) collective-permute-start(bf16[512,512]{1,0:T(8,128)(2,1)S(1)} %get-tuple-element.10), channel_id=1, source_target_pairs={{0,1},{1,0},{2,3},{3,2},{4,5},{5,4},{6,7},{7,6},{8,9},{9,8},{10,11... | collective-permute-start | bytes 1572872 | tf_op jit(solution)/shard_map/ppermute | solution.py:20
  43.8 9.8 %collective-permute-start.11 = (bf16[128,512]{1,0:T(8,128)(2,1)S(1)}, bf16[128,512]{1,0:T(8,128)(2,1)S(1)}, u32[]{:S(2)}, u32[]{:S(2)}) collective-permute-start(bf16[128,512]{1,0:T(8,128)(2,1)S(1)} %get-tuple-element.22), channel_id=1, source_target_pairs={{0,4},{4,8},{8,12},{12,0},{1,5},{5,9},{9,13},{13,1},{2,6},{6,10},{... | collective-permute-start | bytes 393224 | tf_op jit(solution)/shard_map/ppermute | solution.py:20
  45.6 11.5 %collective-permute-start.12 = (bf16[128,512]{1,0:T(8,128)(2,1)S(1)}, bf16[128,512]{1,0:T(8,128)(2,1)S(1)}, u32[]{:S(2)}, u32[]{:S(2)}) collective-permute-start(bf16[128,512]{1,0:T(8,128)(2,1)S(1)} %get-tuple-element.21), channel_id=1, source_target_pairs={{0,8},{4,12},{8,0},{12,4},{1,9},{5,13},{9,1},{13,5},{2,10},{6,14},... | collective-permute-start | bytes 393224 | tf_op jit(solution)/shard_map/ppermute | solution.py:20
  48.2 8.9 %collective-permute-start.13 = (bf16[128,512]{1,0:T(8,128)(2,1)S(1)}, bf16[128,512]{1,0:T(8,128)(2,1)S(1)}, u32[]{:S(2)}, u32[]{:S(2)}) collective-permute-start(bf16[128,512]{1,0:T(8,128)(2,1)S(1)} %get-tuple-element.20), channel_id=1, source_target_pairs={{0,12},{4,0},{8,4},{12,8},{1,13},{5,1},{9,5},{13,9},{2,14},{6,2},{... | collective-permute-start | bytes 393224 | tf_op jit(solution)/shard_map/ppermute | solution.py:20
  58.1 8.5 %collective-permute-start.14 = (bf16[128,512]{1,0:T(8,128)(2,1)S(1)}, bf16[128,512]{1,0:T(8,128)(2,1)S(1)}, u32[]{:S(2)}, u32[]{:S(2)}) collective-permute-start(bf16[128,512]{1,0:T(8,128)(2,1)S(1)} %get-tuple-element.12.refs_2_.refs_0_), channel_id=1, source_target_pairs={{0,4},{4,8},{8,12},{12,0},{1,5},{5,9},{9,13},{13,1},{2,6},{6,10},{... | collective-permute-start | bytes 393224 | tf_op jit(solution)/shard_map/ppermute | solution.py:20
  61.4 9.7 %collective-permute-start.15 = (bf16[128,512]{1,0:T(8,128)(2,1)S(1)}, bf16[128,512]{1,0:T(8,128)(2,1)S(1)}, u32[]{:S(2)}, u32[]{:S(2)}) collective-permute-start(bf16[128,512]{1,0:T(8,128)(2,1)S(1)} %get-tuple-element.12.refs_2_.refs_0_), channel_id=1, source_target_pairs={{0,8},{4,12},{8,0},{12,4},{1,9},{5,13},{9,1},{13,5},{2,10},{6,14},... | collective-permute-start | bytes 393224 | tf_op jit(solution)/shard_map/ppermute | solution.py:20
  63.0 8.1 %collective-permute-start.16 = (bf16[128,512]{1,0:T(8,128)(2,1)S(1)}, bf16[128,512]{1,0:T(8,128)(2,1)S(1)}, u32[]{:S(2)}, u32[]{:S(2)}) collective-permute-start(bf16[128,512]{1,0:T(8,128)(2,1)S(1)} %get-tuple-element.12.refs_2_.refs_0_), channel_id=1, source_target_pairs={{0,12},{4,0},{8,4},{12,8},{1,13},{5,1},{9,5},{13,9},{2,14},{6,2},{... | collective-permute-start | bytes 393224 | tf_op jit(solution)/shard_map/ppermute | solution.py:20
  63.7 7.9 %collective-permute-start.17 = (bf16[128,512]{1,0:T(8,128)(2,1)S(1)}, bf16[128,512]{1,0:T(8,128)(2,1)S(1)}, u32[]{:S(2)}, u32[]{:S(2)}) collective-permute-start(bf16[128,512]{1,0:T(8,128)(2,1)S(1)} %get-tuple-element.12.refs_2_.refs_0_), channel_id=1, source_target_pairs={{0,1},{1,0},{2,3},{3,2},{4,5},{5,4},{6,7},{7,6},{8,9},{9,8},{10,11... | collective-permute-start | bytes 393224 | tf_op jit(solution)/shard_map/ppermute | solution.py:20
  66.6 5.1 %collective-permute-start.18 = (bf16[128,512]{1,0:T(8,128)(2,1)S(1)}, bf16[128,512]{1,0:T(8,128)(2,1)S(1)}, u32[]{:S(2)}, u32[]{:S(2)}) collective-permute-start(bf16[128,512]{1,0:T(8,128)(2,1)S(1)} %collective-permute-done.14.refs_3_.refs_1_), channel_id=1, source_target_pairs={{0,1},{1,0},{2,3},{3,2},{4,5},{5,4},{6,7},{7,6},{8,9},{9,8},{10,11... | collective-permute-start | bytes 393224 | tf_op jit(solution)/shard_map/ppermute | solution.py:20
  71.1 1.3 %collective-permute-start.19 = (bf16[128,512]{1,0:T(8,128)(2,1)S(1)}, bf16[128,512]{1,0:T(8,128)(2,1)S(1)}, u32[]{:S(2)}, u32[]{:S(2)}) collective-permute-start(bf16[128,512]{1,0:T(8,128)(2,1)S(1)} %collective-permute-done.15.refs_4_.refs_2_), channel_id=1, source_target_pairs={{0,1},{1,0},{2,3},{3,2},{4,5},{5,4},{6,7},{7,6},{8,9},{9,8},{10,11... | collective-permute-start | bytes 393224 | tf_op jit(solution)/shard_map/ppermute | solution.py:20
  71.1 1.5 %collective-permute-start.20 = (bf16[128,512]{1,0:T(8,128)(2,1)S(1)}, bf16[128,512]{1,0:T(8,128)(2,1)S(1)}, u32[]{:S(2)}, u32[]{:S(2)}) collective-permute-start(bf16[128,512]{1,0:T(8,128)(2,1)S(1)} %collective-permute-done.16.refs_5_.refs_3_), channel_id=1, source_target_pairs={{0,1},{1,0},{2,3},{3,2},{4,5},{5,4},{6,7},{7,6},{8,9},{9,8},{10,11... | collective-permute-start | bytes 393224 | tf_op jit(solution)/shard_map/ppermute | solution.py:20
  76.7 2.0 %collective-permute-start.21 = (bf16[512,512]{1,0:T(8,128)(2,1)S(1)}, bf16[512,512]{1,0:T(8,128)(2,1)S(1)}, u32[]{:S(2)}, u32[]{:S(2)}) collective-permute-start(bf16[512,512]{1,0:T(8,128)(2,1)S(1)} %get-tuple-element.14), channel_id=1, source_target_pairs={{0,1},{1,0},{2,3},{3,2},{4,5},{5,4},{6,7},{7,6},{8,9},{9,8},{10,11... | collective-permute-start | bytes 1572872 | tf_op jit(solution)/shard_map/ppermute | solution.py:20
  78.9 9.5 %collective-permute-start.22 = (bf16[128,512]{1,0:T(8,128)(2,1)S(1)}, bf16[128,512]{1,0:T(8,128)(2,1)S(1)}, u32[]{:S(2)}, u32[]{:S(2)}) collective-permute-start(bf16[128,512]{1,0:T(8,128)(2,1)S(1)} %get-tuple-element.18), channel_id=1, source_target_pairs={{0,4},{4,8},{8,12},{12,0},{1,5},{5,9},{9,13},{13,1},{2,6},{6,10},{... | collective-permute-start | bytes 393224 | tf_op jit(solution)/shard_map/ppermute | solution.py:20
  82.0 11.3 %collective-permute-start.23 = (bf16[128,512]{1,0:T(8,128)(2,1)S(1)}, bf16[128,512]{1,0:T(8,128)(2,1)S(1)}, u32[]{:S(2)}, u32[]{:S(2)}) collective-permute-start(bf16[128,512]{1,0:T(8,128)(2,1)S(1)} %get-tuple-element.17), channel_id=1, source_target_pairs={{0,8},{4,12},{8,0},{12,4},{1,9},{5,13},{9,1},{13,5},{2,10},{6,14},... | collective-permute-start | bytes 393224 | tf_op jit(solution)/shard_map/ppermute | solution.py:20
  84.2 9.1 %collective-permute-start.24 = (bf16[128,512]{1,0:T(8,128)(2,1)S(1)}, bf16[128,512]{1,0:T(8,128)(2,1)S(1)}, u32[]{:S(2)}, u32[]{:S(2)}) collective-permute-start(bf16[128,512]{1,0:T(8,128)(2,1)S(1)} %get-tuple-element.16), channel_id=1, source_target_pairs={{0,12},{4,0},{8,4},{12,8},{1,13},{5,1},{9,5},{13,9},{2,14},{6,2},{... | collective-permute-start | bytes 393224 | tf_op jit(solution)/shard_map/ppermute | solution.py:20

commit v4 on v0

v4 whole, which is shorter than its diff:
```python
import functools

import jax
import jax.numpy as jnp
from jax import lax
from jax.experimental import pallas as pl
from jax.experimental.pallas import tpu as pltpu
from jax.sharding import PartitionSpec as P

BLK = 512
RMAX = 64
JOIN = 10
EARLY = 10
JB = 128
NCHUNK = 256
BF16 = jnp.bfloat16
F32 = jnp.float32


def hint(us):
    return pl.CostEstimate(flops=int(us * 1e9) + 1, transcendentals=0, bytes_accessed=1)


CONTRACT_LAST = (((1,), (1,)), ((), ()))


def shifted(value, axis, size, amount):
    return lax.ppermute(value, axis, [(i, (i + amount) % size) for i in range(size)])


def on_chip(kernel, scalars, arrays, out_shapes, scratch, cost, limit, name):
    scalars, scalar_tree = jax.tree.flatten(scalars)
    arrays, array_tree = jax.tree.flatten(arrays)
    n_scalars, n_in, n_out = len(scalars), len(arrays), len(out_shapes)
    whole = pl.BlockSpec(memory_space=pltpu.VMEM)
    in_smem = pl.BlockSpec(memory_space=pltpu.SMEM)

    def body(*refs):
        numbers = jax.tree.unflatten(scalar_tree, refs[:n_scalars])
        inputs = jax.tree.unflatten(array_tree, refs[n_scalars : n_scalars + n_in])
        rest = refs[n_scalars + n_in :]
        kernel(numbers, inputs, rest[:n_out], rest[n_out:])

    moved = sum(a.size * a.dtype.itemsize for a in [*arrays, *out_shapes])
    return pl.pallas_call(
        body,
        out_shape=tuple(out_shapes),
        in_specs=[in_smem] * n_scalars + [whole] * n_in,
        out_specs=(whole,) * n_out,
        scratch_shapes=scratch,
        compiler_params=pltpu.CompilerParams(vmem_limit_bytes=limit + moved),
        cost_estimate=hint(cost),
        name=name,
    )(*scalars, *arrays)


def stack(pieces, stacked):
    rows = pieces[0].shape[0]
    for i, piece in enumerate(pieces):
        stacked[i * rows : (i + 1) * rows, :] = piece[...]


def spread(values):
    tile = lax.broadcasted_iota(jnp.int32, (1, NCHUNK), 1) // RMAX
    out = jnp.full((1, NCHUNK), values[0], jnp.int32)
    for i, value in enumerate(values[1:], 1):
        out = jnp.where(tile == i, value, out)
    return out


def slots_of(place, table, tiles, sizes):
    n_tiles, n_sub = sizes
    z, s = place[0], place[1]
    lane = lax.broadcasted_iota(jnp.int32, (1, NCHUNK), 1) % RMAX
    column = spread(
        [
            lax.rem(s + n_sub - lax.rem(table[2, t], n_sub), n_sub) * n_tiles
            + lax.rem(z + n_tiles - lax.div(table[2, t], n_sub), n_tiles)
            for t in tiles
        ]
    )
    target = spread(
        [
            lax.rem(lax.rem(table[1, t], n_sub) + n_sub - s, n_sub) * n_tiles
            + lax.rem(lax.div(table[1, t], n_sub) + n_tiles - z, n_tiles)
            for t in tiles
        ]
    )
    return column, jnp.where(lane < spread([table[0, t] for t in tiles]), target, -1)


def first_stage(numbers, sizes, stacked, ins, lanes, previous, coeff, masked):
    place, tables = numbers
    n_pieces = sizes[0] * sizes[1]
    rows = stacked.shape[0] // n_pieces
    first = 0
    for table, basis in zip(tables, ins):
        for start in range(0, basis.shape[0], NCHUNK):
            tiles = range(start // RMAX, (start + NCHUNK) // RMAX)
            column, target = slots_of(place, table, tiles, sizes)
            products = lax.dot_general(
                stacked[...],
                basis[start : start + NCHUNK, lanes],
                CONTRACT_LAST,
                preferred_element_type=F32,
            )
            chosen = products[:rows]
            for piece in range(1, n_pieces):
                chosen = jnp.where(
                    column == piece, products[piece * rows : (piece + 1) * rows], chosen
                )
            there = slice(first, first + NCHUNK)
            if previous is not None:
                chosen = chosen + previous[:, there]
            if coeff is not None:
                coeff[:, there] = chosen
            if masked is not None:
                for piece in range(n_pieces):
                    masked[piece * rows : (piece + 1) * rows, there] = jnp.where(
                        target == piece, chosen, 0.0
                    ).astype(BF16)
            first += NCHUNK


def second_stage(masked, outs, lanes, total):
    first = 0
    for basis in outs:
        values = basis[...] if basis.shape[1] == lanes.stop - lanes.start else basis[:, lanes]
        added = jnp.dot(
            masked[:, first : first + basis.shape[0]], values, preferred_element_type=F32
        )
        total = added if total is None else total + added
        first += basis.shape[0]
    return total


def split_sums(total, keep_ref, send_ref, lanes):
    kept = keep_ref.shape[0]
    total = total.astype(BF16)
    keep_ref[:, lanes] = total[:kept]
    send_ref[:, lanes] = total[kept:]


def opening_kernel(sizes, numbers, inputs, results, scratch):
    pieces, ins, outs = inputs
    total, stacked = results
    (masked,) = scratch
    every = slice(0, BLK)
    stack(pieces, stacked)
    first_stage(numbers, sizes, stacked, ins, every, None, None, masked)
    total[...] = second_stage(masked, outs, every, None)


def masked_kernel(sizes, numbers, inputs, results, scratch):
    stacked, ins = inputs
    first_stage(numbers, sizes, stacked, ins, slice(0, BLK), None, None, results[0])


def joining_kernel(lanes, numbers, inputs, results, scratch):
    masked, partial, outs = inputs
    total = second_stage(masked, outs, lanes, partial[:, lanes])
    split_sums(total, *results, slice(0, lanes.stop - lanes.start))


def early_kernel(sizes, lanes, numbers, inputs, results, scratch):
    pieces, ins = inputs
    coeff, stacked = results
    stack(pieces, stacked)
    first_stage(numbers, sizes, stacked, ins, lanes, None, coeff, None)


def late_kernel(sizes, lanes, numbers, inputs, results, scratch):
    pieces, ins, previous, outs_by_lanes = inputs
    keep_ref, send_ref, stacked = results
    (masked,) = scratch
    stack(pieces, stacked)
    first_stage(numbers, sizes, stacked, ins, lanes[-1], previous, None, masked)
    for here, outs in zip(lanes, outs_by_lanes):
        split_sums(second_stage(masked, outs, here, None), keep_ref, send_ref, here)


def near_kernel(n_stacks, per_step, slot_ref, *refs):
    stacks, (blocks_ref, out_ref, *own, total) = refs[:n_stacks], refs[n_stacks:]
    rows = out_ref.shape[0]
    step = pl.program_id(0)

    @pl.when(step == 0)
    def _():
        total[...] = jnp.zeros_like(total)

    added = total[...]
    for k in range(per_step):
        start = pl.multiple_of(slot_ref[step * per_step + k] * rows, rows)
        first = 0
        for stacked in stacks:
            width = stacked.shape[1]
            added += lax.dot_general(
                stacked[pl.ds(start, rows), :],
                blocks_ref[k, :, first : first + width],
                CONTRACT_LAST,
                preferred_element_type=F32,
            )
            first += width
    total[...] = added

    @pl.when(step == pl.num_programs(0) - 1)
    def _():
        out_ref[...] = total[...]
        for ref in own:
            first = 0
            for stacked in stacks:
                ref[:, first : first + stacked.shape[1]] = stacked[:rows, :]
                first += stacked.shape[1]


def near_field(rows, stacks, near_blocks, slots, with_own):
    near = near_blocks.shape[0]
    per_step = 4 if near % 4 == 0 else 1
    whole = pl.BlockSpec(memory_space=pltpu.VMEM)
    out_shape = [jax.ShapeDtypeStruct((rows, BLK), F32)]
    if with_own:
        out_shape.append(jax.ShapeDtypeStruct((rows, BLK), BF16))
    return pl.pallas_call(
        functools.partial(near_kernel, len(stacks), per_step),
        out_shape=tuple(out_shape),
        grid_spec=pltpu.PrefetchScalarGridSpec(
            num_scalar_prefetch=1,
            grid=(near // per_step,),
            in_specs=[whole] * len(stacks)
            + [pl.BlockSpec((per_step, BLK, BLK), lambda step, slot: (step, 0, 0))],
            out_specs=(whole,) * len(out_shape),
            scratch_shapes=[pltpu.VMEM((rows, BLK), F32)],
        ),
        compiler_params=pltpu.CompilerParams(vmem_limit_bytes=14 << 20),
        cost_estimate=hint(0),
        name="near_field",
    )(slots, *stacks, near_blocks)


def finish_kernel(lanes, numbers, inputs, results, scratch):
    sums, near_ref, jacobi_ref = inputs
    total = near_ref[:, lanes]
    for part in sums:
        total += part[...].astype(F32)
    field = total.astype(BF16)
    for start in range(0, lanes.stop - lanes.start, JB):
        here = slice(start, start + JB)
        results[0][:, here] = lax.dot_general(
            field[:, here],
            jacobi_ref[(lanes.start + start) // JB],
            CONTRACT_LAST,
            preferred_element_type=F32,
        ).astype(BF16)


def finish(sums, near, jacobi_inverse, lanes):
    return on_chip(
        functools.partial(finish_kernel, lanes),
        (),
        (sums, near, jacobi_inverse),
        [jax.ShapeDtypeStruct(sums[0].shape, BF16)],
        [],
        0,
        2 << 20,
        "finish",
    )[0]


def local(
    n_tiles,
    n_rhs,
    n_sub,
    sources,
    basis_out,
    basis_in,
    tile_rank,
    tile_row,
    tile_col,
    near_blocks,
    near_col,
    jacobi_inverse,
):
    z = lax.axis_index("tiles")
    s = lax.axis_index("sub")
    rows = sources.shape[0]
    basis_in = basis_in.reshape(-1, BLK)
    basis_out = basis_out.reshape(-1, BLK)
    width = basis_in.shape[0]
    sizes = (n_tiles, n_sub)
    n_pieces = n_tiles * n_sub
    stack_rows = n_pieces * rows
    cuts = [slice(0, BLK // 2), slice(BLK // 2, BLK)]
    place = jnp.stack([z, s])
    near_slots = (s - near_col[0] % n_sub) % n_sub * n_tiles + (z - near_col[0] // n_sub) % n_tiles
    near_blocks = near_blocks[0]
    temporary = stack_rows * (16 * BLK + 8 * NCHUNK) + (2 << 20)

    def gather(field):
        along = [field] + [shifted(field, "tiles", n_tiles, d) for d in range(1, n_tiles)]
        pieces = list(along)
        for e in range(1, n_sub):
            pieces += [shifted(piece, "sub", n_sub, e) for piece in along]
        return pieces

    def others(array):
        return [shifted(array, "rhs", n_rhs, e) for e in range(1, n_rhs)]

    def reduced(keep, send):
        total = keep.astype(F32)
        for e in range(1, n_sub):
            size = n_tiles * rows
            total += shifted(send[(e - 1) * size : e * size], "sub", n_sub, e).astype(F32)
        return [total[d * rows : (d + 1) * rows].astype(BF16) for d in range(n_tiles)]

    def spread_out(parts):
        return [shifted(part, "tiles", n_tiles, d) if d else part for d, part in enumerate(parts)]

    def stacked_shape(lanes, dtype=BF16):
        return jax.ShapeDtypeStruct((stack_rows, lanes.stop - lanes.start), dtype)

    def split_shapes(columns):
        return [
            jax.ShapeDtypeStruct((n_tiles * rows, columns), BF16),
            jax.ShapeDtypeStruct((stack_rows - n_tiles * rows, columns), BF16),
        ]

    numbers = jnp.stack([tile_rank, tile_row, tile_col])
    other_tables = others(numbers)
    other_ins = others(basis_in)
    other_outs = [others(basis_out[:, lanes]) for lanes in cuts]
    every = slice(0, BLK)

    partial, stacked = on_chip(
        functools.partial(opening_kernel, sizes),
        (place, [numbers]),
        (gather(sources), [basis_in], [basis_out]),
        [stacked_shape(every, F32), stacked_shape(every)],
        [pltpu.VMEM((stack_rows, width), BF16)],
        0,
        temporary,
        "far_own",
    )
    (near,) = near_field(rows, [stacked], near_blocks, near_slots, False)
    stacked, near = lax.optimization_barrier((stacked, near))
    (masked,) = on_chip(
        functools.partial(masked_kernel, sizes),
        (place, other_tables),
        (stacked, other_ins),
        [jax.ShapeDtypeStruct((stack_rows, (n_rhs - 1) * width), BF16)],
        [],
        0,
        temporary,
        "far_first_stage",
    )
    fields, parts = [], ()
    for lanes, outs in zip(cuts, other_outs):
        if parts:
            fields.append(finish(spread_out(parts), near, jacobi_inverse, cuts[len(fields)]))
        keep, send = on_chip(
            functools.partial(joining_kernel, lanes),
            (),
            (masked, partial, outs),
            split_shapes(lanes.stop - lanes.start),
            [],
            JOIN if parts else 0,
            temporary,
            "far_second_stage",
        )
        parts = reduced(keep, send)
    fields.append(finish(spread_out(parts), near, jacobi_inverse, cuts[-1]))

    tables = (place, [numbers] + other_tables)
    ins = [basis_in] + other_ins
    coeff, first_stack = on_chip(
        functools.partial(early_kernel, sizes, cuts[0]),
        tables,
        (gather(fields[0]), ins),
        [jax.ShapeDtypeStruct((rows, n_rhs * width), F32), stacked_shape(cuts[0])],
        [],
        EARLY,
        temporary,
        "far_early",
    )
    keep, send, second_stack = on_chip(
        functools.partial(late_kernel, sizes, cuts),
        tables,
        (gather(fields[1]), ins, coeff, [[basis_out] + outs for outs in other_outs]),
        split_shapes(BLK) + [stacked_shape(cuts[1])],
        [pltpu.VMEM((stack_rows, n_rhs * width), BF16)],
        0,
        temporary,
        "far_late",
    )
    near, first_result = near_field(
        rows, [first_stack, second_stack], near_blocks, near_slots, True
    )
    second_result = finish(spread_out(reduced(keep, send)), near, jacobi_inverse, every)
    return (first_result, second_result)


def solution(mesh):
    sizes = mesh.shape
    return jax.shard_map(
        functools.partial(local, sizes["tiles"], sizes["rhs"], sizes["sub"]),
        mesh=mesh,
        in_specs=(
            P("rhs", ("groups", "tiles", "sub")),
            P(("groups", "tiles", "rhs", "sub"), None, None),
            P(("groups", "tiles", "rhs", "sub"), None, None),
            P(("groups", "tiles", "rhs", "sub")),
            P(("groups", "tiles", "rhs", "sub")),
            P(("groups", "tiles", "rhs", "sub")),
            P(("groups", "tiles", "sub"), None, None, None),
            P(("groups", "tiles", "sub"), None),
            P(("groups", "tiles", "sub"), None, None),
        ),
        out_specs=(P("rhs", ("groups", "tiles", "sub")), P("rhs", ("groups", "tiles", "sub"))),
        check_vma=False,
    )
```

time: 234 us -> 89 us (0.38)
  waiting for transfers between devices: 150 us -> 20.2 us
  matrix products: 41.5 us -> 0 us
  starting transfers between devices: 0.42 us -> 40.3 us
  Pallas kernels: 0 us -> 19.8 us
  local copies, waits for them, and re-layouts: 20.9 us -> 5.55 us
  between operations: 14.9 us -> 0.88 us
  blocking collectives: 5.19 us -> 0 us
    all_gather x4 -> x0, waiting for transfers between devices: 88.2 us -> none  [the longest x2 35 us: apply_operator(): lax.all_gather(vector, ('tiles', 'sub'), axis=1, tiled=True)]
    reduce_scatter x2 -> x0, waiting for transfers between devices: 60.7 us -> none  [apply_operator(): lax.psum_scatter(far_field.astype(jnp.bfloat16), ('tiles', 'sub'), scatte...]
    dot_general x10 -> x0, matrix products: 41.5 us -> none  [the longest x2 14.4 us: tile_terms(): jnp.einsum('ctr,trp->ctp', coefficients, basis_out, preferred_element_typ...]
    ppermute x0 -> x37, starting transfers between devices: none -> 40.3 us  [shifted(): lax.ppermute(value, axis, [(i, (i + amount) % size) for i in range(size)])]
    ppermute x0 -> x37, waiting for transfers between devices: none -> 20.2 us  [shifted(): lax.ppermute(value, axis, [(i, (i + amount) % size) for i in range(size)])]
    pallas_call x0 -> x11, Pallas kernels: none -> 19.8 us  [the longest x9 11.4 us: on_chip(): pl.pallas_call(body, out_shape=tuple(out_shapes), in_specs=[in_smem] * n_...]
    gather x4 -> x0, local copies, waits for them, and re-layouts: 9.13 us -> none  [the longest x2 6.43 us: tile_terms(): picked = jnp.take(gathered, tile_col, axis=1)]
    unnamed x22 -> x14, local copies, waits for them, and re-layouts: 9.77 us -> 4.31 us
  transfers between devices with their start and end apart: 6 -> 37, of which waited for: 6 -> 9; matrix products, arithmetic and copies ran while one was open for 5% -> 3% of each run, Pallas kernels for 0% -> 18%
where the time goes in v4:
time: 89 us; the launch traced here: 88.4 us
  starting transfers between devices  40.3 us (45%)
  waiting for transfers between devices  20.2 us (23%)
  Pallas kernels  19.8 us (22%)
  local copies, waits for them, and re-layouts  5.55 us (6%)
  other arithmetic  1.73 us (2%)
    ppermute x37, starting transfers between devices, shifted(): lax.ppermute(value, axis, [(i, (i + amount) % size) for i in range(size)])  40.3 us
    ppermute x37, waiting for transfers between devices, shifted(): lax.ppermute(value, axis, [(i, (i + amount) % size) for i in range(size)])  20.2 us
    pallas_call x9, Pallas kernels, on_chip(): pl.pallas_call(body, out_shape=tuple(out_shapes), in_specs=[in_smem] * n_...  11.4 us
    pallas_call x2, Pallas kernels, near_field(): pl.pallas_call(functools.partial(near_kernel, len(stacks), per_step), out...  8.35 us
    unnamed x14, local copies, waits for them, and re-layouts  4.31 us
  transfers between devices with their start and end apart: 37, of which 9 were waited for; matrix products, arithmetic and copies ran while one was open for 3% of the time, Pallas kernels for 18%

profile of v4, /device:TPU:0, one launch (start us, length us, event | category | flops | bytes accessed | tf_op | source)
XLA Modules:
  0.0 88.4 jit_solution(17876402373024898167)
XLA Ops:
  0.6 3.0 %collective-permute-start.8 = (bf16[768,512]{1,0:T(8,128)(2,1)}, bf16[768,512]{1,0:T(8,128)(2,1)S(1)}, u32[]{:S(2)}, u32[]{:S(2)}) collective-permute-start(bf16[768,512]{1,0:T(8,128)(2,1)} %bitcast.29), channel_id=1, source_target_pairs={{0,2},{2,0},{1,3},{3,1},{4,6},{6,4},{5,7},{7,5},{8,10},{10,8},{9,1... | collective-permute-start | bytes 2359304 | tf_op jit(solution)/shard_map/ppermute | solution.py:28
  3.7 1.6 %collective-permute-start.1 = (bf16[128,512]{1,0:T(8,128)(2,1)}, bf16[128,512]{1,0:T(8,128)(2,1)S(1)}, u32[]{:S(2)}, u32[]{:S(2)}) collective-permute-start(bf16[128,512]{1,0:T(8,128)(2,1)} %refs_2_.1), channel_id=1, source_target_pairs={{0,4},{4,8},{8,12},{12,0},{1,5},{5,9},{9,13},{13,1},{2,6},{6,10},{... | collective-permute-start | bytes 393224 | tf_op jit(solution)/shard_map/ppermute | solution.py:28
  5.2 2.6 %collective-permute-start.2 = (bf16[128,512]{1,0:T(8,128)(2,1)}, bf16[128,512]{1,0:T(8,128)(2,1)S(1)}, u32[]{:S(2)}, u32[]{:S(2)}) collective-permute-start(bf16[128,512]{1,0:T(8,128)(2,1)} %refs_2_.1), channel_id=1, source_target_pairs={{0,8},{4,12},{8,0},{12,4},{1,9},{5,13},{9,1},{13,5},{2,10},{6,14},... | collective-permute-start | bytes 393224 | tf_op jit(solution)/shard_map/ppermute | solution.py:28
  7.8 1.3 %collective-permute-start.3 = (bf16[128,512]{1,0:T(8,128)(2,1)}, bf16[128,512]{1,0:T(8,128)(2,1)S(1)}, u32[]{:S(2)}, u32[]{:S(2)}) collective-permute-start(bf16[128,512]{1,0:T(8,128)(2,1)} %refs_2_.1), channel_id=1, source_target_pairs={{0,12},{4,0},{8,4},{12,8},{1,13},{5,1},{9,5},{13,9},{2,14},{6,2},{... | collective-permute-start | bytes 393224 | tf_op jit(solution)/shard_map/ppermute | solution.py:28
  9.2 1.2 %fusion.5 = (bf16[768,256]{1,0:T(8,128)(2,1)S(1)}, bf16[768,256]{1,0:T(8,128)(2,1)S(1)}) fusion(bf16[768,512]{1,0:T(8,128)(2,1)} %bitcast.25), kind=kLoop, calls=%fused_computation.22 | loop fusion | bytes 1572864 | tf_op jit(solution)/shard_map/slice | solution.py:330
  10.3 1.8 %collective-permute-done.1.refs_3_ = bf16[128,512]{1,0:T(8,128)(2,1)S(1)} collective-permute-done((bf16[128,512]{1,0:T(8,128)(2,1)}, bf16[128,512]{1,0:T(8,128)(2,1)S(1)}, u32[]{:S(2)}, u32[]{:S(2)}) %collective-permute-start.1) | collective-permute-done | bytes 131104 | tf_op jit(solution)/shard_map/ppermute | solution.py:28
  12.2 0.3 collective-permute-start.21
  12.5 0.7 fusion.slot_ref
  13.1 3.3 %collective-permute-done.2.refs_4_ = bf16[128,512]{1,0:T(8,128)(2,1)S(1)} collective-permute-done((bf16[128,512]{1,0:T(8,128)(2,1)}, bf16[128,512]{1,0:T(8,128)(2,1)S(1)}, u32[]{:S(2)}, u32[]{:S(2)}) %collective-permute-start.2) | collective-permute-done | bytes 131104 | tf_op jit(solution)/shard_map/ppermute | solution.py:28
  16.4 0.5 collective-permute-start.6
  17.1 0.7 pad_add_fusion.refs_1_
  17.8 0.6 collective-permute-start
  18.4 1.5 %collective-permute-start.9 = (bf16[768,256]{1,0:T(8,128)(2,1)S(1)}, bf16[768,256]{1,0:T(8,128)(2,1)S(1)}, u32[]{:S(2)}, u32[]{:S(2)}) collective-permute-start(bf16[768,256]{1,0:T(8,128)(2,1)S(1)} %get-tuple-element.33), channel_id=1, source_target_pairs={{0,2},{2,0},{1,3},{3,1},{4,6},{6,4},{5,7},{7,5},{8,10},{10,8},{9,1... | collective-permute-start | bytes 1179656 | tf_op jit(solution)/shard_map/ppermute | solution.py:28
  19.9 0.9 %copy-done.4 = bf16[128,512]{1,0:T(8,128)(2,1)S(1)} copy-done((bf16[128,512]{1,0:T(8,128)(2,1)S(1)}, bf16[128,512]{1,0:T(8,128)(2,1)}, u32[]{:S(2)}) %copy-start.4) | copy-done | bytes 131096
  20.8 2.4 %far_own.1 = (f32[1024,512]{1,0:T(8,128)S(1)}, bf16[1024,512]{1,0:T(8,128)(2,1)S(1)}) custom-call(s32[2]{0:T(128)S(1)} %pad_add_fusion.1.refs_0_, s32[3,12]{1,0:T(4,128)S(1)} %pad_add_fusion.refs_1_, bf16[128,512]{1,0:T(8,128)(2,1)S(1)} %copy-done.4, bf16[128,512]{1,0:T(8,128)(2,1)S(1)} %collective-permute-done.1.refs_3_, ...), custom_call_target="tpu_custom_call" | custom-call | flops 1 | bytes 1 | tf_op jit(solution)/shard_map/far_own/pallas_call | solution.py:45
  23.2 3.4 %copy-done = bf16[1,16,512,512]{3,2,1,0:T(8,128)(2,1)S(1)} copy-done((bf16[1,16,512,512]{3,2,1,0:T(8,128)(2,1)S(1)}, bf16[1,16,512,512]{3,2,1,0:T(8,128)(2,1)}, u32[]{:S(2)}) %copy-start) | copy-done | bytes 8388632
  26.6 3.9 %near_field.2.refs_4_ = f32[128,512]{1,0:T(8,128)S(1)} custom-call(s32[16]{0:T(128)S(1)} %fusion.slot_ref, bf16[1024,512]{1,0:T(8,128)(2,1)S(1)} %get-tuple-element.18.refs_0_.refs_2_, bf16[16,512,512]{2,1,0:T(8,128)(2,1)S(1)} %bitcast.21), custom_call_target="tpu_custom_call" | custom-call | flops 1 | bytes 1 | tf_op jit(solution)/shard_map/near_field/pallas_call | solution.py:223
  30.5 0.2 collective-permute-done.refs_1_.refs_2_
  30.7 1.7 %far_first_stage.1.refs_0_ = bf16[1024,768]{1,0:T(8,128)(2,1)S(1)} custom-call(s32[2]{0:T(128)S(1)} %pad_add_fusion.1.refs_0_, s32[3,12]{1,0:T(4,128)S(1)} %collective-permute-done.refs_1_.refs_2_, bf16[1024,512]{1,0:T(8,128)(2,1)S(1)} %get-tuple-element.18.refs_0_.refs_2_, bf16[768,512]{1,0:T(8,128)(2,1)S(1)} %collective-permute-done.8.refs_3_.refs_12_), custom_call_target="tpu_custom_call" | custom-call | flops 1 | bytes 1 | tf_op jit(solution)/shard_map/far_first_stage/pallas_call | solution.py:45
  32.4 0.6 far_second_stage.3
  33.1 5.2 %collective-permute-done.9.refs_2_.refs_15_ = bf16[768,256]{1,0:T(8,128)(2,1)S(1)} collective-permute-done((bf16[768,256]{1,0:T(8,128)(2,1)S(1)}, bf16[768,256]{1,0:T(8,128)(2,1)S(1)}, u32[]{:S(2)}, u32[]{:S(2)}) %collective-permute-start.9) | collective-permute-done | bytes 393248 | tf_op jit(solution)/shard_map/ppermute | solution.py:28
  38.3 0.6 far_second_stage.2
  39.1 1.9 %collective-permute-start.23 = (bf16[128,256]{1,0:T(8,128)(2,1)S(1)}, bf16[128,256]{1,0:T(8,128)(2,1)S(1)}, u32[]{:S(2)}, u32[]{:S(2)}) collective-permute-start(bf16[128,256]{1,0:T(8,128)(2,1)S(1)} %get-tuple-element.40), channel_id=1, source_target_pairs={{0,4},{4,8},{8,12},{12,0},{1,5},{5,9},{9,13},{13,1},{2,6},{6,10},{... | collective-permute-start | bytes 196616 | tf_op jit(solution)/shard_map/ppermute | solution.py:28
  41.0 2.6 %collective-permute-start.24 = (bf16[128,256]{1,0:T(8,128)(2,1)S(1)}, bf16[128,256]{1,0:T(8,128)(2,1)S(1)}, u32[]{:S(2)}, u32[]{:S(2)}) collective-permute-start(bf16[128,256]{1,0:T(8,128)(2,1)S(1)} %get-tuple-element.39), channel_id=1, source_target_pairs={{0,8},{4,12},{8,0},{12,4},{1,9},{5,13},{9,1},{13,5},{2,10},{6,14},... | collective-permute-start | bytes 196616 | tf_op jit(solution)/shard_map/ppermute | solution.py:28
  43.6 1.3 %collective-permute-start.25 = (bf16[128,256]{1,0:T(8,128)(2,1)S(1)}, bf16[128,256]{1,0:T(8,128)(2,1)S(1)}, u32[]{:S(2)}, u32[]{:S(2)}) collective-permute-start(bf16[128,256]{1,0:T(8,128)(2,1)S(1)} %get-tuple-element.38), channel_id=1, source_target_pairs={{0,12},{4,0},{8,4},{12,8},{1,13},{5,1},{9,5},{13,9},{2,14},{6,2},{... | collective-permute-start | bytes 196616 | tf_op jit(solution)/shard_map/ppermute | solution.py:28
  45.0 0.7 collective-permute-start.11
  45.8 0.3 collective-permute-start.12
  46.1 2.8 %collective-permute-start.13 = (bf16[128,256]{1,0:T(8,128)(2,1)S(1)}, bf16[128,256]{1,0:T(8,128)(2,1)S(1)}, u32[]{:S(2)}, u32[]{:S(2)}) collective-permute-start(bf16[128,256]{1,0:T(8,128)(2,1)S(1)} %get-tuple-element.42), channel_id=1, source_target_pairs={{0,12},{4,0},{8,4},{12,8},{1,13},{5,1},{9,5},{13,9},{2,14},{6,2},{... | collective-permute-start | bytes 196616 | tf_op jit(solution)/shard_map/ppermute | solution.py:28
  49.1 4.5 %collective-permute-start.26 = (bf16[128,256]{1,0:T(8,128)(2,1)S(1)}, bf16[128,256]{1,0:T(8,128)(2,1)S(1)}, u32[]{:S(2)}, u32[]{:S(2)}) collective-permute-start(bf16[128,256]{1,0:T(8,128)(2,1)S(1)} %finish.4.refs_3_), channel_id=1, source_target_pairs={{0,4},{4,8},{8,12},{12,0},{1,5},{5,9},{9,13},{13,1},{2,6},{6,10},{... | collective-permute-start | bytes 196616 | tf_op jit(solution)/shard_map/ppermute | solution.py:28
  53.6 2.0 %collective-permute-done.12.refs_2_ = bf16[128,256]{1,0:T(8,128)(2,1)S(1)} collective-permute-done((bf16[128,256]{1,0:T(8,128)(2,1)S(1)}, bf16[128,256]{1,0:T(8,128)(2,1)S(1)}, u32[]{:S(2)}, u32[]{:S(2)}) %collective-permute-start.12) | collective-permute-done | bytes 65568 | tf_op jit(solution)/shard_map/ppermute | solution.py:28
  55.8 3.4 %collective-permute-start.14 = (bf16[128,256]{1,0:T(8,128)(2,1)S(1)}, bf16[128,256]{1,0:T(8,128)(2,1)S(1)}, u32[]{:S(2)}, u32[]{:S(2)}) collective-permute-start(bf16[128,256]{1,0:T(8,128)(2,1)S(1)} %finish.3.refs_3_), channel_id=1, source_target_pairs={{0,4},{4,8},{8,12},{12,0},{1,5},{5,9},{9,13},{13,1},{2,6},{6,10},{... | collective-permute-start | bytes 196616 | tf_op jit(solution)/shard_map/ppermute | solution.py:28
  59.3 2.4 %collective-permute-start.16 = (bf16[128,256]{1,0:T(8,128)(2,1)S(1)}, bf16[128,256]{1,0:T(8,128)(2,1)S(1)}, u32[]{:S(2)}, u32[]{:S(2)}) collective-permute-start(bf16[128,256]{1,0:T(8,128)(2,1)S(1)} %finish.3.refs_3_), channel_id=1, source_target_pairs={{0,12},{4,0},{8,4},{12,8},{1,13},{5,1},{9,5},{13,9},{2,14},{6,2},{... | collective-permute-start | bytes 196616 | tf_op jit(solution)/shard_map/ppermute | solution.py:28
  61.7 1.9 %collective-permute-start.28 = (bf16[128,256]{1,0:T(8,128)(2,1)S(1)}, bf16[128,256]{1,0:T(8,128)(2,1)S(1)}, u32[]{:S(2)}, u32[]{:S(2)}) collective-permute-start(bf16[128,256]{1,0:T(8,128)(2,1)S(1)} %finish.4.refs_3_), channel_id=1, source_target_pairs={{0,12},{4,0},{8,4},{12,8},{1,13},{5,1},{9,5},{13,9},{2,14},{6,2},{... | collective-permute-start | bytes 196616 | tf_op jit(solution)/shard_map/ppermute | solution.py:28
  63.7 0.5 collective-permute-start.18
  64.2 1.5 %collective-permute-done.15.refs_5_ = bf16[128,256]{1,0:T(8,128)(2,1)S(1)} collective-permute-done((bf16[128,256]{1,0:T(8,128)(2,1)S(1)}, bf16[128,256]{1,0:T(8,128)(2,1)S(1)}, u32[]{:S(2)}, u32[]{:S(2)}) %collective-permute-start.15) | collective-permute-done | bytes 65568 | tf_op jit(solution)/shard_map/ppermute | solution.py:28
  65.7 0.5 collective-permute-start.20
  66.2 0.4 collective-permute-start.30
  66.9 0.3 collective-permute-start.32
  67.2 1.6 %far_early.1 = (f32[128,1536]{1,0:T(8,128)S(1)}, bf16[1024,256]{1,0:T(8,128)(2,1)S(1)}) custom-call(s32[2]{0:T(128)S(1)} %pad_add_fusion.1.refs_0_, s32[3,12]{1,0:T(4,128)S(1)} %pad_add_fusion.refs_1_, s32[3,12]{1,0:T(4,128)S(1)} %collective-permute-done.refs_1_.refs_2_, bf16[128,256]{1,0:T(8,128)(2,1)S(1)} %finish.3.refs_3_, ...), custom_call_target="tpu_custom_call" | custom-call | flops 10000000000 | bytes 1 | tf_op jit(solution)/shard_map/far_early/pallas_call | solution.py:45
  68.9 3.3 %far_late.1 = (bf16[512,512]{1,0:T(8,128)(2,1)S(1)}, bf16[512,512]{1,0:T(8,128)(2,1)S(1)}, bf16[1024,256]{1,0:T(8,128)(2,1)S(1)}) custom-call(s32[2]{0:T(128)S(1)} %pad_add_fusion.1.refs_0_, s32[3,12]{1,0:T(4,128)S(1)} %pad_add_fusion.refs_1_, s32[3,12]{1,0:T(4,128)S(1)} %collective-permute-done.refs_1_.refs_2_, bf16[128,256]{1,0:T(8,128)(2,1)S(1)} %finish.4.refs_3_, ...), custom_call_target="tpu_custom_call" | custom-call | flops 1 | bytes 1 | tf_op jit(solution)/shard_map/far_late/pallas_call | solution.py:45
  72.2 0.3 collective-permute-start.33
  72.4 1.7 %collective-permute-done.33 = bf16[512,512]{1,0:T(8,128)(2,1)S(1)} collective-permute-done((bf16[512,512]{1,0:T(8,128)(2,1)S(1)}, bf16[512,512]{1,0:T(8,128)(2,1)S(1)}, u32[]{:S(2)}, u32[]{:S(2)}) %collective-permute-start.33) | collective-permute-done | bytes 524320 | tf_op jit(solution)/shard_map/ppermute | solution.py:28
  74.3 2.0 %collective-permute-start.34 = (bf16[128,512]{1,0:T(8,128)(2,1)S(1)}, bf16[128,512]{1,0:T(8,128)(2,1)S(1)}, u32[]{:S(2)}, u32[]{:S(2)}) collective-permute-start(bf16[128,512]{1,0:T(8,128)(2,1)S(1)} %get-tuple-element.36), channel_id=1, source_target_pairs={{0,4},{4,8},{8,12},{12,0},{1,5},{5,9},{9,13},{13,1},{2,6},{6,10},{... | collective-permute-start | bytes 393224 | tf_op jit(solution)/shard_map/ppermute | solution.py:28
  76.3 2.1 %collective-permute-start.35 = (bf16[128,512]{1,0:T(8,128)(2,1)S(1)}, bf16[128,512]{1,0:T(8,128)(2,1)S(1)}, u32[]{:S(2)}, u32[]{:S(2)}) collective-permute-start(bf16[128,512]{1,0:T(8,128)(2,1)S(1)} %get-tuple-element.35), channel_id=1, source_target_pairs={{0,8},{4,12},{8,0},{12,4},{1,9},{5,13},{9,1},{13,5},{2,10},{6,14},... | collective-permute-start | bytes 393224 | tf_op jit(solution)/shard_map/ppermute | solution.py:28
  78.5 0.3 collective-permute-start.36
  78.8 4.5 %near_field.3 = (f32[128,512]{1,0:T(8,128)S(1)}, bf16[128,512]{1,0:T(8,128)(2,1)}) custom-call(s32[16]{0:T(128)S(1)} %fusion.slot_ref, bf16[1024,256]{1,0:T(8,128)(2,1)S(1)} %get-tuple-element.23.refs_0_, bf16[1024,256]{1,0:T(8,128)(2,1)S(1)} %get-tuple-element.27.refs_1_, bf16[16,512,512]{2,1,0:T(8,128)(2,1)S(1)} %bitcast.24), custom_call_target="tpu_custom_call" | custom-call | flops 1 | bytes 1 | tf_op jit(solution)/shard_map/near_field/pallas_call | solution.py:223
  83.3 4.2 %collective-permute-done.35.refs_2_ = bf16[128,512]{1,0:T(8,128)(2,1)S(1)} collective-permute-done((bf16[128,512]{1,0:T(8,128)(2,1)S(1)}, bf16[128,512]{1,0:T(8,128)(2,1)S(1)}, u32[]{:S(2)}, u32[]{:S(2)}) %collective-permute-start.35) | collective-permute-done | bytes 131104 | tf_op jit(solution)/shard_map/ppermute | solution.py:28
  87.5 0.9 finish.5
  (62 shorter events, 1.4 us)
Async XLA Ops:
  0.6 19.3 %copy-start.2 = (bf16[12,64,512]{2,1,0:T(8,128)(2,1)S(1)}, bf16[12,64,512]{2,1,0:T(8,128)(2,1)}, u32[]{:S(2)}) copy-start(bf16[12,64,512]{2,1,0:T(8,128)(2,1)} %param.11) | copy-start | bytes 2359300
  0.6 19.3 %copy-start.1 = (bf16[12,64,512]{2,1,0:T(8,128)(2,1)S(1)}, bf16[12,64,512]{2,1,0:T(8,128)(2,1)}, u32[]{:S(2)}) copy-start(bf16[12,64,512]{2,1,0:T(8,128)(2,1)} %param.10) | copy-start | bytes 2359300
  0.6 30.1 %collective-permute-start.8 = (bf16[768,512]{1,0:T(8,128)(2,1)}, bf16[768,512]{1,0:T(8,128)(2,1)S(1)}, u32[]{:S(2)}, u32[]{:S(2)}) collective-permute-start(bf16[768,512]{1,0:T(8,128)(2,1)} %bitcast.29), channel_id=1, source_target_pairs={{0,2},{2,0},{1,3},{3,1},{4,6},{6,4},{5,7},{7,5},{8,10},{10,8},{9,1... | collective-permute-start | bytes 2359304 | tf_op jit(solution)/shard_map/ppermute | solution.py:28
  3.7 8.5 %collective-permute-start.1 = (bf16[128,512]{1,0:T(8,128)(2,1)}, bf16[128,512]{1,0:T(8,128)(2,1)S(1)}, u32[]{:S(2)}, u32[]{:S(2)}) collective-permute-start(bf16[128,512]{1,0:T(8,128)(2,1)} %refs_2_.1), channel_id=1, source_target_pairs={{0,4},{4,8},{8,12},{12,0},{1,5},{5,9},{9,13},{13,1},{2,6},{6,10},{... | collective-permute-start | bytes 393224 | tf_op jit(solution)/shard_map/ppermute | solution.py:28
  5.2 11.2 %collective-permute-start.2 = (bf16[128,512]{1,0:T(8,128)(2,1)}, bf16[128,512]{1,0:T(8,128)(2,1)S(1)}, u32[]{:S(2)}, u32[]{:S(2)}) collective-permute-start(bf16[128,512]{1,0:T(8,128)(2,1)} %refs_2_.1), channel_id=1, source_target_pairs={{0,8},{4,12},{8,0},{12,4},{1,9},{5,13},{9,1},{13,5},{2,10},{6,14},... | collective-permute-start | bytes 393224 | tf_op jit(solution)/shard_map/ppermute | solution.py:28
  7.8 8.6 %collective-permute-start.3 = (bf16[128,512]{1,0:T(8,128)(2,1)}, bf16[128,512]{1,0:T(8,128)(2,1)S(1)}, u32[]{:S(2)}, u32[]{:S(2)}) collective-permute-start(bf16[128,512]{1,0:T(8,128)(2,1)} %refs_2_.1), channel_id=1, source_target_pairs={{0,12},{4,0},{8,4},{12,8},{1,13},{5,1},{9,5},{13,9},{2,14},{6,2},{... | collective-permute-start | bytes 393224 | tf_op jit(solution)/shard_map/ppermute | solution.py:28
  9.2 7.8 %collective-permute-start.4 = (bf16[128,512]{1,0:T(8,128)(2,1)}, bf16[128,512]{1,0:T(8,128)(2,1)S(1)}, u32[]{:S(2)}, u32[]{:S(2)}) collective-permute-start(bf16[128,512]{1,0:T(8,128)(2,1)} %refs_2_.1), channel_id=1, source_target_pairs={{0,1},{1,0},{2,3},{3,2},{4,5},{5,4},{6,7},{7,6},{8,9},{9,8},{10,11... | collective-permute-start | bytes 393224 | tf_op jit(solution)/shard_map/ppermute | solution.py:28
  12.2 20.3 %collective-permute-start.21 = (bf16[768,256]{1,0:T(8,128)(2,1)S(1)}, bf16[768,256]{1,0:T(8,128)(2,1)S(1)}, u32[]{:S(2)}, u32[]{:S(2)}) collective-permute-start(bf16[768,256]{1,0:T(8,128)(2,1)S(1)} %get-tuple-element.32), channel_id=1, source_target_pairs={{0,2},{2,0},{1,3},{3,1},{4,6},{6,4},{5,7},{7,5},{8,10},{10,8},{9,1... | collective-permute-start | bytes 1179656 | tf_op jit(solution)/shard_map/ppermute | solution.py:28
  16.4 1.4 %collective-permute-start.5 = (bf16[128,512]{1,0:T(8,128)(2,1)S(1)}, bf16[128,512]{1,0:T(8,128)(2,1)S(1)}, u32[]{:S(2)}, u32[]{:S(2)}) collective-permute-start(bf16[128,512]{1,0:T(8,128)(2,1)S(1)} %collective-permute-done.1.refs_3_), channel_id=1, source_target_pairs={{0,1},{1,0},{2,3},{3,2},{4,5},{5,4},{6,7},{7,6},{8,9},{9,8},{10,11... | collective-permute-start | bytes 393224 | tf_op jit(solution)/shard_map/ppermute | solution.py:28
  16.4 1.9 %collective-permute-start.6 = (bf16[128,512]{1,0:T(8,128)(2,1)S(1)}, bf16[128,512]{1,0:T(8,128)(2,1)S(1)}, u32[]{:S(2)}, u32[]{:S(2)}) collective-permute-start(bf16[128,512]{1,0:T(8,128)(2,1)S(1)} %collective-permute-done.2.refs_4_), channel_id=1, source_target_pairs={{0,1},{1,0},{2,3},{3,2},{4,5},{5,4},{6,7},{7,6},{8,9},{9,8},{10,11... | collective-permute-start | bytes 393224 | tf_op jit(solution)/shard_map/ppermute | solution.py:28
  17.0 2.9 %collective-permute-start.7 = (bf16[128,512]{1,0:T(8,128)(2,1)S(1)}, bf16[128,512]{1,0:T(8,128)(2,1)S(1)}, u32[]{:S(2)}, u32[]{:S(2)}) collective-permute-start(bf16[128,512]{1,0:T(8,128)(2,1)S(1)} %collective-permute-done.3.refs_5_), channel_id=1, source_target_pairs={{0,1},{1,0},{2,3},{3,2},{4,5},{5,4},{6,7},{7,6},{8,9},{9,8},{10,11... | collective-permute-start | bytes 393224 | tf_op jit(solution)/shard_map/ppermute | solution.py:28
  17.8 12.9 %collective-permute-start = (s32[3,12]{1,0:T(4,128)S(1)}, s32[3,12]{1,0:T(4,128)S(1)}, u32[]{:S(2)}, u32[]{:S(2)}) collective-permute-start(s32[3,12]{1,0:T(4,128)S(1)} %pad_add_fusion.refs_1_), channel_id=1, source_target_pairs={{0,2},{2,0},{1,3},{3,1},{4,6},{6,4},{5,7},{7,5},{8,10},{10,8},{9,1... | collective-permute-start | bytes 440 | tf_op jit(solution)/shard_map/ppermute | solution.py:28
  18.4 19.9 %collective-permute-start.9 = (bf16[768,256]{1,0:T(8,128)(2,1)S(1)}, bf16[768,256]{1,0:T(8,128)(2,1)S(1)}, u32[]{:S(2)}, u32[]{:S(2)}) collective-permute-start(bf16[768,256]{1,0:T(8,128)(2,1)S(1)} %get-tuple-element.33), channel_id=1, source_target_pairs={{0,2},{2,0},{1,3},{3,1},{4,6},{6,4},{5,7},{7,5},{8,10},{10,8},{9,1... | collective-permute-start | bytes 1179656 | tf_op jit(solution)/shard_map/ppermute | solution.py:28
  19.9 0.9 %copy-start.4 = (bf16[128,512]{1,0:T(8,128)(2,1)S(1)}, bf16[128,512]{1,0:T(8,128)(2,1)}, u32[]{:S(2)}) copy-start(bf16[128,512]{1,0:T(8,128)(2,1)} %refs_2_.1) | copy-start | bytes 393220
  23.2 3.4 %copy-start = (bf16[1,16,512,512]{3,2,1,0:T(8,128)(2,1)S(1)}, bf16[1,16,512,512]{3,2,1,0:T(8,128)(2,1)}, u32[]{:S(2)}) copy-start(bf16[1,16,512,512]{3,2,1,0:T(8,128)(2,1)} %param.15) | copy-start | bytes 25165828
  33.1 5.9 %collective-permute-start.22 = (bf16[512,256]{1,0:T(8,128)(2,1)S(1)}, bf16[512,256]{1,0:T(8,128)(2,1)S(1)}, u32[]{:S(2)}, u32[]{:S(2)}) collective-permute-start(bf16[512,256]{1,0:T(8,128)(2,1)S(1)} %get-tuple-element.25), channel_id=1, source_target_pairs={{0,1},{1,0},{2,3},{3,2},{4,5},{5,4},{6,7},{7,6},{8,9},{9,8},{10,11... | collective-permute-start | bytes 786440 | tf_op jit(solution)/shard_map/ppermute | solution.py:28
  38.9 10.0 %copy-start.3 = (bf16[4,128,128]{2,1,0:T(8,128)(2,1)S(1)}, bf16[4,128,128]{2,1,0:T(8,128)(2,1)}, u32[]{:S(2)}) copy-start(bf16[4,128,128]{2,1,0:T(8,128)(2,1)} %refs_5_.5) | copy-start | bytes 393220
  38.9 6.0 %collective-permute-start.10 = (bf16[512,256]{1,0:T(8,128)(2,1)S(1)}, bf16[512,256]{1,0:T(8,128)(2,1)S(1)}, u32[]{:S(2)}, u32[]{:S(2)}) collective-permute-start(bf16[512,256]{1,0:T(8,128)(2,1)S(1)} %get-tuple-element.21), channel_id=1, source_target_pairs={{0,1},{1,0},{2,3},{3,2},{4,5},{5,4},{6,7},{7,6},{8,9},{9,8},{10,11... | collective-permute-start | bytes 786440 | tf_op jit(solution)/shard_map/ppermute | solution.py:28
  39.1 7.0 %collective-permute-start.23 = (bf16[128,256]{1,0:T(8,128)(2,1)S(1)}, bf16[128,256]{1,0:T(8,128)(2,1)S(1)}, u32[]{:S(2)}, u32[]{:S(2)}) collective-permute-start(bf16[128,256]{1,0:T(8,128)(2,1)S(1)} %get-tuple-element.40), channel_id=1, source_target_pairs={{0,4},{4,8},{8,12},{12,0},{1,5},{5,9},{9,13},{13,1},{2,6},{6,10},{... | collective-permute-start | bytes 196616 | tf_op jit(solution)/shard_map/ppermute | solution.py:28
  41.0 7.9 %collective-permute-start.24 = (bf16[128,256]{1,0:T(8,128)(2,1)S(1)}, bf16[128,256]{1,0:T(8,128)(2,1)S(1)}, u32[]{:S(2)}, u32[]{:S(2)}) collective-permute-start(bf16[128,256]{1,0:T(8,128)(2,1)S(1)} %get-tuple-element.39), channel_id=1, source_target_pairs={{0,8},{4,12},{8,0},{12,4},{1,9},{5,13},{9,1},{13,5},{2,10},{6,14},... | collective-permute-start | bytes 196616 | tf_op jit(solution)/shard_map/ppermute | solution.py:28
  43.6 5.3 %collective-permute-start.25 = (bf16[128,256]{1,0:T(8,128)(2,1)S(1)}, bf16[128,256]{1,0:T(8,128)(2,1)S(1)}, u32[]{:S(2)}, u32[]{:S(2)}) collective-permute-start(bf16[128,256]{1,0:T(8,128)(2,1)S(1)} %get-tuple-element.38), channel_id=1, source_target_pairs={{0,12},{4,0},{8,4},{12,8},{1,13},{5,1},{9,5},{13,9},{2,14},{6,2},{... | collective-permute-start | bytes 196616 | tf_op jit(solution)/shard_map/ppermute | solution.py:28
  45.0 8.6 %collective-permute-start.11 = (bf16[128,256]{1,0:T(8,128)(2,1)S(1)}, bf16[128,256]{1,0:T(8,128)(2,1)S(1)}, u32[]{:S(2)}, u32[]{:S(2)}) collective-permute-start(bf16[128,256]{1,0:T(8,128)(2,1)S(1)} %get-tuple-element.44), channel_id=1, source_target_pairs={{0,4},{4,8},{8,12},{12,0},{1,5},{5,9},{9,13},{13,1},{2,6},{6,10},{... | collective-permute-start | bytes 196616 | tf_op jit(solution)/shard_map/ppermute | solution.py:28
  45.8 9.9 %collective-permute-start.12 = (bf16[128,256]{1,0:T(8,128)(2,1)S(1)}, bf16[128,256]{1,0:T(8,128)(2,1)S(1)}, u32[]{:S(2)}, u32[]{:S(2)}) collective-permute-start(bf16[128,256]{1,0:T(8,128)(2,1)S(1)} %get-tuple-element.43), channel_id=1, source_target_pairs={{0,8},{4,12},{8,0},{12,4},{1,9},{5,13},{9,1},{13,5},{2,10},{6,14},... | collective-permute-start | bytes 196616 | tf_op jit(solution)/shard_map/ppermute | solution.py:28
  46.1 9.6 %collective-permute-start.13 = (bf16[128,256]{1,0:T(8,128)(2,1)S(1)}, bf16[128,256]{1,0:T(8,128)(2,1)S(1)}, u32[]{:S(2)}, u32[]{:S(2)}) collective-permute-start(bf16[128,256]{1,0:T(8,128)(2,1)S(1)} %get-tuple-element.42), channel_id=1, source_target_pairs={{0,12},{4,0},{8,4},{12,8},{1,13},{5,1},{9,5},{13,9},{2,14},{6,2},{... | collective-permute-start | bytes 196616 | tf_op jit(solution)/shard_map/ppermute | solution.py:28
  48.9 29.9 %slice-start = ((s8[8388608]{0:T(1024)(128)(4,1)}), s8[4194304]{0:T(1024)(128)(4,1)S(1)}, s32[]{:S(2)}) async-start(s8[8388608]{0:T(1024)(128)(4,1)} %bitcast.22), calls=%async_computation | async-start | bytes 8388608
  49.1 12.6 %collective-permute-start.26 = (bf16[128,256]{1,0:T(8,128)(2,1)S(1)}, bf16[128,256]{1,0:T(8,128)(2,1)S(1)}, u32[]{:S(2)}, u32[]{:S(2)}) collective-permute-start(bf16[128,256]{1,0:T(8,128)(2,1)S(1)} %finish.4.refs_3_), channel_id=1, source_target_pairs={{0,4},{4,8},{8,12},{12,0},{1,5},{5,9},{9,13},{13,1},{2,6},{6,10},{... | collective-permute-start | bytes 196616 | tf_op jit(solution)/shard_map/ppermute | solution.py:28
  53.6 10.0 %collective-permute-start.27 = (bf16[128,256]{1,0:T(8,128)(2,1)S(1)}, bf16[128,256]{1,0:T(8,128)(2,1)S(1)}, u32[]{:S(2)}, u32[]{:S(2)}) collective-permute-start(bf16[128,256]{1,0:T(8,128)(2,1)S(1)} %finish.4.refs_3_), channel_id=1, source_target_pairs={{0,8},{4,12},{8,0},{12,4},{1,9},{5,13},{9,1},{13,5},{2,10},{6,14},... | collective-permute-start | bytes 196616 | tf_op jit(solution)/shard_map/ppermute | solution.py:28
  55.8 23.0 %slice-start.1 = ((s8[8388608]{0:T(1024)(128)(4,1)}), s8[4194304]{0:T(1024)(128)(4,1)S(1)}, s32[]{:S(2)}) async-start(s8[8388608]{0:T(1024)(128)(4,1)} %bitcast.22), calls=%async_computation.1 | async-start | bytes 8388608
  55.8 7.8 %collective-permute-start.14 = (bf16[128,256]{1,0:T(8,128)(2,1)S(1)}, bf16[128,256]{1,0:T(8,128)(2,1)S(1)}, u32[]{:S(2)}, u32[]{:S(2)}) collective-permute-start(bf16[128,256]{1,0:T(8,128)(2,1)S(1)} %finish.3.refs_3_), channel_id=1, source_target_pairs={{0,4},{4,8},{8,12},{12,0},{1,5},{5,9},{9,13},{13,1},{2,6},{6,10},{... | collective-permute-start | bytes 196616 | tf_op jit(solution)/shard_map/ppermute | solution.py:28
  59.3 6.4 %collective-permute-start.15 = (bf16[128,256]{1,0:T(8,128)(2,1)S(1)}, bf16[128,256]{1,0:T(8,128)(2,1)S(1)}, u32[]{:S(2)}, u32[]{:S(2)}) collective-permute-start(bf16[128,256]{1,0:T(8,128)(2,1)S(1)} %finish.3.refs_3_), channel_id=1, source_target_pairs={{0,8},{4,12},{8,0},{12,4},{1,9},{5,13},{9,1},{13,5},{2,10},{6,14},... | collective-permute-start | bytes 196616 | tf_op jit(solution)/shard_map/ppermute | solution.py:28
  59.3 6.4 %collective-permute-start.16 = (bf16[128,256]{1,0:T(8,128)(2,1)S(1)}, bf16[128,256]{1,0:T(8,128)(2,1)S(1)}, u32[]{:S(2)}, u32[]{:S(2)}) collective-permute-start(bf16[128,256]{1,0:T(8,128)(2,1)S(1)} %finish.3.refs_3_), channel_id=1, source_target_pairs={{0,12},{4,0},{8,4},{12,8},{1,13},{5,1},{9,5},{13,9},{2,14},{6,2},{... | collective-permute-start | bytes 196616 | tf_op jit(solution)/shard_map/ppermute | solution.py:28
  61.7 4.5 %collective-permute-start.28 = (bf16[128,256]{1,0:T(8,128)(2,1)S(1)}, bf16[128,256]{1,0:T(8,128)(2,1)S(1)}, u32[]{:S(2)}, u32[]{:S(2)}) collective-permute-start(bf16[128,256]{1,0:T(8,128)(2,1)S(1)} %finish.4.refs_3_), channel_id=1, source_target_pairs={{0,12},{4,0},{8,4},{12,8},{1,13},{5,1},{9,5},{13,9},{2,14},{6,2},{... | collective-permute-start | bytes 196616 | tf_op jit(solution)/shard_map/ppermute | solution.py:28
  63.7 2.6 %collective-permute-start.17 = (bf16[128,256]{1,0:T(8,128)(2,1)S(1)}, bf16[128,256]{1,0:T(8,128)(2,1)S(1)}, u32[]{:S(2)}, u32[]{:S(2)}) collective-permute-start(bf16[128,256]{1,0:T(8,128)(2,1)S(1)} %finish.3.refs_3_), channel_id=1, source_target_pairs={{0,1},{1,0},{2,3},{3,2},{4,5},{5,4},{6,7},{7,6},{8,9},{9,8},{10,11... | collective-permute-start | bytes 196616 | tf_op jit(solution)/shard_map/ppermute | solution.py:28
  63.7 3.0 %collective-permute-start.18 = (bf16[128,256]{1,0:T(8,128)(2,1)S(1)}, bf16[128,256]{1,0:T(8,128)(2,1)S(1)}, u32[]{:S(2)}, u32[]{:S(2)}) collective-permute-start(bf16[128,256]{1,0:T(8,128)(2,1)S(1)} %collective-permute-done.14.refs_4_), channel_id=1, source_target_pairs={{0,1},{1,0},{2,3},{3,2},{4,5},{5,4},{6,7},{7,6},{8,9},{9,8},{10,11... | collective-permute-start | bytes 196616 | tf_op jit(solution)/shard_map/ppermute | solution.py:28
  65.7 1.3 %collective-permute-start.19 = (bf16[128,256]{1,0:T(8,128)(2,1)S(1)}, bf16[128,256]{1,0:T(8,128)(2,1)S(1)}, u32[]{:S(2)}, u32[]{:S(2)}) collective-permute-start(bf16[128,256]{1,0:T(8,128)(2,1)S(1)} %collective-permute-done.15.refs_5_), channel_id=1, source_target_pairs={{0,1},{1,0},{2,3},{3,2},{4,5},{5,4},{6,7},{7,6},{8,9},{9,8},{10,11... | collective-permute-start | bytes 196616 | tf_op jit(solution)/shard_map/ppermute | solution.py:28
  65.7 1.6 %collective-permute-start.20 = (bf16[128,256]{1,0:T(8,128)(2,1)S(1)}, bf16[128,256]{1,0:T(8,128)(2,1)S(1)}, u32[]{:S(2)}, u32[]{:S(2)}) collective-permute-start(bf16[128,256]{1,0:T(8,128)(2,1)S(1)} %collective-permute-done.16.refs_6_), channel_id=1, source_target_pairs={{0,1},{1,0},{2,3},{3,2},{4,5},{5,4},{6,7},{7,6},{8,9},{9,8},{10,11... | collective-permute-start | bytes 196616 | tf_op jit(solution)/shard_map/ppermute | solution.py:28
  66.2 2.7 %collective-permute-start.29 = (bf16[128,256]{1,0:T(8,128)(2,1)S(1)}, bf16[128,256]{1,0:T(8,128)(2,1)S(1)}, u32[]{:S(2)}, u32[]{:S(2)}) collective-permute-start(bf16[128,256]{1,0:T(8,128)(2,1)S(1)} %finish.4.refs_3_), channel_id=1, source_target_pairs={{0,1},{1,0},{2,3},{3,2},{4,5},{5,4},{6,7},{7,6},{8,9},{9,8},{10,11... | collective-permute-start | bytes 196616 | tf_op jit(solution)/shard_map/ppermute | solution.py:28
  66.2 2.6 %collective-permute-start.30 = (bf16[128,256]{1,0:T(8,128)(2,1)S(1)}, bf16[128,256]{1,0:T(8,128)(2,1)S(1)}, u32[]{:S(2)}, u32[]{:S(2)}) collective-permute-start(bf16[128,256]{1,0:T(8,128)(2,1)S(1)} %collective-permute-done.26.refs_4_), channel_id=1, source_target_pairs={{0,1},{1,0},{2,3},{3,2},{4,5},{5,4},{6,7},{7,6},{8,9},{9,8},{10,11... | collective-permute-start | bytes 196616 | tf_op jit(solution)/shard_map/ppermute | solution.py:28
  66.7 2.2 %collective-permute-start.31 = (bf16[128,256]{1,0:T(8,128)(2,1)S(1)}, bf16[128,256]{1,0:T(8,128)(2,1)S(1)}, u32[]{:S(2)}, u32[]{:S(2)}) collective-permute-start(bf16[128,256]{1,0:T(8,128)(2,1)S(1)} %collective-permute-done.27.refs_5_), channel_id=1, source_target_pairs={{0,1},{1,0},{2,3},{3,2},{4,5},{5,4},{6,7},{7,6},{8,9},{9,8},{10,11... | collective-permute-start | bytes 196616 | tf_op jit(solution)/shard_map/ppermute | solution.py:28
  66.9 2.0 %collective-permute-start.32 = (bf16[128,256]{1,0:T(8,128)(2,1)S(1)}, bf16[128,256]{1,0:T(8,128)(2,1)S(1)}, u32[]{:S(2)}, u32[]{:S(2)}) collective-permute-start(bf16[128,256]{1,0:T(8,128)(2,1)S(1)} %collective-permute-done.28.refs_6_), channel_id=1, source_target_pairs={{0,1},{1,0},{2,3},{3,2},{4,5},{5,4},{6,7},{7,6},{8,9},{9,8},{10,11... | collective-permute-start | bytes 196616 | tf_op jit(solution)/shard_map/ppermute | solution.py:28
  72.2 2.0 %collective-permute-start.33 = (bf16[512,512]{1,0:T(8,128)(2,1)S(1)}, bf16[512,512]{1,0:T(8,128)(2,1)S(1)}, u32[]{:S(2)}, u32[]{:S(2)}) collective-permute-start(bf16[512,512]{1,0:T(8,128)(2,1)S(1)} %get-tuple-element.30), channel_id=1, source_target_pairs={{0,1},{1,0},{2,3},{3,2},{4,5},{5,4},{6,7},{7,6},{8,9},{9,8},{10,11... | collective-permute-start | bytes 1572872 | tf_op jit(solution)/shard_map/ppermute | solution.py:28
  74.3 9.0 %collective-permute-start.34 = (bf16[128,512]{1,0:T(8,128)(2,1)S(1)}, bf16[128,512]{1,0:T(8,128)(2,1)S(1)}, u32[]{:S(2)}, u32[]{:S(2)}) collective-permute-start(bf16[128,512]{1,0:T(8,128)(2,1)S(1)} %get-tuple-element.36), channel_id=1, source_target_pairs={{0,4},{4,8},{8,12},{12,0},{1,5},{5,9},{9,13},{13,1},{2,6},{6,10},{... | collective-permute-start | bytes 393224 | tf_op jit(solution)/shard_map/ppermute | solution.py:28
  76.3 11.2 %collective-permute-start.35 = (bf16[128,512]{1,0:T(8,128)(2,1)S(1)}, bf16[128,512]{1,0:T(8,128)(2,1)S(1)}, u32[]{:S(2)}, u32[]{:S(2)}) collective-permute-start(bf16[128,512]{1,0:T(8,128)(2,1)S(1)} %get-tuple-element.35), channel_id=1, source_target_pairs={{0,8},{4,12},{8,0},{12,4},{1,9},{5,13},{9,1},{13,5},{2,10},{6,14},... | collective-permute-start | bytes 393224 | tf_op jit(solution)/shard_map/ppermute | solution.py:28
  78.5 9.0 %collective-permute-start.36 = (bf16[128,512]{1,0:T(8,128)(2,1)S(1)}, bf16[128,512]{1,0:T(8,128)(2,1)S(1)}, u32[]{:S(2)}, u32[]{:S(2)}) collective-permute-start(bf16[128,512]{1,0:T(8,128)(2,1)S(1)} %get-tuple-element.34), channel_id=1, source_target_pairs={{0,12},{4,0},{8,4},{12,8},{1,13},{5,1},{9,5},{13,9},{2,14},{6,2},{... | collective-permute-start | bytes 393224 | tf_op jit(solution)/shard_map/ppermute | solution.py:28

commit v5 on v4

--- a/solution.py
+++ b/solution.py
@@ -10,7 +10,7 @@
 BLK = 512
 RMAX = 64
 JOIN = 10
-EARLY = 10
+KEPT = 10
 JB = 128
 NCHUNK = 256
 BF16 = jnp.bfloat16
@@ -162,21 +162,24 @@
     split_sums(total, *results, slice(0, lanes.stop - lanes.start))
 
 
-def early_kernel(sizes, lanes, numbers, inputs, results, scratch):
-    pieces, ins = inputs
-    coeff, stacked = results
-    stack(pieces, stacked)
-    first_stage(numbers, sizes, stacked, ins, lanes, None, coeff, None)
-
-
-def late_kernel(sizes, lanes, numbers, inputs, results, scratch):
-    pieces, ins, previous, outs_by_lanes = inputs
-    keep_ref, send_ref, stacked = results
+def sent_kernel(sizes, lanes, numbers, inputs, results, scratch):
+    pieces_by_lanes, ins, outs_by_lanes = inputs
+    send_ref, stacked, kept = results
     (masked,) = scratch
-    stack(pieces, stacked)
-    first_stage(numbers, sizes, stacked, ins, lanes[-1], previous, None, masked)
+    for here, pieces in zip(lanes, pieces_by_lanes):
+        stack(pieces, stacked.at[:, here])
+    first_stage(numbers, sizes, stacked, ins, slice(0, BLK), None, None, masked)
+    n_kept = kept.shape[0]
     for here, outs in zip(lanes, outs_by_lanes):
-        split_sums(second_stage(masked, outs, here, None), keep_ref, send_ref, here)
+        total = second_stage(masked.at[n_kept:, :], outs, here, None)
+        send_ref[:, here] = total.astype(BF16)
+    kept[...] = masked[:n_kept, :]
+
+
+def kept_kernel(lanes, numbers, inputs, results, scratch):
+    masked, outs_by_lanes = inputs
+    for here, outs in zip(lanes, outs_by_lanes):
+        results[0][:, here] = second_stage(masked, outs, here, None).astype(BF16)
 
 
 def near_kernel(n_stacks, per_step, slot_ref, *refs):
@@ -371,29 +374,30 @@
 
     tables = (place, [numbers] + other_tables)
     ins = [basis_in] + other_ins
-    coeff, first_stack = on_chip(
-        functools.partial(early_kernel, sizes, cuts[0]),
+    outs = [[basis_out] + arrays for arrays in other_outs]
+    keep_shape, send_shape = split_shapes(BLK)
+    send, stacked, kept = on_chip(
+        functools.partial(sent_kernel, sizes, cuts),
         tables,
-        (gather(fields[0]), ins),
-        [jax.ShapeDtypeStruct((rows, n_rhs * width), F32), stacked_shape(cuts[0])],
-        [],
-        EARLY,
-        temporary,
-        "far_early",
-    )
-    keep, send, second_stack = on_chip(
-        functools.partial(late_kernel, sizes, cuts),
-        tables,
-        (gather(fields[1]), ins, coeff, [[basis_out] + outs for outs in other_outs]),
-        split_shapes(BLK) + [stacked_shape(cuts[1])],
+        ([gather(field) for field in fields], ins, outs),
+        [send_shape, stacked_shape(every)]
+        + [jax.ShapeDtypeStruct((n_tiles * rows, n_rhs * width), BF16)],
         [pltpu.VMEM((stack_rows, n_rhs * width), BF16)],
         0,
         temporary,
-        "far_late",
-    )
-    near, first_result = near_field(
-        rows, [first_stack, second_stack], near_blocks, near_slots, True
-    )
+        "far_sent",
+    )
+    (keep,) = on_chip(
+        functools.partial(kept_kernel, cuts),
+        (),
+        (kept, outs),
+        [keep_shape],
+        [],
+        KEPT,
+        temporary,
+        "far_kept",
+    )
+    near, first_result = near_field(rows, [stacked], near_blocks, near_slots, True)
     second_result = finish(spread_out(reduced(keep, send)), near, jacobi_inverse, every)
     return (first_result, second_result)
 

time: 89 us -> 87.8 us (0.987)
  transfers between devices with their start and end apart: 37 -> 37, of which waited for: 9 -> 12; matrix products, arithmetic and copies ran while one was open for 3% -> 3% of each run, Pallas kernels for 18% -> 17%
where the time goes in v5:
time: 87.8 us; the launch traced here: 87.1 us
  starting transfers between devices  40.2 us (46%)
  waiting for transfers between devices  19.7 us (22%)
  Pallas kernels  19.2 us (22%)
  local copies, waits for them, and re-layouts  5.54 us (6%)
  other arithmetic  1.73 us (2%)
    ppermute x37, starting transfers between devices, shifted(): lax.ppermute(value, axis, [(i, (i + amount) % size) for i in range(size)])  40.2 us
    ppermute x37, waiting for transfers between devices, shifted(): lax.ppermute(value, axis, [(i, (i + amount) % size) for i in range(size)])  19.7 us
    pallas_call x9, Pallas kernels, on_chip(): pl.pallas_call(body, out_shape=tuple(out_shapes), in_specs=[in_smem] * n_...  10.8 us
    pallas_call x2, Pallas kernels, near_field(): pl.pallas_call(functools.partial(near_kernel, len(stacks), per_step), out...  8.35 us
    unnamed x14, local copies, waits for them, and re-layouts  4.3 us
  transfers between devices with their start and end apart: 37, of which 12 were waited for; matrix products, arithmetic and copies ran while one was open for 3% of the time, Pallas kernels for 17%

profile of v5, /device:TPU:0, one launch (start us, length us, event | category | flops | bytes accessed | tf_op | source)
XLA Modules:
  0.0 87.1 jit_solution(17128101088475417451)
XLA Ops:
  0.6 3.0 %collective-permute-start.8 = (bf16[768,512]{1,0:T(8,128)(2,1)}, bf16[768,512]{1,0:T(8,128)(2,1)S(1)}, u32[]{:S(2)}, u32[]{:S(2)}) collective-permute-start(bf16[768,512]{1,0:T(8,128)(2,1)} %bitcast.31), channel_id=1, source_target_pairs={{0,2},{2,0},{1,3},{3,1},{4,6},{6,4},{5,7},{7,5},{8,10},{10,8},{9,1... | collective-permute-start | bytes 2359304 | tf_op jit(solution)/shard_map/ppermute | solution.py:28
  3.7 1.6 %collective-permute-start.1 = (bf16[128,512]{1,0:T(8,128)(2,1)}, bf16[128,512]{1,0:T(8,128)(2,1)S(1)}, u32[]{:S(2)}, u32[]{:S(2)}) collective-permute-start(bf16[128,512]{1,0:T(8,128)(2,1)} %refs_2_.1), channel_id=1, source_target_pairs={{0,4},{4,8},{8,12},{12,0},{1,5},{5,9},{9,13},{13,1},{2,6},{6,10},{... | collective-permute-start | bytes 393224 | tf_op jit(solution)/shard_map/ppermute | solution.py:28
  5.2 2.6 %collective-permute-start.2 = (bf16[128,512]{1,0:T(8,128)(2,1)}, bf16[128,512]{1,0:T(8,128)(2,1)S(1)}, u32[]{:S(2)}, u32[]{:S(2)}) collective-permute-start(bf16[128,512]{1,0:T(8,128)(2,1)} %refs_2_.1), channel_id=1, source_target_pairs={{0,8},{4,12},{8,0},{12,4},{1,9},{5,13},{9,1},{13,5},{2,10},{6,14},... | collective-permute-start | bytes 393224 | tf_op jit(solution)/shard_map/ppermute | solution.py:28
  7.8 1.3 %collective-permute-start.3 = (bf16[128,512]{1,0:T(8,128)(2,1)}, bf16[128,512]{1,0:T(8,128)(2,1)S(1)}, u32[]{:S(2)}, u32[]{:S(2)}) collective-permute-start(bf16[128,512]{1,0:T(8,128)(2,1)} %refs_2_.1), channel_id=1, source_target_pairs={{0,12},{4,0},{8,4},{12,8},{1,13},{5,1},{9,5},{13,9},{2,14},{6,2},{... | collective-permute-start | bytes 393224 | tf_op jit(solution)/shard_map/ppermute | solution.py:28
  9.2 1.2 %fusion.5 = (bf16[768,256]{1,0:T(8,128)(2,1)S(1)}, bf16[768,256]{1,0:T(8,128)(2,1)S(1)}) fusion(bf16[768,512]{1,0:T(8,128)(2,1)} %bitcast.25), kind=kLoop, calls=%fused_computation.22 | loop fusion | bytes 1572864 | tf_op jit(solution)/shard_map/slice | solution.py:333
  10.3 1.8 %collective-permute-done.1.refs_3_ = bf16[128,512]{1,0:T(8,128)(2,1)S(1)} collective-permute-done((bf16[128,512]{1,0:T(8,128)(2,1)}, bf16[128,512]{1,0:T(8,128)(2,1)S(1)}, u32[]{:S(2)}, u32[]{:S(2)}) %collective-permute-start.1) | collective-permute-done | bytes 131104 | tf_op jit(solution)/shard_map/ppermute | solution.py:28
  12.2 0.3 collective-permute-start.21
  12.5 0.7 fusion.slot_ref
  13.1 3.3 %collective-permute-done.2.refs_4_ = bf16[128,512]{1,0:T(8,128)(2,1)S(1)} collective-permute-done((bf16[128,512]{1,0:T(8,128)(2,1)}, bf16[128,512]{1,0:T(8,128)(2,1)S(1)}, u32[]{:S(2)}, u32[]{:S(2)}) %collective-permute-start.2) | collective-permute-done | bytes 131104 | tf_op jit(solution)/shard_map/ppermute | solution.py:28
  16.4 0.5 collective-permute-start.6
  17.1 0.7 pad_add_fusion.refs_1_
  17.8 0.6 collective-permute-start
  18.4 1.5 %collective-permute-start.9 = (bf16[768,256]{1,0:T(8,128)(2,1)S(1)}, bf16[768,256]{1,0:T(8,128)(2,1)S(1)}, u32[]{:S(2)}, u32[]{:S(2)}) collective-permute-start(bf16[768,256]{1,0:T(8,128)(2,1)S(1)} %get-tuple-element.29), channel_id=1, source_target_pairs={{0,2},{2,0},{1,3},{3,1},{4,6},{6,4},{5,7},{7,5},{8,10},{10,8},{9,1... | collective-permute-start | bytes 1179656 | tf_op jit(solution)/shard_map/ppermute | solution.py:28
  19.9 0.9 %copy-done.4 = bf16[128,512]{1,0:T(8,128)(2,1)S(1)} copy-done((bf16[128,512]{1,0:T(8,128)(2,1)S(1)}, bf16[128,512]{1,0:T(8,128)(2,1)}, u32[]{:S(2)}) %copy-start.4) | copy-done | bytes 131096
  20.8 2.4 %far_own.1 = (f32[1024,512]{1,0:T(8,128)S(1)}, bf16[1024,512]{1,0:T(8,128)(2,1)S(1)}) custom-call(s32[2]{0:T(128)S(1)} %pad_add_fusion.1.refs_0_, s32[3,12]{1,0:T(4,128)S(1)} %pad_add_fusion.refs_1_, bf16[128,512]{1,0:T(8,128)(2,1)S(1)} %copy-done.4, bf16[128,512]{1,0:T(8,128)(2,1)S(1)} %collective-permute-done.1.refs_3_, ...), custom_call_target="tpu_custom_call" | custom-call | flops 1 | bytes 1 | tf_op jit(solution)/shard_map/far_own/pallas_call | solution.py:45
  23.2 3.4 %copy-done = bf16[1,16,512,512]{3,2,1,0:T(8,128)(2,1)S(1)} copy-done((bf16[1,16,512,512]{3,2,1,0:T(8,128)(2,1)S(1)}, bf16[1,16,512,512]{3,2,1,0:T(8,128)(2,1)}, u32[]{:S(2)}) %copy-start) | copy-done | bytes 8388632
  26.6 3.9 %near_field.2.refs_4_ = f32[128,512]{1,0:T(8,128)S(1)} custom-call(s32[16]{0:T(128)S(1)} %fusion.slot_ref, bf16[1024,512]{1,0:T(8,128)(2,1)S(1)} %get-tuple-element.16.refs_0_.refs_2_, bf16[16,512,512]{2,1,0:T(8,128)(2,1)S(1)} %bitcast.21), custom_call_target="tpu_custom_call" | custom-call | flops 1 | bytes 1 | tf_op jit(solution)/shard_map/near_field/pallas_call | solution.py:226
  30.5 0.2 collective-permute-done.refs_1_.refs_2_
  30.7 1.7 %far_first_stage.1.refs_0_ = bf16[1024,768]{1,0:T(8,128)(2,1)S(1)} custom-call(s32[2]{0:T(128)S(1)} %pad_add_fusion.1.refs_0_, s32[3,12]{1,0:T(4,128)S(1)} %collective-permute-done.refs_1_.refs_2_, bf16[1024,512]{1,0:T(8,128)(2,1)S(1)} %get-tuple-element.16.refs_0_.refs_2_, bf16[768,512]{1,0:T(8,128)(2,1)S(1)} %collective-permute-done.8.refs_3_.refs_20_), custom_call_target="tpu_custom_call" | custom-call | flops 1 | bytes 1 | tf_op jit(solution)/shard_map/far_first_stage/pallas_call | solution.py:45
  32.4 0.6 far_second_stage.3
  33.1 5.2 %collective-permute-done.9.refs_2_.refs_22_ = bf16[768,256]{1,0:T(8,128)(2,1)S(1)} collective-permute-done((bf16[768,256]{1,0:T(8,128)(2,1)S(1)}, bf16[768,256]{1,0:T(8,128)(2,1)S(1)}, u32[]{:S(2)}, u32[]{:S(2)}) %collective-permute-start.9) | collective-permute-done | bytes 393248 | tf_op jit(solution)/shard_map/ppermute | solution.py:28
  38.3 0.6 far_second_stage.2
  39.1 1.9 %collective-permute-start.23 = (bf16[128,256]{1,0:T(8,128)(2,1)S(1)}, bf16[128,256]{1,0:T(8,128)(2,1)S(1)}, u32[]{:S(2)}, u32[]{:S(2)}) collective-permute-start(bf16[128,256]{1,0:T(8,128)(2,1)S(1)} %get-tuple-element.36), channel_id=1, source_target_pairs={{0,4},{4,8},{8,12},{12,0},{1,5},{5,9},{9,13},{13,1},{2,6},{6,10},{... | collective-permute-start | bytes 196616 | tf_op jit(solution)/shard_map/ppermute | solution.py:28
  41.0 2.6 %collective-permute-start.24 = (bf16[128,256]{1,0:T(8,128)(2,1)S(1)}, bf16[128,256]{1,0:T(8,128)(2,1)S(1)}, u32[]{:S(2)}, u32[]{:S(2)}) collective-permute-start(bf16[128,256]{1,0:T(8,128)(2,1)S(1)} %get-tuple-element.35), channel_id=1, source_target_pairs={{0,8},{4,12},{8,0},{12,4},{1,9},{5,13},{9,1},{13,5},{2,10},{6,14},... | collective-permute-start | bytes 196616 | tf_op jit(solution)/shard_map/ppermute | solution.py:28
  43.6 1.3 %collective-permute-start.25 = (bf16[128,256]{1,0:T(8,128)(2,1)S(1)}, bf16[128,256]{1,0:T(8,128)(2,1)S(1)}, u32[]{:S(2)}, u32[]{:S(2)}) collective-permute-start(bf16[128,256]{1,0:T(8,128)(2,1)S(1)} %get-tuple-element.34), channel_id=1, source_target_pairs={{0,12},{4,0},{8,4},{12,8},{1,13},{5,1},{9,5},{13,9},{2,14},{6,2},{... | collective-permute-start | bytes 196616 | tf_op jit(solution)/shard_map/ppermute | solution.py:28
  45.0 0.7 collective-permute-start.11
  45.8 0.3 collective-permute-start.12
  46.1 2.8 %collective-permute-start.13 = (bf16[128,256]{1,0:T(8,128)(2,1)S(1)}, bf16[128,256]{1,0:T(8,128)(2,1)S(1)}, u32[]{:S(2)}, u32[]{:S(2)}) collective-permute-start(bf16[128,256]{1,0:T(8,128)(2,1)S(1)} %get-tuple-element.38), channel_id=1, source_target_pairs={{0,12},{4,0},{8,4},{12,8},{1,13},{5,1},{9,5},{13,9},{2,14},{6,2},{... | collective-permute-start | bytes 196616 | tf_op jit(solution)/shard_map/ppermute | solution.py:28
  49.1 4.5 %collective-permute-start.26 = (bf16[128,256]{1,0:T(8,128)(2,1)S(1)}, bf16[128,256]{1,0:T(8,128)(2,1)S(1)}, u32[]{:S(2)}, u32[]{:S(2)}) collective-permute-start(bf16[128,256]{1,0:T(8,128)(2,1)S(1)} %finish.4.refs_11_), channel_id=1, source_target_pairs={{0,4},{4,8},{8,12},{12,0},{1,5},{5,9},{9,13},{13,1},{2,6},{6,10},{... | collective-permute-start | bytes 196616 | tf_op jit(solution)/shard_map/ppermute | solution.py:28
  53.6 2.4 %collective-permute-start.28 = (bf16[128,256]{1,0:T(8,128)(2,1)S(1)}, bf16[128,256]{1,0:T(8,128)(2,1)S(1)}, u32[]{:S(2)}, u32[]{:S(2)}) collective-permute-start(bf16[128,256]{1,0:T(8,128)(2,1)S(1)} %finish.4.refs_11_), channel_id=1, source_target_pairs={{0,12},{4,0},{8,4},{12,8},{1,13},{5,1},{9,5},{13,9},{2,14},{6,2},{... | collective-permute-start | bytes 196616 | tf_op jit(solution)/shard_map/ppermute | solution.py:28
  56.3 2.4 %collective-permute-start.14 = (bf16[128,256]{1,0:T(8,128)(2,1)S(1)}, bf16[128,256]{1,0:T(8,128)(2,1)S(1)}, u32[]{:S(2)}, u32[]{:S(2)}) collective-permute-start(bf16[128,256]{1,0:T(8,128)(2,1)S(1)} %finish.3.refs_3_), channel_id=1, source_target_pairs={{0,4},{4,8},{8,12},{12,0},{1,5},{5,9},{9,13},{13,1},{2,6},{6,10},{... | collective-permute-start | bytes 196616 | tf_op jit(solution)/shard_map/ppermute | solution.py:28
  58.8 1.2 %collective-permute-done.27.refs_13_ = bf16[128,256]{1,0:T(8,128)(2,1)S(1)} collective-permute-done((bf16[128,256]{1,0:T(8,128)(2,1)S(1)}, bf16[128,256]{1,0:T(8,128)(2,1)S(1)}, u32[]{:S(2)}, u32[]{:S(2)}) %collective-permute-start.27) | collective-permute-done | bytes 65568 | tf_op jit(solution)/shard_map/ppermute | solution.py:28
  60.0 3.2 %collective-permute-start.16 = (bf16[128,256]{1,0:T(8,128)(2,1)S(1)}, bf16[128,256]{1,0:T(8,128)(2,1)S(1)}, u32[]{:S(2)}, u32[]{:S(2)}) collective-permute-start(bf16[128,256]{1,0:T(8,128)(2,1)S(1)} %finish.3.refs_3_), channel_id=1, source_target_pairs={{0,12},{4,0},{8,4},{12,8},{1,13},{5,1},{9,5},{13,9},{2,14},{6,2},{... | collective-permute-start | bytes 196616 | tf_op jit(solution)/shard_map/ppermute | solution.py:28
  63.2 0.5 collective-permute-start.30
  63.8 1.8 %collective-permute-done.15.refs_5_ = bf16[128,256]{1,0:T(8,128)(2,1)S(1)} collective-permute-done((bf16[128,256]{1,0:T(8,128)(2,1)S(1)}, bf16[128,256]{1,0:T(8,128)(2,1)S(1)}, u32[]{:S(2)}, u32[]{:S(2)}) %collective-permute-start.15) | collective-permute-done | bytes 65568 | tf_op jit(solution)/shard_map/ppermute | solution.py:28
  65.6 0.5 collective-permute-start.18
  66.1 0.4 collective-permute-start.20
  66.6 0.2 collective-permute-done.32.refs_18_
  67.0 0.4 collective-permute-done.19.refs_9_
  67.5 3.3 %far_sent.1 = (bf16[512,512]{1,0:T(8,128)(2,1)S(1)}, bf16[1024,512]{1,0:T(8,128)(2,1)S(1)}, bf16[512,1536]{1,0:T(8,128)(2,1)S(1)}) custom-call(s32[2]{0:T(128)S(1)} %pad_add_fusion.1.refs_0_, s32[3,12]{1,0:T(4,128)S(1)} %pad_add_fusion.refs_1_, s32[3,12]{1,0:T(4,128)S(1)} %collective-permute-done.refs_1_.refs_2_, bf16[128,256]{1,0:T(8,128)(2,1)S(1)} %finish.3.refs_3_, ...), custom_call_target="tpu_custom_call" | custom-call | flops 1 | bytes 1 | tf_op jit(solution)/shard_map/far_sent/pallas_call | solution.py:45
  70.8 0.4 collective-permute-start.33
  71.2 1.0 %far_kept.1 = bf16[512,512]{1,0:T(8,128)(2,1)S(1)} custom-call(bf16[512,1536]{1,0:T(8,128)(2,1)S(1)} %get-tuple-element.25.refs_0_, bf16[768,512]{1,0:T(8,128)(2,1)S(1)} %bitcast.29, bf16[768,256]{1,0:T(8,128)(2,1)S(1)} %collective-permute-done.9.refs_2_.refs_22_, bf16[768,512]{1,0:T(8,128)(2,1)S(1)} %bitcast.30, ...), custom_call_target="tpu_custom_call" | custom-call | flops 10000000000 | bytes 1 | tf_op jit(solution)/shard_map/far_kept/pallas_call | solution.py:45
  72.2 0.6 collective-permute-done.33
  72.9 1.7 %collective-permute-start.34 = (bf16[128,512]{1,0:T(8,128)(2,1)S(1)}, bf16[128,512]{1,0:T(8,128)(2,1)S(1)}, u32[]{:S(2)}, u32[]{:S(2)}) collective-permute-start(bf16[128,512]{1,0:T(8,128)(2,1)S(1)} %get-tuple-element.32), channel_id=1, source_target_pairs={{0,4},{4,8},{8,12},{12,0},{1,5},{5,9},{9,13},{13,1},{2,6},{6,10},{... | collective-permute-start | bytes 393224 | tf_op jit(solution)/shard_map/ppermute | solution.py:28
  74.7 2.4 %collective-permute-start.35 = (bf16[128,512]{1,0:T(8,128)(2,1)S(1)}, bf16[128,512]{1,0:T(8,128)(2,1)S(1)}, u32[]{:S(2)}, u32[]{:S(2)}) collective-permute-start(bf16[128,512]{1,0:T(8,128)(2,1)S(1)} %get-tuple-element.31), channel_id=1, source_target_pairs={{0,8},{4,12},{8,0},{12,4},{1,9},{5,13},{9,1},{13,5},{2,10},{6,14},... | collective-permute-start | bytes 393224 | tf_op jit(solution)/shard_map/ppermute | solution.py:28
  77.1 4.5 %near_field.3 = (f32[128,512]{1,0:T(8,128)S(1)}, bf16[128,512]{1,0:T(8,128)(2,1)}) custom-call(s32[16]{0:T(128)S(1)} %fusion.slot_ref, bf16[1024,512]{1,0:T(8,128)(2,1)S(1)} %get-tuple-element.23.refs_0_, bf16[16,512,512]{2,1,0:T(8,128)(2,1)S(1)} %bitcast.24), custom_call_target="tpu_custom_call" | custom-call | flops 1 | bytes 1 | tf_op jit(solution)/shard_map/near_field/pallas_call | solution.py:226
  81.6 4.6 %collective-permute-done.35.refs_2_ = bf16[128,512]{1,0:T(8,128)(2,1)S(1)} collective-permute-done((bf16[128,512]{1,0:T(8,128)(2,1)S(1)}, bf16[128,512]{1,0:T(8,128)(2,1)S(1)}, u32[]{:S(2)}, u32[]{:S(2)}) %collective-permute-start.35) | collective-permute-done | bytes 131104 | tf_op jit(solution)/shard_map/ppermute | solution.py:28
  86.3 0.9 finish.5
  (62 shorter events, 1.8 us)
Async XLA Ops:
  0.6 19.3 %copy-start.2 = (bf16[12,64,512]{2,1,0:T(8,128)(2,1)S(1)}, bf16[12,64,512]{2,1,0:T(8,128)(2,1)}, u32[]{:S(2)}) copy-start(bf16[12,64,512]{2,1,0:T(8,128)(2,1)} %param.11) | copy-start | bytes 2359300
  0.6 19.3 %copy-start.1 = (bf16[12,64,512]{2,1,0:T(8,128)(2,1)S(1)}, bf16[12,64,512]{2,1,0:T(8,128)(2,1)}, u32[]{:S(2)}) copy-start(bf16[12,64,512]{2,1,0:T(8,128)(2,1)} %param.10) | copy-start | bytes 2359300
  0.6 30.1 %collective-permute-start.8 = (bf16[768,512]{1,0:T(8,128)(2,1)}, bf16[768,512]{1,0:T(8,128)(2,1)S(1)}, u32[]{:S(2)}, u32[]{:S(2)}) collective-permute-start(bf16[768,512]{1,0:T(8,128)(2,1)} %bitcast.31), channel_id=1, source_target_pairs={{0,2},{2,0},{1,3},{3,1},{4,6},{6,4},{5,7},{7,5},{8,10},{10,8},{9,1... | collective-permute-start | bytes 2359304 | tf_op jit(solution)/shard_map/ppermute | solution.py:28
  3.7 8.5 %collective-permute-start.1 = (bf16[128,512]{1,0:T(8,128)(2,1)}, bf16[128,512]{1,0:T(8,128)(2,1)S(1)}, u32[]{:S(2)}, u32[]{:S(2)}) collective-permute-start(bf16[128,512]{1,0:T(8,128)(2,1)} %refs_2_.1), channel_id=1, source_target_pairs={{0,4},{4,8},{8,12},{12,0},{1,5},{5,9},{9,13},{13,1},{2,6},{6,10},{... | collective-permute-start | bytes 393224 | tf_op jit(solution)/shard_map/ppermute | solution.py:28
  5.2 11.2 %collective-permute-start.2 = (bf16[128,512]{1,0:T(8,128)(2,1)}, bf16[128,512]{1,0:T(8,128)(2,1)S(1)}, u32[]{:S(2)}, u32[]{:S(2)}) collective-permute-start(bf16[128,512]{1,0:T(8,128)(2,1)} %refs_2_.1), channel_id=1, source_target_pairs={{0,8},{4,12},{8,0},{12,4},{1,9},{5,13},{9,1},{13,5},{2,10},{6,14},... | collective-permute-start | bytes 393224 | tf_op jit(solution)/shard_map/ppermute | solution.py:28
  7.8 8.6 %collective-permute-start.3 = (bf16[128,512]{1,0:T(8,128)(2,1)}, bf16[128,512]{1,0:T(8,128)(2,1)S(1)}, u32[]{:S(2)}, u32[]{:S(2)}) collective-permute-start(bf16[128,512]{1,0:T(8,128)(2,1)} %refs_2_.1), channel_id=1, source_target_pairs={{0,12},{4,0},{8,4},{12,8},{1,13},{5,1},{9,5},{13,9},{2,14},{6,2},{... | collective-permute-start | bytes 393224 | tf_op jit(solution)/shard_map/ppermute | solution.py:28
  9.2 7.8 %collective-permute-start.4 = (bf16[128,512]{1,0:T(8,128)(2,1)}, bf16[128,512]{1,0:T(8,128)(2,1)S(1)}, u32[]{:S(2)}, u32[]{:S(2)}) collective-permute-start(bf16[128,512]{1,0:T(8,128)(2,1)} %refs_2_.1), channel_id=1, source_target_pairs={{0,1},{1,0},{2,3},{3,2},{4,5},{5,4},{6,7},{7,6},{8,9},{9,8},{10,11... | collective-permute-start | bytes 393224 | tf_op jit(solution)/shard_map/ppermute | solution.py:28
  12.2 20.3 %collective-permute-start.21 = (bf16[768,256]{1,0:T(8,128)(2,1)S(1)}, bf16[768,256]{1,0:T(8,128)(2,1)S(1)}, u32[]{:S(2)}, u32[]{:S(2)}) collective-permute-start(bf16[768,256]{1,0:T(8,128)(2,1)S(1)} %get-tuple-element.28), channel_id=1, source_target_pairs={{0,2},{2,0},{1,3},{3,1},{4,6},{6,4},{5,7},{7,5},{8,10},{10,8},{9,1... | collective-permute-start | bytes 1179656 | tf_op jit(solution)/shard_map/ppermute | solution.py:28
  16.4 1.4 %collective-permute-start.5 = (bf16[128,512]{1,0:T(8,128)(2,1)S(1)}, bf16[128,512]{1,0:T(8,128)(2,1)S(1)}, u32[]{:S(2)}, u32[]{:S(2)}) collective-permute-start(bf16[128,512]{1,0:T(8,128)(2,1)S(1)} %collective-permute-done.1.refs_3_), channel_id=1, source_target_pairs={{0,1},{1,0},{2,3},{3,2},{4,5},{5,4},{6,7},{7,6},{8,9},{9,8},{10,11... | collective-permute-start | bytes 393224 | tf_op jit(solution)/shard_map/ppermute | solution.py:28
  16.4 1.9 %collective-permute-start.6 = (bf16[128,512]{1,0:T(8,128)(2,1)S(1)}, bf16[128,512]{1,0:T(8,128)(2,1)S(1)}, u32[]{:S(2)}, u32[]{:S(2)}) collective-permute-start(bf16[128,512]{1,0:T(8,128)(2,1)S(1)} %collective-permute-done.2.refs_4_), channel_id=1, source_target_pairs={{0,1},{1,0},{2,3},{3,2},{4,5},{5,4},{6,7},{7,6},{8,9},{9,8},{10,11... | collective-permute-start | bytes 393224 | tf_op jit(solution)/shard_map/ppermute | solution.py:28
  17.0 2.9 %collective-permute-start.7 = (bf16[128,512]{1,0:T(8,128)(2,1)S(1)}, bf16[128,512]{1,0:T(8,128)(2,1)S(1)}, u32[]{:S(2)}, u32[]{:S(2)}) collective-permute-start(bf16[128,512]{1,0:T(8,128)(2,1)S(1)} %collective-permute-done.3.refs_5_), channel_id=1, source_target_pairs={{0,1},{1,0},{2,3},{3,2},{4,5},{5,4},{6,7},{7,6},{8,9},{9,8},{10,11... | collective-permute-start | bytes 393224 | tf_op jit(solution)/shard_map/ppermute | solution.py:28
  17.8 12.9 %collective-permute-start = (s32[3,12]{1,0:T(4,128)S(1)}, s32[3,12]{1,0:T(4,128)S(1)}, u32[]{:S(2)}, u32[]{:S(2)}) collective-permute-start(s32[3,12]{1,0:T(4,128)S(1)} %pad_add_fusion.refs_1_), channel_id=1, source_target_pairs={{0,2},{2,0},{1,3},{3,1},{4,6},{6,4},{5,7},{7,5},{8,10},{10,8},{9,1... | collective-permute-start | bytes 440 | tf_op jit(solution)/shard_map/ppermute | solution.py:28
  18.4 19.9 %collective-permute-start.9 = (bf16[768,256]{1,0:T(8,128)(2,1)S(1)}, bf16[768,256]{1,0:T(8,128)(2,1)S(1)}, u32[]{:S(2)}, u32[]{:S(2)}) collective-permute-start(bf16[768,256]{1,0:T(8,128)(2,1)S(1)} %get-tuple-element.29), channel_id=1, source_target_pairs={{0,2},{2,0},{1,3},{3,1},{4,6},{6,4},{5,7},{7,5},{8,10},{10,8},{9,1... | collective-permute-start | bytes 1179656 | tf_op jit(solution)/shard_map/ppermute | solution.py:28
  19.9 0.9 %copy-start.4 = (bf16[128,512]{1,0:T(8,128)(2,1)S(1)}, bf16[128,512]{1,0:T(8,128)(2,1)}, u32[]{:S(2)}) copy-start(bf16[128,512]{1,0:T(8,128)(2,1)} %refs_2_.1) | copy-start | bytes 393220
  23.2 3.4 %copy-start = (bf16[1,16,512,512]{3,2,1,0:T(8,128)(2,1)S(1)}, bf16[1,16,512,512]{3,2,1,0:T(8,128)(2,1)}, u32[]{:S(2)}) copy-start(bf16[1,16,512,512]{3,2,1,0:T(8,128)(2,1)} %param.15) | copy-start | bytes 25165828
  33.1 5.9 %collective-permute-start.22 = (bf16[512,256]{1,0:T(8,128)(2,1)S(1)}, bf16[512,256]{1,0:T(8,128)(2,1)S(1)}, u32[]{:S(2)}, u32[]{:S(2)}) collective-permute-start(bf16[512,256]{1,0:T(8,128)(2,1)S(1)} %get-tuple-element.22), channel_id=1, source_target_pairs={{0,1},{1,0},{2,3},{3,2},{4,5},{5,4},{6,7},{7,6},{8,9},{9,8},{10,11... | collective-permute-start | bytes 786440 | tf_op jit(solution)/shard_map/ppermute | solution.py:28
  38.9 10.0 %copy-start.3 = (bf16[4,128,128]{2,1,0:T(8,128)(2,1)S(1)}, bf16[4,128,128]{2,1,0:T(8,128)(2,1)}, u32[]{:S(2)}) copy-start(bf16[4,128,128]{2,1,0:T(8,128)(2,1)} %refs_5_.5) | copy-start | bytes 393220
  38.9 6.0 %collective-permute-start.10 = (bf16[512,256]{1,0:T(8,128)(2,1)S(1)}, bf16[512,256]{1,0:T(8,128)(2,1)S(1)}, u32[]{:S(2)}, u32[]{:S(2)}) collective-permute-start(bf16[512,256]{1,0:T(8,128)(2,1)S(1)} %get-tuple-element.19), channel_id=1, source_target_pairs={{0,1},{1,0},{2,3},{3,2},{4,5},{5,4},{6,7},{7,6},{8,9},{9,8},{10,11... | collective-permute-start | bytes 786440 | tf_op jit(solution)/shard_map/ppermute | solution.py:28
  39.1 7.0 %collective-permute-start.23 = (bf16[128,256]{1,0:T(8,128)(2,1)S(1)}, bf16[128,256]{1,0:T(8,128)(2,1)S(1)}, u32[]{:S(2)}, u32[]{:S(2)}) collective-permute-start(bf16[128,256]{1,0:T(8,128)(2,1)S(1)} %get-tuple-element.36), channel_id=1, source_target_pairs={{0,4},{4,8},{8,12},{12,0},{1,5},{5,9},{9,13},{13,1},{2,6},{6,10},{... | collective-permute-start | bytes 196616 | tf_op jit(solution)/shard_map/ppermute | solution.py:28
  41.0 7.9 %collective-permute-start.24 = (bf16[128,256]{1,0:T(8,128)(2,1)S(1)}, bf16[128,256]{1,0:T(8,128)(2,1)S(1)}, u32[]{:S(2)}, u32[]{:S(2)}) collective-permute-start(bf16[128,256]{1,0:T(8,128)(2,1)S(1)} %get-tuple-element.35), channel_id=1, source_target_pairs={{0,8},{4,12},{8,0},{12,4},{1,9},{5,13},{9,1},{13,5},{2,10},{6,14},... | collective-permute-start | bytes 196616 | tf_op jit(solution)/shard_map/ppermute | solution.py:28
  43.6 5.3 %collective-permute-start.25 = (bf16[128,256]{1,0:T(8,128)(2,1)S(1)}, bf16[128,256]{1,0:T(8,128)(2,1)S(1)}, u32[]{:S(2)}, u32[]{:S(2)}) collective-permute-start(bf16[128,256]{1,0:T(8,128)(2,1)S(1)} %get-tuple-element.34), channel_id=1, source_target_pairs={{0,12},{4,0},{8,4},{12,8},{1,13},{5,1},{9,5},{13,9},{2,14},{6,2},{... | collective-permute-start | bytes 196616 | tf_op jit(solution)/shard_map/ppermute | solution.py:28
  45.0 8.6 %collective-permute-start.11 = (bf16[128,256]{1,0:T(8,128)(2,1)S(1)}, bf16[128,256]{1,0:T(8,128)(2,1)S(1)}, u32[]{:S(2)}, u32[]{:S(2)}) collective-permute-start(bf16[128,256]{1,0:T(8,128)(2,1)S(1)} %get-tuple-element.40), channel_id=1, source_target_pairs={{0,4},{4,8},{8,12},{12,0},{1,5},{5,9},{9,13},{13,1},{2,6},{6,10},{... | collective-permute-start | bytes 196616 | tf_op jit(solution)/shard_map/ppermute | solution.py:28
  45.8 10.3 %collective-permute-start.12 = (bf16[128,256]{1,0:T(8,128)(2,1)S(1)}, bf16[128,256]{1,0:T(8,128)(2,1)S(1)}, u32[]{:S(2)}, u32[]{:S(2)}) collective-permute-start(bf16[128,256]{1,0:T(8,128)(2,1)S(1)} %get-tuple-element.39), channel_id=1, source_target_pairs={{0,8},{4,12},{8,0},{12,4},{1,9},{5,13},{9,1},{13,5},{2,10},{6,14},... | collective-permute-start | bytes 196616 | tf_op jit(solution)/shard_map/ppermute | solution.py:28
  46.1 10.0 %collective-permute-start.13 = (bf16[128,256]{1,0:T(8,128)(2,1)S(1)}, bf16[128,256]{1,0:T(8,128)(2,1)S(1)}, u32[]{:S(2)}, u32[]{:S(2)}) collective-permute-start(bf16[128,256]{1,0:T(8,128)(2,1)S(1)} %get-tuple-element.38), channel_id=1, source_target_pairs={{0,12},{4,0},{8,4},{12,8},{1,13},{5,1},{9,5},{13,9},{2,14},{6,2},{... | collective-permute-start | bytes 196616 | tf_op jit(solution)/shard_map/ppermute | solution.py:28
  49.1 9.6 %collective-permute-start.26 = (bf16[128,256]{1,0:T(8,128)(2,1)S(1)}, bf16[128,256]{1,0:T(8,128)(2,1)S(1)}, u32[]{:S(2)}, u32[]{:S(2)}) collective-permute-start(bf16[128,256]{1,0:T(8,128)(2,1)S(1)} %finish.4.refs_11_), channel_id=1, source_target_pairs={{0,4},{4,8},{8,12},{12,0},{1,5},{5,9},{9,13},{13,1},{2,6},{6,10},{... | collective-permute-start | bytes 196616 | tf_op jit(solution)/shard_map/ppermute | solution.py:28
  53.6 6.4 %collective-permute-start.27 = (bf16[128,256]{1,0:T(8,128)(2,1)S(1)}, bf16[128,256]{1,0:T(8,128)(2,1)S(1)}, u32[]{:S(2)}, u32[]{:S(2)}) collective-permute-start(bf16[128,256]{1,0:T(8,128)(2,1)S(1)} %finish.4.refs_11_), channel_id=1, source_target_pairs={{0,8},{4,12},{8,0},{12,4},{1,9},{5,13},{9,1},{13,5},{2,10},{6,14},... | collective-permute-start | bytes 196616 | tf_op jit(solution)/shard_map/ppermute | solution.py:28
  53.6 9.6 %collective-permute-start.28 = (bf16[128,256]{1,0:T(8,128)(2,1)S(1)}, bf16[128,256]{1,0:T(8,128)(2,1)S(1)}, u32[]{:S(2)}, u32[]{:S(2)}) collective-permute-start(bf16[128,256]{1,0:T(8,128)(2,1)S(1)} %finish.4.refs_11_), channel_id=1, source_target_pairs={{0,12},{4,0},{8,4},{12,8},{1,13},{5,1},{9,5},{13,9},{2,14},{6,2},{... | collective-permute-start | bytes 196616 | tf_op jit(solution)/shard_map/ppermute | solution.py:28
  56.1 7.1 %collective-permute-start.29 = (bf16[128,256]{1,0:T(8,128)(2,1)S(1)}, bf16[128,256]{1,0:T(8,128)(2,1)S(1)}, u32[]{:S(2)}, u32[]{:S(2)}) collective-permute-start(bf16[128,256]{1,0:T(8,128)(2,1)S(1)} %finish.4.refs_11_), channel_id=1, source_target_pairs={{0,1},{1,0},{2,3},{3,2},{4,5},{5,4},{6,7},{7,6},{8,9},{9,8},{10,11... | collective-permute-start | bytes 196616 | tf_op jit(solution)/shard_map/ppermute | solution.py:28
  56.3 7.4 %collective-permute-start.14 = (bf16[128,256]{1,0:T(8,128)(2,1)S(1)}, bf16[128,256]{1,0:T(8,128)(2,1)S(1)}, u32[]{:S(2)}, u32[]{:S(2)}) collective-permute-start(bf16[128,256]{1,0:T(8,128)(2,1)S(1)} %finish.3.refs_3_), channel_id=1, source_target_pairs={{0,4},{4,8},{8,12},{12,0},{1,5},{5,9},{9,13},{13,1},{2,6},{6,10},{... | collective-permute-start | bytes 196616 | tf_op jit(solution)/shard_map/ppermute | solution.py:28
  58.7 6.8 %collective-permute-start.15 = (bf16[128,256]{1,0:T(8,128)(2,1)S(1)}, bf16[128,256]{1,0:T(8,128)(2,1)S(1)}, u32[]{:S(2)}, u32[]{:S(2)}) collective-permute-start(bf16[128,256]{1,0:T(8,128)(2,1)S(1)} %finish.3.refs_3_), channel_id=1, source_target_pairs={{0,8},{4,12},{8,0},{12,4},{1,9},{5,13},{9,1},{13,5},{2,10},{6,14},... | collective-permute-start | bytes 196616 | tf_op jit(solution)/shard_map/ppermute | solution.py:28
  60.0 5.6 %collective-permute-start.16 = (bf16[128,256]{1,0:T(8,128)(2,1)S(1)}, bf16[128,256]{1,0:T(8,128)(2,1)S(1)}, u32[]{:S(2)}, u32[]{:S(2)}) collective-permute-start(bf16[128,256]{1,0:T(8,128)(2,1)S(1)} %finish.3.refs_3_), channel_id=1, source_target_pairs={{0,12},{4,0},{8,4},{12,8},{1,13},{5,1},{9,5},{13,9},{2,14},{6,2},{... | collective-permute-start | bytes 196616 | tf_op jit(solution)/shard_map/ppermute | solution.py:28
  63.2 2.9 %collective-permute-start.17 = (bf16[128,256]{1,0:T(8,128)(2,1)S(1)}, bf16[128,256]{1,0:T(8,128)(2,1)S(1)}, u32[]{:S(2)}, u32[]{:S(2)}) collective-permute-start(bf16[128,256]{1,0:T(8,128)(2,1)S(1)} %finish.3.refs_3_), channel_id=1, source_target_pairs={{0,1},{1,0},{2,3},{3,2},{4,5},{5,4},{6,7},{7,6},{8,9},{9,8},{10,11... | collective-permute-start | bytes 196616 | tf_op jit(solution)/shard_map/ppermute | solution.py:28
  63.2 2.9 %collective-permute-start.30 = (bf16[128,256]{1,0:T(8,128)(2,1)S(1)}, bf16[128,256]{1,0:T(8,128)(2,1)S(1)}, u32[]{:S(2)}, u32[]{:S(2)}) collective-permute-start(bf16[128,256]{1,0:T(8,128)(2,1)S(1)} %collective-permute-done.26.refs_12_), channel_id=1, source_target_pairs={{0,1},{1,0},{2,3},{3,2},{4,5},{5,4},{6,7},{7,6},{8,9},{9,8},{10,11... | collective-permute-start | bytes 196616 | tf_op jit(solution)/shard_map/ppermute | solution.py:28
  63.7 2.9 %collective-permute-start.31 = (bf16[128,256]{1,0:T(8,128)(2,1)S(1)}, bf16[128,256]{1,0:T(8,128)(2,1)S(1)}, u32[]{:S(2)}, u32[]{:S(2)}) collective-permute-start(bf16[128,256]{1,0:T(8,128)(2,1)S(1)} %collective-permute-done.27.refs_13_), channel_id=1, source_target_pairs={{0,1},{1,0},{2,3},{3,2},{4,5},{5,4},{6,7},{7,6},{8,9},{9,8},{10,11... | collective-permute-start | bytes 196616 | tf_op jit(solution)/shard_map/ppermute | solution.py:28
  65.5 1.3 %collective-permute-start.32 = (bf16[128,256]{1,0:T(8,128)(2,1)S(1)}, bf16[128,256]{1,0:T(8,128)(2,1)S(1)}, u32[]{:S(2)}, u32[]{:S(2)}) collective-permute-start(bf16[128,256]{1,0:T(8,128)(2,1)S(1)} %collective-permute-done.28.refs_14_), channel_id=1, source_target_pairs={{0,1},{1,0},{2,3},{3,2},{4,5},{5,4},{6,7},{7,6},{8,9},{9,8},{10,11... | collective-permute-start | bytes 196616 | tf_op jit(solution)/shard_map/ppermute | solution.py:28
  65.6 1.4 %collective-permute-start.18 = (bf16[128,256]{1,0:T(8,128)(2,1)S(1)}, bf16[128,256]{1,0:T(8,128)(2,1)S(1)}, u32[]{:S(2)}, u32[]{:S(2)}) collective-permute-start(bf16[128,256]{1,0:T(8,128)(2,1)S(1)} %collective-permute-done.14.refs_4_), channel_id=1, source_target_pairs={{0,1},{1,0},{2,3},{3,2},{4,5},{5,4},{6,7},{7,6},{8,9},{9,8},{10,11... | collective-permute-start | bytes 196616 | tf_op jit(solution)/shard_map/ppermute | solution.py:28
  66.1 1.3 %collective-permute-start.19 = (bf16[128,256]{1,0:T(8,128)(2,1)S(1)}, bf16[128,256]{1,0:T(8,128)(2,1)S(1)}, u32[]{:S(2)}, u32[]{:S(2)}) collective-permute-start(bf16[128,256]{1,0:T(8,128)(2,1)S(1)} %collective-permute-done.15.refs_5_), channel_id=1, source_target_pairs={{0,1},{1,0},{2,3},{3,2},{4,5},{5,4},{6,7},{7,6},{8,9},{9,8},{10,11... | collective-permute-start | bytes 196616 | tf_op jit(solution)/shard_map/ppermute | solution.py:28
  66.1 1.3 %collective-permute-start.20 = (bf16[128,256]{1,0:T(8,128)(2,1)S(1)}, bf16[128,256]{1,0:T(8,128)(2,1)S(1)}, u32[]{:S(2)}, u32[]{:S(2)}) collective-permute-start(bf16[128,256]{1,0:T(8,128)(2,1)S(1)} %collective-permute-done.16.refs_6_), channel_id=1, source_target_pairs={{0,1},{1,0},{2,3},{3,2},{4,5},{5,4},{6,7},{7,6},{8,9},{9,8},{10,11... | collective-permute-start | bytes 196616 | tf_op jit(solution)/shard_map/ppermute | solution.py:28
  70.8 2.0 %collective-permute-start.33 = (bf16[512,512]{1,0:T(8,128)(2,1)S(1)}, bf16[512,512]{1,0:T(8,128)(2,1)S(1)}, u32[]{:S(2)}, u32[]{:S(2)}) collective-permute-start(bf16[512,512]{1,0:T(8,128)(2,1)S(1)} %get-tuple-element.26), channel_id=1, source_target_pairs={{0,1},{1,0},{2,3},{3,2},{4,5},{5,4},{6,7},{7,6},{8,9},{9,8},{10,11... | collective-permute-start | bytes 1572872 | tf_op jit(solution)/shard_map/ppermute | solution.py:28
  71.2 5.9 %slice-start = ((s8[8388608]{0:T(1024)(128)(4,1)}), s8[4194304]{0:T(1024)(128)(4,1)S(1)}, s32[]{:S(2)}) async-start(s8[8388608]{0:T(1024)(128)(4,1)} %bitcast.22), calls=%async_computation | async-start | bytes 8388608
  71.2 5.9 %slice-start.1 = ((s8[8388608]{0:T(1024)(128)(4,1)}), s8[4194304]{0:T(1024)(128)(4,1)S(1)}, s32[]{:S(2)}) async-start(s8[8388608]{0:T(1024)(128)(4,1)} %bitcast.22), calls=%async_computation.1 | async-start | bytes 8388608
  72.9 8.7 %collective-permute-start.34 = (bf16[128,512]{1,0:T(8,128)(2,1)S(1)}, bf16[128,512]{1,0:T(8,128)(2,1)S(1)}, u32[]{:S(2)}, u32[]{:S(2)}) collective-permute-start(bf16[128,512]{1,0:T(8,128)(2,1)S(1)} %get-tuple-element.32), channel_id=1, source_target_pairs={{0,4},{4,8},{8,12},{12,0},{1,5},{5,9},{9,13},{13,1},{2,6},{6,10},{... | collective-permute-start | bytes 393224 | tf_op jit(solution)/shard_map/ppermute | solution.py:28
  74.7 11.6 %collective-permute-start.35 = (bf16[128,512]{1,0:T(8,128)(2,1)S(1)}, bf16[128,512]{1,0:T(8,128)(2,1)S(1)}, u32[]{:S(2)}, u32[]{:S(2)}) collective-permute-start(bf16[128,512]{1,0:T(8,128)(2,1)S(1)} %get-tuple-element.31), channel_id=1, source_target_pairs={{0,8},{4,12},{8,0},{12,4},{1,9},{5,13},{9,1},{13,5},{2,10},{6,14},... | collective-permute-start | bytes 393224 | tf_op jit(solution)/shard_map/ppermute | solution.py:28
  77.1 9.1 %collective-permute-start.36 = (bf16[128,512]{1,0:T(8,128)(2,1)S(1)}, bf16[128,512]{1,0:T(8,128)(2,1)S(1)}, u32[]{:S(2)}, u32[]{:S(2)}) collective-permute-start(bf16[128,512]{1,0:T(8,128)(2,1)S(1)} %get-tuple-element.30), channel_id=1, source_target_pairs={{0,12},{4,0},{8,4},{12,8},{1,13},{5,1},{9,5},{13,9},{2,14},{6,2},{... | collective-permute-start | bytes 393224 | tf_op jit(solution)/shard_map/ppermute | solution.py:28

commit v6 on v5

--- a/solution.py
+++ b/solution.py
@@ -91,33 +91,34 @@
 
 def first_stage(numbers, sizes, stacked, ins, lanes, previous, coeff, masked):
     place, tables = numbers
-    n_pieces = sizes[0] * sizes[1]
-    rows = stacked.shape[0] // n_pieces
+    n_tiles, n_sub = sizes
+    rows = stacked.shape[0] // (n_tiles * n_sub)
     first = 0
     for table, basis in zip(tables, ins):
         for start in range(0, basis.shape[0], NCHUNK):
             tiles = range(start // RMAX, (start + NCHUNK) // RMAX)
-            column, target = slots_of(place, table, tiles, sizes)
-            products = lax.dot_general(
-                stacked[...],
-                basis[start : start + NCHUNK, lanes],
-                CONTRACT_LAST,
-                preferred_element_type=F32,
-            )
-            chosen = products[:rows]
-            for piece in range(1, n_pieces):
-                chosen = jnp.where(
-                    column == piece, products[piece * rows : (piece + 1) * rows], chosen
+            target = slots_of(place, table, tiles, sizes)[1]
+            found = []
+            for t in tiles:
+                block = table[2, t]
+                slot = lax.rem(place[1] + n_sub - lax.rem(block, n_sub), n_sub) * n_tiles
+                slot += lax.rem(place[0] + n_tiles - lax.div(block, n_sub), n_tiles)
+                begin = pl.multiple_of(slot * rows, rows)
+                found.append(
+                    lax.dot_general(
+                        stacked[pl.ds(begin, rows), :],
+                        basis[t * RMAX : (t + 1) * RMAX, :],
+                        CONTRACT_LAST,
+                        preferred_element_type=F32,
+                    )
                 )
+            chosen = jnp.concatenate(found, axis=1)
             there = slice(first, first + NCHUNK)
-            if previous is not None:
-                chosen = chosen + previous[:, there]
-            if coeff is not None:
-                coeff[:, there] = chosen
-            if masked is not None:
-                for piece in range(n_pieces):
-                    masked[piece * rows : (piece + 1) * rows, there] = jnp.where(
-                        target == piece, chosen, 0.0
+            for i, part in enumerate(masked):
+                held = part.shape[0] // rows
+                for piece in range(held):
+                    part[piece * rows : (piece + 1) * rows, there] = jnp.where(
+                        target == i * held + piece, chosen, 0.0
                     ).astype(BF16)
             first += NCHUNK
 
@@ -147,13 +148,13 @@
     (masked,) = scratch
     every = slice(0, BLK)
     stack(pieces, stacked)
-    first_stage(numbers, sizes, stacked, ins, every, None, None, masked)
+    first_stage(numbers, sizes, stacked, ins, every, None, None, [masked])
     total[...] = second_stage(masked, outs, every, None)
 
 
 def masked_kernel(sizes, numbers, inputs, results, scratch):
     stacked, ins = inputs
-    first_stage(numbers, sizes, stacked, ins, slice(0, BLK), None, None, results[0])
+    first_stage(numbers, sizes, stacked, ins, slice(0, BLK), None, None, results)
 
 
 def joining_kernel(lanes, numbers, inputs, results, scratch):
@@ -164,16 +165,15 @@
 
 def sent_kernel(sizes, lanes, numbers, inputs, results, scratch):
     pieces_by_lanes, ins, outs_by_lanes = inputs
-    send_ref, stacked, kept = results
-    (masked,) = scratch
+    send_ref, stacked, *masked = results
     for here, pieces in zip(lanes, pieces_by_lanes):
         stack(pieces, stacked.at[:, here])
-    first_stage(numbers, sizes, stacked, ins, slice(0, BLK), None, None, masked)
-    n_kept = kept.shape[0]
+    first_stage(numbers, sizes, stacked, ins, slice(0, BLK), None, None, [*masked, *scratch])
+    size = masked[0].shape[0]
     for here, outs in zip(lanes, outs_by_lanes):
-        total = second_stage(masked.at[n_kept:, :], outs, here, None)
-        send_ref[:, here] = total.astype(BF16)
-    kept[...] = masked[:n_kept, :]
+        for i, part in enumerate(scratch):
+            total = second_stage(part, outs, here, None)
+            send_ref[i * size : (i + 1) * size, here] = total.astype(BF16)
 
 
 def kept_kernel(lanes, numbers, inputs, results, scratch):
@@ -382,7 +382,7 @@
         ([gather(field) for field in fields], ins, outs),
         [send_shape, stacked_shape(every)]
         + [jax.ShapeDtypeStruct((n_tiles * rows, n_rhs * width), BF16)],
-        [pltpu.VMEM((stack_rows, n_rhs * width), BF16)],
+        [pltpu.VMEM((n_tiles * rows, n_rhs * width), BF16)] * (n_sub - 1),
         0,
         temporary,
         "far_sent",

time: 87.8 us -> 87 us (level)
  Pallas kernels: 19.2 us -> 17.5 us
  waiting for transfers between devices: 19.7 us -> 20.6 us
    pallas_call x9, Pallas kernels: 10.8 us -> 9.14 us  [on_chip(): pl.pallas_call(body, out_shape=tuple(out_shapes), in_specs=[in_smem] * n_...]
    ppermute x37, waiting for transfers between devices: 19.7 us -> 20.6 us  [shifted(): lax.ppermute(value, axis, [(i, (i + amount) % size) for i in range(size)])]
  transfers between devices with their start and end apart: 37 -> 37, of which waited for: 12 -> 12; matrix products, arithmetic and copies ran while one was open for 3% -> 3% of each run, Pallas kernels for 17% -> 16%
where the time goes in v6:
time: 87 us; the launch traced here: 86.4 us
  starting transfers between devices  40.2 us (46%)
  waiting for transfers between devices  20.6 us (24%)
  Pallas kernels  17.5 us (20%)
  local copies, waits for them, and re-layouts  5.54 us (6%)
  other arithmetic  1.73 us (2%)
    ppermute x37, starting transfers between devices, shifted(): lax.ppermute(value, axis, [(i, (i + amount) % size) for i in range(size)])  40.2 us
    ppermute x37, waiting for transfers between devices, shifted(): lax.ppermute(value, axis, [(i, (i + amount) % size) for i in range(size)])  20.6 us
    pallas_call x9, Pallas kernels, on_chip(): pl.pallas_call(body, out_shape=tuple(out_shapes), in_specs=[in_smem] * n_...  9.14 us
    pallas_call x2, Pallas kernels, near_field(): pl.pallas_call(functools.partial(near_kernel, len(stacks), per_step), out...  8.36 us
    unnamed x14, local copies, waits for them, and re-layouts  4.3 us
  transfers between devices with their start and end apart: 37, of which 12 were waited for; matrix products, arithmetic and copies ran while one was open for 3% of the time, Pallas kernels for 16%

profile of v6, /device:TPU:0, one launch (start us, length us, event | category | flops | bytes accessed | tf_op | source)
XLA Modules:
  0.0 86.4 jit_solution(9962657241012909250)
XLA Ops:
  0.6 3.0 %collective-permute-start.8 = (bf16[768,512]{1,0:T(8,128)(2,1)}, bf16[768,512]{1,0:T(8,128)(2,1)S(1)}, u32[]{:S(2)}, u32[]{:S(2)}) collective-permute-start(bf16[768,512]{1,0:T(8,128)(2,1)} %bitcast.31), channel_id=1, source_target_pairs={{0,2},{2,0},{1,3},{3,1},{4,6},{6,4},{5,7},{7,5},{8,10},{10,8},{9,1... | collective-permute-start | bytes 2359304 | tf_op jit(solution)/shard_map/ppermute | solution.py:28
  3.7 1.6 %collective-permute-start.1 = (bf16[128,512]{1,0:T(8,128)(2,1)}, bf16[128,512]{1,0:T(8,128)(2,1)S(1)}, u32[]{:S(2)}, u32[]{:S(2)}) collective-permute-start(bf16[128,512]{1,0:T(8,128)(2,1)} %refs_2_.1), channel_id=1, source_target_pairs={{0,4},{4,8},{8,12},{12,0},{1,5},{5,9},{9,13},{13,1},{2,6},{6,10},{... | collective-permute-start | bytes 393224 | tf_op jit(solution)/shard_map/ppermute | solution.py:28
  5.2 2.6 %collective-permute-start.2 = (bf16[128,512]{1,0:T(8,128)(2,1)}, bf16[128,512]{1,0:T(8,128)(2,1)S(1)}, u32[]{:S(2)}, u32[]{:S(2)}) collective-permute-start(bf16[128,512]{1,0:T(8,128)(2,1)} %refs_2_.1), channel_id=1, source_target_pairs={{0,8},{4,12},{8,0},{12,4},{1,9},{5,13},{9,1},{13,5},{2,10},{6,14},... | collective-permute-start | bytes 393224 | tf_op jit(solution)/shard_map/ppermute | solution.py:28
  7.8 1.3 %collective-permute-start.3 = (bf16[128,512]{1,0:T(8,128)(2,1)}, bf16[128,512]{1,0:T(8,128)(2,1)S(1)}, u32[]{:S(2)}, u32[]{:S(2)}) collective-permute-start(bf16[128,512]{1,0:T(8,128)(2,1)} %refs_2_.1), channel_id=1, source_target_pairs={{0,12},{4,0},{8,4},{12,8},{1,13},{5,1},{9,5},{13,9},{2,14},{6,2},{... | collective-permute-start | bytes 393224 | tf_op jit(solution)/shard_map/ppermute | solution.py:28
  9.2 1.2 %fusion.5 = (bf16[768,256]{1,0:T(8,128)(2,1)S(1)}, bf16[768,256]{1,0:T(8,128)(2,1)S(1)}) fusion(bf16[768,512]{1,0:T(8,128)(2,1)} %bitcast.25), kind=kLoop, calls=%fused_computation.22 | loop fusion | bytes 1572864 | tf_op jit(solution)/shard_map/slice | solution.py:333
  10.3 1.8 %collective-permute-done.1.refs_3_ = bf16[128,512]{1,0:T(8,128)(2,1)S(1)} collective-permute-done((bf16[128,512]{1,0:T(8,128)(2,1)}, bf16[128,512]{1,0:T(8,128)(2,1)S(1)}, u32[]{:S(2)}, u32[]{:S(2)}) %collective-permute-start.1) | collective-permute-done | bytes 131104 | tf_op jit(solution)/shard_map/ppermute | solution.py:28
  12.2 0.3 collective-permute-start.21
  12.5 0.7 fusion.slot_ref
  13.1 3.3 %collective-permute-done.2.refs_4_ = bf16[128,512]{1,0:T(8,128)(2,1)S(1)} collective-permute-done((bf16[128,512]{1,0:T(8,128)(2,1)}, bf16[128,512]{1,0:T(8,128)(2,1)S(1)}, u32[]{:S(2)}, u32[]{:S(2)}) %collective-permute-start.2) | collective-permute-done | bytes 131104 | tf_op jit(solution)/shard_map/ppermute | solution.py:28
  16.4 0.5 collective-permute-start.6
  17.1 0.7 pad_add_fusion.refs_1_
  17.8 0.6 collective-permute-start
  18.4 1.5 %collective-permute-start.9 = (bf16[768,256]{1,0:T(8,128)(2,1)S(1)}, bf16[768,256]{1,0:T(8,128)(2,1)S(1)}, u32[]{:S(2)}, u32[]{:S(2)}) collective-permute-start(bf16[768,256]{1,0:T(8,128)(2,1)S(1)} %get-tuple-element.29), channel_id=1, source_target_pairs={{0,2},{2,0},{1,3},{3,1},{4,6},{6,4},{5,7},{7,5},{8,10},{10,8},{9,1... | collective-permute-start | bytes 1179656 | tf_op jit(solution)/shard_map/ppermute | solution.py:28
  19.9 0.9 %copy-done.4 = bf16[128,512]{1,0:T(8,128)(2,1)S(1)} copy-done((bf16[128,512]{1,0:T(8,128)(2,1)S(1)}, bf16[128,512]{1,0:T(8,128)(2,1)}, u32[]{:S(2)}) %copy-start.4) | copy-done | bytes 131096
  20.8 2.0 %far_own.1 = (f32[1024,512]{1,0:T(8,128)S(1)}, bf16[1024,512]{1,0:T(8,128)(2,1)S(1)}) custom-call(s32[2]{0:T(128)S(1)} %pad_add_fusion.1.refs_0_, s32[3,12]{1,0:T(4,128)S(1)} %pad_add_fusion.refs_1_, bf16[128,512]{1,0:T(8,128)(2,1)S(1)} %copy-done.4, bf16[128,512]{1,0:T(8,128)(2,1)S(1)} %collective-permute-done.1.refs_3_, ...), custom_call_target="tpu_custom_call" | custom-call | flops 1 | bytes 1 | tf_op jit(solution)/shard_map/far_own/pallas_call | solution.py:45
  22.8 3.4 %copy-done = bf16[1,16,512,512]{3,2,1,0:T(8,128)(2,1)S(1)} copy-done((bf16[1,16,512,512]{3,2,1,0:T(8,128)(2,1)S(1)}, bf16[1,16,512,512]{3,2,1,0:T(8,128)(2,1)}, u32[]{:S(2)}) %copy-start) | copy-done | bytes 8388632
  26.2 3.9 %near_field.2.refs_4_ = f32[128,512]{1,0:T(8,128)S(1)} custom-call(s32[16]{0:T(128)S(1)} %fusion.slot_ref, bf16[1024,512]{1,0:T(8,128)(2,1)S(1)} %get-tuple-element.16.refs_0_.refs_2_, bf16[16,512,512]{2,1,0:T(8,128)(2,1)S(1)} %bitcast.21), custom_call_target="tpu_custom_call" | custom-call | flops 1 | bytes 1 | tf_op jit(solution)/shard_map/near_field/pallas_call | solution.py:226
  30.1 0.6 collective-permute-done.refs_1_.refs_2_
  30.7 1.2 %far_first_stage.1.refs_0_ = bf16[1024,768]{1,0:T(8,128)(2,1)S(1)} custom-call(s32[2]{0:T(128)S(1)} %pad_add_fusion.1.refs_0_, s32[3,12]{1,0:T(4,128)S(1)} %collective-permute-done.refs_1_.refs_2_, bf16[1024,512]{1,0:T(8,128)(2,1)S(1)} %get-tuple-element.16.refs_0_.refs_2_, bf16[768,512]{1,0:T(8,128)(2,1)S(1)} %collective-permute-done.8.refs_3_.refs_20_), custom_call_target="tpu_custom_call" | custom-call | flops 1 | bytes 1 | tf_op jit(solution)/shard_map/far_first_stage/pallas_call | solution.py:45
  31.9 0.6 far_second_stage.3
  32.6 5.7 %collective-permute-done.9.refs_2_.refs_22_ = bf16[768,256]{1,0:T(8,128)(2,1)S(1)} collective-permute-done((bf16[768,256]{1,0:T(8,128)(2,1)S(1)}, bf16[768,256]{1,0:T(8,128)(2,1)S(1)}, u32[]{:S(2)}, u32[]{:S(2)}) %collective-permute-start.9) | collective-permute-done | bytes 393248 | tf_op jit(solution)/shard_map/ppermute | solution.py:28
  38.3 0.6 far_second_stage.2
  39.1 1.9 %collective-permute-start.23 = (bf16[128,256]{1,0:T(8,128)(2,1)S(1)}, bf16[128,256]{1,0:T(8,128)(2,1)S(1)}, u32[]{:S(2)}, u32[]{:S(2)}) collective-permute-start(bf16[128,256]{1,0:T(8,128)(2,1)S(1)} %get-tuple-element.36), channel_id=1, source_target_pairs={{0,4},{4,8},{8,12},{12,0},{1,5},{5,9},{9,13},{13,1},{2,6},{6,10},{... | collective-permute-start | bytes 196616 | tf_op jit(solution)/shard_map/ppermute | solution.py:28
  41.0 2.6 %collective-permute-start.24 = (bf16[128,256]{1,0:T(8,128)(2,1)S(1)}, bf16[128,256]{1,0:T(8,128)(2,1)S(1)}, u32[]{:S(2)}, u32[]{:S(2)}) collective-permute-start(bf16[128,256]{1,0:T(8,128)(2,1)S(1)} %get-tuple-element.35), channel_id=1, source_target_pairs={{0,8},{4,12},{8,0},{12,4},{1,9},{5,13},{9,1},{13,5},{2,10},{6,14},... | collective-permute-start | bytes 196616 | tf_op jit(solution)/shard_map/ppermute | solution.py:28
  43.6 1.3 %collective-permute-start.25 = (bf16[128,256]{1,0:T(8,128)(2,1)S(1)}, bf16[128,256]{1,0:T(8,128)(2,1)S(1)}, u32[]{:S(2)}, u32[]{:S(2)}) collective-permute-start(bf16[128,256]{1,0:T(8,128)(2,1)S(1)} %get-tuple-element.34), channel_id=1, source_target_pairs={{0,12},{4,0},{8,4},{12,8},{1,13},{5,1},{9,5},{13,9},{2,14},{6,2},{... | collective-permute-start | bytes 196616 | tf_op jit(solution)/shard_map/ppermute | solution.py:28
  45.0 0.7 collective-permute-start.11
  45.8 0.3 collective-permute-start.12
  46.1 2.8 %collective-permute-start.13 = (bf16[128,256]{1,0:T(8,128)(2,1)S(1)}, bf16[128,256]{1,0:T(8,128)(2,1)S(1)}, u32[]{:S(2)}, u32[]{:S(2)}) collective-permute-start(bf16[128,256]{1,0:T(8,128)(2,1)S(1)} %get-tuple-element.38), channel_id=1, source_target_pairs={{0,12},{4,0},{8,4},{12,8},{1,13},{5,1},{9,5},{13,9},{2,14},{6,2},{... | collective-permute-start | bytes 196616 | tf_op jit(solution)/shard_map/ppermute | solution.py:28
  49.1 4.5 %collective-permute-start.26 = (bf16[128,256]{1,0:T(8,128)(2,1)S(1)}, bf16[128,256]{1,0:T(8,128)(2,1)S(1)}, u32[]{:S(2)}, u32[]{:S(2)}) collective-permute-start(bf16[128,256]{1,0:T(8,128)(2,1)S(1)} %finish.4.refs_11_), channel_id=1, source_target_pairs={{0,4},{4,8},{8,12},{12,0},{1,5},{5,9},{9,13},{13,1},{2,6},{6,10},{... | collective-permute-start | bytes 196616 | tf_op jit(solution)/shard_map/ppermute | solution.py:28
  53.6 2.4 %collective-permute-start.28 = (bf16[128,256]{1,0:T(8,128)(2,1)S(1)}, bf16[128,256]{1,0:T(8,128)(2,1)S(1)}, u32[]{:S(2)}, u32[]{:S(2)}) collective-permute-start(bf16[128,256]{1,0:T(8,128)(2,1)S(1)} %finish.4.refs_11_), channel_id=1, source_target_pairs={{0,12},{4,0},{8,4},{12,8},{1,13},{5,1},{9,5},{13,9},{2,14},{6,2},{... | collective-permute-start | bytes 196616 | tf_op jit(solution)/shard_map/ppermute | solution.py:28
  56.3 2.4 %collective-permute-start.14 = (bf16[128,256]{1,0:T(8,128)(2,1)S(1)}, bf16[128,256]{1,0:T(8,128)(2,1)S(1)}, u32[]{:S(2)}, u32[]{:S(2)}) collective-permute-start(bf16[128,256]{1,0:T(8,128)(2,1)S(1)} %finish.3.refs_3_), channel_id=1, source_target_pairs={{0,4},{4,8},{8,12},{12,0},{1,5},{5,9},{9,13},{13,1},{2,6},{6,10},{... | collective-permute-start | bytes 196616 | tf_op jit(solution)/shard_map/ppermute | solution.py:28
  58.8 1.2 %collective-permute-done.27.refs_13_ = bf16[128,256]{1,0:T(8,128)(2,1)S(1)} collective-permute-done((bf16[128,256]{1,0:T(8,128)(2,1)S(1)}, bf16[128,256]{1,0:T(8,128)(2,1)S(1)}, u32[]{:S(2)}, u32[]{:S(2)}) %collective-permute-start.27) | collective-permute-done | bytes 65568 | tf_op jit(solution)/shard_map/ppermute | solution.py:28
  60.0 3.2 %collective-permute-start.16 = (bf16[128,256]{1,0:T(8,128)(2,1)S(1)}, bf16[128,256]{1,0:T(8,128)(2,1)S(1)}, u32[]{:S(2)}, u32[]{:S(2)}) collective-permute-start(bf16[128,256]{1,0:T(8,128)(2,1)S(1)} %finish.3.refs_3_), channel_id=1, source_target_pairs={{0,12},{4,0},{8,4},{12,8},{1,13},{5,1},{9,5},{13,9},{2,14},{6,2},{... | collective-permute-start | bytes 196616 | tf_op jit(solution)/shard_map/ppermute | solution.py:28
  63.2 0.5 collective-permute-start.30
  63.8 1.8 %collective-permute-done.15.refs_5_ = bf16[128,256]{1,0:T(8,128)(2,1)S(1)} collective-permute-done((bf16[128,256]{1,0:T(8,128)(2,1)S(1)}, bf16[128,256]{1,0:T(8,128)(2,1)S(1)}, u32[]{:S(2)}, u32[]{:S(2)}) %collective-permute-start.15) | collective-permute-done | bytes 65568 | tf_op jit(solution)/shard_map/ppermute | solution.py:28
  65.6 0.5 collective-permute-start.18
  66.1 0.4 collective-permute-start.20
  66.6 0.2 collective-permute-done.32.refs_18_
  67.0 0.4 collective-permute-done.19.refs_9_
  67.5 2.5 %far_sent.1 = (bf16[512,512]{1,0:T(8,128)(2,1)S(1)}, bf16[1024,512]{1,0:T(8,128)(2,1)S(1)}, bf16[512,1536]{1,0:T(8,128)(2,1)S(1)}) custom-call(s32[2]{0:T(128)S(1)} %pad_add_fusion.1.refs_0_, s32[3,12]{1,0:T(4,128)S(1)} %pad_add_fusion.refs_1_, s32[3,12]{1,0:T(4,128)S(1)} %collective-permute-done.refs_1_.refs_2_, bf16[128,256]{1,0:T(8,128)(2,1)S(1)} %finish.3.refs_3_, ...), custom_call_target="tpu_custom_call" | custom-call | flops 1 | bytes 1 | tf_op jit(solution)/shard_map/far_sent/pallas_call | solution.py:45
  70.0 0.4 collective-permute-start.33
  70.4 1.0 %far_kept.1 = bf16[512,512]{1,0:T(8,128)(2,1)S(1)} custom-call(bf16[512,1536]{1,0:T(8,128)(2,1)S(1)} %get-tuple-element.25.refs_0_, bf16[768,512]{1,0:T(8,128)(2,1)S(1)} %bitcast.29, bf16[768,256]{1,0:T(8,128)(2,1)S(1)} %collective-permute-done.9.refs_2_.refs_22_, bf16[768,512]{1,0:T(8,128)(2,1)S(1)} %bitcast.30, ...), custom_call_target="tpu_custom_call" | custom-call | flops 10000000000 | bytes 1 | tf_op jit(solution)/shard_map/far_kept/pallas_call | solution.py:45
  71.4 0.6 collective-permute-done.33
  72.2 1.8 %collective-permute-start.34 = (bf16[128,512]{1,0:T(8,128)(2,1)S(1)}, bf16[128,512]{1,0:T(8,128)(2,1)S(1)}, u32[]{:S(2)}, u32[]{:S(2)}) collective-permute-start(bf16[128,512]{1,0:T(8,128)(2,1)S(1)} %get-tuple-element.32), channel_id=1, source_target_pairs={{0,4},{4,8},{8,12},{12,0},{1,5},{5,9},{9,13},{13,1},{2,6},{6,10},{... | collective-permute-start | bytes 393224 | tf_op jit(solution)/shard_map/ppermute | solution.py:28
  73.9 2.4 %collective-permute-start.35 = (bf16[128,512]{1,0:T(8,128)(2,1)S(1)}, bf16[128,512]{1,0:T(8,128)(2,1)S(1)}, u32[]{:S(2)}, u32[]{:S(2)}) collective-permute-start(bf16[128,512]{1,0:T(8,128)(2,1)S(1)} %get-tuple-element.31), channel_id=1, source_target_pairs={{0,8},{4,12},{8,0},{12,4},{1,9},{5,13},{9,1},{13,5},{2,10},{6,14},... | collective-permute-start | bytes 393224 | tf_op jit(solution)/shard_map/ppermute | solution.py:28
  76.4 4.5 %near_field.3 = (f32[128,512]{1,0:T(8,128)S(1)}, bf16[128,512]{1,0:T(8,128)(2,1)}) custom-call(s32[16]{0:T(128)S(1)} %fusion.slot_ref, bf16[1024,512]{1,0:T(8,128)(2,1)S(1)} %get-tuple-element.23.refs_0_, bf16[16,512,512]{2,1,0:T(8,128)(2,1)S(1)} %bitcast.24), custom_call_target="tpu_custom_call" | custom-call | flops 1 | bytes 1 | tf_op jit(solution)/shard_map/near_field/pallas_call | solution.py:226
  80.9 4.6 %collective-permute-done.35.refs_2_ = bf16[128,512]{1,0:T(8,128)(2,1)S(1)} collective-permute-done((bf16[128,512]{1,0:T(8,128)(2,1)S(1)}, bf16[128,512]{1,0:T(8,128)(2,1)S(1)}, u32[]{:S(2)}, u32[]{:S(2)}) %collective-permute-start.35) | collective-permute-done | bytes 131104 | tf_op jit(solution)/shard_map/ppermute | solution.py:28
  85.5 0.9 %finish.5 = bf16[128,512]{1,0:T(8,128)(2,1)} custom-call(bf16[128,512]{1,0:T(8,128)(2,1)S(1)} %get-tuple-element.33.refs_0_, bf16[128,512]{1,0:T(8,128)(2,1)S(1)} %collective-permute-done.34.refs_1_, bf16[128,512]{1,0:T(8,128)(2,1)S(1)} %collective-permute-done.35.refs_2_, bf16[128,512]{1,0:T(8,128)(2,1)S(1)} %collective-permute-done.36.refs_3_, ...), custom_call_target="tpu_custom_call" | custom-call | flops 1 | bytes 1 | tf_op jit(solution)/shard_map/finish/pallas_call | solution.py:45
  (62 shorter events, 1.8 us)
Async XLA Ops:
  0.6 19.3 %copy-start.2 = (bf16[12,64,512]{2,1,0:T(8,128)(2,1)S(1)}, bf16[12,64,512]{2,1,0:T(8,128)(2,1)}, u32[]{:S(2)}) copy-start(bf16[12,64,512]{2,1,0:T(8,128)(2,1)} %param.11) | copy-start | bytes 2359300
  0.6 19.3 %copy-start.1 = (bf16[12,64,512]{2,1,0:T(8,128)(2,1)S(1)}, bf16[12,64,512]{2,1,0:T(8,128)(2,1)}, u32[]{:S(2)}) copy-start(bf16[12,64,512]{2,1,0:T(8,128)(2,1)} %param.10) | copy-start | bytes 2359300
  0.6 30.1 %collective-permute-start.8 = (bf16[768,512]{1,0:T(8,128)(2,1)}, bf16[768,512]{1,0:T(8,128)(2,1)S(1)}, u32[]{:S(2)}, u32[]{:S(2)}) collective-permute-start(bf16[768,512]{1,0:T(8,128)(2,1)} %bitcast.31), channel_id=1, source_target_pairs={{0,2},{2,0},{1,3},{3,1},{4,6},{6,4},{5,7},{7,5},{8,10},{10,8},{9,1... | collective-permute-start | bytes 2359304 | tf_op jit(solution)/shard_map/ppermute | solution.py:28
  3.7 8.5 %collective-permute-start.1 = (bf16[128,512]{1,0:T(8,128)(2,1)}, bf16[128,512]{1,0:T(8,128)(2,1)S(1)}, u32[]{:S(2)}, u32[]{:S(2)}) collective-permute-start(bf16[128,512]{1,0:T(8,128)(2,1)} %refs_2_.1), channel_id=1, source_target_pairs={{0,4},{4,8},{8,12},{12,0},{1,5},{5,9},{9,13},{13,1},{2,6},{6,10},{... | collective-permute-start | bytes 393224 | tf_op jit(solution)/shard_map/ppermute | solution.py:28
  5.2 11.2 %collective-permute-start.2 = (bf16[128,512]{1,0:T(8,128)(2,1)}, bf16[128,512]{1,0:T(8,128)(2,1)S(1)}, u32[]{:S(2)}, u32[]{:S(2)}) collective-permute-start(bf16[128,512]{1,0:T(8,128)(2,1)} %refs_2_.1), channel_id=1, source_target_pairs={{0,8},{4,12},{8,0},{12,4},{1,9},{5,13},{9,1},{13,5},{2,10},{6,14},... | collective-permute-start | bytes 393224 | tf_op jit(solution)/shard_map/ppermute | solution.py:28
  7.8 8.6 %collective-permute-start.3 = (bf16[128,512]{1,0:T(8,128)(2,1)}, bf16[128,512]{1,0:T(8,128)(2,1)S(1)}, u32[]{:S(2)}, u32[]{:S(2)}) collective-permute-start(bf16[128,512]{1,0:T(8,128)(2,1)} %refs_2_.1), channel_id=1, source_target_pairs={{0,12},{4,0},{8,4},{12,8},{1,13},{5,1},{9,5},{13,9},{2,14},{6,2},{... | collective-permute-start | bytes 393224 | tf_op jit(solution)/shard_map/ppermute | solution.py:28
  9.2 7.8 %collective-permute-start.4 = (bf16[128,512]{1,0:T(8,128)(2,1)}, bf16[128,512]{1,0:T(8,128)(2,1)S(1)}, u32[]{:S(2)}, u32[]{:S(2)}) collective-permute-start(bf16[128,512]{1,0:T(8,128)(2,1)} %refs_2_.1), channel_id=1, source_target_pairs={{0,1},{1,0},{2,3},{3,2},{4,5},{5,4},{6,7},{7,6},{8,9},{9,8},{10,11... | collective-permute-start | bytes 393224 | tf_op jit(solution)/shard_map/ppermute | solution.py:28
  12.2 19.8 %collective-permute-start.21 = (bf16[768,256]{1,0:T(8,128)(2,1)S(1)}, bf16[768,256]{1,0:T(8,128)(2,1)S(1)}, u32[]{:S(2)}, u32[]{:S(2)}) collective-permute-start(bf16[768,256]{1,0:T(8,128)(2,1)S(1)} %get-tuple-element.28), channel_id=1, source_target_pairs={{0,2},{2,0},{1,3},{3,1},{4,6},{6,4},{5,7},{7,5},{8,10},{10,8},{9,1... | collective-permute-start | bytes 1179656 | tf_op jit(solution)/shard_map/ppermute | solution.py:28
  16.4 1.4 %collective-permute-start.5 = (bf16[128,512]{1,0:T(8,128)(2,1)S(1)}, bf16[128,512]{1,0:T(8,128)(2,1)S(1)}, u32[]{:S(2)}, u32[]{:S(2)}) collective-permute-start(bf16[128,512]{1,0:T(8,128)(2,1)S(1)} %collective-permute-done.1.refs_3_), channel_id=1, source_target_pairs={{0,1},{1,0},{2,3},{3,2},{4,5},{5,4},{6,7},{7,6},{8,9},{9,8},{10,11... | collective-permute-start | bytes 393224 | tf_op jit(solution)/shard_map/ppermute | solution.py:28
  16.4 1.9 %collective-permute-start.6 = (bf16[128,512]{1,0:T(8,128)(2,1)S(1)}, bf16[128,512]{1,0:T(8,128)(2,1)S(1)}, u32[]{:S(2)}, u32[]{:S(2)}) collective-permute-start(bf16[128,512]{1,0:T(8,128)(2,1)S(1)} %collective-permute-done.2.refs_4_), channel_id=1, source_target_pairs={{0,1},{1,0},{2,3},{3,2},{4,5},{5,4},{6,7},{7,6},{8,9},{9,8},{10,11... | collective-permute-start | bytes 393224 | tf_op jit(solution)/shard_map/ppermute | solution.py:28
  17.0 2.9 %collective-permute-start.7 = (bf16[128,512]{1,0:T(8,128)(2,1)S(1)}, bf16[128,512]{1,0:T(8,128)(2,1)S(1)}, u32[]{:S(2)}, u32[]{:S(2)}) collective-permute-start(bf16[128,512]{1,0:T(8,128)(2,1)S(1)} %collective-permute-done.3.refs_5_), channel_id=1, source_target_pairs={{0,1},{1,0},{2,3},{3,2},{4,5},{5,4},{6,7},{7,6},{8,9},{9,8},{10,11... | collective-permute-start | bytes 393224 | tf_op jit(solution)/shard_map/ppermute | solution.py:28
  17.8 12.9 %collective-permute-start = (s32[3,12]{1,0:T(4,128)S(1)}, s32[3,12]{1,0:T(4,128)S(1)}, u32[]{:S(2)}, u32[]{:S(2)}) collective-permute-start(s32[3,12]{1,0:T(4,128)S(1)} %pad_add_fusion.refs_1_), channel_id=1, source_target_pairs={{0,2},{2,0},{1,3},{3,1},{4,6},{6,4},{5,7},{7,5},{8,10},{10,8},{9,1... | collective-permute-start | bytes 440 | tf_op jit(solution)/shard_map/ppermute | solution.py:28
  18.4 19.9 %collective-permute-start.9 = (bf16[768,256]{1,0:T(8,128)(2,1)S(1)}, bf16[768,256]{1,0:T(8,128)(2,1)S(1)}, u32[]{:S(2)}, u32[]{:S(2)}) collective-permute-start(bf16[768,256]{1,0:T(8,128)(2,1)S(1)} %get-tuple-element.29), channel_id=1, source_target_pairs={{0,2},{2,0},{1,3},{3,1},{4,6},{6,4},{5,7},{7,5},{8,10},{10,8},{9,1... | collective-permute-start | bytes 1179656 | tf_op jit(solution)/shard_map/ppermute | solution.py:28
  19.9 0.9 %copy-start.4 = (bf16[128,512]{1,0:T(8,128)(2,1)S(1)}, bf16[128,512]{1,0:T(8,128)(2,1)}, u32[]{:S(2)}) copy-start(bf16[128,512]{1,0:T(8,128)(2,1)} %refs_2_.1) | copy-start | bytes 393220
  22.8 3.4 %copy-start = (bf16[1,16,512,512]{3,2,1,0:T(8,128)(2,1)S(1)}, bf16[1,16,512,512]{3,2,1,0:T(8,128)(2,1)}, u32[]{:S(2)}) copy-start(bf16[1,16,512,512]{3,2,1,0:T(8,128)(2,1)} %param.15) | copy-start | bytes 25165828
  32.5 6.4 %collective-permute-start.22 = (bf16[512,256]{1,0:T(8,128)(2,1)S(1)}, bf16[512,256]{1,0:T(8,128)(2,1)S(1)}, u32[]{:S(2)}, u32[]{:S(2)}) collective-permute-start(bf16[512,256]{1,0:T(8,128)(2,1)S(1)} %get-tuple-element.22), channel_id=1, source_target_pairs={{0,1},{1,0},{2,3},{3,2},{4,5},{5,4},{6,7},{7,6},{8,9},{9,8},{10,11... | collective-permute-start | bytes 786440 | tf_op jit(solution)/shard_map/ppermute | solution.py:28
  38.9 10.0 %copy-start.3 = (bf16[4,128,128]{2,1,0:T(8,128)(2,1)S(1)}, bf16[4,128,128]{2,1,0:T(8,128)(2,1)}, u32[]{:S(2)}) copy-start(bf16[4,128,128]{2,1,0:T(8,128)(2,1)} %refs_5_.5) | copy-start | bytes 393220
  38.9 6.0 %collective-permute-start.10 = (bf16[512,256]{1,0:T(8,128)(2,1)S(1)}, bf16[512,256]{1,0:T(8,128)(2,1)S(1)}, u32[]{:S(2)}, u32[]{:S(2)}) collective-permute-start(bf16[512,256]{1,0:T(8,128)(2,1)S(1)} %get-tuple-element.19), channel_id=1, source_target_pairs={{0,1},{1,0},{2,3},{3,2},{4,5},{5,4},{6,7},{7,6},{8,9},{9,8},{10,11... | collective-permute-start | bytes 786440 | tf_op jit(solution)/shard_map/ppermute | solution.py:28
  39.1 7.0 %collective-permute-start.23 = (bf16[128,256]{1,0:T(8,128)(2,1)S(1)}, bf16[128,256]{1,0:T(8,128)(2,1)S(1)}, u32[]{:S(2)}, u32[]{:S(2)}) collective-permute-start(bf16[128,256]{1,0:T(8,128)(2,1)S(1)} %get-tuple-element.36), channel_id=1, source_target_pairs={{0,4},{4,8},{8,12},{12,0},{1,5},{5,9},{9,13},{13,1},{2,6},{6,10},{... | collective-permute-start | bytes 196616 | tf_op jit(solution)/shard_map/ppermute | solution.py:28
  41.0 7.9 %collective-permute-start.24 = (bf16[128,256]{1,0:T(8,128)(2,1)S(1)}, bf16[128,256]{1,0:T(8,128)(2,1)S(1)}, u32[]{:S(2)}, u32[]{:S(2)}) collective-permute-start(bf16[128,256]{1,0:T(8,128)(2,1)S(1)} %get-tuple-element.35), channel_id=1, source_target_pairs={{0,8},{4,12},{8,0},{12,4},{1,9},{5,13},{9,1},{13,5},{2,10},{6,14},... | collective-permute-start | bytes 196616 | tf_op jit(solution)/shard_map/ppermute | solution.py:28
  43.6 5.3 %collective-permute-start.25 = (bf16[128,256]{1,0:T(8,128)(2,1)S(1)}, bf16[128,256]{1,0:T(8,128)(2,1)S(1)}, u32[]{:S(2)}, u32[]{:S(2)}) collective-permute-start(bf16[128,256]{1,0:T(8,128)(2,1)S(1)} %get-tuple-element.34), channel_id=1, source_target_pairs={{0,12},{4,0},{8,4},{12,8},{1,13},{5,1},{9,5},{13,9},{2,14},{6,2},{... | collective-permute-start | bytes 196616 | tf_op jit(solution)/shard_map/ppermute | solution.py:28
  45.0 8.6 %collective-permute-start.11 = (bf16[128,256]{1,0:T(8,128)(2,1)S(1)}, bf16[128,256]{1,0:T(8,128)(2,1)S(1)}, u32[]{:S(2)}, u32[]{:S(2)}) collective-permute-start(bf16[128,256]{1,0:T(8,128)(2,1)S(1)} %get-tuple-element.40), channel_id=1, source_target_pairs={{0,4},{4,8},{8,12},{12,0},{1,5},{5,9},{9,13},{13,1},{2,6},{6,10},{... | collective-permute-start | bytes 196616 | tf_op jit(solution)/shard_map/ppermute | solution.py:28
  45.8 10.3 %collective-permute-start.12 = (bf16[128,256]{1,0:T(8,128)(2,1)S(1)}, bf16[128,256]{1,0:T(8,128)(2,1)S(1)}, u32[]{:S(2)}, u32[]{:S(2)}) collective-permute-start(bf16[128,256]{1,0:T(8,128)(2,1)S(1)} %get-tuple-element.39), channel_id=1, source_target_pairs={{0,8},{4,12},{8,0},{12,4},{1,9},{5,13},{9,1},{13,5},{2,10},{6,14},... | collective-permute-start | bytes 196616 | tf_op jit(solution)/shard_map/ppermute | solution.py:28
  46.1 10.0 %collective-permute-start.13 = (bf16[128,256]{1,0:T(8,128)(2,1)S(1)}, bf16[128,256]{1,0:T(8,128)(2,1)S(1)}, u32[]{:S(2)}, u32[]{:S(2)}) collective-permute-start(bf16[128,256]{1,0:T(8,128)(2,1)S(1)} %get-tuple-element.38), channel_id=1, source_target_pairs={{0,12},{4,0},{8,4},{12,8},{1,13},{5,1},{9,5},{13,9},{2,14},{6,2},{... | collective-permute-start | bytes 196616 | tf_op jit(solution)/shard_map/ppermute | solution.py:28
  49.1 9.6 %collective-permute-start.26 = (bf16[128,256]{1,0:T(8,128)(2,1)S(1)}, bf16[128,256]{1,0:T(8,128)(2,1)S(1)}, u32[]{:S(2)}, u32[]{:S(2)}) collective-permute-start(bf16[128,256]{1,0:T(8,128)(2,1)S(1)} %finish.4.refs_11_), channel_id=1, source_target_pairs={{0,4},{4,8},{8,12},{12,0},{1,5},{5,9},{9,13},{13,1},{2,6},{6,10},{... | collective-permute-start | bytes 196616 | tf_op jit(solution)/shard_map/ppermute | solution.py:28
  53.6 6.4 %collective-permute-start.27 = (bf16[128,256]{1,0:T(8,128)(2,1)S(1)}, bf16[128,256]{1,0:T(8,128)(2,1)S(1)}, u32[]{:S(2)}, u32[]{:S(2)}) collective-permute-start(bf16[128,256]{1,0:T(8,128)(2,1)S(1)} %finish.4.refs_11_), channel_id=1, source_target_pairs={{0,8},{4,12},{8,0},{12,4},{1,9},{5,13},{9,1},{13,5},{2,10},{6,14},... | collective-permute-start | bytes 196616 | tf_op jit(solution)/shard_map/ppermute | solution.py:28
  53.6 9.6 %collective-permute-start.28 = (bf16[128,256]{1,0:T(8,128)(2,1)S(1)}, bf16[128,256]{1,0:T(8,128)(2,1)S(1)}, u32[]{:S(2)}, u32[]{:S(2)}) collective-permute-start(bf16[128,256]{1,0:T(8,128)(2,1)S(1)} %finish.4.refs_11_), channel_id=1, source_target_pairs={{0,12},{4,0},{8,4},{12,8},{1,13},{5,1},{9,5},{13,9},{2,14},{6,2},{... | collective-permute-start | bytes 196616 | tf_op jit(solution)/shard_map/ppermute | solution.py:28
  56.1 7.1 %collective-permute-start.29 = (bf16[128,256]{1,0:T(8,128)(2,1)S(1)}, bf16[128,256]{1,0:T(8,128)(2,1)S(1)}, u32[]{:S(2)}, u32[]{:S(2)}) collective-permute-start(bf16[128,256]{1,0:T(8,128)(2,1)S(1)} %finish.4.refs_11_), channel_id=1, source_target_pairs={{0,1},{1,0},{2,3},{3,2},{4,5},{5,4},{6,7},{7,6},{8,9},{9,8},{10,11... | collective-permute-start | bytes 196616 | tf_op jit(solution)/shard_map/ppermute | solution.py:28
  56.3 7.4 %collective-permute-start.14 = (bf16[128,256]{1,0:T(8,128)(2,1)S(1)}, bf16[128,256]{1,0:T(8,128)(2,1)S(1)}, u32[]{:S(2)}, u32[]{:S(2)}) collective-permute-start(bf16[128,256]{1,0:T(8,128)(2,1)S(1)} %finish.3.refs_3_), channel_id=1, source_target_pairs={{0,4},{4,8},{8,12},{12,0},{1,5},{5,9},{9,13},{13,1},{2,6},{6,10},{... | collective-permute-start | bytes 196616 | tf_op jit(solution)/shard_map/ppermute | solution.py:28
  58.7 6.8 %collective-permute-start.15 = (bf16[128,256]{1,0:T(8,128)(2,1)S(1)}, bf16[128,256]{1,0:T(8,128)(2,1)S(1)}, u32[]{:S(2)}, u32[]{:S(2)}) collective-permute-start(bf16[128,256]{1,0:T(8,128)(2,1)S(1)} %finish.3.refs_3_), channel_id=1, source_target_pairs={{0,8},{4,12},{8,0},{12,4},{1,9},{5,13},{9,1},{13,5},{2,10},{6,14},... | collective-permute-start | bytes 196616 | tf_op jit(solution)/shard_map/ppermute | solution.py:28
  60.0 5.6 %collective-permute-start.16 = (bf16[128,256]{1,0:T(8,128)(2,1)S(1)}, bf16[128,256]{1,0:T(8,128)(2,1)S(1)}, u32[]{:S(2)}, u32[]{:S(2)}) collective-permute-start(bf16[128,256]{1,0:T(8,128)(2,1)S(1)} %finish.3.refs_3_), channel_id=1, source_target_pairs={{0,12},{4,0},{8,4},{12,8},{1,13},{5,1},{9,5},{13,9},{2,14},{6,2},{... | collective-permute-start | bytes 196616 | tf_op jit(solution)/shard_map/ppermute | solution.py:28
  63.2 2.9 %collective-permute-start.17 = (bf16[128,256]{1,0:T(8,128)(2,1)S(1)}, bf16[128,256]{1,0:T(8,128)(2,1)S(1)}, u32[]{:S(2)}, u32[]{:S(2)}) collective-permute-start(bf16[128,256]{1,0:T(8,128)(2,1)S(1)} %finish.3.refs_3_), channel_id=1, source_target_pairs={{0,1},{1,0},{2,3},{3,2},{4,5},{5,4},{6,7},{7,6},{8,9},{9,8},{10,11... | collective-permute-start | bytes 196616 | tf_op jit(solution)/shard_map/ppermute | solution.py:28
  63.2 2.9 %collective-permute-start.30 = (bf16[128,256]{1,0:T(8,128)(2,1)S(1)}, bf16[128,256]{1,0:T(8,128)(2,1)S(1)}, u32[]{:S(2)}, u32[]{:S(2)}) collective-permute-start(bf16[128,256]{1,0:T(8,128)(2,1)S(1)} %collective-permute-done.26.refs_12_), channel_id=1, source_target_pairs={{0,1},{1,0},{2,3},{3,2},{4,5},{5,4},{6,7},{7,6},{8,9},{9,8},{10,11... | collective-permute-start | bytes 196616 | tf_op jit(solution)/shard_map/ppermute | solution.py:28
  63.7 2.9 %collective-permute-start.31 = (bf16[128,256]{1,0:T(8,128)(2,1)S(1)}, bf16[128,256]{1,0:T(8,128)(2,1)S(1)}, u32[]{:S(2)}, u32[]{:S(2)}) collective-permute-start(bf16[128,256]{1,0:T(8,128)(2,1)S(1)} %collective-permute-done.27.refs_13_), channel_id=1, source_target_pairs={{0,1},{1,0},{2,3},{3,2},{4,5},{5,4},{6,7},{7,6},{8,9},{9,8},{10,11... | collective-permute-start | bytes 196616 | tf_op jit(solution)/shard_map/ppermute | solution.py:28
  65.5 1.3 %collective-permute-start.32 = (bf16[128,256]{1,0:T(8,128)(2,1)S(1)}, bf16[128,256]{1,0:T(8,128)(2,1)S(1)}, u32[]{:S(2)}, u32[]{:S(2)}) collective-permute-start(bf16[128,256]{1,0:T(8,128)(2,1)S(1)} %collective-permute-done.28.refs_14_), channel_id=1, source_target_pairs={{0,1},{1,0},{2,3},{3,2},{4,5},{5,4},{6,7},{7,6},{8,9},{9,8},{10,11... | collective-permute-start | bytes 196616 | tf_op jit(solution)/shard_map/ppermute | solution.py:28
  65.6 1.4 %collective-permute-start.18 = (bf16[128,256]{1,0:T(8,128)(2,1)S(1)}, bf16[128,256]{1,0:T(8,128)(2,1)S(1)}, u32[]{:S(2)}, u32[]{:S(2)}) collective-permute-start(bf16[128,256]{1,0:T(8,128)(2,1)S(1)} %collective-permute-done.14.refs_4_), channel_id=1, source_target_pairs={{0,1},{1,0},{2,3},{3,2},{4,5},{5,4},{6,7},{7,6},{8,9},{9,8},{10,11... | collective-permute-start | bytes 196616 | tf_op jit(solution)/shard_map/ppermute | solution.py:28
  66.1 1.3 %collective-permute-start.19 = (bf16[128,256]{1,0:T(8,128)(2,1)S(1)}, bf16[128,256]{1,0:T(8,128)(2,1)S(1)}, u32[]{:S(2)}, u32[]{:S(2)}) collective-permute-start(bf16[128,256]{1,0:T(8,128)(2,1)S(1)} %collective-permute-done.15.refs_5_), channel_id=1, source_target_pairs={{0,1},{1,0},{2,3},{3,2},{4,5},{5,4},{6,7},{7,6},{8,9},{9,8},{10,11... | collective-permute-start | bytes 196616 | tf_op jit(solution)/shard_map/ppermute | solution.py:28
  66.1 1.3 %collective-permute-start.20 = (bf16[128,256]{1,0:T(8,128)(2,1)S(1)}, bf16[128,256]{1,0:T(8,128)(2,1)S(1)}, u32[]{:S(2)}, u32[]{:S(2)}) collective-permute-start(bf16[128,256]{1,0:T(8,128)(2,1)S(1)} %collective-permute-done.16.refs_6_), channel_id=1, source_target_pairs={{0,1},{1,0},{2,3},{3,2},{4,5},{5,4},{6,7},{7,6},{8,9},{9,8},{10,11... | collective-permute-start | bytes 196616 | tf_op jit(solution)/shard_map/ppermute | solution.py:28
  70.0 2.0 %collective-permute-start.33 = (bf16[512,512]{1,0:T(8,128)(2,1)S(1)}, bf16[512,512]{1,0:T(8,128)(2,1)S(1)}, u32[]{:S(2)}, u32[]{:S(2)}) collective-permute-start(bf16[512,512]{1,0:T(8,128)(2,1)S(1)} %get-tuple-element.26), channel_id=1, source_target_pairs={{0,1},{1,0},{2,3},{3,2},{4,5},{5,4},{6,7},{7,6},{8,9},{9,8},{10,11... | collective-permute-start | bytes 1572872 | tf_op jit(solution)/shard_map/ppermute | solution.py:28
  70.4 5.9 %slice-start = ((s8[8388608]{0:T(1024)(128)(4,1)}), s8[4194304]{0:T(1024)(128)(4,1)S(1)}, s32[]{:S(2)}) async-start(s8[8388608]{0:T(1024)(128)(4,1)} %bitcast.22), calls=%async_computation | async-start | bytes 8388608
  70.4 5.9 %slice-start.1 = ((s8[8388608]{0:T(1024)(128)(4,1)}), s8[4194304]{0:T(1024)(128)(4,1)S(1)}, s32[]{:S(2)}) async-start(s8[8388608]{0:T(1024)(128)(4,1)} %bitcast.22), calls=%async_computation.1 | async-start | bytes 8388608
  72.2 8.7 %collective-permute-start.34 = (bf16[128,512]{1,0:T(8,128)(2,1)S(1)}, bf16[128,512]{1,0:T(8,128)(2,1)S(1)}, u32[]{:S(2)}, u32[]{:S(2)}) collective-permute-start(bf16[128,512]{1,0:T(8,128)(2,1)S(1)} %get-tuple-element.32), channel_id=1, source_target_pairs={{0,4},{4,8},{8,12},{12,0},{1,5},{5,9},{9,13},{13,1},{2,6},{6,10},{... | collective-permute-start | bytes 393224 | tf_op jit(solution)/shard_map/ppermute | solution.py:28
  73.9 11.6 %collective-permute-start.35 = (bf16[128,512]{1,0:T(8,128)(2,1)S(1)}, bf16[128,512]{1,0:T(8,128)(2,1)S(1)}, u32[]{:S(2)}, u32[]{:S(2)}) collective-permute-start(bf16[128,512]{1,0:T(8,128)(2,1)S(1)} %get-tuple-element.31), channel_id=1, source_target_pairs={{0,8},{4,12},{8,0},{12,4},{1,9},{5,13},{9,1},{13,5},{2,10},{6,14},... | collective-permute-start | bytes 393224 | tf_op jit(solution)/shard_map/ppermute | solution.py:28
  76.4 9.1 %collective-permute-start.36 = (bf16[128,512]{1,0:T(8,128)(2,1)S(1)}, bf16[128,512]{1,0:T(8,128)(2,1)S(1)}, u32[]{:S(2)}, u32[]{:S(2)}) collective-permute-start(bf16[128,512]{1,0:T(8,128)(2,1)S(1)} %get-tuple-element.30), channel_id=1, source_target_pairs={{0,12},{4,0},{8,4},{12,8},{1,13},{5,1},{9,5},{13,9},{2,14},{6,2},{... | collective-permute-start | bytes 393224 | tf_op jit(solution)/shard_map/ppermute | solution.py:28

commit v7 on v6

--- a/solution.py
+++ b/solution.py
@@ -240,6 +240,17 @@
     )(slots, *stacks, near_blocks)
 
 
+def combine_kernel(numbers, inputs, results, scratch):
+    keep, received = inputs
+    rows = results[0].shape[0]
+    for d, result in enumerate(results):
+        here = slice(d * rows, (d + 1) * rows)
+        total = keep[here, :].astype(F32)
+        for part in received:
+            total += part[here, :].astype(F32)
+        result[...] = total.astype(BF16)
+
+
 def finish_kernel(lanes, numbers, inputs, results, scratch):
     sums, near_ref, jacobi_ref = inputs
     total = near_ref[:, lanes]
@@ -309,11 +320,20 @@
         return [shifted(array, "rhs", n_rhs, e) for e in range(1, n_rhs)]
 
     def reduced(keep, send):
-        total = keep.astype(F32)
-        for e in range(1, n_sub):
-            size = n_tiles * rows
-            total += shifted(send[(e - 1) * size : e * size], "sub", n_sub, e).astype(F32)
-        return [total[d * rows : (d + 1) * rows].astype(BF16) for d in range(n_tiles)]
+        size = n_tiles * rows
+        received = [
+            shifted(send[(e - 1) * size : e * size], "sub", n_sub, e) for e in range(1, n_sub)
+        ]
+        return on_chip(
+            combine_kernel,
+            (),
+            (keep, received),
+            [jax.ShapeDtypeStruct((rows, keep.shape[1]), BF16)] * n_tiles,
+            [],
+            0,
+            2 << 20,
+            "combine",
+        )
 
     def spread_out(parts):
         return [shifted(part, "tiles", n_tiles, d) if d else part for d, part in enumerate(parts)]

time: 87 us -> 86.9 us (level)
    pallas_call x9 -> x12, Pallas kernels: 9.14 us -> 9.41 us  [on_chip(): pl.pallas_call(body, out_shape=tuple(out_shapes), in_specs=[in_smem] * n_...]
where the time goes in v7:
time: 86.9 us; the launch traced here: 86.3 us
  starting transfers between devices  40.6 us (47%)
  waiting for transfers between devices  20.1 us (23%)
  Pallas kernels  17.8 us (20%)
  local copies, waits for them, and re-layouts  5.46 us (6%)
  other arithmetic  1.45 us (2%)
    ppermute x37, starting transfers between devices, shifted(): lax.ppermute(value, axis, [(i, (i + amount) % size) for i in range(size)])  40.6 us
    ppermute x37, waiting for transfers between devices, shifted(): lax.ppermute(value, axis, [(i, (i + amount) % size) for i in range(size)])  20.1 us
    pallas_call x12, Pallas kernels, on_chip(): pl.pallas_call(body, out_shape=tuple(out_shapes), in_specs=[in_smem] * n_...  9.41 us
    pallas_call x2, Pallas kernels, near_field(): pl.pallas_call(functools.partial(near_kernel, len(stacks), per_step), out...  8.36 us
    unnamed x14, local copies, waits for them, and re-layouts  4.3 us
  transfers between devices with their start and end apart: 37, of which 12 were waited for; matrix products, arithmetic and copies ran while one was open for 3% of the time, Pallas kernels for 16%

profile of v7, /device:TPU:0, one launch (start us, length us, event | category | flops | bytes accessed | tf_op | source)
XLA Modules:
  0.0 86.3 jit_solution(8488245097429406575)
XLA Ops:
  0.6 3.0 %collective-permute-start.8 = (bf16[768,512]{1,0:T(8,128)(2,1)}, bf16[768,512]{1,0:T(8,128)(2,1)S(1)}, u32[]{:S(2)}, u32[]{:S(2)}) collective-permute-start(bf16[768,512]{1,0:T(8,128)(2,1)} %bitcast.31), channel_id=1, source_target_pairs={{0,2},{2,0},{1,3},{3,1},{4,6},{6,4},{5,7},{7,5},{8,10},{10,8},{9,1... | collective-permute-start | bytes 2359304 | tf_op jit(solution)/shard_map/ppermute | solution.py:28
  3.7 1.6 %collective-permute-start.1 = (bf16[128,512]{1,0:T(8,128)(2,1)}, bf16[128,512]{1,0:T(8,128)(2,1)S(1)}, u32[]{:S(2)}, u32[]{:S(2)}) collective-permute-start(bf16[128,512]{1,0:T(8,128)(2,1)} %refs_2_.1), channel_id=1, source_target_pairs={{0,4},{4,8},{8,12},{12,0},{1,5},{5,9},{9,13},{13,1},{2,6},{6,10},{... | collective-permute-start | bytes 393224 | tf_op jit(solution)/shard_map/ppermute | solution.py:28
  5.2 2.6 %collective-permute-start.2 = (bf16[128,512]{1,0:T(8,128)(2,1)}, bf16[128,512]{1,0:T(8,128)(2,1)S(1)}, u32[]{:S(2)}, u32[]{:S(2)}) collective-permute-start(bf16[128,512]{1,0:T(8,128)(2,1)} %refs_2_.1), channel_id=1, source_target_pairs={{0,8},{4,12},{8,0},{12,4},{1,9},{5,13},{9,1},{13,5},{2,10},{6,14},... | collective-permute-start | bytes 393224 | tf_op jit(solution)/shard_map/ppermute | solution.py:28
  7.8 1.3 %collective-permute-start.3 = (bf16[128,512]{1,0:T(8,128)(2,1)}, bf16[128,512]{1,0:T(8,128)(2,1)S(1)}, u32[]{:S(2)}, u32[]{:S(2)}) collective-permute-start(bf16[128,512]{1,0:T(8,128)(2,1)} %refs_2_.1), channel_id=1, source_target_pairs={{0,12},{4,0},{8,4},{12,8},{1,13},{5,1},{9,5},{13,9},{2,14},{6,2},{... | collective-permute-start | bytes 393224 | tf_op jit(solution)/shard_map/ppermute | solution.py:28
  9.2 1.2 %fusion.5 = (bf16[768,256]{1,0:T(8,128)(2,1)S(1)}, bf16[768,256]{1,0:T(8,128)(2,1)S(1)}) fusion(bf16[768,512]{1,0:T(8,128)(2,1)} %bitcast.25), kind=kLoop, calls=%fused_computation.19 | loop fusion | bytes 1572864 | tf_op jit(solution)/shard_map/slice | solution.py:353
  10.3 1.8 %collective-permute-done.1.refs_3_ = bf16[128,512]{1,0:T(8,128)(2,1)S(1)} collective-permute-done((bf16[128,512]{1,0:T(8,128)(2,1)}, bf16[128,512]{1,0:T(8,128)(2,1)S(1)}, u32[]{:S(2)}, u32[]{:S(2)}) %collective-permute-start.1) | collective-permute-done | bytes 131104 | tf_op jit(solution)/shard_map/ppermute | solution.py:28
  12.2 0.3 collective-permute-start.21
  12.5 0.7 fusion.slot_ref
  13.1 3.3 %collective-permute-done.2.refs_4_ = bf16[128,512]{1,0:T(8,128)(2,1)S(1)} collective-permute-done((bf16[128,512]{1,0:T(8,128)(2,1)}, bf16[128,512]{1,0:T(8,128)(2,1)S(1)}, u32[]{:S(2)}, u32[]{:S(2)}) %collective-permute-start.2) | collective-permute-done | bytes 131104 | tf_op jit(solution)/shard_map/ppermute | solution.py:28
  16.4 0.5 collective-permute-start.6
  17.1 0.7 pad_add_fusion.refs_1_
  17.8 0.6 collective-permute-start
  18.4 1.5 %collective-permute-start.9 = (bf16[768,256]{1,0:T(8,128)(2,1)S(1)}, bf16[768,256]{1,0:T(8,128)(2,1)S(1)}, u32[]{:S(2)}, u32[]{:S(2)}) collective-permute-start(bf16[768,256]{1,0:T(8,128)(2,1)S(1)} %get-tuple-element.53), channel_id=1, source_target_pairs={{0,2},{2,0},{1,3},{3,1},{4,6},{6,4},{5,7},{7,5},{8,10},{10,8},{9,1... | collective-permute-start | bytes 1179656 | tf_op jit(solution)/shard_map/ppermute | solution.py:28
  19.9 0.9 %copy-done.4 = bf16[128,512]{1,0:T(8,128)(2,1)S(1)} copy-done((bf16[128,512]{1,0:T(8,128)(2,1)S(1)}, bf16[128,512]{1,0:T(8,128)(2,1)}, u32[]{:S(2)}) %copy-start.4) | copy-done | bytes 131096
  20.8 2.0 %far_own.1 = (f32[1024,512]{1,0:T(8,128)S(1)}, bf16[1024,512]{1,0:T(8,128)(2,1)S(1)}) custom-call(s32[2]{0:T(128)S(1)} %pad_add_fusion.1.refs_0_, s32[3,12]{1,0:T(4,128)S(1)} %pad_add_fusion.refs_1_, bf16[128,512]{1,0:T(8,128)(2,1)S(1)} %copy-done.4, bf16[128,512]{1,0:T(8,128)(2,1)S(1)} %collective-permute-done.1.refs_3_, ...), custom_call_target="tpu_custom_call" | custom-call | flops 1 | bytes 1 | tf_op jit(solution)/shard_map/far_own/pallas_call | solution.py:45
  22.8 3.4 %copy-done = bf16[1,16,512,512]{3,2,1,0:T(8,128)(2,1)S(1)} copy-done((bf16[1,16,512,512]{3,2,1,0:T(8,128)(2,1)S(1)}, bf16[1,16,512,512]{3,2,1,0:T(8,128)(2,1)}, u32[]{:S(2)}) %copy-start) | copy-done | bytes 8388632
  26.2 3.9 %near_field.2.refs_4_ = f32[128,512]{1,0:T(8,128)S(1)} custom-call(s32[16]{0:T(128)S(1)} %fusion.slot_ref, bf16[1024,512]{1,0:T(8,128)(2,1)S(1)} %get-tuple-element.28.refs_0_.refs_2_, bf16[16,512,512]{2,1,0:T(8,128)(2,1)S(1)} %bitcast.21), custom_call_target="tpu_custom_call" | custom-call | flops 1 | bytes 1 | tf_op jit(solution)/shard_map/near_field/pallas_call | solution.py:226
  30.1 0.6 collective-permute-done.refs_1_.refs_2_
  30.7 1.2 %far_first_stage.1.refs_0_ = bf16[1024,768]{1,0:T(8,128)(2,1)S(1)} custom-call(s32[2]{0:T(128)S(1)} %pad_add_fusion.1.refs_0_, s32[3,12]{1,0:T(4,128)S(1)} %collective-permute-done.refs_1_.refs_2_, bf16[1024,512]{1,0:T(8,128)(2,1)S(1)} %get-tuple-element.28.refs_0_.refs_2_, bf16[768,512]{1,0:T(8,128)(2,1)S(1)} %collective-permute-done.8.refs_3_.refs_20_), custom_call_target="tpu_custom_call" | custom-call | flops 1 | bytes 1 | tf_op jit(solution)/shard_map/far_first_stage/pallas_call | solution.py:45
  31.9 0.6 far_second_stage.3
  32.6 5.7 %collective-permute-done.9.refs_2_.refs_22_ = bf16[768,256]{1,0:T(8,128)(2,1)S(1)} collective-permute-done((bf16[768,256]{1,0:T(8,128)(2,1)S(1)}, bf16[768,256]{1,0:T(8,128)(2,1)S(1)}, u32[]{:S(2)}, u32[]{:S(2)}) %collective-permute-start.9) | collective-permute-done | bytes 393248 | tf_op jit(solution)/shard_map/ppermute | solution.py:28
  38.3 0.6 far_second_stage.2
  39.1 1.9 %collective-permute-start.23 = (bf16[128,256]{1,0:T(8,128)(2,1)S(1)}, bf16[128,256]{1,0:T(8,128)(2,1)S(1)}, u32[]{:S(2)}, u32[]{:S(2)}) collective-permute-start(bf16[128,256]{1,0:T(8,128)(2,1)S(1)} %get-tuple-element.40), channel_id=1, source_target_pairs={{0,4},{4,8},{8,12},{12,0},{1,5},{5,9},{9,13},{13,1},{2,6},{6,10},{... | collective-permute-start | bytes 196616 | tf_op jit(solution)/shard_map/ppermute | solution.py:28
  40.9 2.6 %collective-permute-start.24 = (bf16[128,256]{1,0:T(8,128)(2,1)S(1)}, bf16[128,256]{1,0:T(8,128)(2,1)S(1)}, u32[]{:S(2)}, u32[]{:S(2)}) collective-permute-start(bf16[128,256]{1,0:T(8,128)(2,1)S(1)} %get-tuple-element.41), channel_id=1, source_target_pairs={{0,8},{4,12},{8,0},{12,4},{1,9},{5,13},{9,1},{13,5},{2,10},{6,14},... | collective-permute-start | bytes 196616 | tf_op jit(solution)/shard_map/ppermute | solution.py:28
  43.5 1.3 %collective-permute-start.25 = (bf16[128,256]{1,0:T(8,128)(2,1)S(1)}, bf16[128,256]{1,0:T(8,128)(2,1)S(1)}, u32[]{:S(2)}, u32[]{:S(2)}) collective-permute-start(bf16[128,256]{1,0:T(8,128)(2,1)S(1)} %get-tuple-element.42), channel_id=1, source_target_pairs={{0,12},{4,0},{8,4},{12,8},{1,13},{5,1},{9,5},{13,9},{2,14},{6,2},{... | collective-permute-start | bytes 196616 | tf_op jit(solution)/shard_map/ppermute | solution.py:28
  44.9 0.7 collective-permute-start.11
  45.7 0.3 collective-permute-start.12
  46.0 2.8 %collective-permute-start.13 = (bf16[128,256]{1,0:T(8,128)(2,1)S(1)}, bf16[128,256]{1,0:T(8,128)(2,1)S(1)}, u32[]{:S(2)}, u32[]{:S(2)}) collective-permute-start(bf16[128,256]{1,0:T(8,128)(2,1)S(1)} %get-tuple-element.35), channel_id=1, source_target_pairs={{0,12},{4,0},{8,4},{12,8},{1,13},{5,1},{9,5},{13,9},{2,14},{6,2},{... | collective-permute-start | bytes 196616 | tf_op jit(solution)/shard_map/ppermute | solution.py:28
  49.0 4.5 %collective-permute-start.26 = (bf16[128,256]{1,0:T(8,128)(2,1)S(1)}, bf16[128,256]{1,0:T(8,128)(2,1)S(1)}, u32[]{:S(2)}, u32[]{:S(2)}) collective-permute-start(bf16[128,256]{1,0:T(8,128)(2,1)S(1)} %finish.4.refs_11_), channel_id=1, source_target_pairs={{0,4},{4,8},{8,12},{12,0},{1,5},{5,9},{9,13},{13,1},{2,6},{6,10},{... | collective-permute-start | bytes 196616 | tf_op jit(solution)/shard_map/ppermute | solution.py:28
  53.6 2.4 %collective-permute-start.28 = (bf16[128,256]{1,0:T(8,128)(2,1)S(1)}, bf16[128,256]{1,0:T(8,128)(2,1)S(1)}, u32[]{:S(2)}, u32[]{:S(2)}) collective-permute-start(bf16[128,256]{1,0:T(8,128)(2,1)S(1)} %finish.4.refs_11_), channel_id=1, source_target_pairs={{0,12},{4,0},{8,4},{12,8},{1,13},{5,1},{9,5},{13,9},{2,14},{6,2},{... | collective-permute-start | bytes 196616 | tf_op jit(solution)/shard_map/ppermute | solution.py:28
  56.2 2.7 %collective-permute-start.14 = (bf16[128,256]{1,0:T(8,128)(2,1)S(1)}, bf16[128,256]{1,0:T(8,128)(2,1)S(1)}, u32[]{:S(2)}, u32[]{:S(2)}) collective-permute-start(bf16[128,256]{1,0:T(8,128)(2,1)S(1)} %finish.3.refs_3_), channel_id=1, source_target_pairs={{0,4},{4,8},{8,12},{12,0},{1,5},{5,9},{9,13},{13,1},{2,6},{6,10},{... | collective-permute-start | bytes 196616 | tf_op jit(solution)/shard_map/ppermute | solution.py:28
  58.9 0.9 %collective-permute-done.27.refs_13_ = bf16[128,256]{1,0:T(8,128)(2,1)S(1)} collective-permute-done((bf16[128,256]{1,0:T(8,128)(2,1)S(1)}, bf16[128,256]{1,0:T(8,128)(2,1)S(1)}, u32[]{:S(2)}, u32[]{:S(2)}) %collective-permute-start.27) | collective-permute-done | bytes 65568 | tf_op jit(solution)/shard_map/ppermute | solution.py:28
  59.8 3.4 %collective-permute-start.16 = (bf16[128,256]{1,0:T(8,128)(2,1)S(1)}, bf16[128,256]{1,0:T(8,128)(2,1)S(1)}, u32[]{:S(2)}, u32[]{:S(2)}) collective-permute-start(bf16[128,256]{1,0:T(8,128)(2,1)S(1)} %finish.3.refs_3_), channel_id=1, source_target_pairs={{0,12},{4,0},{8,4},{12,8},{1,13},{5,1},{9,5},{13,9},{2,14},{6,2},{... | collective-permute-start | bytes 196616 | tf_op jit(solution)/shard_map/ppermute | solution.py:28
  63.2 0.5 collective-permute-start.30
  63.8 1.7 %collective-permute-done.15.refs_5_ = bf16[128,256]{1,0:T(8,128)(2,1)S(1)} collective-permute-done((bf16[128,256]{1,0:T(8,128)(2,1)S(1)}, bf16[128,256]{1,0:T(8,128)(2,1)S(1)}, u32[]{:S(2)}, u32[]{:S(2)}) %collective-permute-start.15) | collective-permute-done | bytes 65568 | tf_op jit(solution)/shard_map/ppermute | solution.py:28
  65.5 0.5 collective-permute-start.18
  66.1 0.4 collective-permute-start.20
  66.5 0.2 collective-permute-done.32.refs_18_
  66.9 0.4 collective-permute-done.19.refs_9_
  67.4 2.5 %far_sent.1 = (bf16[512,512]{1,0:T(8,128)(2,1)S(1)}, bf16[1024,512]{1,0:T(8,128)(2,1)S(1)}, bf16[512,1536]{1,0:T(8,128)(2,1)S(1)}) custom-call(s32[2]{0:T(128)S(1)} %pad_add_fusion.1.refs_0_, s32[3,12]{1,0:T(4,128)S(1)} %pad_add_fusion.refs_1_, s32[3,12]{1,0:T(4,128)S(1)} %collective-permute-done.refs_1_.refs_2_, bf16[128,256]{1,0:T(8,128)(2,1)S(1)} %finish.3.refs_3_, ...), custom_call_target="tpu_custom_call" | custom-call | flops 1 | bytes 1 | tf_op jit(solution)/shard_map/far_sent/pallas_call | solution.py:45
  70.0 0.4 collective-permute-start.33
  70.4 1.0 %far_kept.1.refs_0_ = bf16[512,512]{1,0:T(8,128)(2,1)S(1)} custom-call(bf16[512,1536]{1,0:T(8,128)(2,1)S(1)} %get-tuple-element.45.refs_0_, bf16[768,512]{1,0:T(8,128)(2,1)S(1)} %bitcast.29, bf16[768,256]{1,0:T(8,128)(2,1)S(1)} %collective-permute-done.9.refs_2_.refs_22_, bf16[768,512]{1,0:T(8,128)(2,1)S(1)} %bitcast.30, ...), custom_call_target="tpu_custom_call" | custom-call | flops 10000000000 | bytes 1 | tf_op jit(solution)/shard_map/far_kept/pallas_call | solution.py:45
  71.4 0.6 collective-permute-done.33.refs_1_
  72.1 1.8 %collective-permute-start.34 = (bf16[128,512]{1,0:T(8,128)(2,1)S(1)}, bf16[128,512]{1,0:T(8,128)(2,1)S(1)}, u32[]{:S(2)}, u32[]{:S(2)}) collective-permute-start(bf16[128,512]{1,0:T(8,128)(2,1)S(1)} %get-tuple-element.48), channel_id=1, source_target_pairs={{0,4},{4,8},{8,12},{12,0},{1,5},{5,9},{9,13},{13,1},{2,6},{6,10},{... | collective-permute-start | bytes 393224 | tf_op jit(solution)/shard_map/ppermute | solution.py:28
  73.8 2.5 %collective-permute-start.35 = (bf16[128,512]{1,0:T(8,128)(2,1)S(1)}, bf16[128,512]{1,0:T(8,128)(2,1)S(1)}, u32[]{:S(2)}, u32[]{:S(2)}) collective-permute-start(bf16[128,512]{1,0:T(8,128)(2,1)S(1)} %get-tuple-element.49), channel_id=1, source_target_pairs={{0,8},{4,12},{8,0},{12,4},{1,9},{5,13},{9,1},{13,5},{2,10},{6,14},... | collective-permute-start | bytes 393224 | tf_op jit(solution)/shard_map/ppermute | solution.py:28
  76.3 4.5 %near_field.3 = (f32[128,512]{1,0:T(8,128)S(1)}, bf16[128,512]{1,0:T(8,128)(2,1)}) custom-call(s32[16]{0:T(128)S(1)} %fusion.slot_ref, bf16[1024,512]{1,0:T(8,128)(2,1)S(1)} %get-tuple-element.43.refs_0_, bf16[16,512,512]{2,1,0:T(8,128)(2,1)S(1)} %bitcast.24), custom_call_target="tpu_custom_call" | custom-call | flops 1 | bytes 1 | tf_op jit(solution)/shard_map/near_field/pallas_call | solution.py:226
  80.8 4.5 %collective-permute-done.35.refs_2_ = bf16[128,512]{1,0:T(8,128)(2,1)S(1)} collective-permute-done((bf16[128,512]{1,0:T(8,128)(2,1)S(1)}, bf16[128,512]{1,0:T(8,128)(2,1)S(1)}, u32[]{:S(2)}, u32[]{:S(2)}) %collective-permute-start.35) | collective-permute-done | bytes 131104 | tf_op jit(solution)/shard_map/ppermute | solution.py:28
  85.4 0.9 %finish.5 = bf16[128,512]{1,0:T(8,128)(2,1)} custom-call(bf16[128,512]{1,0:T(8,128)(2,1)S(1)} %get-tuple-element.47.refs_0_, bf16[128,512]{1,0:T(8,128)(2,1)S(1)} %collective-permute-done.34.refs_1_, bf16[128,512]{1,0:T(8,128)(2,1)S(1)} %collective-permute-done.35.refs_2_, bf16[128,512]{1,0:T(8,128)(2,1)S(1)} %collective-permute-done.36.refs_3_, ...), custom_call_target="tpu_custom_call" | custom-call | flops 1 | bytes 1 | tf_op jit(solution)/shard_map/finish/pallas_call | solution.py:45
  (59 shorter events, 1.5 us)
Async XLA Ops:
  0.6 19.3 %copy-start.2 = (bf16[12,64,512]{2,1,0:T(8,128)(2,1)S(1)}, bf16[12,64,512]{2,1,0:T(8,128)(2,1)}, u32[]{:S(2)}) copy-start(bf16[12,64,512]{2,1,0:T(8,128)(2,1)} %param.11) | copy-start | bytes 2359300
  0.6 19.3 %copy-start.1 = (bf16[12,64,512]{2,1,0:T(8,128)(2,1)S(1)}, bf16[12,64,512]{2,1,0:T(8,128)(2,1)}, u32[]{:S(2)}) copy-start(bf16[12,64,512]{2,1,0:T(8,128)(2,1)} %param.10) | copy-start | bytes 2359300
  0.6 30.1 %collective-permute-start.8 = (bf16[768,512]{1,0:T(8,128)(2,1)}, bf16[768,512]{1,0:T(8,128)(2,1)S(1)}, u32[]{:S(2)}, u32[]{:S(2)}) collective-permute-start(bf16[768,512]{1,0:T(8,128)(2,1)} %bitcast.31), channel_id=1, source_target_pairs={{0,2},{2,0},{1,3},{3,1},{4,6},{6,4},{5,7},{7,5},{8,10},{10,8},{9,1... | collective-permute-start | bytes 2359304 | tf_op jit(solution)/shard_map/ppermute | solution.py:28
  3.7 8.5 %collective-permute-start.1 = (bf16[128,512]{1,0:T(8,128)(2,1)}, bf16[128,512]{1,0:T(8,128)(2,1)S(1)}, u32[]{:S(2)}, u32[]{:S(2)}) collective-permute-start(bf16[128,512]{1,0:T(8,128)(2,1)} %refs_2_.1), channel_id=1, source_target_pairs={{0,4},{4,8},{8,12},{12,0},{1,5},{5,9},{9,13},{13,1},{2,6},{6,10},{... | collective-permute-start | bytes 393224 | tf_op jit(solution)/shard_map/ppermute | solution.py:28
  5.2 11.2 %collective-permute-start.2 = (bf16[128,512]{1,0:T(8,128)(2,1)}, bf16[128,512]{1,0:T(8,128)(2,1)S(1)}, u32[]{:S(2)}, u32[]{:S(2)}) collective-permute-start(bf16[128,512]{1,0:T(8,128)(2,1)} %refs_2_.1), channel_id=1, source_target_pairs={{0,8},{4,12},{8,0},{12,4},{1,9},{5,13},{9,1},{13,5},{2,10},{6,14},... | collective-permute-start | bytes 393224 | tf_op jit(solution)/shard_map/ppermute | solution.py:28
  7.8 8.6 %collective-permute-start.3 = (bf16[128,512]{1,0:T(8,128)(2,1)}, bf16[128,512]{1,0:T(8,128)(2,1)S(1)}, u32[]{:S(2)}, u32[]{:S(2)}) collective-permute-start(bf16[128,512]{1,0:T(8,128)(2,1)} %refs_2_.1), channel_id=1, source_target_pairs={{0,12},{4,0},{8,4},{12,8},{1,13},{5,1},{9,5},{13,9},{2,14},{6,2},{... | collective-permute-start | bytes 393224 | tf_op jit(solution)/shard_map/ppermute | solution.py:28
  9.2 7.8 %collective-permute-start.4 = (bf16[128,512]{1,0:T(8,128)(2,1)}, bf16[128,512]{1,0:T(8,128)(2,1)S(1)}, u32[]{:S(2)}, u32[]{:S(2)}) collective-permute-start(bf16[128,512]{1,0:T(8,128)(2,1)} %refs_2_.1), channel_id=1, source_target_pairs={{0,1},{1,0},{2,3},{3,2},{4,5},{5,4},{6,7},{7,6},{8,9},{9,8},{10,11... | collective-permute-start | bytes 393224 | tf_op jit(solution)/shard_map/ppermute | solution.py:28
  12.2 19.8 %collective-permute-start.21 = (bf16[768,256]{1,0:T(8,128)(2,1)S(1)}, bf16[768,256]{1,0:T(8,128)(2,1)S(1)}, u32[]{:S(2)}, u32[]{:S(2)}) collective-permute-start(bf16[768,256]{1,0:T(8,128)(2,1)S(1)} %get-tuple-element.52), channel_id=1, source_target_pairs={{0,2},{2,0},{1,3},{3,1},{4,6},{6,4},{5,7},{7,5},{8,10},{10,8},{9,1... | collective-permute-start | bytes 1179656 | tf_op jit(solution)/shard_map/ppermute | solution.py:28
  16.4 1.4 %collective-permute-start.5 = (bf16[128,512]{1,0:T(8,128)(2,1)S(1)}, bf16[128,512]{1,0:T(8,128)(2,1)S(1)}, u32[]{:S(2)}, u32[]{:S(2)}) collective-permute-start(bf16[128,512]{1,0:T(8,128)(2,1)S(1)} %collective-permute-done.1.refs_3_), channel_id=1, source_target_pairs={{0,1},{1,0},{2,3},{3,2},{4,5},{5,4},{6,7},{7,6},{8,9},{9,8},{10,11... | collective-permute-start | bytes 393224 | tf_op jit(solution)/shard_map/ppermute | solution.py:28
  16.4 1.9 %collective-permute-start.6 = (bf16[128,512]{1,0:T(8,128)(2,1)S(1)}, bf16[128,512]{1,0:T(8,128)(2,1)S(1)}, u32[]{:S(2)}, u32[]{:S(2)}) collective-permute-start(bf16[128,512]{1,0:T(8,128)(2,1)S(1)} %collective-permute-done.2.refs_4_), channel_id=1, source_target_pairs={{0,1},{1,0},{2,3},{3,2},{4,5},{5,4},{6,7},{7,6},{8,9},{9,8},{10,11... | collective-permute-start | bytes 393224 | tf_op jit(solution)/shard_map/ppermute | solution.py:28
  17.0 2.9 %collective-permute-start.7 = (bf16[128,512]{1,0:T(8,128)(2,1)S(1)}, bf16[128,512]{1,0:T(8,128)(2,1)S(1)}, u32[]{:S(2)}, u32[]{:S(2)}) collective-permute-start(bf16[128,512]{1,0:T(8,128)(2,1)S(1)} %collective-permute-done.3.refs_5_), channel_id=1, source_target_pairs={{0,1},{1,0},{2,3},{3,2},{4,5},{5,4},{6,7},{7,6},{8,9},{9,8},{10,11... | collective-permute-start | bytes 393224 | tf_op jit(solution)/shard_map/ppermute | solution.py:28
  17.8 12.9 %collective-permute-start = (s32[3,12]{1,0:T(4,128)S(1)}, s32[3,12]{1,0:T(4,128)S(1)}, u32[]{:S(2)}, u32[]{:S(2)}) collective-permute-start(s32[3,12]{1,0:T(4,128)S(1)} %pad_add_fusion.refs_1_), channel_id=1, source_target_pairs={{0,2},{2,0},{1,3},{3,1},{4,6},{6,4},{5,7},{7,5},{8,10},{10,8},{9,1... | collective-permute-start | bytes 440 | tf_op jit(solution)/shard_map/ppermute | solution.py:28
  18.4 19.9 %collective-permute-start.9 = (bf16[768,256]{1,0:T(8,128)(2,1)S(1)}, bf16[768,256]{1,0:T(8,128)(2,1)S(1)}, u32[]{:S(2)}, u32[]{:S(2)}) collective-permute-start(bf16[768,256]{1,0:T(8,128)(2,1)S(1)} %get-tuple-element.53), channel_id=1, source_target_pairs={{0,2},{2,0},{1,3},{3,1},{4,6},{6,4},{5,7},{7,5},{8,10},{10,8},{9,1... | collective-permute-start | bytes 1179656 | tf_op jit(solution)/shard_map/ppermute | solution.py:28
  19.9 0.9 %copy-start.4 = (bf16[128,512]{1,0:T(8,128)(2,1)S(1)}, bf16[128,512]{1,0:T(8,128)(2,1)}, u32[]{:S(2)}) copy-start(bf16[128,512]{1,0:T(8,128)(2,1)} %refs_2_.1) | copy-start | bytes 393220
  22.8 3.4 %copy-start = (bf16[1,16,512,512]{3,2,1,0:T(8,128)(2,1)S(1)}, bf16[1,16,512,512]{3,2,1,0:T(8,128)(2,1)}, u32[]{:S(2)}) copy-start(bf16[1,16,512,512]{3,2,1,0:T(8,128)(2,1)} %param.15) | copy-start | bytes 25165828
  32.5 16.3 %copy-start.3 = (bf16[4,128,128]{2,1,0:T(8,128)(2,1)S(1)}, bf16[4,128,128]{2,1,0:T(8,128)(2,1)}, u32[]{:S(2)}) copy-start(bf16[4,128,128]{2,1,0:T(8,128)(2,1)} %refs_5_.5) | copy-start | bytes 393220
  32.6 6.4 %collective-permute-start.22 = (bf16[512,256]{1,0:T(8,128)(2,1)S(1)}, bf16[512,256]{1,0:T(8,128)(2,1)S(1)}, u32[]{:S(2)}, u32[]{:S(2)}) collective-permute-start(bf16[512,256]{1,0:T(8,128)(2,1)S(1)} %get-tuple-element.38), channel_id=1, source_target_pairs={{0,1},{1,0},{2,3},{3,2},{4,5},{5,4},{6,7},{7,6},{8,9},{9,8},{10,11... | collective-permute-start | bytes 786440 | tf_op jit(solution)/shard_map/ppermute | solution.py:28
  38.9 6.0 %collective-permute-start.10 = (bf16[512,256]{1,0:T(8,128)(2,1)S(1)}, bf16[512,256]{1,0:T(8,128)(2,1)S(1)}, u32[]{:S(2)}, u32[]{:S(2)}) collective-permute-start(bf16[512,256]{1,0:T(8,128)(2,1)S(1)} %get-tuple-element.31), channel_id=1, source_target_pairs={{0,1},{1,0},{2,3},{3,2},{4,5},{5,4},{6,7},{7,6},{8,9},{9,8},{10,11... | collective-permute-start | bytes 786440 | tf_op jit(solution)/shard_map/ppermute | solution.py:28
  39.1 7.0 %collective-permute-start.23 = (bf16[128,256]{1,0:T(8,128)(2,1)S(1)}, bf16[128,256]{1,0:T(8,128)(2,1)S(1)}, u32[]{:S(2)}, u32[]{:S(2)}) collective-permute-start(bf16[128,256]{1,0:T(8,128)(2,1)S(1)} %get-tuple-element.40), channel_id=1, source_target_pairs={{0,4},{4,8},{8,12},{12,0},{1,5},{5,9},{9,13},{13,1},{2,6},{6,10},{... | collective-permute-start | bytes 196616 | tf_op jit(solution)/shard_map/ppermute | solution.py:28
  40.9 7.9 %collective-permute-start.24 = (bf16[128,256]{1,0:T(8,128)(2,1)S(1)}, bf16[128,256]{1,0:T(8,128)(2,1)S(1)}, u32[]{:S(2)}, u32[]{:S(2)}) collective-permute-start(bf16[128,256]{1,0:T(8,128)(2,1)S(1)} %get-tuple-element.41), channel_id=1, source_target_pairs={{0,8},{4,12},{8,0},{12,4},{1,9},{5,13},{9,1},{13,5},{2,10},{6,14},... | collective-permute-start | bytes 196616 | tf_op jit(solution)/shard_map/ppermute | solution.py:28
  43.5 5.3 %collective-permute-start.25 = (bf16[128,256]{1,0:T(8,128)(2,1)S(1)}, bf16[128,256]{1,0:T(8,128)(2,1)S(1)}, u32[]{:S(2)}, u32[]{:S(2)}) collective-permute-start(bf16[128,256]{1,0:T(8,128)(2,1)S(1)} %get-tuple-element.42), channel_id=1, source_target_pairs={{0,12},{4,0},{8,4},{12,8},{1,13},{5,1},{9,5},{13,9},{2,14},{6,2},{... | collective-permute-start | bytes 196616 | tf_op jit(solution)/shard_map/ppermute | solution.py:28
  44.9 8.6 %collective-permute-start.11 = (bf16[128,256]{1,0:T(8,128)(2,1)S(1)}, bf16[128,256]{1,0:T(8,128)(2,1)S(1)}, u32[]{:S(2)}, u32[]{:S(2)}) collective-permute-start(bf16[128,256]{1,0:T(8,128)(2,1)S(1)} %get-tuple-element.33), channel_id=1, source_target_pairs={{0,4},{4,8},{8,12},{12,0},{1,5},{5,9},{9,13},{13,1},{2,6},{6,10},{... | collective-permute-start | bytes 196616 | tf_op jit(solution)/shard_map/ppermute | solution.py:28
  45.7 10.4 %collective-permute-start.12 = (bf16[128,256]{1,0:T(8,128)(2,1)S(1)}, bf16[128,256]{1,0:T(8,128)(2,1)S(1)}, u32[]{:S(2)}, u32[]{:S(2)}) collective-permute-start(bf16[128,256]{1,0:T(8,128)(2,1)S(1)} %get-tuple-element.34), channel_id=1, source_target_pairs={{0,8},{4,12},{8,0},{12,4},{1,9},{5,13},{9,1},{13,5},{2,10},{6,14},... | collective-permute-start | bytes 196616 | tf_op jit(solution)/shard_map/ppermute | solution.py:28
  46.0 10.0 %collective-permute-start.13 = (bf16[128,256]{1,0:T(8,128)(2,1)S(1)}, bf16[128,256]{1,0:T(8,128)(2,1)S(1)}, u32[]{:S(2)}, u32[]{:S(2)}) collective-permute-start(bf16[128,256]{1,0:T(8,128)(2,1)S(1)} %get-tuple-element.35), channel_id=1, source_target_pairs={{0,12},{4,0},{8,4},{12,8},{1,13},{5,1},{9,5},{13,9},{2,14},{6,2},{... | collective-permute-start | bytes 196616 | tf_op jit(solution)/shard_map/ppermute | solution.py:28
  49.0 9.9 %collective-permute-start.26 = (bf16[128,256]{1,0:T(8,128)(2,1)S(1)}, bf16[128,256]{1,0:T(8,128)(2,1)S(1)}, u32[]{:S(2)}, u32[]{:S(2)}) collective-permute-start(bf16[128,256]{1,0:T(8,128)(2,1)S(1)} %finish.4.refs_11_), channel_id=1, source_target_pairs={{0,4},{4,8},{8,12},{12,0},{1,5},{5,9},{9,13},{13,1},{2,6},{6,10},{... | collective-permute-start | bytes 196616 | tf_op jit(solution)/shard_map/ppermute | solution.py:28
  53.6 6.2 %collective-permute-start.27 = (bf16[128,256]{1,0:T(8,128)(2,1)S(1)}, bf16[128,256]{1,0:T(8,128)(2,1)S(1)}, u32[]{:S(2)}, u32[]{:S(2)}) collective-permute-start(bf16[128,256]{1,0:T(8,128)(2,1)S(1)} %finish.4.refs_11_), channel_id=1, source_target_pairs={{0,8},{4,12},{8,0},{12,4},{1,9},{5,13},{9,1},{13,5},{2,10},{6,14},... | collective-permute-start | bytes 196616 | tf_op jit(solution)/shard_map/ppermute | solution.py:28
  53.6 9.6 %collective-permute-start.28 = (bf16[128,256]{1,0:T(8,128)(2,1)S(1)}, bf16[128,256]{1,0:T(8,128)(2,1)S(1)}, u32[]{:S(2)}, u32[]{:S(2)}) collective-permute-start(bf16[128,256]{1,0:T(8,128)(2,1)S(1)} %finish.4.refs_11_), channel_id=1, source_target_pairs={{0,12},{4,0},{8,4},{12,8},{1,13},{5,1},{9,5},{13,9},{2,14},{6,2},{... | collective-permute-start | bytes 196616 | tf_op jit(solution)/shard_map/ppermute | solution.py:28
  56.0 7.2 %collective-permute-start.29 = (bf16[128,256]{1,0:T(8,128)(2,1)S(1)}, bf16[128,256]{1,0:T(8,128)(2,1)S(1)}, u32[]{:S(2)}, u32[]{:S(2)}) collective-permute-start(bf16[128,256]{1,0:T(8,128)(2,1)S(1)} %finish.4.refs_11_), channel_id=1, source_target_pairs={{0,1},{1,0},{2,3},{3,2},{4,5},{5,4},{6,7},{7,6},{8,9},{9,8},{10,11... | collective-permute-start | bytes 196616 | tf_op jit(solution)/shard_map/ppermute | solution.py:28
  56.2 7.5 %collective-permute-start.14 = (bf16[128,256]{1,0:T(8,128)(2,1)S(1)}, bf16[128,256]{1,0:T(8,128)(2,1)S(1)}, u32[]{:S(2)}, u32[]{:S(2)}) collective-permute-start(bf16[128,256]{1,0:T(8,128)(2,1)S(1)} %finish.3.refs_3_), channel_id=1, source_target_pairs={{0,4},{4,8},{8,12},{12,0},{1,5},{5,9},{9,13},{13,1},{2,6},{6,10},{... | collective-permute-start | bytes 196616 | tf_op jit(solution)/shard_map/ppermute | solution.py:28
  58.9 6.5 %collective-permute-start.15 = (bf16[128,256]{1,0:T(8,128)(2,1)S(1)}, bf16[128,256]{1,0:T(8,128)(2,1)S(1)}, u32[]{:S(2)}, u32[]{:S(2)}) collective-permute-start(bf16[128,256]{1,0:T(8,128)(2,1)S(1)} %finish.3.refs_3_), channel_id=1, source_target_pairs={{0,8},{4,12},{8,0},{12,4},{1,9},{5,13},{9,1},{13,5},{2,10},{6,14},... | collective-permute-start | bytes 196616 | tf_op jit(solution)/shard_map/ppermute | solution.py:28
  59.8 5.7 %collective-permute-start.16 = (bf16[128,256]{1,0:T(8,128)(2,1)S(1)}, bf16[128,256]{1,0:T(8,128)(2,1)S(1)}, u32[]{:S(2)}, u32[]{:S(2)}) collective-permute-start(bf16[128,256]{1,0:T(8,128)(2,1)S(1)} %finish.3.refs_3_), channel_id=1, source_target_pairs={{0,12},{4,0},{8,4},{12,8},{1,13},{5,1},{9,5},{13,9},{2,14},{6,2},{... | collective-permute-start | bytes 196616 | tf_op jit(solution)/shard_map/ppermute | solution.py:28
  63.2 2.8 %collective-permute-start.17 = (bf16[128,256]{1,0:T(8,128)(2,1)S(1)}, bf16[128,256]{1,0:T(8,128)(2,1)S(1)}, u32[]{:S(2)}, u32[]{:S(2)}) collective-permute-start(bf16[128,256]{1,0:T(8,128)(2,1)S(1)} %finish.3.refs_3_), channel_id=1, source_target_pairs={{0,1},{1,0},{2,3},{3,2},{4,5},{5,4},{6,7},{7,6},{8,9},{9,8},{10,11... | collective-permute-start | bytes 196616 | tf_op jit(solution)/shard_map/ppermute | solution.py:28
  63.2 2.9 %collective-permute-start.30 = (bf16[128,256]{1,0:T(8,128)(2,1)S(1)}, bf16[128,256]{1,0:T(8,128)(2,1)S(1)}, u32[]{:S(2)}, u32[]{:S(2)}) collective-permute-start(bf16[128,256]{1,0:T(8,128)(2,1)S(1)} %collective-permute-done.26.refs_12_), channel_id=1, source_target_pairs={{0,1},{1,0},{2,3},{3,2},{4,5},{5,4},{6,7},{7,6},{8,9},{9,8},{10,11... | collective-permute-start | bytes 196616 | tf_op jit(solution)/shard_map/ppermute | solution.py:28
  63.7 2.8 %collective-permute-start.31 = (bf16[128,256]{1,0:T(8,128)(2,1)S(1)}, bf16[128,256]{1,0:T(8,128)(2,1)S(1)}, u32[]{:S(2)}, u32[]{:S(2)}) collective-permute-start(bf16[128,256]{1,0:T(8,128)(2,1)S(1)} %collective-permute-done.27.refs_13_), channel_id=1, source_target_pairs={{0,1},{1,0},{2,3},{3,2},{4,5},{5,4},{6,7},{7,6},{8,9},{9,8},{10,11... | collective-permute-start | bytes 196616 | tf_op jit(solution)/shard_map/ppermute | solution.py:28
  65.5 1.3 %collective-permute-start.32 = (bf16[128,256]{1,0:T(8,128)(2,1)S(1)}, bf16[128,256]{1,0:T(8,128)(2,1)S(1)}, u32[]{:S(2)}, u32[]{:S(2)}) collective-permute-start(bf16[128,256]{1,0:T(8,128)(2,1)S(1)} %collective-permute-done.28.refs_14_), channel_id=1, source_target_pairs={{0,1},{1,0},{2,3},{3,2},{4,5},{5,4},{6,7},{7,6},{8,9},{9,8},{10,11... | collective-permute-start | bytes 196616 | tf_op jit(solution)/shard_map/ppermute | solution.py:28
  65.5 1.4 %collective-permute-start.18 = (bf16[128,256]{1,0:T(8,128)(2,1)S(1)}, bf16[128,256]{1,0:T(8,128)(2,1)S(1)}, u32[]{:S(2)}, u32[]{:S(2)}) collective-permute-start(bf16[128,256]{1,0:T(8,128)(2,1)S(1)} %collective-permute-done.14.refs_4_), channel_id=1, source_target_pairs={{0,1},{1,0},{2,3},{3,2},{4,5},{5,4},{6,7},{7,6},{8,9},{9,8},{10,11... | collective-permute-start | bytes 196616 | tf_op jit(solution)/shard_map/ppermute | solution.py:28
  66.0 1.3 %collective-permute-start.19 = (bf16[128,256]{1,0:T(8,128)(2,1)S(1)}, bf16[128,256]{1,0:T(8,128)(2,1)S(1)}, u32[]{:S(2)}, u32[]{:S(2)}) collective-permute-start(bf16[128,256]{1,0:T(8,128)(2,1)S(1)} %collective-permute-done.15.refs_5_), channel_id=1, source_target_pairs={{0,1},{1,0},{2,3},{3,2},{4,5},{5,4},{6,7},{7,6},{8,9},{9,8},{10,11... | collective-permute-start | bytes 196616 | tf_op jit(solution)/shard_map/ppermute | solution.py:28
  66.1 1.3 %collective-permute-start.20 = (bf16[128,256]{1,0:T(8,128)(2,1)S(1)}, bf16[128,256]{1,0:T(8,128)(2,1)S(1)}, u32[]{:S(2)}, u32[]{:S(2)}) collective-permute-start(bf16[128,256]{1,0:T(8,128)(2,1)S(1)} %collective-permute-done.16.refs_6_), channel_id=1, source_target_pairs={{0,1},{1,0},{2,3},{3,2},{4,5},{5,4},{6,7},{7,6},{8,9},{9,8},{10,11... | collective-permute-start | bytes 196616 | tf_op jit(solution)/shard_map/ppermute | solution.py:28
  70.0 2.0 %collective-permute-start.33 = (bf16[512,512]{1,0:T(8,128)(2,1)S(1)}, bf16[512,512]{1,0:T(8,128)(2,1)S(1)}, u32[]{:S(2)}, u32[]{:S(2)}) collective-permute-start(bf16[512,512]{1,0:T(8,128)(2,1)S(1)} %get-tuple-element.46), channel_id=1, source_target_pairs={{0,1},{1,0},{2,3},{3,2},{4,5},{5,4},{6,7},{7,6},{8,9},{9,8},{10,11... | collective-permute-start | bytes 1572872 | tf_op jit(solution)/shard_map/ppermute | solution.py:28
  70.4 5.9 %slice-start = ((s8[8388608]{0:T(1024)(128)(4,1)}), s8[4194304]{0:T(1024)(128)(4,1)S(1)}, s32[]{:S(2)}) async-start(s8[8388608]{0:T(1024)(128)(4,1)} %bitcast.22), calls=%async_computation | async-start | bytes 8388608
  70.4 5.9 %slice-start.1 = ((s8[8388608]{0:T(1024)(128)(4,1)}), s8[4194304]{0:T(1024)(128)(4,1)S(1)}, s32[]{:S(2)}) async-start(s8[8388608]{0:T(1024)(128)(4,1)} %bitcast.22), calls=%async_computation.1 | async-start | bytes 8388608
  72.1 8.8 %collective-permute-start.34 = (bf16[128,512]{1,0:T(8,128)(2,1)S(1)}, bf16[128,512]{1,0:T(8,128)(2,1)S(1)}, u32[]{:S(2)}, u32[]{:S(2)}) collective-permute-start(bf16[128,512]{1,0:T(8,128)(2,1)S(1)} %get-tuple-element.48), channel_id=1, source_target_pairs={{0,4},{4,8},{8,12},{12,0},{1,5},{5,9},{9,13},{13,1},{2,6},{6,10},{... | collective-permute-start | bytes 393224 | tf_op jit(solution)/shard_map/ppermute | solution.py:28
  73.8 11.5 %collective-permute-start.35 = (bf16[128,512]{1,0:T(8,128)(2,1)S(1)}, bf16[128,512]{1,0:T(8,128)(2,1)S(1)}, u32[]{:S(2)}, u32[]{:S(2)}) collective-permute-start(bf16[128,512]{1,0:T(8,128)(2,1)S(1)} %get-tuple-element.49), channel_id=1, source_target_pairs={{0,8},{4,12},{8,0},{12,4},{1,9},{5,13},{9,1},{13,5},{2,10},{6,14},... | collective-permute-start | bytes 393224 | tf_op jit(solution)/shard_map/ppermute | solution.py:28
  76.3 9.1 %collective-permute-start.36 = (bf16[128,512]{1,0:T(8,128)(2,1)S(1)}, bf16[128,512]{1,0:T(8,128)(2,1)S(1)}, u32[]{:S(2)}, u32[]{:S(2)}) collective-permute-start(bf16[128,512]{1,0:T(8,128)(2,1)S(1)} %get-tuple-element.50), channel_id=1, source_target_pairs={{0,12},{4,0},{8,4},{12,8},{1,13},{5,1},{9,5},{13,9},{2,14},{6,2},{... | collective-permute-start | bytes 393224 | tf_op jit(solution)/shard_map/ppermute | solution.py:28

commit v8 on v6

--- a/solution.py
+++ b/solution.py
@@ -165,7 +165,7 @@
 
 def sent_kernel(sizes, lanes, numbers, inputs, results, scratch):
     pieces_by_lanes, ins, outs_by_lanes = inputs
-    send_ref, stacked, *masked = results
+    low_ref, high_ref, stacked, *masked = results
     for here, pieces in zip(lanes, pieces_by_lanes):
         stack(pieces, stacked.at[:, here])
     first_stage(numbers, sizes, stacked, ins, slice(0, BLK), None, None, [*masked, *scratch])
@@ -173,7 +173,9 @@
     for here, outs in zip(lanes, outs_by_lanes):
         for i, part in enumerate(scratch):
             total = second_stage(part, outs, here, None)
-            send_ref[i * size : (i + 1) * size, here] = total.astype(BF16)
+            total, half = total.astype(BF16), size // 2
+            low_ref[i * half : (i + 1) * half, here] = total[:half]
+            high_ref[i * half : (i + 1) * half, here] = total[half:]
 
 
 def kept_kernel(lanes, numbers, inputs, results, scratch):
@@ -376,11 +378,12 @@
     ins = [basis_in] + other_ins
     outs = [[basis_out] + arrays for arrays in other_outs]
     keep_shape, send_shape = split_shapes(BLK)
-    send, stacked, kept = on_chip(
+    half_shape = jax.ShapeDtypeStruct((send_shape.shape[0] // 2, BLK), BF16)
+    low, high, stacked, kept = on_chip(
         functools.partial(sent_kernel, sizes, cuts),
         tables,
         ([gather(field) for field in fields], ins, outs),
-        [send_shape, stacked_shape(every)]
+        [half_shape, half_shape, stacked_shape(every)]
         + [jax.ShapeDtypeStruct((n_tiles * rows, n_rhs * width), BF16)],
         [pltpu.VMEM((n_tiles * rows, n_rhs * width), BF16)] * (n_sub - 1),
         0,
@@ -398,7 +401,15 @@
         "far_kept",
     )
     near, first_result = near_field(rows, [stacked], near_blocks, near_slots, True)
-    second_result = finish(spread_out(reduced(keep, send)), near, jacobi_inverse, every)
+    half = n_tiles * rows // 2
+    parts = []
+    for held, send in ((keep[:half], low), (keep[half:], high)):
+        total = held.astype(F32)
+        for e in range(1, n_sub):
+            here = slice((e - 1) * half, e * half)
+            total += shifted(send[here], "sub", n_sub, e).astype(F32)
+        parts += [total[d * rows : (d + 1) * rows].astype(BF16) for d in range(n_tiles // 2)]
+    second_result = finish(spread_out(parts), near, jacobi_inverse, every)
     return (first_result, second_result)
 
 

time: 87 us -> 87 us (level)
    ppermute x37 -> x38, waiting for transfers between devices: 20.6 us -> 20.3 us  [shifted(): lax.ppermute(value, axis, [(i, (i + amount) % size) for i in range(size)])]
    ppermute x37 -> x38, starting transfers between devices: 40.2 us -> 40.4 us  [shifted(): lax.ppermute(value, axis, [(i, (i + amount) % size) for i in range(size)])]
  transfers between devices with their start and end apart: 37 -> 38, of which waited for: 12 -> 12; matrix products, arithmetic and copies ran while one was open for 3% -> 3% of each run, Pallas kernels for 16% -> 16%
where the time goes in v8:
time: 87 us; the launch traced here: 86.4 us
  starting transfers between devices  40.4 us (46%)
  waiting for transfers between devices  20.3 us (23%)
  Pallas kernels  17.5 us (20%)
  local copies, waits for them, and re-layouts  5.54 us (6%)
  other arithmetic  1.73 us (2%)
    ppermute x38, starting transfers between devices, shifted(): lax.ppermute(value, axis, [(i, (i + amount) % size) for i in range(size)])  40.4 us
    ppermute x38, waiting for transfers between devices, shifted(): lax.ppermute(value, axis, [(i, (i + amount) % size) for i in range(size)])  20.3 us
    pallas_call x9, Pallas kernels, on_chip(): pl.pallas_call(body, out_shape=tuple(out_shapes), in_specs=[in_smem] * n_...  9.15 us
    pallas_call x2, Pallas kernels, near_field(): pl.pallas_call(functools.partial(near_kernel, len(stacks), per_step), out...  8.35 us
    unnamed x14, local copies, waits for them, and re-layouts  4.3 us
  transfers between devices with their start and end apart: 38, of which 12 were waited for; matrix products, arithmetic and copies ran while one was open for 3% of the time, Pallas kernels for 16%

profile of v8, /device:TPU:0, one launch (start us, length us, event | category | flops | bytes accessed | tf_op | source)
XLA Modules:
  0.0 86.4 jit_solution(6751023234588943923)
XLA Ops:
  0.6 3.0 %collective-permute-start.8 = (bf16[768,512]{1,0:T(8,128)(2,1)}, bf16[768,512]{1,0:T(8,128)(2,1)S(1)}, u32[]{:S(2)}, u32[]{:S(2)}) collective-permute-start(bf16[768,512]{1,0:T(8,128)(2,1)} %bitcast.31), channel_id=1, source_target_pairs={{0,2},{2,0},{1,3},{3,1},{4,6},{6,4},{5,7},{7,5},{8,10},{10,8},{9,1... | collective-permute-start | bytes 2359304 | tf_op jit(solution)/shard_map/ppermute | solution.py:28
  3.7 1.6 %collective-permute-start.1 = (bf16[128,512]{1,0:T(8,128)(2,1)}, bf16[128,512]{1,0:T(8,128)(2,1)S(1)}, u32[]{:S(2)}, u32[]{:S(2)}) collective-permute-start(bf16[128,512]{1,0:T(8,128)(2,1)} %refs_2_.1), channel_id=1, source_target_pairs={{0,4},{4,8},{8,12},{12,0},{1,5},{5,9},{9,13},{13,1},{2,6},{6,10},{... | collective-permute-start | bytes 393224 | tf_op jit(solution)/shard_map/ppermute | solution.py:28
  5.2 2.6 %collective-permute-start.2 = (bf16[128,512]{1,0:T(8,128)(2,1)}, bf16[128,512]{1,0:T(8,128)(2,1)S(1)}, u32[]{:S(2)}, u32[]{:S(2)}) collective-permute-start(bf16[128,512]{1,0:T(8,128)(2,1)} %refs_2_.1), channel_id=1, source_target_pairs={{0,8},{4,12},{8,0},{12,4},{1,9},{5,13},{9,1},{13,5},{2,10},{6,14},... | collective-permute-start | bytes 393224 | tf_op jit(solution)/shard_map/ppermute | solution.py:28
  7.8 1.3 %collective-permute-start.3 = (bf16[128,512]{1,0:T(8,128)(2,1)}, bf16[128,512]{1,0:T(8,128)(2,1)S(1)}, u32[]{:S(2)}, u32[]{:S(2)}) collective-permute-start(bf16[128,512]{1,0:T(8,128)(2,1)} %refs_2_.1), channel_id=1, source_target_pairs={{0,12},{4,0},{8,4},{12,8},{1,13},{5,1},{9,5},{13,9},{2,14},{6,2},{... | collective-permute-start | bytes 393224 | tf_op jit(solution)/shard_map/ppermute | solution.py:28
  9.2 1.2 %fusion.5 = (bf16[768,256]{1,0:T(8,128)(2,1)S(1)}, bf16[768,256]{1,0:T(8,128)(2,1)S(1)}) fusion(bf16[768,512]{1,0:T(8,128)(2,1)} %bitcast.25), kind=kLoop, calls=%fused_computation.23 | loop fusion | bytes 1572864 | tf_op jit(solution)/shard_map/slice | solution.py:335
  10.3 1.8 %collective-permute-done.1.refs_3_ = bf16[128,512]{1,0:T(8,128)(2,1)S(1)} collective-permute-done((bf16[128,512]{1,0:T(8,128)(2,1)}, bf16[128,512]{1,0:T(8,128)(2,1)S(1)}, u32[]{:S(2)}, u32[]{:S(2)}) %collective-permute-start.1) | collective-permute-done | bytes 131104 | tf_op jit(solution)/shard_map/ppermute | solution.py:28
  12.2 0.3 collective-permute-start.21
  12.5 0.7 fusion.slot_ref
  13.1 3.3 %collective-permute-done.2.refs_4_ = bf16[128,512]{1,0:T(8,128)(2,1)S(1)} collective-permute-done((bf16[128,512]{1,0:T(8,128)(2,1)}, bf16[128,512]{1,0:T(8,128)(2,1)S(1)}, u32[]{:S(2)}, u32[]{:S(2)}) %collective-permute-start.2) | collective-permute-done | bytes 131104 | tf_op jit(solution)/shard_map/ppermute | solution.py:28
  16.4 0.5 collective-permute-start.6
  17.1 0.7 pad_add_fusion.refs_1_
  17.8 0.6 collective-permute-start
  18.4 1.5 %collective-permute-start.9 = (bf16[768,256]{1,0:T(8,128)(2,1)S(1)}, bf16[768,256]{1,0:T(8,128)(2,1)S(1)}, u32[]{:S(2)}, u32[]{:S(2)}) collective-permute-start(bf16[768,256]{1,0:T(8,128)(2,1)S(1)} %get-tuple-element.31), channel_id=1, source_target_pairs={{0,2},{2,0},{1,3},{3,1},{4,6},{6,4},{5,7},{7,5},{8,10},{10,8},{9,1... | collective-permute-start | bytes 1179656 | tf_op jit(solution)/shard_map/ppermute | solution.py:28
  19.9 0.9 %copy-done.4 = bf16[128,512]{1,0:T(8,128)(2,1)S(1)} copy-done((bf16[128,512]{1,0:T(8,128)(2,1)S(1)}, bf16[128,512]{1,0:T(8,128)(2,1)}, u32[]{:S(2)}) %copy-start.4) | copy-done | bytes 131096
  20.8 2.0 %far_own.1 = (f32[1024,512]{1,0:T(8,128)S(1)}, bf16[1024,512]{1,0:T(8,128)(2,1)S(1)}) custom-call(s32[2]{0:T(128)S(1)} %pad_add_fusion.1.refs_0_, s32[3,12]{1,0:T(4,128)S(1)} %pad_add_fusion.refs_1_, bf16[128,512]{1,0:T(8,128)(2,1)S(1)} %copy-done.4, bf16[128,512]{1,0:T(8,128)(2,1)S(1)} %collective-permute-done.1.refs_3_, ...), custom_call_target="tpu_custom_call" | custom-call | flops 1 | bytes 1 | tf_op jit(solution)/shard_map/far_own/pallas_call | solution.py:45
  22.8 3.4 %copy-done = bf16[1,16,512,512]{3,2,1,0:T(8,128)(2,1)S(1)} copy-done((bf16[1,16,512,512]{3,2,1,0:T(8,128)(2,1)S(1)}, bf16[1,16,512,512]{3,2,1,0:T(8,128)(2,1)}, u32[]{:S(2)}) %copy-start) | copy-done | bytes 8388632
  26.2 3.9 %near_field.2.refs_4_ = f32[128,512]{1,0:T(8,128)S(1)} custom-call(s32[16]{0:T(128)S(1)} %fusion.slot_ref, bf16[1024,512]{1,0:T(8,128)(2,1)S(1)} %get-tuple-element.17.refs_0_.refs_2_, bf16[16,512,512]{2,1,0:T(8,128)(2,1)S(1)} %bitcast.21), custom_call_target="tpu_custom_call" | custom-call | flops 1 | bytes 1 | tf_op jit(solution)/shard_map/near_field/pallas_call | solution.py:228
  30.1 0.6 collective-permute-done.refs_1_.refs_2_
  30.7 1.2 %far_first_stage.1.refs_0_ = bf16[1024,768]{1,0:T(8,128)(2,1)S(1)} custom-call(s32[2]{0:T(128)S(1)} %pad_add_fusion.1.refs_0_, s32[3,12]{1,0:T(4,128)S(1)} %collective-permute-done.refs_1_.refs_2_, bf16[1024,512]{1,0:T(8,128)(2,1)S(1)} %get-tuple-element.17.refs_0_.refs_2_, bf16[768,512]{1,0:T(8,128)(2,1)S(1)} %collective-permute-done.8.refs_3_.refs_20_), custom_call_target="tpu_custom_call" | custom-call | flops 1 | bytes 1 | tf_op jit(solution)/shard_map/far_first_stage/pallas_call | solution.py:45
  31.9 0.6 far_second_stage.3
  32.6 5.7 %collective-permute-done.9.refs_2_.refs_22_ = bf16[768,256]{1,0:T(8,128)(2,1)S(1)} collective-permute-done((bf16[768,256]{1,0:T(8,128)(2,1)S(1)}, bf16[768,256]{1,0:T(8,128)(2,1)S(1)}, u32[]{:S(2)}, u32[]{:S(2)}) %collective-permute-start.9) | collective-permute-done | bytes 393248 | tf_op jit(solution)/shard_map/ppermute | solution.py:28
  38.3 0.6 far_second_stage.2
  39.1 1.9 %collective-permute-start.23 = (bf16[128,256]{1,0:T(8,128)(2,1)S(1)}, bf16[128,256]{1,0:T(8,128)(2,1)S(1)}, u32[]{:S(2)}, u32[]{:S(2)}) collective-permute-start(bf16[128,256]{1,0:T(8,128)(2,1)S(1)} %get-tuple-element.40), channel_id=1, source_target_pairs={{0,4},{4,8},{8,12},{12,0},{1,5},{5,9},{9,13},{13,1},{2,6},{6,10},{... | collective-permute-start | bytes 196616 | tf_op jit(solution)/shard_map/ppermute | solution.py:28
  41.0 2.6 %collective-permute-start.24 = (bf16[128,256]{1,0:T(8,128)(2,1)S(1)}, bf16[128,256]{1,0:T(8,128)(2,1)S(1)}, u32[]{:S(2)}, u32[]{:S(2)}) collective-permute-start(bf16[128,256]{1,0:T(8,128)(2,1)S(1)} %get-tuple-element.39), channel_id=1, source_target_pairs={{0,8},{4,12},{8,0},{12,4},{1,9},{5,13},{9,1},{13,5},{2,10},{6,14},... | collective-permute-start | bytes 196616 | tf_op jit(solution)/shard_map/ppermute | solution.py:28
  43.6 1.3 %collective-permute-start.25 = (bf16[128,256]{1,0:T(8,128)(2,1)S(1)}, bf16[128,256]{1,0:T(8,128)(2,1)S(1)}, u32[]{:S(2)}, u32[]{:S(2)}) collective-permute-start(bf16[128,256]{1,0:T(8,128)(2,1)S(1)} %get-tuple-element.38), channel_id=1, source_target_pairs={{0,12},{4,0},{8,4},{12,8},{1,13},{5,1},{9,5},{13,9},{2,14},{6,2},{... | collective-permute-start | bytes 196616 | tf_op jit(solution)/shard_map/ppermute | solution.py:28
  45.0 0.7 collective-permute-start.11
  45.8 0.3 collective-permute-start.12
  46.1 2.8 %collective-permute-start.13 = (bf16[128,256]{1,0:T(8,128)(2,1)S(1)}, bf16[128,256]{1,0:T(8,128)(2,1)S(1)}, u32[]{:S(2)}, u32[]{:S(2)}) collective-permute-start(bf16[128,256]{1,0:T(8,128)(2,1)S(1)} %get-tuple-element.42), channel_id=1, source_target_pairs={{0,12},{4,0},{8,4},{12,8},{1,13},{5,1},{9,5},{13,9},{2,14},{6,2},{... | collective-permute-start | bytes 196616 | tf_op jit(solution)/shard_map/ppermute | solution.py:28
  49.1 4.5 %collective-permute-start.26 = (bf16[128,256]{1,0:T(8,128)(2,1)S(1)}, bf16[128,256]{1,0:T(8,128)(2,1)S(1)}, u32[]{:S(2)}, u32[]{:S(2)}) collective-permute-start(bf16[128,256]{1,0:T(8,128)(2,1)S(1)} %finish.4.refs_11_), channel_id=1, source_target_pairs={{0,4},{4,8},{8,12},{12,0},{1,5},{5,9},{9,13},{13,1},{2,6},{6,10},{... | collective-permute-start | bytes 196616 | tf_op jit(solution)/shard_map/ppermute | solution.py:28
  53.6 2.4 %collective-permute-start.28 = (bf16[128,256]{1,0:T(8,128)(2,1)S(1)}, bf16[128,256]{1,0:T(8,128)(2,1)S(1)}, u32[]{:S(2)}, u32[]{:S(2)}) collective-permute-start(bf16[128,256]{1,0:T(8,128)(2,1)S(1)} %finish.4.refs_11_), channel_id=1, source_target_pairs={{0,12},{4,0},{8,4},{12,8},{1,13},{5,1},{9,5},{13,9},{2,14},{6,2},{... | collective-permute-start | bytes 196616 | tf_op jit(solution)/shard_map/ppermute | solution.py:28
  56.3 2.4 %collective-permute-start.14 = (bf16[128,256]{1,0:T(8,128)(2,1)S(1)}, bf16[128,256]{1,0:T(8,128)(2,1)S(1)}, u32[]{:S(2)}, u32[]{:S(2)}) collective-permute-start(bf16[128,256]{1,0:T(8,128)(2,1)S(1)} %finish.3.refs_3_), channel_id=1, source_target_pairs={{0,4},{4,8},{8,12},{12,0},{1,5},{5,9},{9,13},{13,1},{2,6},{6,10},{... | collective-permute-start | bytes 196616 | tf_op jit(solution)/shard_map/ppermute | solution.py:28
  58.8 1.2 %collective-permute-done.27.refs_13_ = bf16[128,256]{1,0:T(8,128)(2,1)S(1)} collective-permute-done((bf16[128,256]{1,0:T(8,128)(2,1)S(1)}, bf16[128,256]{1,0:T(8,128)(2,1)S(1)}, u32[]{:S(2)}, u32[]{:S(2)}) %collective-permute-start.27) | collective-permute-done | bytes 65568 | tf_op jit(solution)/shard_map/ppermute | solution.py:28
  60.0 3.2 %collective-permute-start.16 = (bf16[128,256]{1,0:T(8,128)(2,1)S(1)}, bf16[128,256]{1,0:T(8,128)(2,1)S(1)}, u32[]{:S(2)}, u32[]{:S(2)}) collective-permute-start(bf16[128,256]{1,0:T(8,128)(2,1)S(1)} %finish.3.refs_3_), channel_id=1, source_target_pairs={{0,12},{4,0},{8,4},{12,8},{1,13},{5,1},{9,5},{13,9},{2,14},{6,2},{... | collective-permute-start | bytes 196616 | tf_op jit(solution)/shard_map/ppermute | solution.py:28
  63.2 0.5 collective-permute-start.30
  63.8 1.8 %collective-permute-done.15.refs_5_ = bf16[128,256]{1,0:T(8,128)(2,1)S(1)} collective-permute-done((bf16[128,256]{1,0:T(8,128)(2,1)S(1)}, bf16[128,256]{1,0:T(8,128)(2,1)S(1)}, u32[]{:S(2)}, u32[]{:S(2)}) %collective-permute-start.15) | collective-permute-done | bytes 65568 | tf_op jit(solution)/shard_map/ppermute | solution.py:28
  65.6 0.5 collective-permute-start.18
  66.1 0.4 collective-permute-start.20
  66.6 0.2 collective-permute-done.32.refs_18_
  67.0 0.4 collective-permute-done.19.refs_9_
  67.5 2.5 %far_sent.1 = (bf16[256,512]{1,0:T(8,128)(2,1)S(1)}, bf16[256,512]{1,0:T(8,128)(2,1)S(1)}, bf16[1024,512]{1,0:T(8,128)(2,1)S(1)}, bf16[512,1536]{1,0:T(8,128)(2,1)S(1)}) custom-call(s32[2]{0:T(128)S(1)} %pad_add_fusion.1.refs_0_, s32[3,12]{1,0:T(4,128)S(1)} %pad_add_fusion.refs_1_, s32[3,12]{1,0:T(4,128)S(1)} %collective-permute-done.refs_1_.refs_2_, ...), custom_call_target="tpu_custom_call" | custom-call | flops 1 | bytes 1 | tf_op jit(solution)/shard_map/far_sent/pallas_call | solution.py:45
  70.0 0.4 collective-permute-start.33
  70.6 1.0 %far_kept.1 = bf16[512,512]{1,0:T(8,128)(2,1)S(1)} custom-call(bf16[512,1536]{1,0:T(8,128)(2,1)S(1)} %get-tuple-element.26.refs_0_, bf16[768,512]{1,0:T(8,128)(2,1)S(1)} %bitcast.29, bf16[768,256]{1,0:T(8,128)(2,1)S(1)} %collective-permute-done.9.refs_2_.refs_22_, bf16[768,512]{1,0:T(8,128)(2,1)S(1)} %bitcast.30, ...), custom_call_target="tpu_custom_call" | custom-call | flops 10000000000 | bytes 1 | tf_op jit(solution)/shard_map/far_kept/pallas_call | solution.py:45
  71.6 0.4 collective-permute-done.35
  72.2 1.8 %collective-permute-start.34 = (bf16[128,512]{1,0:T(8,128)(2,1)S(1)}, bf16[128,512]{1,0:T(8,128)(2,1)S(1)}, u32[]{:S(2)}, u32[]{:S(2)}) collective-permute-start(bf16[128,512]{1,0:T(8,128)(2,1)S(1)} %get-tuple-element.36), channel_id=1, source_target_pairs={{0,4},{4,8},{8,12},{12,0},{1,5},{5,9},{9,13},{13,1},{2,6},{6,10},{... | collective-permute-start | bytes 393224 | tf_op jit(solution)/shard_map/ppermute | solution.py:28
  73.9 2.5 %collective-permute-start.36 = (bf16[128,512]{1,0:T(8,128)(2,1)S(1)}, bf16[128,512]{1,0:T(8,128)(2,1)S(1)}, u32[]{:S(2)}, u32[]{:S(2)}) collective-permute-start(bf16[128,512]{1,0:T(8,128)(2,1)S(1)} %get-tuple-element.35), channel_id=1, source_target_pairs={{0,8},{4,12},{8,0},{12,4},{1,9},{5,13},{9,1},{13,5},{2,10},{6,14},... | collective-permute-start | bytes 393224 | tf_op jit(solution)/shard_map/ppermute | solution.py:28
  76.5 4.5 %near_field.3 = (f32[128,512]{1,0:T(8,128)S(1)}, bf16[128,512]{1,0:T(8,128)(2,1)}) custom-call(s32[16]{0:T(128)S(1)} %fusion.slot_ref, bf16[1024,512]{1,0:T(8,128)(2,1)S(1)} %get-tuple-element.24.refs_0_, bf16[16,512,512]{2,1,0:T(8,128)(2,1)S(1)} %bitcast.24), custom_call_target="tpu_custom_call" | custom-call | flops 1 | bytes 1 | tf_op jit(solution)/shard_map/near_field/pallas_call | solution.py:228
  81.0 4.5 %collective-permute-done.36.refs_2_ = bf16[128,512]{1,0:T(8,128)(2,1)S(1)} collective-permute-done((bf16[128,512]{1,0:T(8,128)(2,1)S(1)}, bf16[128,512]{1,0:T(8,128)(2,1)S(1)}, u32[]{:S(2)}, u32[]{:S(2)}) %collective-permute-start.36) | collective-permute-done | bytes 131104 | tf_op jit(solution)/shard_map/ppermute | solution.py:28
  85.5 0.9 %finish.5 = bf16[128,512]{1,0:T(8,128)(2,1)} custom-call(bf16[128,512]{1,0:T(8,128)(2,1)S(1)} %get-tuple-element.37.refs_0_, bf16[128,512]{1,0:T(8,128)(2,1)S(1)} %collective-permute-done.34.refs_1_, bf16[128,512]{1,0:T(8,128)(2,1)S(1)} %collective-permute-done.36.refs_2_, bf16[128,512]{1,0:T(8,128)(2,1)S(1)} %collective-permute-done.37.refs_3_, ...), custom_call_target="tpu_custom_call" | custom-call | flops 1 | bytes 1 | tf_op jit(solution)/shard_map/finish/pallas_call | solution.py:45
  (65 shorter events, 1.9 us)
Async XLA Ops:
  0.6 19.3 %copy-start.2 = (bf16[12,64,512]{2,1,0:T(8,128)(2,1)S(1)}, bf16[12,64,512]{2,1,0:T(8,128)(2,1)}, u32[]{:S(2)}) copy-start(bf16[12,64,512]{2,1,0:T(8,128)(2,1)} %param.11) | copy-start | bytes 2359300
  0.6 19.3 %copy-start.1 = (bf16[12,64,512]{2,1,0:T(8,128)(2,1)S(1)}, bf16[12,64,512]{2,1,0:T(8,128)(2,1)}, u32[]{:S(2)}) copy-start(bf16[12,64,512]{2,1,0:T(8,128)(2,1)} %param.10) | copy-start | bytes 2359300
  0.6 30.1 %collective-permute-start.8 = (bf16[768,512]{1,0:T(8,128)(2,1)}, bf16[768,512]{1,0:T(8,128)(2,1)S(1)}, u32[]{:S(2)}, u32[]{:S(2)}) collective-permute-start(bf16[768,512]{1,0:T(8,128)(2,1)} %bitcast.31), channel_id=1, source_target_pairs={{0,2},{2,0},{1,3},{3,1},{4,6},{6,4},{5,7},{7,5},{8,10},{10,8},{9,1... | collective-permute-start | bytes 2359304 | tf_op jit(solution)/shard_map/ppermute | solution.py:28
  3.7 8.5 %collective-permute-start.1 = (bf16[128,512]{1,0:T(8,128)(2,1)}, bf16[128,512]{1,0:T(8,128)(2,1)S(1)}, u32[]{:S(2)}, u32[]{:S(2)}) collective-permute-start(bf16[128,512]{1,0:T(8,128)(2,1)} %refs_2_.1), channel_id=1, source_target_pairs={{0,4},{4,8},{8,12},{12,0},{1,5},{5,9},{9,13},{13,1},{2,6},{6,10},{... | collective-permute-start | bytes 393224 | tf_op jit(solution)/shard_map/ppermute | solution.py:28
  5.2 11.2 %collective-permute-start.2 = (bf16[128,512]{1,0:T(8,128)(2,1)}, bf16[128,512]{1,0:T(8,128)(2,1)S(1)}, u32[]{:S(2)}, u32[]{:S(2)}) collective-permute-start(bf16[128,512]{1,0:T(8,128)(2,1)} %refs_2_.1), channel_id=1, source_target_pairs={{0,8},{4,12},{8,0},{12,4},{1,9},{5,13},{9,1},{13,5},{2,10},{6,14},... | collective-permute-start | bytes 393224 | tf_op jit(solution)/shard_map/ppermute | solution.py:28
  7.8 8.6 %collective-permute-start.3 = (bf16[128,512]{1,0:T(8,128)(2,1)}, bf16[128,512]{1,0:T(8,128)(2,1)S(1)}, u32[]{:S(2)}, u32[]{:S(2)}) collective-permute-start(bf16[128,512]{1,0:T(8,128)(2,1)} %refs_2_.1), channel_id=1, source_target_pairs={{0,12},{4,0},{8,4},{12,8},{1,13},{5,1},{9,5},{13,9},{2,14},{6,2},{... | collective-permute-start | bytes 393224 | tf_op jit(solution)/shard_map/ppermute | solution.py:28
  9.2 7.8 %collective-permute-start.4 = (bf16[128,512]{1,0:T(8,128)(2,1)}, bf16[128,512]{1,0:T(8,128)(2,1)S(1)}, u32[]{:S(2)}, u32[]{:S(2)}) collective-permute-start(bf16[128,512]{1,0:T(8,128)(2,1)} %refs_2_.1), channel_id=1, source_target_pairs={{0,1},{1,0},{2,3},{3,2},{4,5},{5,4},{6,7},{7,6},{8,9},{9,8},{10,11... | collective-permute-start | bytes 393224 | tf_op jit(solution)/shard_map/ppermute | solution.py:28
  12.2 19.8 %collective-permute-start.21 = (bf16[768,256]{1,0:T(8,128)(2,1)S(1)}, bf16[768,256]{1,0:T(8,128)(2,1)S(1)}, u32[]{:S(2)}, u32[]{:S(2)}) collective-permute-start(bf16[768,256]{1,0:T(8,128)(2,1)S(1)} %get-tuple-element.30), channel_id=1, source_target_pairs={{0,2},{2,0},{1,3},{3,1},{4,6},{6,4},{5,7},{7,5},{8,10},{10,8},{9,1... | collective-permute-start | bytes 1179656 | tf_op jit(solution)/shard_map/ppermute | solution.py:28
  16.4 1.4 %collective-permute-start.5 = (bf16[128,512]{1,0:T(8,128)(2,1)S(1)}, bf16[128,512]{1,0:T(8,128)(2,1)S(1)}, u32[]{:S(2)}, u32[]{:S(2)}) collective-permute-start(bf16[128,512]{1,0:T(8,128)(2,1)S(1)} %collective-permute-done.1.refs_3_), channel_id=1, source_target_pairs={{0,1},{1,0},{2,3},{3,2},{4,5},{5,4},{6,7},{7,6},{8,9},{9,8},{10,11... | collective-permute-start | bytes 393224 | tf_op jit(solution)/shard_map/ppermute | solution.py:28
  16.4 1.9 %collective-permute-start.6 = (bf16[128,512]{1,0:T(8,128)(2,1)S(1)}, bf16[128,512]{1,0:T(8,128)(2,1)S(1)}, u32[]{:S(2)}, u32[]{:S(2)}) collective-permute-start(bf16[128,512]{1,0:T(8,128)(2,1)S(1)} %collective-permute-done.2.refs_4_), channel_id=1, source_target_pairs={{0,1},{1,0},{2,3},{3,2},{4,5},{5,4},{6,7},{7,6},{8,9},{9,8},{10,11... | collective-permute-start | bytes 393224 | tf_op jit(solution)/shard_map/ppermute | solution.py:28
  17.0 2.9 %collective-permute-start.7 = (bf16[128,512]{1,0:T(8,128)(2,1)S(1)}, bf16[128,512]{1,0:T(8,128)(2,1)S(1)}, u32[]{:S(2)}, u32[]{:S(2)}) collective-permute-start(bf16[128,512]{1,0:T(8,128)(2,1)S(1)} %collective-permute-done.3.refs_5_), channel_id=1, source_target_pairs={{0,1},{1,0},{2,3},{3,2},{4,5},{5,4},{6,7},{7,6},{8,9},{9,8},{10,11... | collective-permute-start | bytes 393224 | tf_op jit(solution)/shard_map/ppermute | solution.py:28
  17.8 12.9 %collective-permute-start = (s32[3,12]{1,0:T(4,128)S(1)}, s32[3,12]{1,0:T(4,128)S(1)}, u32[]{:S(2)}, u32[]{:S(2)}) collective-permute-start(s32[3,12]{1,0:T(4,128)S(1)} %pad_add_fusion.refs_1_), channel_id=1, source_target_pairs={{0,2},{2,0},{1,3},{3,1},{4,6},{6,4},{5,7},{7,5},{8,10},{10,8},{9,1... | collective-permute-start | bytes 440 | tf_op jit(solution)/shard_map/ppermute | solution.py:28
  18.4 19.9 %collective-permute-start.9 = (bf16[768,256]{1,0:T(8,128)(2,1)S(1)}, bf16[768,256]{1,0:T(8,128)(2,1)S(1)}, u32[]{:S(2)}, u32[]{:S(2)}) collective-permute-start(bf16[768,256]{1,0:T(8,128)(2,1)S(1)} %get-tuple-element.31), channel_id=1, source_target_pairs={{0,2},{2,0},{1,3},{3,1},{4,6},{6,4},{5,7},{7,5},{8,10},{10,8},{9,1... | collective-permute-start | bytes 1179656 | tf_op jit(solution)/shard_map/ppermute | solution.py:28
  19.9 0.9 %copy-start.4 = (bf16[128,512]{1,0:T(8,128)(2,1)S(1)}, bf16[128,512]{1,0:T(8,128)(2,1)}, u32[]{:S(2)}) copy-start(bf16[128,512]{1,0:T(8,128)(2,1)} %refs_2_.1) | copy-start | bytes 393220
  22.8 3.4 %copy-start = (bf16[1,16,512,512]{3,2,1,0:T(8,128)(2,1)S(1)}, bf16[1,16,512,512]{3,2,1,0:T(8,128)(2,1)}, u32[]{:S(2)}) copy-start(bf16[1,16,512,512]{3,2,1,0:T(8,128)(2,1)} %param.15) | copy-start | bytes 25165828
  32.5 6.4 %collective-permute-start.22 = (bf16[512,256]{1,0:T(8,128)(2,1)S(1)}, bf16[512,256]{1,0:T(8,128)(2,1)S(1)}, u32[]{:S(2)}, u32[]{:S(2)}) collective-permute-start(bf16[512,256]{1,0:T(8,128)(2,1)S(1)} %get-tuple-element.23), channel_id=1, source_target_pairs={{0,1},{1,0},{2,3},{3,2},{4,5},{5,4},{6,7},{7,6},{8,9},{9,8},{10,11... | collective-permute-start | bytes 786440 | tf_op jit(solution)/shard_map/ppermute | solution.py:28
  38.9 10.0 %copy-start.3 = (bf16[4,128,128]{2,1,0:T(8,128)(2,1)S(1)}, bf16[4,128,128]{2,1,0:T(8,128)(2,1)}, u32[]{:S(2)}) copy-start(bf16[4,128,128]{2,1,0:T(8,128)(2,1)} %refs_5_.5) | copy-start | bytes 393220
  38.9 6.0 %collective-permute-start.10 = (bf16[512,256]{1,0:T(8,128)(2,1)S(1)}, bf16[512,256]{1,0:T(8,128)(2,1)S(1)}, u32[]{:S(2)}, u32[]{:S(2)}) collective-permute-start(bf16[512,256]{1,0:T(8,128)(2,1)S(1)} %get-tuple-element.20), channel_id=1, source_target_pairs={{0,1},{1,0},{2,3},{3,2},{4,5},{5,4},{6,7},{7,6},{8,9},{9,8},{10,11... | collective-permute-start | bytes 786440 | tf_op jit(solution)/shard_map/ppermute | solution.py:28
  39.1 7.0 %collective-permute-start.23 = (bf16[128,256]{1,0:T(8,128)(2,1)S(1)}, bf16[128,256]{1,0:T(8,128)(2,1)S(1)}, u32[]{:S(2)}, u32[]{:S(2)}) collective-permute-start(bf16[128,256]{1,0:T(8,128)(2,1)S(1)} %get-tuple-element.40), channel_id=1, source_target_pairs={{0,4},{4,8},{8,12},{12,0},{1,5},{5,9},{9,13},{13,1},{2,6},{6,10},{... | collective-permute-start | bytes 196616 | tf_op jit(solution)/shard_map/ppermute | solution.py:28
  41.0 7.9 %collective-permute-start.24 = (bf16[128,256]{1,0:T(8,128)(2,1)S(1)}, bf16[128,256]{1,0:T(8,128)(2,1)S(1)}, u32[]{:S(2)}, u32[]{:S(2)}) collective-permute-start(bf16[128,256]{1,0:T(8,128)(2,1)S(1)} %get-tuple-element.39), channel_id=1, source_target_pairs={{0,8},{4,12},{8,0},{12,4},{1,9},{5,13},{9,1},{13,5},{2,10},{6,14},... | collective-permute-start | bytes 196616 | tf_op jit(solution)/shard_map/ppermute | solution.py:28
  43.6 5.3 %collective-permute-start.25 = (bf16[128,256]{1,0:T(8,128)(2,1)S(1)}, bf16[128,256]{1,0:T(8,128)(2,1)S(1)}, u32[]{:S(2)}, u32[]{:S(2)}) collective-permute-start(bf16[128,256]{1,0:T(8,128)(2,1)S(1)} %get-tuple-element.38), channel_id=1, source_target_pairs={{0,12},{4,0},{8,4},{12,8},{1,13},{5,1},{9,5},{13,9},{2,14},{6,2},{... | collective-permute-start | bytes 196616 | tf_op jit(solution)/shard_map/ppermute | solution.py:28
  45.0 8.6 %collective-permute-start.11 = (bf16[128,256]{1,0:T(8,128)(2,1)S(1)}, bf16[128,256]{1,0:T(8,128)(2,1)S(1)}, u32[]{:S(2)}, u32[]{:S(2)}) collective-permute-start(bf16[128,256]{1,0:T(8,128)(2,1)S(1)} %get-tuple-element.44), channel_id=1, source_target_pairs={{0,4},{4,8},{8,12},{12,0},{1,5},{5,9},{9,13},{13,1},{2,6},{6,10},{... | collective-permute-start | bytes 196616 | tf_op jit(solution)/shard_map/ppermute | solution.py:28
  45.8 10.3 %collective-permute-start.12 = (bf16[128,256]{1,0:T(8,128)(2,1)S(1)}, bf16[128,256]{1,0:T(8,128)(2,1)S(1)}, u32[]{:S(2)}, u32[]{:S(2)}) collective-permute-start(bf16[128,256]{1,0:T(8,128)(2,1)S(1)} %get-tuple-element.43), channel_id=1, source_target_pairs={{0,8},{4,12},{8,0},{12,4},{1,9},{5,13},{9,1},{13,5},{2,10},{6,14},... | collective-permute-start | bytes 196616 | tf_op jit(solution)/shard_map/ppermute | solution.py:28
  46.1 10.0 %collective-permute-start.13 = (bf16[128,256]{1,0:T(8,128)(2,1)S(1)}, bf16[128,256]{1,0:T(8,128)(2,1)S(1)}, u32[]{:S(2)}, u32[]{:S(2)}) collective-permute-start(bf16[128,256]{1,0:T(8,128)(2,1)S(1)} %get-tuple-element.42), channel_id=1, source_target_pairs={{0,12},{4,0},{8,4},{12,8},{1,13},{5,1},{9,5},{13,9},{2,14},{6,2},{... | collective-permute-start | bytes 196616 | tf_op jit(solution)/shard_map/ppermute | solution.py:28
  49.1 9.6 %collective-permute-start.26 = (bf16[128,256]{1,0:T(8,128)(2,1)S(1)}, bf16[128,256]{1,0:T(8,128)(2,1)S(1)}, u32[]{:S(2)}, u32[]{:S(2)}) collective-permute-start(bf16[128,256]{1,0:T(8,128)(2,1)S(1)} %finish.4.refs_11_), channel_id=1, source_target_pairs={{0,4},{4,8},{8,12},{12,0},{1,5},{5,9},{9,13},{13,1},{2,6},{6,10},{... | collective-permute-start | bytes 196616 | tf_op jit(solution)/shard_map/ppermute | solution.py:28
  53.6 6.4 %collective-permute-start.27 = (bf16[128,256]{1,0:T(8,128)(2,1)S(1)}, bf16[128,256]{1,0:T(8,128)(2,1)S(1)}, u32[]{:S(2)}, u32[]{:S(2)}) collective-permute-start(bf16[128,256]{1,0:T(8,128)(2,1)S(1)} %finish.4.refs_11_), channel_id=1, source_target_pairs={{0,8},{4,12},{8,0},{12,4},{1,9},{5,13},{9,1},{13,5},{2,10},{6,14},... | collective-permute-start | bytes 196616 | tf_op jit(solution)/shard_map/ppermute | solution.py:28
  53.6 9.6 %collective-permute-start.28 = (bf16[128,256]{1,0:T(8,128)(2,1)S(1)}, bf16[128,256]{1,0:T(8,128)(2,1)S(1)}, u32[]{:S(2)}, u32[]{:S(2)}) collective-permute-start(bf16[128,256]{1,0:T(8,128)(2,1)S(1)} %finish.4.refs_11_), channel_id=1, source_target_pairs={{0,12},{4,0},{8,4},{12,8},{1,13},{5,1},{9,5},{13,9},{2,14},{6,2},{... | collective-permute-start | bytes 196616 | tf_op jit(solution)/shard_map/ppermute | solution.py:28
  56.1 7.1 %collective-permute-start.29 = (bf16[128,256]{1,0:T(8,128)(2,1)S(1)}, bf16[128,256]{1,0:T(8,128)(2,1)S(1)}, u32[]{:S(2)}, u32[]{:S(2)}) collective-permute-start(bf16[128,256]{1,0:T(8,128)(2,1)S(1)} %finish.4.refs_11_), channel_id=1, source_target_pairs={{0,1},{1,0},{2,3},{3,2},{4,5},{5,4},{6,7},{7,6},{8,9},{9,8},{10,11... | collective-permute-start | bytes 196616 | tf_op jit(solution)/shard_map/ppermute | solution.py:28
  56.3 7.4 %collective-permute-start.14 = (bf16[128,256]{1,0:T(8,128)(2,1)S(1)}, bf16[128,256]{1,0:T(8,128)(2,1)S(1)}, u32[]{:S(2)}, u32[]{:S(2)}) collective-permute-start(bf16[128,256]{1,0:T(8,128)(2,1)S(1)} %finish.3.refs_3_), channel_id=1, source_target_pairs={{0,4},{4,8},{8,12},{12,0},{1,5},{5,9},{9,13},{13,1},{2,6},{6,10},{... | collective-permute-start | bytes 196616 | tf_op jit(solution)/shard_map/ppermute | solution.py:28
  58.7 6.8 %collective-permute-start.15 = (bf16[128,256]{1,0:T(8,128)(2,1)S(1)}, bf16[128,256]{1,0:T(8,128)(2,1)S(1)}, u32[]{:S(2)}, u32[]{:S(2)}) collective-permute-start(bf16[128,256]{1,0:T(8,128)(2,1)S(1)} %finish.3.refs_3_), channel_id=1, source_target_pairs={{0,8},{4,12},{8,0},{12,4},{1,9},{5,13},{9,1},{13,5},{2,10},{6,14},... | collective-permute-start | bytes 196616 | tf_op jit(solution)/shard_map/ppermute | solution.py:28
  60.0 5.6 %collective-permute-start.16 = (bf16[128,256]{1,0:T(8,128)(2,1)S(1)}, bf16[128,256]{1,0:T(8,128)(2,1)S(1)}, u32[]{:S(2)}, u32[]{:S(2)}) collective-permute-start(bf16[128,256]{1,0:T(8,128)(2,1)S(1)} %finish.3.refs_3_), channel_id=1, source_target_pairs={{0,12},{4,0},{8,4},{12,8},{1,13},{5,1},{9,5},{13,9},{2,14},{6,2},{... | collective-permute-start | bytes 196616 | tf_op jit(solution)/shard_map/ppermute | solution.py:28
  63.2 2.9 %collective-permute-start.17 = (bf16[128,256]{1,0:T(8,128)(2,1)S(1)}, bf16[128,256]{1,0:T(8,128)(2,1)S(1)}, u32[]{:S(2)}, u32[]{:S(2)}) collective-permute-start(bf16[128,256]{1,0:T(8,128)(2,1)S(1)} %finish.3.refs_3_), channel_id=1, source_target_pairs={{0,1},{1,0},{2,3},{3,2},{4,5},{5,4},{6,7},{7,6},{8,9},{9,8},{10,11... | collective-permute-start | bytes 196616 | tf_op jit(solution)/shard_map/ppermute | solution.py:28
  63.2 2.9 %collective-permute-start.30 = (bf16[128,256]{1,0:T(8,128)(2,1)S(1)}, bf16[128,256]{1,0:T(8,128)(2,1)S(1)}, u32[]{:S(2)}, u32[]{:S(2)}) collective-permute-start(bf16[128,256]{1,0:T(8,128)(2,1)S(1)} %collective-permute-done.26.refs_12_), channel_id=1, source_target_pairs={{0,1},{1,0},{2,3},{3,2},{4,5},{5,4},{6,7},{7,6},{8,9},{9,8},{10,11... | collective-permute-start | bytes 196616 | tf_op jit(solution)/shard_map/ppermute | solution.py:28
  63.7 2.9 %collective-permute-start.31 = (bf16[128,256]{1,0:T(8,128)(2,1)S(1)}, bf16[128,256]{1,0:T(8,128)(2,1)S(1)}, u32[]{:S(2)}, u32[]{:S(2)}) collective-permute-start(bf16[128,256]{1,0:T(8,128)(2,1)S(1)} %collective-permute-done.27.refs_13_), channel_id=1, source_target_pairs={{0,1},{1,0},{2,3},{3,2},{4,5},{5,4},{6,7},{7,6},{8,9},{9,8},{10,11... | collective-permute-start | bytes 196616 | tf_op jit(solution)/shard_map/ppermute | solution.py:28
  65.5 1.3 %collective-permute-start.32 = (bf16[128,256]{1,0:T(8,128)(2,1)S(1)}, bf16[128,256]{1,0:T(8,128)(2,1)S(1)}, u32[]{:S(2)}, u32[]{:S(2)}) collective-permute-start(bf16[128,256]{1,0:T(8,128)(2,1)S(1)} %collective-permute-done.28.refs_14_), channel_id=1, source_target_pairs={{0,1},{1,0},{2,3},{3,2},{4,5},{5,4},{6,7},{7,6},{8,9},{9,8},{10,11... | collective-permute-start | bytes 196616 | tf_op jit(solution)/shard_map/ppermute | solution.py:28
  65.6 1.4 %collective-permute-start.18 = (bf16[128,256]{1,0:T(8,128)(2,1)S(1)}, bf16[128,256]{1,0:T(8,128)(2,1)S(1)}, u32[]{:S(2)}, u32[]{:S(2)}) collective-permute-start(bf16[128,256]{1,0:T(8,128)(2,1)S(1)} %collective-permute-done.14.refs_4_), channel_id=1, source_target_pairs={{0,1},{1,0},{2,3},{3,2},{4,5},{5,4},{6,7},{7,6},{8,9},{9,8},{10,11... | collective-permute-start | bytes 196616 | tf_op jit(solution)/shard_map/ppermute | solution.py:28
  66.1 1.3 %collective-permute-start.19 = (bf16[128,256]{1,0:T(8,128)(2,1)S(1)}, bf16[128,256]{1,0:T(8,128)(2,1)S(1)}, u32[]{:S(2)}, u32[]{:S(2)}) collective-permute-start(bf16[128,256]{1,0:T(8,128)(2,1)S(1)} %collective-permute-done.15.refs_5_), channel_id=1, source_target_pairs={{0,1},{1,0},{2,3},{3,2},{4,5},{5,4},{6,7},{7,6},{8,9},{9,8},{10,11... | collective-permute-start | bytes 196616 | tf_op jit(solution)/shard_map/ppermute | solution.py:28
  66.1 1.3 %collective-permute-start.20 = (bf16[128,256]{1,0:T(8,128)(2,1)S(1)}, bf16[128,256]{1,0:T(8,128)(2,1)S(1)}, u32[]{:S(2)}, u32[]{:S(2)}) collective-permute-start(bf16[128,256]{1,0:T(8,128)(2,1)S(1)} %collective-permute-done.16.refs_6_), channel_id=1, source_target_pairs={{0,1},{1,0},{2,3},{3,2},{4,5},{5,4},{6,7},{7,6},{8,9},{9,8},{10,11... | collective-permute-start | bytes 196616 | tf_op jit(solution)/shard_map/ppermute | solution.py:28
  70.0 1.6 %collective-permute-start.33 = (bf16[256,512]{1,0:T(8,128)(2,1)S(1)}, bf16[256,512]{1,0:T(8,128)(2,1)S(1)}, u32[]{:S(2)}, u32[]{:S(2)}) collective-permute-start(bf16[256,512]{1,0:T(8,128)(2,1)S(1)} %get-tuple-element.27), channel_id=1, source_target_pairs={{0,1},{1,0},{2,3},{3,2},{4,5},{5,4},{6,7},{7,6},{8,9},{9,8},{10,11... | collective-permute-start | bytes 786440 | tf_op jit(solution)/shard_map/ppermute | solution.py:28
  70.4 1.6 %collective-permute-start.35 = (bf16[256,512]{1,0:T(8,128)(2,1)S(1)}, bf16[256,512]{1,0:T(8,128)(2,1)S(1)}, u32[]{:S(2)}, u32[]{:S(2)}) collective-permute-start(bf16[256,512]{1,0:T(8,128)(2,1)S(1)} %get-tuple-element.28), channel_id=1, source_target_pairs={{0,1},{1,0},{2,3},{3,2},{4,5},{5,4},{6,7},{7,6},{8,9},{9,8},{10,11... | collective-permute-start | bytes 786440 | tf_op jit(solution)/shard_map/ppermute | solution.py:28
  70.6 5.8 %slice-start = ((s8[8388608]{0:T(1024)(128)(4,1)}), s8[4194304]{0:T(1024)(128)(4,1)S(1)}, s32[]{:S(2)}) async-start(s8[8388608]{0:T(1024)(128)(4,1)} %bitcast.22), calls=%async_computation | async-start | bytes 8388608
  70.6 5.8 %slice-start.1 = ((s8[8388608]{0:T(1024)(128)(4,1)}), s8[4194304]{0:T(1024)(128)(4,1)S(1)}, s32[]{:S(2)}) async-start(s8[8388608]{0:T(1024)(128)(4,1)} %bitcast.22), calls=%async_computation.1 | async-start | bytes 8388608
  72.2 8.8 %collective-permute-start.34 = (bf16[128,512]{1,0:T(8,128)(2,1)S(1)}, bf16[128,512]{1,0:T(8,128)(2,1)S(1)}, u32[]{:S(2)}, u32[]{:S(2)}) collective-permute-start(bf16[128,512]{1,0:T(8,128)(2,1)S(1)} %get-tuple-element.36), channel_id=1, source_target_pairs={{0,4},{4,8},{8,12},{12,0},{1,5},{5,9},{9,13},{13,1},{2,6},{6,10},{... | collective-permute-start | bytes 393224 | tf_op jit(solution)/shard_map/ppermute | solution.py:28
  73.9 11.5 %collective-permute-start.36 = (bf16[128,512]{1,0:T(8,128)(2,1)S(1)}, bf16[128,512]{1,0:T(8,128)(2,1)S(1)}, u32[]{:S(2)}, u32[]{:S(2)}) collective-permute-start(bf16[128,512]{1,0:T(8,128)(2,1)S(1)} %get-tuple-element.35), channel_id=1, source_target_pairs={{0,8},{4,12},{8,0},{12,4},{1,9},{5,13},{9,1},{13,5},{2,10},{6,14},... | collective-permute-start | bytes 393224 | tf_op jit(solution)/shard_map/ppermute | solution.py:28
  76.4 9.1 %collective-permute-start.37 = (bf16[128,512]{1,0:T(8,128)(2,1)S(1)}, bf16[128,512]{1,0:T(8,128)(2,1)S(1)}, u32[]{:S(2)}, u32[]{:S(2)}) collective-permute-start(bf16[128,512]{1,0:T(8,128)(2,1)S(1)} %get-tuple-element.34), channel_id=1, source_target_pairs={{0,12},{4,0},{8,4},{12,8},{1,13},{5,1},{9,5},{13,9},{2,14},{6,2},{... | collective-permute-start | bytes 393224 | tf_op jit(solution)/shard_map/ppermute | solution.py:28
